TPU v7x, 32 devices: a whole 2x2x4 slice. The times are simulated.
32 devices in a mesh: seq: 4 (over y, x), batch: 8 (over z, core).
Axes of the slice: x: 2, y: 2, z: 4, core: 2. Of those that a mesh axis runs over, the one named last changes fastest.
Arguments:
- hidden_state: bfloat16 [8, 4096, 768], P('batch', 'seq'), may hold values from -6 to 6
- segment_ids: int32 [8, 4096], P('batch', 'seq'), may hold values from 0 to 2, as said below
- valid_mask: int32 [8, 4096], P('batch', 'seq'), may hold values from 0 to 1, as said below
- cotangent: bfloat16 [8, 4096, 768], P('batch', 'seq'), may hold values from -6 to 6
- norm_gain: bfloat16 [768], P(('seq', 'batch')), may hold values from 0.5 to 1.5
- pool_gain: bfloat16 [768], P(('seq', 'batch')), may hold values from 0.5 to 1.5
- feed_gain: bfloat16 [768], P(('seq', 'batch')), may hold values from 0.5 to 1.5
- query_weight: bfloat16 [768, 768], P(('seq', 'batch')), may hold values from -0.0546875 to 0.0546875
- key_weight: bfloat16 [768, 768], P(('seq', 'batch')), may hold values from -0.21875 to 0.21875
- value_weight: bfloat16 [768, 768], P(('seq', 'batch')), may hold values from -0.21875 to 0.21875
- output_weight: bfloat16 [768, 768], P(('seq', 'batch')), may hold values from -1.25 to 1.25
- local_bias: float32 [12, 32], replicated, may hold values from -4 to 4
- global_bias: float32 [12, 32], replicated, may hold values from -4 to 4
- gate_weight: bfloat16 [768, 2048], P(('seq', 'batch')), may hold values from -0.21875 to 0.21875
- up_weight: bfloat16 [768, 2048], P(('seq', 'batch')), may hold values from -0.21875 to 0.21875
- down_weight: bfloat16 [2048, 768], P(('seq', 'batch')), may hold values from -0.25 to 0.25
Outputs:
- layer_output: bfloat16 [8, 4096, 768], P('batch', 'seq')
- input_delta: float32 [8, 4096, 768], P('batch', 'seq')
- norm_delta: float32 [768], P(('seq', 'batch'))
- pool_delta: float32 [768], P(('seq', 'batch'))
- feed_delta: float32 [768], P(('seq', 'batch'))
- query_delta: float32 [768, 768], P(('seq', 'batch'))
- key_delta: float32 [768, 768], P(('seq', 'batch'))
- value_delta: float32 [768, 768], P(('seq', 'batch'))
- output_delta: float32 [768, 768], P(('seq', 'batch'))
- local_delta: float32 [12, 32], replicated
- global_delta: float32 [12, 32], replicated
- gate_delta: float32 [768, 2048], P(('seq', 'batch'))
- up_delta: float32 [768, 2048], P(('seq', 'batch'))
- down_delta: float32 [2048, 768], P(('seq', 'batch'))
Inputs may be any that keep to these rules, and one draw needn't show every extreme that they name: `segment_ids`: each pack holds three documents with ids 0, 1, 2 in order; every document fills whole aligned 16-token slots; the first and the last take 1 to 63 slots each. `valid_mask`: padding stands only at the end of each document's last 16-token slot, which holds 1 to 15 real tokens; all other tokens are real.
All inputs are finite; a program needn't handle non-finite values.
Results may differ from a plain program's by a relative error of at most 0.028.
Values may be sent and summed in bfloat16 or wider, within the bound.
No kernel may reach another device: no remote copies, remote signals or barrier semaphores. Data moves between devices by JAX's collectives and lax.ppermute only.
A program may use at most 320 MiB of HBM per device.

v0:
```python
import jax
import jax.numpy as jnp
from jax import lax
from jax.sharding import PartitionSpec as P

epsilon = 1e-06
highest = lax.Precision.HIGHEST
boundaries = (12, 16, 23, 32, 46, 64, 91)


def with_halo(cells, sides, width):
    for axis, dim in sides:
        count = lax.axis_size(axis)
        ends = count - 1
        head = lax.slice_in_dim(cells, 0, width, axis=dim)
        tail = lax.slice_in_dim(cells, cells.shape[dim] - width, cells.shape[dim], axis=dim)
        cells = jnp.concatenate(
            [
                lax.ppermute(tail, axis, [(i, (i + 1) % count) for i in range(ends)]),
                cells,
                lax.ppermute(head, axis, [((i + 1) % count, i) for i in range(ends)]),
            ],
            axis=dim,
        )
    return cells


def bucket_of(offset):
    distance = jnp.abs(offset)
    far_part = 8 + sum(((distance >= boundary).astype(jnp.int32) for boundary in boundaries))
    return 16 * (offset > 0).astype(jnp.int32) + jnp.where(distance < 8, distance, far_part)


def scaled(values, gain_row):
    return (
        values * lax.rsqrt(jnp.mean(values * values, axis=-1, keepdims=True) + epsilon) * gain_row
    )


def activate(gate_pre, lift_pre):
    return jax.nn.gelu(gate_pre, approximate=True) * lift_pre


def forward_product(left, right):
    return jnp.dot(left, right, preferred_element_type=jnp.float32)


def weight_sum(left, right):
    return jnp.einsum("ra,rb->ab", left, right, preferred_element_type=jnp.float32)


def back_product(left, right):
    return jnp.einsum("ra,ba->rb", left, right, preferred_element_type=jnp.float32)


def fold_windows(window_grad):
    first_part = jnp.pad(window_grad[:, :128], ((0, 2), (0, 0), (0, 0)))
    second_part = jnp.pad(window_grad[:, 128:256], ((1, 1), (0, 0), (0, 0)))
    third_part = jnp.pad(window_grad[:, 256:], ((2, 0), (0, 0), (0, 0)))
    summed = first_part + second_part + third_part
    return summed.reshape(-1, summed.shape[2])


def on_device(
    hidden_state,
    segment_ids,
    valid_mask,
    cotangent,
    norm_gain,
    pool_gain,
    feed_gain,
    query_weight,
    key_weight,
    value_weight,
    output_weight,
    local_bias,
    global_bias,
    gate_weight,
    up_weight,
    down_weight,
):
    all_segments, all_valid = (
        lax.all_gather(segment_ids[0], "seq", axis=0, tiled=True),
        lax.all_gather(valid_mask[0], "seq", axis=0, tiled=True),
    )
    gathered = (
        lax.all_gather(norm_gain, ("seq", "batch"), axis=0, tiled=True),
        lax.all_gather(pool_gain, ("seq", "batch"), axis=0, tiled=True),
        lax.all_gather(feed_gain, ("seq", "batch"), axis=0, tiled=True),
        lax.all_gather(query_weight, ("seq", "batch"), axis=0, tiled=True),
        lax.all_gather(key_weight, ("seq", "batch"), axis=0, tiled=True),
        lax.all_gather(value_weight, ("seq", "batch"), axis=0, tiled=True),
        lax.all_gather(output_weight, ("seq", "batch"), axis=0, tiled=True),
        lax.all_gather(gate_weight, ("seq", "batch"), axis=0, tiled=True),
        lax.all_gather(up_weight, ("seq", "batch"), axis=0, tiled=True),
        lax.all_gather(down_weight, ("seq", "batch"), axis=0, tiled=True),
    )
    gain_one, gain_pool, gain_two, w_query, w_key, w_value, w_output, w_gate, w_up, w_down = (
        gathered
    )
    tok_rows = hidden_state.shape[1]
    model_width = hidden_state.shape[2]
    head_count = local_bias.shape[0]
    bucket_count = local_bias.shape[1]
    inner_width = w_query.shape[1]
    head_size = inner_width // head_count
    block_count = tok_rows // 128
    step_rows = min(512, tok_rows)
    step_blocks = step_rows // 128
    step_count = tok_rows // step_rows
    slot_count = all_segments.shape[0] // 16
    own_slots = tok_rows // 16
    row_start = lax.axis_index("seq") * tok_rows
    own_segments = segment_ids[0]
    valid_float = valid_mask[0].astype(jnp.float32)
    source = hidden_state[0].astype(jnp.float32)
    normed_full, norm_pull = jax.vjp(scaled, source, gain_one.astype(jnp.float32))
    normed = normed_full.astype(jnp.bfloat16)
    queries = forward_product(normed, w_query).astype(jnp.bfloat16)
    key_rows = forward_product(normed, w_key).astype(jnp.bfloat16)
    value_rows = forward_product(normed, w_value).astype(jnp.bfloat16)
    pooled_raw = jnp.sum(
        (normed.astype(jnp.float32) * valid_float[:, None]).reshape(own_slots, 16, model_width),
        axis=1,
    )
    pooled_full, pool_pull = jax.vjp(scaled, pooled_raw, gain_pool.astype(jnp.float32))
    pooled = pooled_full.astype(jnp.bfloat16)
    own_keys = forward_product(pooled, w_key).astype(jnp.bfloat16)
    own_values = forward_product(pooled, w_value).astype(jnp.bfloat16)
    global_keys, global_values = (
        lax.all_gather(own_keys, "seq", axis=0, tiled=True),
        lax.all_gather(own_values, "seq", axis=0, tiled=True),
    )
    global_keys = global_keys.reshape(slot_count, head_count, head_size)
    global_values = global_values.reshape(slot_count, head_count, head_size)
    slot_segments = all_segments.reshape(slot_count, 16)[:, 0]
    slot_live = jnp.sum(all_valid.reshape(slot_count, 16), axis=1) > 0
    kv_ext = with_halo(jnp.stack([key_rows, value_rows]), (("seq", 1),), 128)
    kv_blocks = kv_ext.reshape(2, block_count + 2, 128, inner_width)
    kv_windows = jnp.concatenate(
        [kv_blocks[:, :-2], kv_blocks[:, 1:-1], kv_blocks[:, 2:]], axis=2
    ).reshape(2, block_count, 384, head_count, head_size)
    segment_ext = lax.dynamic_slice_in_dim(
        jnp.pad(all_segments, 128, constant_values=-1), row_start, tok_rows + 256
    ).reshape(block_count + 2, 128)
    valid_ext = lax.dynamic_slice_in_dim(
        jnp.pad(all_valid, 128), row_start, tok_rows + 256
    ).reshape(block_count + 2, 128)
    segment_windows = jnp.concatenate(
        [segment_ext[:-2], segment_ext[1:-1], segment_ext[2:]], axis=1
    )
    valid_windows = jnp.concatenate([valid_ext[:-2], valid_ext[1:-1], valid_ext[2:]], axis=1)
    local_offset = (
        jnp.arange(384, dtype=jnp.int32)[None, :] - 128 - jnp.arange(128, dtype=jnp.int32)[:, None]
    )
    bucket_ids = jnp.arange(bucket_count, dtype=jnp.int32)
    local_table = (bucket_of(local_offset)[:, :, None] == bucket_ids[None, None, :]).astype(
        jnp.float32
    )
    local_shift = jnp.einsum("hb,qkb->hqk", local_bias, local_table, precision=highest)
    local_mask = (
        (jnp.abs(local_offset) <= 127)[None]
        & (own_segments.reshape(block_count, 128)[:, :, None] == segment_windows[:, None, :])
        & (valid_windows[:, None, :] > 0)
    )
    query_blocks = queries.reshape(block_count, 128, head_count, head_size)

    def scores_for(step_index):
        first_block = step_index * step_blocks
        query_part = lax.dynamic_slice_in_dim(query_blocks, first_block, step_blocks, 0)
        window_part = lax.dynamic_slice_in_dim(kv_windows, first_block, step_blocks, 1)
        mask_part = lax.dynamic_slice_in_dim(local_mask, first_block, step_blocks, 0)
        local_scores = (
            jnp.einsum(
                "bqhd,bkhd->hbqk", query_part, window_part[0], preferred_element_type=jnp.float32
            )
            + local_shift[:, None]
        )
        local_scores = jnp.where(mask_part[None], local_scores, -1e30)
        query_flat = query_part.reshape(step_rows, head_count, head_size)
        query_segments = lax.dynamic_slice_in_dim(own_segments, step_index * step_rows, step_rows)
        query_slots = (row_start + step_index * step_rows) // 16 + jnp.arange(
            step_rows // 16, dtype=jnp.int32
        )
        slot_offset = jnp.arange(slot_count, dtype=jnp.int32)[None, :] - query_slots[:, None]
        global_table = (bucket_of(slot_offset)[:, :, None] == bucket_ids[None, None, :]).astype(
            jnp.float32
        )
        global_shift = jnp.einsum("hb,sgb->hsg", global_bias, global_table, precision=highest)
        global_scores = jnp.einsum(
            "qhd,ghd->hqg", query_flat, global_keys, preferred_element_type=jnp.float32
        )
        global_scores = (
            global_scores.reshape(head_count, step_rows // 16, 16, slot_count)
            + global_shift[:, :, None, :]
        ).reshape(head_count, step_rows, slot_count)
        global_mask = (query_segments[:, None] == slot_segments[None, :]) & slot_live[None, :]
        global_scores = jnp.where(global_mask[None], global_scores, -1e30)
        return (query_part, query_flat, window_part, local_scores, global_scores, global_table)

    def forward_step(unused_state, step_index):
        query_part, query_flat, window_part, local_scores, global_scores, global_table = scores_for(
            step_index
        )
        peak = jnp.maximum(
            jnp.max(local_scores, axis=3).reshape(head_count, step_rows),
            jnp.max(global_scores, axis=2),
        )
        local_exp = jnp.exp(local_scores - peak.reshape(head_count, step_blocks, 128)[..., None])
        global_exp = jnp.exp(global_scores - peak[..., None])
        totals = jnp.sum(local_exp, axis=3).reshape(head_count, step_rows) + jnp.sum(
            global_exp, axis=2
        )
        local_weights = (
            local_exp / totals.reshape(head_count, step_blocks, 128)[..., None]
        ).astype(jnp.bfloat16)
        global_weights = (global_exp / totals[..., None]).astype(jnp.bfloat16)
        mixture = jnp.einsum(
            "hbqk,bkhd->bqhd", local_weights, window_part[1], preferred_element_type=jnp.float32
        ).reshape(step_rows, inner_width)
        mixture = mixture + jnp.einsum(
            "hqg,ghd->qhd", global_weights, global_values, preferred_element_type=jnp.float32
        ).reshape(step_rows, inner_width)
        return (unused_state, (mixture.astype(jnp.bfloat16), peak + jnp.log(totals)))

    steps_index = jnp.arange(step_count, dtype=jnp.int32)
    _, (mixture, log_totals) = lax.scan(forward_step, None, steps_index)
    mixture = mixture.reshape(tok_rows, inner_width)
    middle = source + forward_product(mixture, w_output)
    normed_two_full, feed_pull = jax.vjp(scaled, middle, gain_two.astype(jnp.float32))
    normed_two = normed_two_full.astype(jnp.bfloat16)
    gate_pre = forward_product(normed_two, w_gate)
    lift_pre = forward_product(normed_two, w_up)
    product_full, act_pull = jax.vjp(activate, gate_pre, lift_pre)
    product = product_full.astype(jnp.bfloat16)
    layer_output = (middle + forward_product(product, w_down)).astype(jnp.bfloat16)
    upstream = cotangent[0]
    down_delta = weight_sum(product, upstream)
    product_grad = back_product(upstream, w_down)
    gate_grad, lift_grad = act_pull(product_grad)
    gate_low = gate_grad.astype(jnp.bfloat16)
    lift_low = lift_grad.astype(jnp.bfloat16)
    gate_delta = weight_sum(normed_two, gate_low)
    up_delta = weight_sum(normed_two, lift_low)
    normed_two_grad = back_product(gate_low, w_gate) + back_product(lift_low, w_up)
    middle_norm_grad, feed_delta = feed_pull(normed_two_grad)
    middle_grad = upstream.astype(jnp.float32) + middle_norm_grad
    attn_low = middle_grad.astype(jnp.bfloat16)
    output_delta = weight_sum(mixture, attn_low)
    mixture_grad = back_product(attn_low, w_output).astype(jnp.bfloat16)
    grad_blocks = mixture_grad.reshape(block_count, 128, head_count, head_size)

    def backward_step(state, step_index):
        key_sum, value_sum, table_sum, bias_sum = state
        query_part, query_flat, window_part, local_scores, global_scores, global_table = scores_for(
            step_index
        )
        log_rows = log_totals[step_index]
        grad_part = lax.dynamic_slice_in_dim(grad_blocks, step_index * step_blocks, step_blocks, 0)
        grad_flat = grad_part.reshape(step_rows, head_count, head_size)
        local_prob = jnp.exp(
            local_scores - log_rows.reshape(head_count, step_blocks, 128)[..., None]
        )
        global_prob = jnp.exp(global_scores - log_rows[..., None])
        local_weights = local_prob.astype(jnp.bfloat16)
        global_weights = global_prob.astype(jnp.bfloat16)
        local_dprob = jnp.einsum(
            "bqhd,bkhd->hbqk", grad_part, window_part[1], preferred_element_type=jnp.float32
        )
        global_dprob = jnp.einsum(
            "qhd,ghd->hqg", grad_flat, global_values, preferred_element_type=jnp.float32
        )
        centre = jnp.sum(local_prob * local_dprob, axis=3).reshape(head_count, step_rows) + jnp.sum(
            global_prob * global_dprob, axis=2
        )
        local_low = (
            local_prob * (local_dprob - centre.reshape(head_count, step_blocks, 128)[..., None])
        ).astype(jnp.bfloat16)
        global_low = (global_prob * (global_dprob - centre[..., None])).astype(jnp.bfloat16)
        query_grad = jnp.einsum(
            "hbqk,bkhd->bqhd", local_low, window_part[0], preferred_element_type=jnp.float32
        ).reshape(step_rows, inner_width)
        query_grad = query_grad + jnp.einsum(
            "hqg,ghd->qhd", global_low, global_keys, preferred_element_type=jnp.float32
        ).reshape(step_rows, inner_width)
        key_grad = jnp.einsum(
            "hbqk,bqhd->bkhd", local_low, query_part, preferred_element_type=jnp.float32
        ).reshape(step_blocks, 384, inner_width)
        value_grad = jnp.einsum(
            "hbqk,bqhd->bkhd", local_weights, grad_part, preferred_element_type=jnp.float32
        ).reshape(step_blocks, 384, inner_width)
        key_sum = key_sum + jnp.einsum(
            "hqg,qhd->ghd", global_low, query_flat, preferred_element_type=jnp.float32
        )
        value_sum = value_sum + jnp.einsum(
            "hqg,qhd->ghd", global_weights, grad_flat, preferred_element_type=jnp.float32
        )
        table_sum = table_sum + jnp.sum(local_low.astype(jnp.float32), axis=1)
        slot_grads = jnp.sum(
            global_low.astype(jnp.float32).reshape(head_count, step_rows // 16, 16, slot_count),
            axis=2,
        )
        bias_sum = bias_sum + jnp.einsum("hsg,sgb->hb", slot_grads, global_table, precision=highest)
        return ((key_sum, value_sum, table_sum, bias_sum), (query_grad, key_grad, value_grad))

    zero_state = (
        jnp.zeros((slot_count, head_count, head_size), jnp.float32),
        jnp.zeros((slot_count, head_count, head_size), jnp.float32),
        jnp.zeros((head_count, 128, 384), jnp.float32),
        jnp.zeros((head_count, bucket_count), jnp.float32),
    )
    (key_sum, value_sum, table_sum, bias_sum), (query_grad, key_grad, value_grad) = lax.scan(
        backward_step, zero_state, steps_index
    )
    query_low = query_grad.reshape(tok_rows, inner_width).astype(jnp.bfloat16)
    key_fold = fold_windows(key_grad.reshape(block_count, 384, inner_width))
    value_fold = fold_windows(value_grad.reshape(block_count, 384, inner_width))
    rims = jnp.stack(
        [
            jnp.concatenate([key_fold[:128], key_fold[-128:]], axis=0),
            jnp.concatenate([value_fold[:128], value_fold[-128:]], axis=0),
        ]
    )
    returned = with_halo(rims.astype(jnp.bfloat16), (("seq", 1),), 128).astype(rims.dtype)
    key_low = jnp.concatenate(
        [
            key_fold[128:256] + returned[0, :128],
            key_fold[256:-256],
            key_fold[-256:-128] + returned[0, -128:],
        ],
        axis=0,
    ).astype(jnp.bfloat16)
    value_low = jnp.concatenate(
        [
            value_fold[128:256] + returned[1, :128],
            value_fold[256:-256],
            value_fold[-256:-128] + returned[1, -128:],
        ],
        axis=0,
    ).astype(jnp.bfloat16)
    global_key_own, global_value_own = (
        lax.psum_scatter(
            key_sum.reshape(slot_count, inner_width).astype(jnp.bfloat16),
            "seq",
            scatter_dimension=0,
            tiled=True,
        ).astype(jnp.float32),
        lax.psum_scatter(
            value_sum.reshape(slot_count, inner_width).astype(jnp.bfloat16),
            "seq",
            scatter_dimension=0,
            tiled=True,
        ).astype(jnp.float32),
    )
    global_key_low = global_key_own.astype(jnp.bfloat16)
    global_value_low = global_value_own.astype(jnp.bfloat16)
    query_delta = weight_sum(normed, query_low)
    key_delta = weight_sum(normed, key_low) + weight_sum(pooled, global_key_low)
    value_delta = weight_sum(normed, value_low) + weight_sum(pooled, global_value_low)
    pooled_grad = back_product(global_key_low, w_key) + back_product(global_value_low, w_value)
    pooled_raw_grad, pool_delta = pool_pull(pooled_grad)
    normed_grad = (
        back_product(query_low, w_query)
        + back_product(key_low, w_key)
        + back_product(value_low, w_value)
    )
    spread_grad = jnp.broadcast_to(
        pooled_raw_grad[:, None, :], (own_slots, 16, model_width)
    ).reshape(tok_rows, model_width)
    normed_grad = normed_grad + spread_grad * valid_float[:, None]
    source_grad, norm_delta = norm_pull(normed_grad)
    input_delta = middle_grad + source_grad
    local_delta = jnp.einsum("hqk,qkb->hb", table_sum, local_table, precision=highest)
    local_total, global_total = lax.psum((local_delta, bias_sum), ("seq", "batch"))
    reduced = (
        lax.psum_scatter(norm_delta, ("seq", "batch"), scatter_dimension=0, tiled=True),
        lax.psum_scatter(pool_delta, ("seq", "batch"), scatter_dimension=0, tiled=True),
        lax.psum_scatter(feed_delta, ("seq", "batch"), scatter_dimension=0, tiled=True),
        lax.psum_scatter(query_delta, ("seq", "batch"), scatter_dimension=0, tiled=True),
        lax.psum_scatter(key_delta, ("seq", "batch"), scatter_dimension=0, tiled=True),
        lax.psum_scatter(value_delta, ("seq", "batch"), scatter_dimension=0, tiled=True),
        lax.psum_scatter(output_delta, ("seq", "batch"), scatter_dimension=0, tiled=True),
        lax.psum_scatter(gate_delta, ("seq", "batch"), scatter_dimension=0, tiled=True),
        lax.psum_scatter(up_delta, ("seq", "batch"), scatter_dimension=0, tiled=True),
        lax.psum_scatter(down_delta, ("seq", "batch"), scatter_dimension=0, tiled=True),
    )
    return (
        layer_output[None],
        input_delta[None],
        reduced[0],
        reduced[1],
        reduced[2],
        reduced[3],
        reduced[4],
        reduced[5],
        reduced[6],
        local_total,
        global_total,
        reduced[7],
        reduced[8],
        reduced[9],
    )


def solution(mesh):
    placed = (
        P("batch", "seq", None),
        P("batch", "seq"),
        P("batch", "seq"),
        P("batch", "seq", None),
        P(("seq", "batch")),
        P(("seq", "batch")),
        P(("seq", "batch")),
        P(("seq", "batch"), None),
        P(("seq", "batch"), None),
        P(("seq", "batch"), None),
        P(("seq", "batch"), None),
        P(),
        P(),
        P(("seq", "batch"), None),
        P(("seq", "batch"), None),
        P(("seq", "batch"), None),
    )
    return jax.shard_map(
        on_device,
        mesh=mesh,
        in_specs=placed,
        out_specs=(
            P("batch", "seq", None),
            P("batch", "seq", None),
            P(("seq", "batch")),
            P(("seq", "batch")),
            P(("seq", "batch")),
            P(("seq", "batch"), None),
            P(("seq", "batch"), None),
            P(("seq", "batch"), None),
            P(("seq", "batch"), None),
            P(),
            P(),
            P(("seq", "batch"), None),
            P(("seq", "batch"), None),
            P(("seq", "batch"), None),
        ),
        check_vma=False,
    )
```

profile of v0, /device:TPU:0, one launch (start us, length us, event | category | flops | bytes accessed | tf_op | source)
XLA Modules:
  0.0 1517.7 jit_solution(3120688478570913973)
XLA Ops:
  12.7 9.7 all-gather.1
  27.7 39.9 %all-reduce.15 = (bf16[768]{0:T(1024)(128)(2,1)S(1)}, bf16[768]{0:T(1024)(128)(2,1)S(1)}, bf16[768]{0:T(1024)(128)(2,1)S(1)}) all-reduce(bf16[768]{0:T(1024)(128)(2,1)S(1)} %dynamic-update-slice, bf16[768]{0:T(1024)(128)(2,1)S(1)} %dynamic-update-slice.1, ...), channel_id=1, replica_groups=mesh['seq'=4,'batch'=8] {'seq','batch'}, use_global_device_ids=true, to_apply=%add.8 | all-reduce | flops 2304 | bytes 9216
  68.2 9.1 all-gather
  81.3 8.1 copy.146
  104.4 19.8 %all-gather.10.cloned.1.call-done = bf16[768,768]{1,0:T(8,128)(2,1)} async-done(((bf16[24,768]{1,0:T(8,128)(2,1)}), bf16[768,768]{1,0:T(8,128)(2,1)}) %all-gather.10.cloned.1.call-update) | async-done | bytes 1179664 | tf_op jit(solution)/shard_map/all_gather | solution.py:91
  134.5 46.0 %all-gather.14.cloned.1.call-done = bf16[768,768]{1,0:T(8,128)(2,1)} async-done(((bf16[24,768]{1,0:T(8,128)(2,1)}), bf16[768,768]{1,0:T(8,128)(2,1)}) %all-gather.14.cloned.1.call-update) | async-done | bytes 1179664 | tf_op jit(solution)/shard_map/all_gather | solution.py:90
  191.4 9.5 all_gather.49
  202.6 8.8 all_gather.50
  232.5 9.2 pad_maximum_fusion
  241.7 9.2 copy.150
  251.4 119.3 %while.40 = (s32[]{:T(128)}, bf16[2,512,768]{2,1,0:T(8,128)(2,1)}, f32[2,12,512]{2,1,0:T(8,128)}, s32[2]{0:T(128)}, bf16[2,8,384,12,64]{2,4,1,3,0:T(8,128)(2,1)}...) while((s32[]{:T(128)}, bf16[2,512,768]{2,1,0:T(8,128)(2,1)}, ...), condition=%wide.region_9.10_spmd.clone, body=%wide.region_4.9_spmd.clone.sunk | while | flops 1086834688 | bytes 172370656 | solution.py:227
  260.9 6.6 copy.297
  267.5 6.9 fusion.286
  293.8 7.0 fusion.289
  320.3 6.6 copy.297
  326.9 6.9 fusion.286
  353.2 7.0 fusion.289
  378.0 9.0 fusion.166
  387.0 9.2 fusion.165
  396.2 23.4 %all-gather.22.cloned.1.call-done = bf16[2048,768]{1,0:T(8,128)(2,1)} async-done(((bf16[64,768]{1,0:T(8,128)(2,1)}), bf16[2048,768]{1,0:T(8,128)(2,1)}) %all-gather.22.cloned.1.call-update) | async-done | bytes 3145744 | tf_op jit(solution)/shard_map/all_gather | solution.py:96
  419.6 17.3 %multiply_convert_fusion.2 = (bf16[1024,2048]{1,0:T(8,128)(2,1)S(1)}, bf16[1024,2048]{1,0:T(8,128)(2,1)}, bf16[1024,2048]{1,0:T(8,128)(2,1)}) fusion(f32[1024,2048]{1,0:T(8,128)} %fusion.165, f32[1024,2048]{1,0:T(8,128)} %fusion.166, bf16[2048,768]{1,0:T(8,128)(2,1)} %all-gather.22.cloned.1.call-done, bf16[1,1024,768]{2,1,0:T(8,128)(2,1)} %param.23), kind=kOutput, calls=%fused_computation.129 | convolution fusion | flops 3275751424 | bytes 34078720 | tf_op jit(solution)/shard_map/ra,ba->rb/dot_general | solution.py:53
  436.9 6.8 fusion.167
  459.1 219.5 %while.41 = (s32[]{:T(128)}, f32[256,12,64]{0,2,1:T(8,128)}, f32[256,12,64]{0,2,1:T(8,128)}, f32[12,128,384]{2,1,0:T(8,128)}, f32[12,32]{1,0:T(8,128)S(1)}, /*in...) while((s32[]{:T(128)}, f32[256,12,64]{0,2,1:T(8,128)}, ...), condition=%wide.region_17.18_spmd.clone, body=%wide.region_12.17_spmd.clone.sunk | while | flops 2650211072 | bytes 347802112 | solution.py:312
  478.6 13.7 multiply_reduce_fusion.10
  504.3 10.8 convert_reduce_fusion.6
  528.8 6.0 copy.317
  554.2 6.0 copy.316
  560.2 8.1 constant_dynamic-update-slice_fusion.9
  587.6 13.7 multiply_reduce_fusion.10
  614.4 10.8 convert_reduce_fusion.6
  638.9 6.0 copy.317
  670.3 7.9 constant_dynamic-update-slice_fusion.9
  691.4 7.6 fusion.159
  699.1 6.5 fusion.157
  718.2 8.0 collective-permute-done.2
  726.2 11.5 collective-permute-done.3
  755.1 7.6 fusion.171
  762.7 7.9 fusion.170
  772.0 8.4 fusion.102
  782.3 7.8 fusion.110
  814.9 6.6 fusion.94
  827.6 38.8 %all-reduce.14 = (f32[768]{0:T(1024)S(1)}, f32[768]{0:T(1024)S(1)}, f32[768]{0:T(1024)S(1)}, f32[12,32]{1,0:T(8,128)}, f32[12,32]{1,0:T(8,128)}) all-reduce(f32[768]{0:T(1024)S(1)} %get-tuple-element.768, f32[768]{0:T(1024)S(1)} %get-tuple-element.770, ...), channel_id=6, replica_groups=mesh['seq'=4,'batch'=8] {'seq','batch'}, use_global_device_ids=true, to_apply=%region_23.24.clone | all-reduce | flops 3072 | bytes 24576
  868.2 73.9 %reduce-scatter.14.cloned.1.call-done = f32[24,768]{1,0:T(8,128)} async-done(((f32[768,768]{1,0:T(8,128)}), f32[24,768]{1,0:T(8,128)}) %reduce-scatter.14.cloned.1.call-update) | async-done | bytes 73744 | tf_op jit(solution)/shard_map/reduce_scatter | solution.py:379
  942.1 103.8 %reduce-scatter.18.cloned.1.call-done = f32[24,768]{1,0:T(8,128)} async-done(((f32[768,768]{1,0:T(8,128)}), f32[24,768]{1,0:T(8,128)}) %reduce-scatter.18.cloned.1.call-update) | async-done | bytes 73744 | tf_op jit(solution)/shard_map/reduce_scatter | solution.py:381
  1045.8 104.8 %reduce-scatter.16.cloned.1.call-done = f32[24,768]{1,0:T(8,128)} async-done(((f32[768,768]{1,0:T(8,128)}), f32[24,768]{1,0:T(8,128)}) %reduce-scatter.16.cloned.1.call-update) | async-done | bytes 73744 | tf_op jit(solution)/shard_map/reduce_scatter | solution.py:380
  1150.6 119.7 %reduce-scatter.24.cloned.1.call-done = f32[24,2048]{1,0:T(8,128)} async-done(((f32[768,2048]{1,0:T(8,128)}), f32[24,2048]{1,0:T(8,128)}) %reduce-scatter.24.cloned.1.call-update) | async-done | bytes 196624 | tf_op jit(solution)/shard_map/reduce_scatter | solution.py:384
  1270.3 120.8 %reduce-scatter.22.cloned.1.call-done = f32[24,2048]{1,0:T(8,128)} async-done(((f32[768,2048]{1,0:T(8,128)}), f32[24,2048]{1,0:T(8,128)}) %reduce-scatter.22.cloned.1.call-update) | async-done | bytes 196624 | tf_op jit(solution)/shard_map/reduce_scatter | solution.py:383
  1391.1 119.8 %reduce-scatter.26.cloned.1.call-done = f32[64,768]{1,0:T(8,128)} async-done(((f32[2048,768]{1,0:T(8,128)}), f32[64,768]{1,0:T(8,128)}) %reduce-scatter.26.cloned.1.call-update) | async-done | bytes 196624 | tf_op jit(solution)/shard_map/reduce_scatter | solution.py:385
  (575 shorter events, 378.4 us)
Async XLA Ops:
  7.2 82.2 %copy-start = (f32[12,32]{1,0:T(8,128)S(1)}, f32[12,32]{1,0:T(8,128)}, u32[]{:S(2)}) copy-start(f32[12,32]{1,0:T(8,128)} %param.31) | copy-start | bytes 4612
  7.2 92.7 %all-gather.12.cloned.1.call-start = ((), (), s32[]{:S(2)}) async-start(), calls=%async_computation.10 | async-start | bytes 1216512 | tf_op jit(solution)/shard_map/all_gather | solution.py:92
  7.9 116.2 %all-gather.10.cloned.1.call-start = ((), (), s32[]{:S(2)}) async-start(), calls=%async_computation.9 | async-start | bytes 1216512 | tf_op jit(solution)/shard_map/all_gather | solution.py:91
  8.7 171.8 %all-gather.14.cloned.1.call-start = ((), (), s32[]{:S(2)}) async-start(), calls=%async_computation.11 | async-start | bytes 1216512 | tf_op jit(solution)/shard_map/all_gather | solution.py:90
  9.4 361.4 %all-gather.16.cloned.1.call-start = ((), (), s32[]{:S(2)}) async-start(), calls=%async_computation.12 | async-start | bytes 1216512 | tf_op jit(solution)/shard_map/all_gather | solution.py:93
  10.0 368.0 %all-gather.20.cloned.1.call-start = ((), (), s32[]{:S(2)}) async-start(), calls=%async_computation.14 | async-start | bytes 3244032 | tf_op jit(solution)/shard_map/all_gather | solution.py:95
  10.6 376.5 %all-gather.18.cloned.1.call-start = ((), (), s32[]{:S(2)}) async-start(), calls=%async_computation.13 | async-start | bytes 3244032 | tf_op jit(solution)/shard_map/all_gather | solution.py:94
  11.2 408.5 %all-gather.22.cloned.1.call-start = ((), (), s32[]{:S(2)}) async-start(), calls=%async_computation.15 | async-start | bytes 3244032 | tf_op jit(solution)/shard_map/all_gather | solution.py:96
  11.9 730.8 %reduce-scatter.30.cloned.1.call-start = ((), (), s32[]{:S(2)}) async-start(), calls=%async_computation.24 | async-start | bytes 491520
  24.5 43.7 %copy-start.72 = (s32[1,1024]{1,0:T(1,128)S(1)}, s32[1,1024]{1,0:T(1,128)}, u32[]{:S(2)}) copy-start(s32[1,1024]{1,0:T(1,128)} %param.21) | copy-start | bytes 12292
  24.9 56.4 %copy-start.85 = (f32[1024]{0:T(1024)}, f32[1024]{0:T(1024)S(1)}, u32[]{:S(2)}) copy-start(f32[1024]{0:T(1024)S(1)} %fusion.97) | copy-start | bytes 12292
  67.6 112.9 %copy-start.78 = (f32[768]{0:T(1024)}, f32[768]{0:T(1024)S(1)}, u32[]{:S(2)}) copy-start(f32[768]{0:T(1024)S(1)} %convert_element_type.411) | copy-start | bytes 9220
  67.6 29.9 %copy-start.76 = (f32[768]{0:T(1024)}, f32[768]{0:T(1024)S(1)}, u32[]{:S(2)}) copy-start(f32[768]{0:T(1024)S(1)} %convert_element_type.429) | copy-start | bytes 9220
  80.3 9.1 copy-start.54
  80.3 100.1 %copy-start.81 = (f32[1024]{0:T(1024)}, f32[1024]{0:T(1024)S(1)}, u32[]{:S(2)}) copy-start(f32[1024]{0:T(1024)S(1)} %fusion.144) | copy-start | bytes 12292
  98.2 102.9 %copy-start.50 = (bf16[64,768]{1,0:T(8,128)(2,1)}, bf16[64,768]{1,0:T(8,128)(2,1)S(1)}, u32[]{:S(2)}) copy-start(bf16[64,768]{1,0:T(8,128)(2,1)S(1)} %multiply_convert_fusion.6) | copy-start | bytes 294916
  129.1 83.3 %collective-permute-start = (bf16[2,128,768]{2,1,0:T(8,128)(2,1)}, bf16[2,128,768]{2,1,0:T(8,128)(2,1)}, u32[]{:S(2)}, u32[]{:S(2)}) collective-permute-start(bf16[2,128,768]{2,1,0:T(8,128)(2,1)} %get-tuple-element.890), channel_id=1, source_target_pairs={{0,8},{8,16},{16,24},{1,9},{9,17},{17,25},{2,10},{10,18},{18,26},{... | collective-permute-start | bytes 1179656 | tf_op jit(solution)/shard_map/ppermute | solution.py:19
  133.2 79.2 %collective-permute-start.1 = (bf16[2,128,768]{2,1,0:T(8,128)(2,1)}, bf16[2,128,768]{2,1,0:T(8,128)(2,1)}, u32[]{:S(2)}, u32[]{:S(2)}) collective-permute-start(bf16[2,128,768]{2,1,0:T(8,128)(2,1)} %get-tuple-element.891), channel_id=1, source_target_pairs={{8,0},{16,8},{24,16},{9,1},{17,9},{25,17},{10,2},{18,10},{26,18},{... | collective-permute-start | bytes 1179656 | tf_op jit(solution)/shard_map/ppermute | solution.py:21
  241.7 9.7 copy-start.64
  282.4 8.7 copy-start.25
  341.8 8.7 copy-start.25
  419.6 17.3 %copy-start.96 = (bf16[768,2048]{1,0:T(8,128)(2,1)S(1)}, bf16[768,2048]{1,0:T(8,128)(2,1)}, u32[]{:S(2)}) copy-start(bf16[768,2048]{1,0:T(8,128)(2,1)} %all-gather.18.cloned.1.call-done) | copy-start | bytes 9437188
  459.3 13.7 copy-start.3
  478.6 13.7 copy-start.2
  478.6 14.3 copy-start.9
  478.6 14.3 copy-start.33
  504.3 10.8 copy-start.15
  560.2 8.1 copy-start.105
  568.3 13.7 copy-start.3
  587.6 13.7 copy-start.2
  587.6 14.3 copy-start.9
  587.6 14.3 copy-start.33
  614.4 10.8 copy-start.15
  680.8 70.4 %reduce-scatter.28.cloned.1.call-start = ((), (), s32[]{:S(2)}) async-start(), calls=%async_computation.23 | async-start | bytes 491520
  683.0 185.2 %reduce-scatter.20.cloned.1.call-start = ((), (), s32[]{:S(2)}) async-start(), calls=%async_computation.19 | async-start | bytes 2433024 | tf_op jit(solution)/shard_map/reduce_scatter | solution.py:382
  688.5 253.6 %reduce-scatter.14.cloned.1.call-start = ((), (), s32[]{:S(2)}) async-start(), calls=%async_computation.16 | async-start | bytes 2433024 | tf_op jit(solution)/shard_map/reduce_scatter | solution.py:379
  699.1 346.8 %reduce-scatter.18.cloned.1.call-start = ((), (), s32[]{:S(2)}) async-start(), calls=%async_computation.18 | async-start | bytes 2433024 | tf_op jit(solution)/shard_map/reduce_scatter | solution.py:381
  705.6 32.1 %copy-start.39 = (bf16[1,256,768]{2,1,0:T(8,128)(2,1)}, bf16[1,256,768]{2,1,0:T(8,128)(2,1)S(1)}, u32[]{:S(2)}) copy-start(bf16[1,256,768]{2,1,0:T(8,128)(2,1)S(1)} %maximum_bitcast_fusion.1) | copy-start | bytes 1179652
  713.3 25.8 %copy-start.40 = (bf16[1,256,768]{2,1,0:T(8,128)(2,1)}, bf16[1,256,768]{2,1,0:T(8,128)(2,1)S(1)}, u32[]{:S(2)}) copy-start(bf16[1,256,768]{2,1,0:T(8,128)(2,1)S(1)} %maximum_bitcast_fusion) | copy-start | bytes 1179652
  713.4 12.8 collective-permute-start.2
  716.8 21.0 %collective-permute-start.3 = (bf16[2,128,768]{2,1,0:T(8,128)(2,1)S(1)}, bf16[2,128,768]{2,1,0:T(8,128)(2,1)S(1)}, u32[]{:S(2)}, u32[]{:S(2)}) collective-permute-start(bf16[2,128,768]{2,1,0:T(8,128)(2,1)S(1)} %get-tuple-element.897), channel_id=1, source_target_pairs={{8,0},{16,8},{24,16},{9,1},{17,9},{25,17},{10,2},{18,10},{26,18},{... | collective-permute-start | bytes 1179656 | tf_op jit(solution)/shard_map/ppermute | solution.py:21
  718.2 21.0 %copy-start.48 = (bf16[6,128,768]{2,1,0:T(8,128)(2,1)}, bf16[6,128,768]{2,1,0:T(8,128)(2,1)S(1)}, u32[]{:S(2)}) copy-start(bf16[6,128,768]{2,1,0:T(8,128)(2,1)S(1)} %slice.291) | copy-start | bytes 3538948
  726.2 12.9 copy-start.60
  746.4 404.2 %reduce-scatter.16.cloned.1.call-start = ((), (), s32[]{:S(2)}) async-start(), calls=%async_computation.17 | async-start | bytes 2433024 | tf_op jit(solution)/shard_map/reduce_scatter | solution.py:380
  755.0 515.3 %reduce-scatter.24.cloned.1.call-start = ((), (), s32[]{:S(2)}) async-start(), calls=%async_computation.21 | async-start | bytes 6488064 | tf_op jit(solution)/shard_map/reduce_scatter | solution.py:384
  762.7 628.4 %reduce-scatter.22.cloned.1.call-start = ((), (), s32[]{:S(2)}) async-start(), calls=%async_computation.20 | async-start | bytes 6488064 | tf_op jit(solution)/shard_map/reduce_scatter | solution.py:383
  770.6 740.3 %reduce-scatter.26.cloned.1.call-start = ((), (), s32[]{:S(2)}) async-start(), calls=%async_computation.22 | async-start | bytes 6488064 | tf_op jit(solution)/shard_map/reduce_scatter | solution.py:385
  821.5 689.4 %copy-start.1 = (f32[12,32]{1,0:T(8,128)S(1)}, f32[12,32]{1,0:T(8,128)}, u32[]{:S(2)}) copy-start(f32[12,32]{1,0:T(8,128)} %param.31) | copy-start | bytes 4612
  (113 other events, 439.8 us)
Sparse Core Ops, SparseCore 0:
  11.1 56.9 all-gather.11
  71.0 53.1 all-gather.9
  127.2 53.2 all-gather.13
  183.4 53.4 all-gather.15
  239.7 58.0 all-gather.19
  300.7 57.9 all-gather.17
  361.6 57.9 all-gather.21
  680.9 23.2 reduce-scatter.29
  707.0 25.3 reduce-scatter.27
  738.1 99.0 reduce-scatter.19
  843.9 98.0 reduce-scatter.13
  947.8 98.0 reduce-scatter.17
  1052.5 98.0 reduce-scatter.15
  1156.7 113.5 reduce-scatter.23
  1277.3 113.7 reduce-scatter.21
  1397.1 113.7 reduce-scatter.25
where the time goes:
time: 1520 us
  waiting for transfers between devices  756 us (50%)
  matrix products  272 us (18%)
  local copies, waits for them, and re-layouts  229 us (15%)
  blocking collectives  116 us (8%)
  other arithmetic  107 us (7%)
  between operations  15.3 us (1%)
    reduce_scatter x1, waiting for transfers between devices, on_device(): lax.psum_scatter(gate_delta, ('seq', 'batch'), scatter_dimension=0, tiled...  121 us
    reduce_scatter x1, waiting for transfers between devices, on_device(): lax.psum_scatter(down_delta, ('seq', 'batch'), scatter_dimension=0, tiled...  120 us
    reduce_scatter x1, waiting for transfers between devices, on_device(): lax.psum_scatter(up_delta, ('seq', 'batch'), scatter_dimension=0, tiled=T...  120 us
    reduce_scatter x1, waiting for transfers between devices, on_device(): lax.psum_scatter(key_delta, ('seq', 'batch'), scatter_dimension=0, tiled=...  105 us
    reduce_scatter x1, waiting for transfers between devices, on_device(): lax.psum_scatter(value_delta, ('seq', 'batch'), scatter_dimension=0, tile...  104 us
    unnamed x2, blocking collectives  78.8 us
    reduce_scatter x1, waiting for transfers between devices, on_device(): lax.psum_scatter(query_delta, ('seq', 'batch'), scatter_dimension=0, tile...  73.9 us
    unnamed x170, local copies, waits for them, and re-layouts  54.2 us
  transfers between devices with their start and end apart: 20, of which 11 were waited for; matrix products, arithmetic and copies ran while one was open for 22% of the time, Pallas kernels for 0%

commit v1 on v0

v1 whole, which is shorter than its diff:
```python
import functools

import jax
import jax.numpy as jnp
from jax import lax
from jax.experimental import pallas as pl
from jax.experimental.pallas import tpu as pltpu
from jax.sharding import PartitionSpec as P

epsilon = 1e-06
highest = lax.Precision.HIGHEST
boundaries = (12, 16, 23, 32, 46, 64, 91)
never = -1e30
both = ("seq", "batch")
bf16 = jnp.bfloat16
f32 = jnp.float32


def bucket_of(offset):
    distance = jnp.abs(offset)
    far_part = 8 + sum(((distance >= boundary).astype(jnp.int32) for boundary in boundaries))
    return 16 * (offset > 0).astype(jnp.int32) + jnp.where(distance < 8, distance, far_part)


def scaled(values, gain_row):
    return (
        values * lax.rsqrt(jnp.mean(values * values, axis=-1, keepdims=True) + epsilon) * gain_row
    )


def activate(gate_pre, lift_pre):
    return jax.nn.gelu(gate_pre, approximate=True) * lift_pre


def forward_product(left, right):
    return jnp.dot(left, right, preferred_element_type=f32)


def weight_sum(left, right):
    return jnp.einsum("ra,rb->ab", left, right, preferred_element_type=f32)


def back_product(left, right):
    return jnp.einsum("ra,ba->rb", left, right, preferred_element_type=f32)


def dot_nt(left, right):
    return lax.dot_general(left, right, (((1,), (1,)), ((), ())), preferred_element_type=f32)


def dot_nn(left, right):
    return lax.dot_general(left, right, (((1,), (0,)), ((), ())), preferred_element_type=f32)


def stack_heads(rows):
    lane = lax.broadcasted_iota(jnp.int32, rows.shape, 1)
    zero = jnp.zeros_like(rows)
    return jnp.concatenate(
        [jnp.where(lane < 64, rows, zero), jnp.where(lane < 64, zero, rows)], axis=0
    )


def unstack_heads(wide):
    row = lax.broadcasted_iota(jnp.int32, (128, 128), 0)
    return jnp.where(row < 64, wide[:, :128], wide[:, 128:]).T


def upper_band():
    key = lax.broadcasted_iota(jnp.int32, (128, 256), 0)
    query = lax.broadcasted_iota(jnp.int32, (128, 256), 1) & 127
    return key > query


def spread_band(upper, own, merged):
    zero = jnp.zeros_like(merged)
    return jnp.concatenate(
        [jnp.where(upper, merged, zero), own, jnp.where(upper, zero, merged)], axis=0
    ).astype(bf16)


def block_scores(block, upper, query_two, key_ref, gkey_ref, bias_ref, klocal_ref, kglobal_ref, qfeat_ref):
    window = pl.ds(pl.multiple_of(block * 128, 128), 384)
    query_wide = jnp.concatenate([query_two, qfeat_ref[block]], axis=1)
    key_wide = jnp.concatenate([key_ref[window, :], klocal_ref[window, :]], axis=1)
    local = dot_nt(key_wide, query_wide)
    own = local[128:256] + bias_ref[0, 0:128]
    merged = jnp.where(upper, local[0:128], local[256:384]) + bias_ref[0, 128:256]
    gkey_wide = jnp.concatenate([gkey_ref[...], kglobal_ref[0, block]], axis=1)
    return own, merged, dot_nt(gkey_wide, query_wide)


def attend_forward(
    query_ref, key_ref, value_ref, gkey_ref, gvalue_ref, bias_ref, klocal_ref, kglobal_ref, qfeat_ref,
    out_ref, log_ref, value_turned, gvalue_turned,
):
    value_turned[...] = value_ref[...].T
    gvalue_turned[...] = gvalue_ref[...].T
    upper = upper_band()

    def step(block, carry):
        rows = pl.ds(pl.multiple_of(block * 128, 128), 128)
        window = pl.ds(pl.multiple_of(block * 128, 128), 384)
        query_two = stack_heads(query_ref[rows, :])
        own, merged, far = block_scores(
            block, upper, query_two, key_ref, gkey_ref, bias_ref, klocal_ref, kglobal_ref, qfeat_ref
        )
        peak = jnp.maximum(
            jnp.maximum(
                jnp.max(own, axis=0, keepdims=True), jnp.max(merged, axis=0, keepdims=True)
            ),
            jnp.max(far, axis=0, keepdims=True),
        )
        own, merged, far = jnp.exp(own - peak), jnp.exp(merged - peak), jnp.exp(far - peak)
        total = (
            jnp.sum(own, axis=0, keepdims=True)
            + jnp.sum(merged, axis=0, keepdims=True)
            + jnp.sum(far, axis=0, keepdims=True)
        )
        scale = 1.0 / total
        near_low = spread_band(upper, own * scale, merged * scale)
        far_low = (far * scale).astype(bf16)
        wide = dot_nn(value_turned[:, window], near_low) + dot_nn(gvalue_turned[...], far_low)
        out_ref[rows, :] = unstack_heads(wide).astype(bf16)
        log_ref[0, pl.ds(block, 1), :] = peak + jnp.log(total)
        return carry

    lax.fori_loop(0, query_ref.shape[0] // 128, step, 0)


def attend_backward(
    query_ref, grad_ref, key_ref, value_ref, gkey_ref, gvalue_ref, bias_ref, klocal_ref, kglobal_ref, qfeat_ref, log_ref,
    dquery_ref, dkey_ref, dvalue_ref, dgkey_ref, dgvalue_ref, near_ref, far_ref,
    key_turned, gkey_turned, key_sum, value_sum, gkey_sum, gvalue_sum,
):
    key_turned[...] = key_ref[...].T
    gkey_turned[...] = gkey_ref[...].T
    for total_ref in (key_sum, value_sum, gkey_sum, gvalue_sum, near_ref, far_ref):
        total_ref[...] = jnp.zeros_like(total_ref)
    upper = upper_band()
    lane = lax.broadcasted_iota(jnp.int32, (256, 128), 0)
    column = lax.broadcasted_iota(jnp.int32, (256, 128), 1)
    slot_column = (lane // 128) * 8 + (lane % 128) // 16

    def step(block, carry):
        rows = pl.ds(pl.multiple_of(block * 128, 128), 128)
        window = pl.ds(pl.multiple_of(block * 128, 128), 384)
        query_two = stack_heads(query_ref[rows, :])
        grad_two = stack_heads(grad_ref[rows, :])
        own, merged, far = block_scores(
            block, upper, query_two, key_ref, gkey_ref, bias_ref, klocal_ref, kglobal_ref, qfeat_ref
        )
        logs = log_ref[0, pl.ds(block, 1), :]
        own, merged, far = jnp.exp(own - logs), jnp.exp(merged - logs), jnp.exp(far - logs)
        value_sum[window, :] += dot_nn(spread_band(upper, own, merged), grad_two)
        gvalue_sum[...] += dot_nn(far.astype(bf16), grad_two)
        near_dot = dot_nt(value_ref[window, :], grad_two)
        own_dot = near_dot[128:256]
        merged_dot = jnp.where(upper, near_dot[0:128], near_dot[256:384])
        far_dot = dot_nt(gvalue_ref[...], grad_two)
        centre = (
            jnp.sum(own * own_dot, axis=0, keepdims=True)
            + jnp.sum(merged * merged_dot, axis=0, keepdims=True)
            + jnp.sum(far * far_dot, axis=0, keepdims=True)
        )
        own = own * (own_dot - centre)
        merged = merged * (merged_dot - centre)
        far = (far * (far_dot - centre)).astype(bf16)
        near_ref[0, 0:128, :] += own
        near_ref[0, 128:256, :] += merged
        choose = (column == slot_column + block * 16).astype(bf16)
        far_ref[0] += dot_nn(far, choose)
        near_low = spread_band(upper, own, merged)
        key_sum[window, :] += dot_nn(near_low, query_two)
        gkey_sum[...] += dot_nn(far, query_two)
        wide = dot_nn(key_turned[:, window], near_low) + dot_nn(gkey_turned[...], far)
        dquery_ref[rows, :] = unstack_heads(wide).astype(bf16)
        return carry

    lax.fori_loop(0, query_ref.shape[0] // 128, step, 0)
    dkey_ref[...] = key_sum[...].astype(bf16)
    dvalue_ref[...] = value_sum[...].astype(bf16)
    dgkey_ref[...] = gkey_sum[...].astype(bf16)
    dgvalue_ref[...] = gvalue_sum[...].astype(bf16)


def column_block(rows):
    return pl.BlockSpec((rows, 128), lambda pair: (0, pair))


def pair_block(*shape):
    zeros = (0,) * len(shape)
    return pl.BlockSpec((1,) + shape, lambda pair: (pair,) + zeros)


def fixed_block(*shape):
    zeros = (0,) * len(shape)
    return pl.BlockSpec(shape, lambda pair: zeros)


def attention_specs(rows, slots):
    blocks = rows // 128
    return [
        column_block(rows + 256),
        column_block(rows + 256),
        column_block(slots),
        column_block(slots),
        pair_block(256, 256),
        fixed_block(rows + 256, 128),
        pair_block(blocks, slots, 128),
        fixed_block(blocks, 256, 128),
    ]


def attention_forward(queries, keys, values, gkeys, gvalues, bias, klocal, kglobal, qfeat):
    rows, width = queries.shape
    slots = gkeys.shape[0]
    pairs = width // 128
    return pl.pallas_call(
        attend_forward,
        grid=(pairs,),
        in_specs=[column_block(rows)] + attention_specs(rows, slots),
        out_specs=[column_block(rows), pair_block(rows // 128, 256)],
        out_shape=[
            jax.ShapeDtypeStruct((rows, width), bf16),
            jax.ShapeDtypeStruct((pairs, rows // 128, 256), f32),
        ],
        scratch_shapes=[pltpu.VMEM((128, rows + 256), bf16), pltpu.VMEM((128, slots), bf16)],
        compiler_params=pltpu.CompilerParams(vmem_limit_bytes=48 << 20),
        cost_estimate=pl.CostEstimate(
            flops=8 * rows * (384 + slots) * width, bytes_accessed=16 << 20, transcendentals=0
        ),
    )(queries, keys, values, gkeys, gvalues, bias, klocal, kglobal, qfeat)


def attention_backward(queries, grads, keys, values, gkeys, gvalues, bias, klocal, kglobal, qfeat, logs):
    rows, width = queries.shape
    slots = gkeys.shape[0]
    pairs = width // 128
    return pl.pallas_call(
        attend_backward,
        grid=(pairs,),
        in_specs=[column_block(rows), column_block(rows)]
        + attention_specs(rows, slots)
        + [pair_block(rows // 128, 256)],
        out_specs=[
            column_block(rows),
            column_block(rows + 256),
            column_block(rows + 256),
            column_block(slots),
            column_block(slots),
            pair_block(256, 256),
            pair_block(slots, 128),
        ],
        out_shape=[
            jax.ShapeDtypeStruct((rows, width), bf16),
            jax.ShapeDtypeStruct((rows + 256, width), bf16),
            jax.ShapeDtypeStruct((rows + 256, width), bf16),
            jax.ShapeDtypeStruct((slots, width), bf16),
            jax.ShapeDtypeStruct((slots, width), bf16),
            jax.ShapeDtypeStruct((pairs, 256, 256), f32),
            jax.ShapeDtypeStruct((pairs, slots, 128), f32),
        ],
        scratch_shapes=[
            pltpu.VMEM((128, rows + 256), bf16),
            pltpu.VMEM((128, slots), bf16),
            pltpu.VMEM((rows + 256, 128), f32),
            pltpu.VMEM((rows + 256, 128), f32),
            pltpu.VMEM((slots, 128), f32),
            pltpu.VMEM((slots, 128), f32),
        ],
        compiler_params=pltpu.CompilerParams(vmem_limit_bytes=48 << 20),
        cost_estimate=pl.CostEstimate(
            flops=20 * rows * (384 + slots) * width, bytes_accessed=24 << 20, transcendentals=0
        ),
    )(queries, grads, keys, values, gkeys, gvalues, bias, klocal, kglobal, qfeat, logs)


def choose_bias(bucket, table):
    chosen = jnp.zeros((), f32)
    for index in range(table.shape[0]):
        chosen = jnp.where(bucket == index, table[index], chosen)
    return chosen


def near_offset():
    place = lax.broadcasted_iota(jnp.int32, (256, 256), 0)
    query = lax.broadcasted_iota(jnp.int32, (256, 256), 1) & 127
    return ((place - query + 128) & 255) - 128


def near_bias(local_bias):
    heads, buckets = local_bias.shape
    pairs = heads // 2
    offset = near_offset()
    table = jnp.repeat(local_bias.T.reshape(buckets, pairs, 1, 2), 128, axis=3)
    chosen = choose_bias(bucket_of(offset)[None], table)
    return jnp.where((offset == -128)[None], never, chosen)


def far_features(global_bias, slot_segments, slot_live, first_slot, blocks):
    heads, buckets = global_bias.shape
    pairs = heads // 2
    slots = slot_segments.shape[0]
    shape = (1, blocks, slots, 128)
    lane = lax.broadcasted_iota(jnp.int32, shape, 3)
    query_slot = first_slot + lax.broadcasted_iota(jnp.int32, shape, 1) * 8 + (lane & 7)
    bucket = bucket_of(lax.broadcasted_iota(jnp.int32, shape, 2) - query_slot)
    per_lane = jnp.repeat(global_bias.T.reshape(buckets, pairs, 2), 8, axis=2)
    table = jnp.tile(per_lane, (1, 1, 8)).reshape(buckets, pairs, 1, 1, 128)
    chosen = choose_bias(bucket, table)
    high = lax.reduce_precision(chosen, 8, 7)
    middle = lax.reduce_precision(chosen - high, 8, 7)
    lowest = chosen - high - middle
    part = lane // 16
    allowed = (slot_segments[None, None, :, None] == lane - 48) & slot_live[None, None, :, None]
    barred = jnp.where((lane >= 48) & (lane < 51) & ~allowed, never, 0.0)
    picked = jnp.where(part == 0, high, jnp.where(part == 1, middle, jnp.where(part == 2, lowest, barred)))
    return picked.astype(bf16)


def near_features(segments_ext, valid_ext):
    lane = lax.broadcasted_iota(jnp.int32, (segments_ext.shape[0], 128), 1)
    allowed = (segments_ext[:, None] == lane - 48) & (valid_ext[:, None] > 0)
    return jnp.where((lane >= 48) & (lane < 51) & ~allowed, never, 0.0).astype(bf16)


def query_features(own_segments):
    blocks = own_segments.shape[0] // 128
    shape = (blocks, 2, 128, 128)
    lane = lax.broadcasted_iota(jnp.int32, shape, 3)
    head = lax.broadcasted_iota(jnp.int32, shape, 1)
    token = lax.broadcasted_iota(jnp.int32, shape, 2)
    on_slot = (lane < 48) & ((lane & 15) == head * 8 + token // 16)
    on_segment = lane - 48 == own_segments.reshape(blocks, 1, 128, 1)
    return (on_slot | on_segment).astype(bf16).reshape(blocks, 256, 128)


def bucket_totals(near_sums, far_sums, first_slot, buckets):
    pairs, slots, _ = far_sums.shape
    ids = jnp.arange(buckets, dtype=jnp.int32)
    offset = near_offset()[:, :128]
    near_table = (bucket_of(offset)[:, :, None] == ids).astype(f32)
    near = jnp.einsum(
        "pmai,mib->pab", near_sums.reshape(pairs, 256, 2, 128), near_table, precision=highest
    ).reshape(pairs * 2, buckets)
    blocks = far_sums.shape[2] // 16
    own_slot = first_slot + jnp.arange(blocks * 8, dtype=jnp.int32).reshape(blocks, 8)
    far_offset = jnp.arange(slots, dtype=jnp.int32)[:, None, None] - own_slot[None]
    far_table = (bucket_of(far_offset)[..., None] == ids).astype(f32)
    far = jnp.einsum(
        "pgnat,gntb->pab", far_sums.reshape(pairs, slots, blocks, 2, 8), far_table, precision=highest
    ).reshape(pairs * 2, buckets)
    return near, far


def neighbour_rows(rows, width):
    count = lax.axis_size("seq")
    ends = count - 1
    before = lax.ppermute(rows[-width:], "seq", [(i, (i + 1) % count) for i in range(ends)])
    after = lax.ppermute(rows[:width], "seq", [((i + 1) % count, i) for i in range(ends)])
    return before, after


def return_rows(before, after):
    count = lax.axis_size("seq")
    ends = count - 1
    to_tail = lax.ppermute(before, "seq", [((i + 1) % count, i) for i in range(ends)])
    to_head = lax.ppermute(after, "seq", [(i, (i + 1) % count) for i in range(ends)])
    return to_head, to_tail


def gather_rows(array):
    return lax.all_gather(array, both, axis=0, tiled=True)


def scatter_rows(array):
    return lax.psum_scatter(
        array.astype(bf16), both, scatter_dimension=0, tiled=True
    ).astype(f32)


def on_device(
    hidden_state,
    segment_ids,
    valid_mask,
    cotangent,
    norm_gain,
    pool_gain,
    feed_gain,
    query_weight,
    key_weight,
    value_weight,
    output_weight,
    local_bias,
    global_bias,
    gate_weight,
    up_weight,
    down_weight,
):
    inner = query_weight.shape[1]
    hidden = gate_weight.shape[1]
    w_qkv = gather_rows(jnp.concatenate([query_weight, key_weight, value_weight], axis=1))
    w_rest = gather_rows(jnp.concatenate([output_weight, gate_weight, up_weight], axis=1))
    w_down = gather_rows(down_weight)
    w_query, w_key, w_value = w_qkv[:, :inner], w_qkv[:, inner : 2 * inner], w_qkv[:, 2 * inner :]
    model_width = hidden_state.shape[2]
    w_output = w_rest[:, :model_width]
    w_gate = w_rest[:, model_width : model_width + hidden]
    w_up = w_rest[:, model_width + hidden :]
    tok_rows = hidden_state.shape[1]
    bucket_count = local_bias.shape[1]
    block_count = tok_rows // 128
    own_slots = tok_rows // 16
    row_start = lax.axis_index("seq") * tok_rows
    first_slot = row_start // 16

    gains = jnp.stack([norm_gain, pool_gain, feed_gain]).astype(f32)
    gains = lax.all_gather(lax.all_gather(gains, "batch", axis=1, tiled=True), "seq", axis=1, tiled=True)
    gain_one, gain_pool, gain_two = gains[0], gains[1], gains[2]
    marks = lax.all_gather(jnp.concatenate([segment_ids, valid_mask], axis=0), "seq", axis=1, tiled=True)
    all_segments, all_valid = marks[0], marks[1]
    slot_count = all_segments.shape[0] // 16
    own_segments = segment_ids[0]
    valid_float = valid_mask[0].astype(f32)
    slot_segments = all_segments.reshape(slot_count, 16)[:, 0]
    slot_live = jnp.sum(all_valid.reshape(slot_count, 16), axis=1) > 0
    segments_ext = lax.dynamic_slice_in_dim(
        jnp.pad(all_segments, 128, constant_values=-1), row_start, tok_rows + 256
    )
    valid_ext = lax.dynamic_slice_in_dim(jnp.pad(all_valid, 128), row_start, tok_rows + 256)
    bias_near = near_bias(local_bias)
    feat_far = far_features(global_bias, slot_segments, slot_live, first_slot, block_count)
    feat_near = near_features(segments_ext, valid_ext)
    feat_query = query_features(own_segments)

    source = hidden_state[0].astype(f32)
    normed_full, norm_pull = jax.vjp(scaled, source, gain_one)
    normed = normed_full.astype(bf16)
    pooled_raw = jnp.sum(
        (normed.astype(f32) * valid_float[:, None]).reshape(own_slots, 16, model_width), axis=1
    )
    pooled_full, pool_pull = jax.vjp(scaled, pooled_raw, gain_pool)
    pooled = lax.all_gather(pooled_full.astype(bf16), "seq", axis=0, tiled=True)
    before, after = neighbour_rows(normed, 128)
    normed_ext = jnp.concatenate([before, normed, after], axis=0)

    queries = forward_product(normed, w_query).astype(bf16)
    keys = forward_product(normed_ext, w_key).astype(bf16)
    values = forward_product(normed_ext, w_value).astype(bf16)
    gkeys = forward_product(pooled, w_key).astype(bf16)
    gvalues = forward_product(pooled, w_value).astype(bf16)
    mixture, logs = attention_forward(
        queries, keys, values, gkeys, gvalues, bias_near, feat_near, feat_far, feat_query
    )

    middle = source + forward_product(mixture, w_output)
    normed_two_full, feed_pull = jax.vjp(scaled, middle, gain_two)
    normed_two = normed_two_full.astype(bf16)
    gate_pre = forward_product(normed_two, w_gate)
    lift_pre = forward_product(normed_two, w_up)
    product_full, act_pull = jax.vjp(activate, gate_pre, lift_pre)
    product = product_full.astype(bf16)
    layer_output = (middle + forward_product(product, w_down)).astype(bf16)
    upstream = cotangent[0]
    down_delta = scatter_rows(weight_sum(product, upstream))
    product_grad = back_product(upstream, w_down)
    gate_grad, lift_grad = act_pull(product_grad)
    gate_low = gate_grad.astype(bf16)
    lift_low = lift_grad.astype(bf16)
    normed_two_grad = back_product(gate_low, w_gate) + back_product(lift_low, w_up)
    middle_norm_grad, feed_delta = feed_pull(normed_two_grad)
    middle_grad = upstream.astype(f32) + middle_norm_grad
    attn_low = middle_grad.astype(bf16)
    rest_delta = scatter_rows(
        jnp.concatenate(
            [
                weight_sum(mixture, attn_low).astype(bf16),
                weight_sum(normed_two, gate_low).astype(bf16),
                weight_sum(normed_two, lift_low).astype(bf16),
            ],
            axis=1,
        )
    )
    mixture_grad = back_product(attn_low, w_output).astype(bf16)

    query_low, key_low, value_low, gkey_low, gvalue_low, near_sums, far_sums = attention_backward(
        queries, mixture_grad, keys, values, gkeys, gvalues, bias_near, feat_near, feat_far, feat_query, logs
    )
    qkv_delta = scatter_rows(
        jnp.concatenate(
            [
                weight_sum(normed, query_low).astype(bf16),
                (weight_sum(normed_ext, key_low) + weight_sum(pooled, gkey_low)).astype(bf16),
                (weight_sum(normed_ext, value_low) + weight_sum(pooled, gvalue_low)).astype(bf16),
            ],
            axis=1,
        )
    )
    pooled_grad = back_product(gkey_low, w_key) + back_product(gvalue_low, w_value)
    pooled_grad = jnp.sum(
        lax.all_to_all(
            pooled_grad.astype(bf16).reshape(-1, own_slots, model_width), "seq", 0, 0, tiled=True
        ).astype(f32),
        axis=0,
    )
    pooled_raw_grad, pool_delta = pool_pull(pooled_grad)
    key_part = back_product(key_low, w_key) + back_product(value_low, w_value)
    to_head, to_tail = return_rows(key_part[:128].astype(bf16), key_part[-128:].astype(bf16))
    edges = jnp.concatenate(
        [to_head.astype(f32), jnp.zeros((tok_rows - 256, model_width), f32), to_tail.astype(f32)]
    )
    normed_grad = back_product(query_low, w_query) + key_part[128:-128] + edges
    spread_grad = jnp.broadcast_to(
        pooled_raw_grad[:, None, :], (own_slots, 16, model_width)
    ).reshape(tok_rows, model_width)
    normed_grad = normed_grad + spread_grad * valid_float[:, None]
    source_grad, norm_delta = norm_pull(normed_grad)
    input_delta = middle_grad + source_grad
    local_delta, global_delta = bucket_totals(near_sums, far_sums, first_slot, bucket_count)
    small = jnp.concatenate(
        [norm_delta, pool_delta, feed_delta, local_delta.reshape(-1), global_delta.reshape(-1)]
    ).reshape(1, -1)
    small = jnp.sum(lax.all_gather(small, "batch", axis=0, tiled=True), axis=0, keepdims=True)
    small = jnp.sum(lax.all_gather(small, "seq", axis=0, tiled=True), axis=0)
    own_part = norm_gain.shape[0]
    place = (lax.axis_index("seq") * lax.axis_size("batch") + lax.axis_index("batch")) * own_part
    gain_deltas = [
        lax.dynamic_slice_in_dim(small[i * model_width : (i + 1) * model_width], place, own_part)
        for i in range(3)
    ]
    bias_size = local_bias.size
    local_total = small[3 * model_width : 3 * model_width + bias_size].reshape(local_bias.shape)
    global_total = small[3 * model_width + bias_size :].reshape(local_bias.shape)
    return (
        layer_output[None],
        input_delta[None],
        gain_deltas[0],
        gain_deltas[1],
        gain_deltas[2],
        qkv_delta[:, :inner],
        qkv_delta[:, inner : 2 * inner],
        qkv_delta[:, 2 * inner :],
        rest_delta[:, :model_width],
        local_total,
        global_total,
        rest_delta[:, model_width : model_width + hidden],
        rest_delta[:, model_width + hidden :],
        down_delta,
    )


def solution(mesh):
    row = P(both)
    matrix = P(both, None)
    return jax.shard_map(
        on_device,
        mesh=mesh,
        in_specs=(
            P("batch", "seq", None),
            P("batch", "seq"),
            P("batch", "seq"),
            P("batch", "seq", None),
            row,
            row,
            row,
            matrix,
            matrix,
            matrix,
            matrix,
            P(),
            P(),
            matrix,
            matrix,
            matrix,
        ),
        out_specs=(
            P("batch", "seq", None),
            P("batch", "seq", None),
            row,
            row,
            row,
            matrix,
            matrix,
            matrix,
            matrix,
            P(),
            P(),
            matrix,
            matrix,
            matrix,
        ),
        check_vma=False,
    )
```

time: 1520 us -> 606 us (0.40)
  waiting for transfers between devices: 756 us -> 148 us
  local copies, waits for them, and re-layouts: 229 us -> 64.4 us
  matrix products: 272 us -> 122 us
  Pallas kernels: 0 us -> 98.2 us
  blocking collectives: 116 us -> 63.8 us
  other arithmetic: 107 us -> 70.7 us
    reduce_scatter x7 -> x2, waiting for transfers between devices: 643 us -> 122 us  [scatter_rows(): lax.psum_scatter(array.astype(bf16), both, scatter_dimension=0, tiled=True)]
    dot_general x63 -> x29, matrix products: 272 us -> 122 us  [the longest x9 46.8 us: forward_product(): return jnp.dot(left, right, preferred_element_type=f32)]
    pallas_call x0 -> x2, Pallas kernels: none -> 98.2 us  [the longest x1 58.7 us: attention_backward(): pl.pallas_call(attend_backward, grid=(pairs,), in_specs=[column_block(row...]
    unnamed x2 -> x0, blocking collectives: 78.8 us -> none
    all_gather x7 -> x3, waiting for transfers between devices: 89.3 us -> 19.3 us  [gather_rows(): return lax.all_gather(array, both, axis=0, tiled=True)]
    dynamic_update_slice x14 -> x0, local copies, waits for them, and re-layouts: 53.7 us -> none  [the longest x10 49 us: on_device(): lax.scan(backward_step, zero_state, steps_index)]
    reduce_sum x9 -> x5, other arithmetic: 47 us -> 3.05 us  [the longest x1 2.79 us: on_device(): jnp.sum((normed.astype(f32) * valid_float[:, None]).reshape(own_slots, 16...]
    all_gather x4 -> x6, blocking collectives: 37.1 us -> 63.8 us  [the longest x1 14.5 us: on_device(): lax.all_gather(gains, 'batch', axis=1, tiled=True)]
  transfers between devices with their start and end apart: 20 -> 11, of which waited for: 11 -> 3; matrix products, arithmetic and copies ran while one was open for 22% -> 35% of each run, Pallas kernels for 0% -> 16%
where the time goes in v1:
time: 606 us; the launch traced here: 599 us
  waiting for transfers between devices  148 us (24%)
  matrix products  122 us (20%)
  Pallas kernels  98.2 us (16%)
  other arithmetic  70.7 us (12%)
  local copies, waits for them, and re-layouts  64.4 us (11%)
  blocking collectives  63.8 us (11%)
  starting transfers between devices  16.2 us (3%)
  between operations  16.1 us (3%)
    reduce_scatter x2, waiting for transfers between devices, scatter_rows(): lax.psum_scatter(array.astype(bf16), both, scatter_dimension=0, tiled=True)  122 us
    pallas_call x1, Pallas kernels, attention_backward(): pl.pallas_call(attend_backward, grid=(pairs,), in_specs=[column_block(row...  58.7 us
    dot_general x9, matrix products, forward_product(): return jnp.dot(left, right, preferred_element_type=f32)  46.8 us
    dot_general x9, matrix products, back_product(): return jnp.einsum('ra,ba->rb', left, right, preferred_element_type=f32)  42.4 us
    pallas_call x1, Pallas kernels, attention_forward(): pl.pallas_call(attend_forward, grid=(pairs,), in_specs=[column_block(rows...  39.6 us
    unnamed x165, local copies, waits for them, and re-layouts  27.7 us
    dot_general x9, matrix products, weight_sum(): return jnp.einsum('ra,rb->ab', left, right, preferred_element_type=f32)  27.3 us
    convert_element_type x1, other arithmetic, far_features(): return picked.astype(bf16)  25.3 us
  transfers between devices with their start and end apart: 11, of which 3 were waited for; matrix products, arithmetic and copies ran while one was open for 35% of the time, Pallas kernels for 16%

profile of v1, /device:TPU:0, one launch (start us, length us, event | category | flops | bytes accessed | tf_op | source)
XLA Modules:
  0.0 598.9 jit_solution(16610365430259147094)
XLA Ops:
  11.3 14.5 %all-gather.2 = f32[8,24,3]{1,2,0:T(4,128)S(1)} all-gather(f32[1,24,3]{1,2,0:T(4,128)S(1)} %convert_bitcast_fusion), channel_id=1, replica_groups=mesh['seq'=4,'batch'=8] {'batch'}, dimensions={0}, use_global_device_ids=true | all-gather | bytes 2592 | tf_op jit(solution)/shard_map/all_gather | solution.py:418
  25.9 8.2 %all-gather.3 = f32[4,192,3]{1,2,0:T(4,128)S(1)} all-gather(f32[1,192,3]{1,2,0:T(4,128)S(1)} %reshape.1642), channel_id=1, replica_groups=mesh['seq'=4,'batch'=8] {'seq'}, dimensions={0}, use_global_device_ids=true | all-gather | bytes 11520 | tf_op jit(solution)/shard_map/all_gather | solution.py:418
  36.9 4.2 collective-permute-start
  47.5 9.5 %all_gather.31 = s32[2,4096]{1,0:T(2,128)S(1)} all-gather(s32[2,1024]{1,0:T(2,128)S(1)} %pad_add_fusion), channel_id=1, replica_groups=mesh['seq'=4,'batch'=8] {'seq'}, dimensions={1}, use_global_device_ids=true | all-gather | bytes 40960 | tf_op jit(solution)/shard_map/all_gather | solution.py:420
  62.6 2.8 multiply_reduce_fusion.3
  66.2 8.7 %all_gather.30 = bf16[256,768]{1,0:T(8,128)(2,1)S(1)} all-gather(bf16[64,768]{1,0:T(8,128)(2,1)S(1)} %multiply_convert_fusion.4), channel_id=1, replica_groups=mesh['seq'=4,'batch'=8] {'seq'}, dimensions={0}, use_global_device_ids=true | all-gather | bytes 491520 | tf_op jit(solution)/shard_map/all_gather | solution.py:443
  85.3 2.8 copy.123
  92.3 6.8 %select_select_fusion.bias_ref = f32[6,256,256]{2,1,0:T(8,128)} fusion(f32[6,256]{1,0:T(8,128)S(1)} %get-tuple-element.270, f32[6,256]{1,0:T(8,128)S(1)} %get-tuple-element.271, f32[6,256]{1,0:T(8,128)S(1)} %get-tuple-element.272, f32[6,256]{1,0:T(8,128)S(1)} %get-tuple-element.273, f32[6,256]{1,0:T(8,128)S(1)} %get-tuple-element.274, ...), kind=kLoop, calls=%fused_computation.80 | loop fusion | flops 12976128 | bytes 3932160 | tf_op jit(solution)/shard_map/jit(_where)/select_n | solution.py:297
  99.0 7.6 %broadcast_compare_fusion.26 = (pred[8,256,128]{2,1,0:T(8,128)(4,1)S(1)}, pred[8,256,128]{2,1,0:T(8,128)(4,1)S(1)}, pred[8,256,128]{2,1,0:T(8,128)(4,1)S(1)}, pr...) fusion(s32[128]{0:T(128)S(1)} %iota_and_fusion.2, ...), kind=kLoop, calls=%fused_computation.153 | loop fusion | flops 15990784 | bytes 8389152 | tf_op jit(solution)/shard_map/eq | solution.py:281
  106.6 25.3 %fusion.7.kglobal_ref = bf16[6,8,256,128]{3,2,1,0:T(8,128)(2,1)} fusion(bf16[8,256,128]{2,1,0:T(8,128)(2,1)S(1)} %and_select_fusion, f32[6,128]{1,0:T(8,128)S(1)} %tile.194, f32[6,128]{1,0:T(8,128)S(1)} %tile.192, f32[6,128]{1,0:T(8,128)S(1)} %tile.190, f32[6,128]{1,0:T(8,128)S(1)} %tile.188, f32[6,128]{1,0:T(8,128)S(1)} %tile.186, f32[6,128]{1,0:T(8,128)S(1)} %tile.184, ...), kind=kLoop, calls=%fused_computation.17 | loop fusion | flops 61341696 | bytes 12943360 | tf_op jit(solution)/shard_map/convert_element_type | solution.py:318
  131.9 9.2 %fusion.39 = f32[1024,2048]{1,0:T(8,128)} fusion(bf16[2048,768]{1,0:T(8,128)(2,1)} %all-gather.12.cloned.1.call-done, bf16[1,1024,768]{2,1,0:T(8,128)(2,1)} %param.19), kind=kOutput, calls=%fused_computation.78 | convolution fusion | flops 3221225472 | bytes 13107200 | tf_op jit(solution)/shard_map/ra,ba->rb/dot_general | solution.py:44
  142.9 2.9 convolution_convert_fusion.6.query_ref
  146.3 4.2 convolution_convert_fusion.3.value_ref
  150.4 4.0 convolution_convert_fusion.4.key_ref
  154.4 39.6 %shard_map.263 = (bf16[1024,768]{1,0:T(8,128)(2,1)S(1)}, f32[6,8,256]{2,1,0:T(8,128)S(1)}) custom-call(bf16[1024,768]{1,0:T(8,128)(2,1)S(1)} %convolution_convert_fusion.6.query_ref, bf16[1280,768]{1,0:T(8,128)(2,1)} %convolution_convert_fusion.4.key_ref, bf16[1280,768]{1,0:T(8,128)(2,1)} %convolution_convert_fusion.3.value_ref, ...), custom_call_target="tpu_custom_call" | custom-call | flops 4026531840 | bytes 16777216 | tf_op jit(solution)/shard_map/pallas_call | solution.py:218
  194.0 19.3 %all-gather.10.cloned.1.call-done = bf16[768,4864]{1,0:T(8,128)(2,1)} async-done(((bf16[24,4864]{1,0:T(8,128)(2,1)}), bf16[768,4864]{1,0:T(8,128)(2,1)}) %all-gather.10.cloned.1.call-update) | async-done | bytes 7471120 | tf_op jit(solution)/shard_map/all_gather | solution.py:373
  213.3 3.5 multiply_reduce_fusion.2
  217.3 5.8 fusion.25
  223.1 15.2 %fusion.6 = (bf16[1024,2048]{1,0:T(8,128)(2,1)}, bf16[1024,2048]{1,0:T(8,128)(2,1)}, bf16[1024,2048]{1,0:T(8,128)(2,1)}) fusion(f32[1024,2048]{1,0:T(8,128)} %fusion.39, f32[1024,2048]{1,0:T(8,128)} %fusion.25, bf16[1024,768]{0,1:T(8,128)(2,1)S(1)} %multiply_convert_fusion.2, bf16[768,4864]{1,0:T(8,128)(2,1)S(1)} %bitcast.259), kind=kOutput, calls=%fused_computation.12 | convolution fusion | flops 3275751424 | bytes 34078720 | tf_op jit(solution)/shard_map/dot_general | solution.py:36
  238.3 5.4 fusion.23
  243.8 6.2 %multiply_reduce_fusion = (f32[768]{0:T(1024)}, f32[1024]{0:T(1024)S(1)}, f32[1024,768]{0,1:T(8,128)}) fusion(f32[1024,768]{0,1:T(8,128)S(1)} %get-tuple-element.265, f32[1024]{0:T(1024)S(1)} %fusion.95, f32[768]{0:T(1024)S(1)} %get-tuple-element.110, f32[1024,768]{0,1:T(8,128)S(1)} %fusion.23, bf16[1024,2048]{1,0:T(8,128)(2,1)S(1)} %copy-done.54, ...), kind=kOutput, calls=%fused_computation.48 | convolution fusion | flops 3226728704 | bytes 16792576 | tf_op jit(solution)/shard_map/ra,ba->rb/dot_general | solution.py:44
  250.0 5.0 convolution_convert_fusion
  256.4 3.6 fusion.12
  260.0 4.9 convolution_convert_fusion.5.grad_ref
  264.9 58.7 %shard_map.264 = (bf16[1024,768]{1,0:T(8,128)(2,1)S(1)}, bf16[1280,768]{1,0:T(8,128)(2,1)}, bf16[1280,768]{1,0:T(8,128)(2,1)}, bf16[256,768]{1,0:T(8,128)(2,1)S(...) custom-call(bf16[1024,768]{1,0:T(8,128)(2,1)} %copy-done.2, ...), custom_call_target="tpu_custom_call" | custom-call | flops 10066329600 | bytes 25165824 | tf_op jit(solution)/shard_map/pallas_call | solution.py:239
  327.1 2.9 add_convert_fusion.2
  330.0 2.8 add_convert_fusion.1
  332.8 2.1 pad_maximum_fusion.1
  335.0 5.8 copy.151
  342.2 4.3 convolution_convert_fusion.7
  348.1 6.2 %convolution_convert_fusion.1 = bf16[768,2048]{1,0:T(8,128)(2,1)S(1)} fusion(bf16[1024,768]{0,1:T(8,128)(2,1)} %copy-done.27, bf16[1024,2048]{1,0:T(8,128)(2,1)} %get-tuple-element.178), kind=kOutput, calls=%fused_computation.27 | convolution fusion | flops 3222798336 | bytes 8912896 | tf_op jit(solution)/shard_map/ra,rb->ab/dot_general | solution.py:40
  354.4 3.6 convolution_convert_fusion.2
  358.0 3.4 pad_maximum_fusion
  363.1 3.7 fusion.76
  366.9 3.7 fusion.103
  371.3 4.4 collective-permute-start.2
  378.7 4.4 all-to-all-start
  385.0 9.0 %fusion.41 = bf16[1,1024,768]{1,2,0:T(8,128)(2,1)} fusion(f32[1024,768]{0,1:T(8,128)} %copy-done.7, bf16[1024,2048]{1,0:T(8,128)(2,1)} %get-tuple-element.179, bf16[2048,768]{1,0:T(8,128)(2,1)} %all-gather.12.cloned.1.call-done), kind=kOutput, calls=%fused_computation.83 | convolution fusion | flops 3222798336 | bytes 12058624 | tf_op jit(solution)/shard_map/dot_general | solution.py:36
  394.1 3.1 fusion.46
  400.9 2.6 copy.137
  408.4 3.7 copy.129
  412.2 7.7 %fusion.20 = (f32[768]{0:T(1024)S(1)}, f32[1024]{0:T(1024)}, f32[1024,768]{0,1:T(8,128)}) fusion(bf16[1,1024,768]{1,2,0:T(8,128)(2,1)S(1)} %copy-done.6, f32[1024]{0:T(1024)S(1)} %copy-done.36, f32[768]{0:T(1024)S(1)} %copy-done.32, f32[1024,768]{0,1:T(8,128)} %copy.129, f32[1024]{0:T(1024)} %bitcast.254, f32[128,768]{0,1:T(8,128)} %convert_element_type.2103, ...), kind=kOutput, calls=%fused_computation.45 | convolution fusion | flops 1218181376 | bytes 14571520 | tf_op jit(solution)/shard_map/ra,ba->rb/dot_general | solution.py:44
  420.0 13.9 %all-gather = f32[24576]{0:T(1024)S(1)} all-gather(f32[3072]{0:T(1024)S(1)} %constant_dynamic-update-slice_fusion), channel_id=2, replica_groups=mesh['seq'=4,'batch'=8] {'batch'}, dimensions={0}, use_global_device_ids=true | all-gather | bytes 110592 | tf_op jit(solution)/shard_map/all_gather | solution.py:523
  434.0 8.9 %all-gather.1 = f32[12288]{0:T(1024)S(1)} all-gather(f32[3072]{0:T(1024)S(1)} %reduce_sum.162), channel_id=3, replica_groups=mesh['seq'=4,'batch'=8] {'seq'}, dimensions={0}, use_global_device_ids=true | all-gather | bytes 61440 | tf_op jit(solution)/shard_map/all_gather | solution.py:524
  446.8 5.3 fusion.14
  452.0 3.5 copy.138
  457.2 6.0 %reduce-scatter.10.cloned.1.call-done = bf16[24,2304]{1,0:T(8,128)(2,1)} async-done(((bf16[768,2304]{1,0:T(8,128)(2,1)}), bf16[24,2304]{1,0:T(8,128)(2,1)}) %reduce-scatter.10.cloned.1.call-update) | async-done | bytes 110608
  466.9 121.6 %reduce-scatter.6.cloned.1.call-done = bf16[24,4864]{1,0:T(8,128)(2,1)} async-done(((bf16[768,4864]{1,0:T(8,128)(2,1)}), bf16[24,4864]{1,0:T(8,128)(2,1)}) %reduce-scatter.6.cloned.1.call-update) | async-done | bytes 233488 | tf_op jit(solution)/shard_map/reduce_scatter | solution.py:377
  (493 shorter events, 72.3 us)
Async XLA Ops:
  7.2 124.7 %all-gather.12.cloned.1.call-start = ((), (), s32[]{:S(2)}) async-start(), calls=%async_computation.6 | async-start | bytes 3244032 | tf_op jit(solution)/shard_map/all_gather | solution.py:373
  7.9 133.1 %all-gather.8.cloned.1.call-start = ((), (), s32[]{:S(2)}) async-start(), calls=%async_computation.4 | async-start | bytes 3649536 | tf_op jit(solution)/shard_map/all_gather | solution.py:373
  9.5 203.8 %all-gather.10.cloned.1.call-start = ((), (), s32[]{:S(2)}) async-start(), calls=%async_computation.5 | async-start | bytes 7704576 | tf_op jit(solution)/shard_map/all_gather | solution.py:373
  11.2 68.8 %copy-start.5 = (bf16[1,1024,768]{1,2,0:T(8,128)(2,1)}, bf16[1,1024,768]{1,2,0:T(8,128)(2,1)S(1)}, u32[]{:S(2)}) copy-start(bf16[1,1024,768]{1,2,0:T(8,128)(2,1)S(1)} %copy.118) | copy-start | bytes 4718596
  11.3 31.2 %copy-start.29 = (bf16[24,2048]{1,0:T(8,128)(2,1)S(1)}, bf16[24,2048]{1,0:T(8,128)(2,1)}, u32[]{:S(2)}) copy-start(bf16[24,2048]{1,0:T(8,128)(2,1)} %param.30) | copy-start | bytes 294916
  11.3 31.2 %copy-start.30 = (bf16[24,2048]{1,0:T(8,128)(2,1)S(1)}, bf16[24,2048]{1,0:T(8,128)(2,1)}, u32[]{:S(2)}) copy-start(bf16[24,2048]{1,0:T(8,128)(2,1)} %param.29) | copy-start | bytes 294916
  11.3 31.2 %copy-start.39 = (bf16[24,768]{1,0:T(8,128)(2,1)S(1)}, bf16[24,768]{1,0:T(8,128)(2,1)}, u32[]{:S(2)}) copy-start(bf16[24,768]{1,0:T(8,128)(2,1)} %param.26) | copy-start | bytes 110596
  34.1 9.2 %copy-start.10 = (f32[12,32]{1,0:T(8,128)S(1)}, f32[12,32]{1,0:T(8,128)}, u32[]{:S(2)}) copy-start(f32[12,32]{1,0:T(8,128)} %param.28) | copy-start | bytes 4612
  34.2 28.4 %copy-start.31 = (f32[768]{0:T(1024)}, f32[768]{0:T(1024)S(1)}, u32[]{:S(2)}) copy-start(f32[768]{0:T(1024)S(1)} %get-tuple-element.112) | copy-start | bytes 9220
  34.2 31.9 %copy-start.33 = (f32[768]{0:T(1024)}, f32[768]{0:T(1024)S(1)}, u32[]{:S(2)}) copy-start(f32[768]{0:T(1024)S(1)} %get-tuple-element.111) | copy-start | bytes 9220
  34.3 10.0 %copy-start.11 = (f32[12,32]{1,0:T(8,128)S(1)}, f32[12,32]{1,0:T(8,128)}, u32[]{:S(2)}) copy-start(f32[12,32]{1,0:T(8,128)} %param.27) | copy-start | bytes 4612
  34.6 12.8 %copy-start.37 = (f32[1024]{0:T(1024)}, f32[1024]{0:T(1024)S(1)}, u32[]{:S(2)}) copy-start(f32[1024]{0:T(1024)S(1)} %fusion.21) | copy-start | bytes 12292
  34.7 12.8 %copy-start.35 = (f32[1024]{0:T(1024)}, f32[1024]{0:T(1024)S(1)}, u32[]{:S(2)}) copy-start(f32[1024]{0:T(1024)S(1)} %fusion.94) | copy-start | bytes 12292
  36.9 10.5 %copy-start.40 = (s32[1,1024]{1,0:T(1,128)S(1)}, s32[1,1024]{1,0:T(1,128)}, u32[]{:S(2)}) copy-start(s32[1,1024]{1,0:T(1,128)} %param.18) | copy-start | bytes 12292
  36.9 10.5 %copy-start.41 = (s32[1,1024]{1,0:T(1,128)S(1)}, s32[1,1024]{1,0:T(1,128)}, u32[]{:S(2)}) copy-start(s32[1,1024]{1,0:T(1,128)} %param.17) | copy-start | bytes 12292
  36.9 109.3 %collective-permute-start = (bf16[128,768]{0,1:T(8,128)(2,1)}, bf16[128,768]{0,1:T(8,128)(2,1)}, u32[]{:S(2)}, u32[]{:S(2)}) collective-permute-start(bf16[128,768]{0,1:T(8,128)(2,1)} %get-tuple-element.182), channel_id=1, source_target_pairs={{0,8},{8,16},{16,24},{1,9},{9,17},{17,25},{2,10},{10,18},{18,26},{... | collective-permute-start | bytes 589832 | tf_op jit(solution)/shard_map/ppermute | solution.py:359
  41.2 105.1 %collective-permute-start.1 = (bf16[128,768]{0,1:T(8,128)(2,1)S(1)}, bf16[128,768]{0,1:T(8,128)(2,1)}, u32[]{:S(2)}, u32[]{:S(2)}) collective-permute-start(bf16[128,768]{0,1:T(8,128)(2,1)S(1)} %get-tuple-element.183), channel_id=1, source_target_pairs={{8,0},{16,8},{24,16},{9,1},{17,9},{25,17},{10,2},{18,10},{26,18},{... | collective-permute-start | bytes 589832 | tf_op jit(solution)/shard_map/ppermute | solution.py:360
  43.2 412.4 %reduce-scatter.8.cloned.1.call-start = ((), (), s32[]{:S(2)}) async-start(), calls=%async_computation.8 | async-start | bytes 3244032 | tf_op jit(solution)/shard_map/reduce_scatter | solution.py:377
  65.4 22.7 %copy-start.15 = (f32[64,768]{1,0:T(8,128)}, f32[64,768]{1,0:T(8,128)S(1)}, u32[]{:S(2)}) copy-start(f32[64,768]{1,0:T(8,128)S(1)} %multiply_reduce_fusion.3) | copy-start | bytes 589828
  65.6 22.5 %copy-start.45 = (f32[64]{0:T(128)}, f32[64]{0:T(128)S(1)}, u32[]{:S(2)}) copy-start(f32[64]{0:T(128)S(1)} %fusion.96) | copy-start | bytes 772
  74.9 66.2 %copy-start.19 = (bf16[256,768]{1,0:T(8,128)(2,1)}, bf16[256,768]{1,0:T(8,128)(2,1)S(1)}, u32[]{:S(2)}) copy-start(bf16[256,768]{1,0:T(8,128)(2,1)S(1)} %all_gather.30) | copy-start | bytes 1179652
  131.9 10.9 %copy-start.23 = (bf16[1024,768]{0,1:T(8,128)(2,1)S(1)}, bf16[1024,768]{0,1:T(8,128)(2,1)}, u32[]{:S(2)}) copy-start(bf16[1024,768]{0,1:T(8,128)(2,1)} %copy-done.22) | copy-start | bytes 4718596
  145.7 8.7 %copy-start.2 = (bf16[1024,768]{1,0:T(8,128)(2,1)}, bf16[1024,768]{1,0:T(8,128)(2,1)S(1)}, u32[]{:S(2)}) copy-start(bf16[1024,768]{1,0:T(8,128)(2,1)S(1)} %convolution_convert_fusion.6.query_ref) | copy-start | bytes 4718596
  194.0 22.8 %copy-start = (bf16[1024,768]{1,0:T(8,128)(2,1)}, bf16[1024,768]{1,0:T(8,128)(2,1)S(1)}, u32[]{:S(2)}) copy-start(bf16[1024,768]{1,0:T(8,128)(2,1)S(1)} %get-tuple-element.23) | copy-start | bytes 4718596
  216.8 26.9 %copy-start.7 = (f32[1024,768]{0,1:T(8,128)}, f32[1024,768]{0,1:T(8,128)S(1)}, u32[]{:S(2)}) copy-start(f32[1024,768]{0,1:T(8,128)S(1)} %get-tuple-element.265) | copy-start | bytes 9437188
  217.3 5.8 copy-start.27
  238.3 5.4 copy-start.54
  243.7 6.2 %copy-start.26 = (bf16[1,1024,768]{2,1,0:T(8,128)(2,1)S(1)}, bf16[1,1024,768]{2,1,0:T(8,128)(2,1)}, u32[]{:S(2)}) copy-start(bf16[1,1024,768]{2,1,0:T(8,128)(2,1)} %param.19) | copy-start | bytes 4718596
  243.7 6.2 %copy-start.56 = (bf16[1024,2048]{1,0:T(8,128)(2,1)S(1)}, bf16[1024,2048]{1,0:T(8,128)(2,1)}, u32[]{:S(2)}) copy-start(bf16[1024,2048]{1,0:T(8,128)(2,1)} %get-tuple-element.179) | copy-start | bytes 12582916
  255.0 208.2 %reduce-scatter.10.cloned.1.call-start = ((), (), s32[]{:S(2)}) async-start(), calls=%async_computation.9 | async-start | bytes 3649536
  264.9 58.7 %copy-start.21 = (bf16[256,768]{1,0:T(8,128)(2,1)S(1)}, bf16[256,768]{1,0:T(8,128)(2,1)}, u32[]{:S(2)}) copy-start(bf16[256,768]{1,0:T(8,128)(2,1)} %copy-done.19) | copy-start | bytes 1179652
  340.8 247.7 %reduce-scatter.6.cloned.1.call-start = ((), (), s32[]{:S(2)}) async-start(), calls=%async_computation.7 | async-start | bytes 7704576 | tf_op jit(solution)/shard_map/reduce_scatter | solution.py:377
  348.1 6.3 %copy-start.28 = (bf16[1024,768]{0,1:T(8,128)(2,1)S(1)}, bf16[1024,768]{0,1:T(8,128)(2,1)}, u32[]{:S(2)}) copy-start(bf16[1024,768]{0,1:T(8,128)(2,1)} %copy-done.27) | copy-start | bytes 4718596
  348.1 6.3 %copy-start.55 = (bf16[1024,2048]{1,0:T(8,128)(2,1)S(1)}, bf16[1024,2048]{1,0:T(8,128)(2,1)}, u32[]{:S(2)}) copy-start(bf16[1024,2048]{1,0:T(8,128)(2,1)} %get-tuple-element.177) | copy-start | bytes 12582916
  371.3 11.8 %copy-start.25 = (f32[6,256,256]{2,1,0:T(8,128)S(1)}, f32[6,256,256]{2,1,0:T(8,128)}, u32[]{:S(2)}) copy-start(f32[6,256,256]{2,1,0:T(8,128)} %get-tuple-element.30) | copy-start | bytes 4718596
  371.3 32.2 %collective-permute-start.2 = (bf16[128,768]{0,1:T(8,128)(2,1)S(1)}, bf16[128,768]{0,1:T(8,128)(2,1)}, u32[]{:S(2)}, u32[]{:S(2)}) collective-permute-start(bf16[128,768]{0,1:T(8,128)(2,1)S(1)} %get-tuple-element.180), channel_id=1, source_target_pairs={{0,8},{8,16},{16,24},{1,9},{9,17},{17,25},{2,10},{10,18},{18,26},{... | collective-permute-start | bytes 589832 | tf_op jit(solution)/shard_map/ppermute | solution.py:368
  375.7 28.8 %collective-permute-start.3 = (bf16[128,768]{0,1:T(8,128)(2,1)}, bf16[128,768]{0,1:T(8,128)(2,1)}, u32[]{:S(2)}, u32[]{:S(2)}) collective-permute-start(bf16[128,768]{0,1:T(8,128)(2,1)} %get-tuple-element.181), channel_id=1, source_target_pairs={{8,0},{16,8},{24,16},{9,1},{17,9},{25,17},{10,2},{18,10},{26,18},{... | collective-permute-start | bytes 589832 | tf_op jit(solution)/shard_map/ppermute | solution.py:367
  378.7 27.4 %all-to-all-start = ((bf16[4,64,768]{2,1,0:T(8,128)(2,1)}), bf16[4,64,768]{2,1,0:T(8,128)(2,1)S(1)}, u32[]{:S(2)}, u32[]{:S(2)}) async-start(bf16[4,64,768]{2,1,0:T(8,128)(2,1)} %bitcast.20), calls=%async_computation | async-start | bytes 786432 | tf_op jit(solution)/shard_map/all_to_all | solution.py:501
  385.0 9.0 %copy-start.9 = (f32[6,256,256]{1,0,2:T(8,128)S(1)}, f32[6,256,256]{1,0,2:T(8,128)}, u32[]{:S(2)}) copy-start(f32[6,256,256]{1,0,2:T(8,128)} %copy.150) | copy-start | bytes 4718596
  398.1 8.1 %copy-start.16 = (f32[64,768]{1,0:T(8,128)S(1)}, f32[64,768]{1,0:T(8,128)}, u32[]{:S(2)}) copy-start(f32[64,768]{1,0:T(8,128)} %copy-done.15) | copy-start | bytes 589828
  398.2 8.1 %copy-start.34 = (f32[768]{0:T(1024)S(1)}, f32[768]{0:T(1024)}, u32[]{:S(2)}) copy-start(f32[768]{0:T(1024)} %copy-done.33) | copy-start | bytes 9220
  398.2 8.1 %copy-start.46 = (f32[64]{0:T(128)S(1)}, f32[64]{0:T(128)}, u32[]{:S(2)}) copy-start(f32[64]{0:T(128)} %copy-done.45) | copy-start | bytes 772
  398.2 8.2 %copy-start.49 = (f32[64]{0:T(128)S(1)}, f32[64]{0:T(128)}, u32[]{:S(2)}) copy-start(f32[64]{0:T(128)} %copy-done.48) | copy-start | bytes 772
  412.2 7.7 %copy-start.42 = (f32[3072]{0:T(1024)S(1)}, f32[3072]{0:T(1024)}, u32[]{:S(2)}) copy-start(f32[3072]{0:T(1024)} %custom-call) | copy-start | bytes 36868
  412.2 7.7 %copy-start.47 = (f32[768]{0:T(1024)S(1)}, f32[768]{0:T(1024)}, u32[]{:S(2)}) copy-start(f32[768]{0:T(1024)} %get-tuple-element.102) | copy-start | bytes 9220
  412.2 7.7 %copy-start.43 = (f32[384]{0:T(512)S(1)}, f32[384]{0:T(512)}, u32[]{:S(2)}) copy-start(f32[384]{0:T(512)} %reshape_reshape.6) | copy-start | bytes 4612
  412.2 7.7 %copy-start.44 = (f32[384]{0:T(512)S(1)}, f32[384]{0:T(512)}, u32[]{:S(2)}) copy-start(f32[384]{0:T(512)} %reshape_reshape.7) | copy-start | bytes 4612
  412.2 33.9 %copy-start.38 = (f32[1024]{0:T(1024)S(1)}, f32[1024]{0:T(1024)}, u32[]{:S(2)}) copy-start(f32[1024]{0:T(1024)} %copy-done.37) | copy-start | bytes 12292
  (22 other events, 65.5 us)
Sparse Core Ops, SparseCore 0:
  11.1 63.3 all-gather.11
  78.1 59.2 all-gather.7
  140.4 72.8 all-gather.9
  255.1 100.4 reduce-scatter.7
  360.9 102.2 reduce-scatter.9
  468.8 119.6 reduce-scatter.5

commit v2 on v1

v2 whole, which is shorter than its diff:
```python
import jax
import jax.numpy as jnp
from jax import lax
from jax.experimental import pallas as pl
from jax.experimental.pallas import tpu as pltpu
from jax.sharding import Mesh
from jax.sharding import PartitionSpec as P

epsilon = 1e-06
boundaries = (12, 16, 23, 32, 46, 64, 91)
never = -1e30
seq = ("y", "x")
batch = ("z", "core")
everyone = seq + batch
bf16 = jnp.bfloat16
f32 = jnp.float32
i32 = jnp.int32
highest = lax.Precision.HIGHEST


def bucket_of(offset):
    distance = jnp.abs(offset)
    far_part = 8 + sum(((distance >= boundary).astype(i32) for boundary in boundaries))
    return 16 * (offset > 0).astype(i32) + jnp.where(distance < 8, distance, far_part)


def dot_nt(left, right):
    return lax.dot_general(left, right, (((1,), (1,)), ((), ())), preferred_element_type=f32)


def dot_nn(left, right):
    return lax.dot_general(left, right, (((1,), (0,)), ((), ())), preferred_element_type=f32)


def inverse_rms(values):
    return lax.rsqrt(jnp.mean(values * values, axis=-1, keepdims=True) + epsilon)


def norm_gradient(values, inverse, gain, grad):
    weighted = grad * gain
    mean = jnp.mean(weighted * values, axis=-1, keepdims=True)
    return inverse * weighted - (inverse * inverse * inverse * mean) * values


def stack_heads(rows):
    lane = lax.broadcasted_iota(i32, rows.shape, 1)
    zero = jnp.zeros_like(rows)
    return jnp.concatenate(
        [jnp.where(lane < 64, rows, zero), jnp.where(lane < 64, zero, rows)], axis=0
    )


def unstack_heads(wide):
    row = lax.broadcasted_iota(i32, (128, 128), 0)
    return jnp.where(row < 64, wide[:, :128], wide[:, 128:]).T


def upper_band():
    key = lax.broadcasted_iota(i32, (128, 256), 0)
    query = lax.broadcasted_iota(i32, (128, 256), 1) & 127
    return key > query


def spread_band(upper, own, merged):
    zero = jnp.zeros_like(merged)
    return jnp.concatenate(
        [jnp.where(upper, merged, zero), own, jnp.where(upper, zero, merged)], axis=0
    ).astype(bf16)


def window_of(block):
    return pl.ds(pl.multiple_of(block * 128, 128), 384)


def rows_of(block):
    return pl.ds(pl.multiple_of(block * 128, 128), 128)


def slot_lanes():
    row = lax.broadcasted_iota(i32, (256, 128), 0)
    lane = lax.broadcasted_iota(i32, (256, 128), 1)
    hit = (lane < 48) & ((lane & 15) == (row // 128) * 8 + (row % 128) // 16)
    return hit.astype(f32).astype(bf16)


def block_scores(block, upper, on_slot, query_two, key_ref, gkey_ref, bias_ref, klocal_ref, kglobal_ref, qfeat_ref):
    slots = gkey_ref.shape[0]
    window = window_of(block)
    segment_lanes = qfeat_ref[rows_of(block), :]
    features = jnp.concatenate([segment_lanes, segment_lanes], axis=0) + on_slot
    query_wide = jnp.concatenate([query_two, features], axis=1)
    key_wide = jnp.concatenate([key_ref[window, :], klocal_ref[window, :]], axis=1)
    local = dot_nt(key_wide, query_wide)
    own = local[128:256] + bias_ref[0, 0:128]
    merged = jnp.where(upper, local[0:128], local[256:384]) + bias_ref[0, 128:256]
    far_rows = pl.ds(pl.multiple_of(block * slots, 128), slots)
    gkey_wide = jnp.concatenate([gkey_ref[...], kglobal_ref[far_rows, :]], axis=1)
    return own, merged, dot_nt(gkey_wide, query_wide)


def attend_forward(
    source_ref, raw_ref, gain_ref, wq_ref, wk_ref, wv_ref, offsets_ref, klocal_ref, kglobal_ref, qfeat_ref,
    bias_ref, out_ref, log_ref, query_ref, key_ref, value_ref, gkey_ref, gvalue_ref, normed_ref, pooled_ref, gains_ref,
    value_turned, gvalue_turned,
):
    rows = query_ref.shape[0]
    slots = gkey_ref.shape[0]

    @pl.when(pl.program_id(0) == 0)
    def start():
        turned = gain_ref[...].astype(f32).T
        gains_ref[...] = turned[0:8]
        gain_one, gain_pool = turned[0:1], turned[1:2]

        def norm_rows(index, carry):
            part = pl.ds(pl.multiple_of(index * 128, 128), 128)
            values = source_ref[part, :].astype(f32)
            normed_ref[part, :] = (values * inverse_rms(values) * gain_one).astype(bf16)
            return carry

        lax.fori_loop(0, (rows + 256) // 128, norm_rows, 0)

        def pool_rows(index, carry):
            part = pl.ds(pl.multiple_of(index * 128, 128), 128)
            values = raw_ref[part, :].astype(f32) * gain_one
            pooled_ref[part, :] = (values * inverse_rms(values) * gain_pool).astype(bf16)
            return carry

        lax.fori_loop(0, slots // 128, pool_rows, 0)

    lane = lax.broadcasted_iota(i32, (256, 128), 1)
    spread = []
    for head in range(2):
        mine = jnp.where(lane == 2 * pl.program_id(0) + head, offsets_ref[...], 0.0)
        spread.append(jnp.broadcast_to(jnp.sum(mine, axis=1, keepdims=True), (256, 128)))
    lane_of = lax.broadcasted_iota(i32, (256, 256), 1)
    bias_ref[0] = align_offsets(jnp.concatenate(spread, axis=1), lane_of & 127, 7, -1)

    query_ref[...] = dot_nn(normed_ref[128 : 128 + rows, :], wq_ref[...]).astype(bf16)
    w_two = jnp.concatenate([wk_ref[...], wv_ref[...]], axis=1)
    two = dot_nn(normed_ref[...], w_two).astype(bf16)
    key_ref[...] = two[:, :128]
    value_ref[...] = two[:, 128:]
    value_turned[...] = two[:, 128:].T
    two = dot_nn(pooled_ref[...], w_two).astype(bf16)
    gkey_ref[...] = two[:, :128]
    gvalue_ref[...] = two[:, 128:]
    gvalue_turned[...] = two[:, 128:].T
    upper = upper_band()
    on_slot = slot_lanes()

    def step(block, carry):
        window = window_of(block)
        query_two = stack_heads(query_ref[rows_of(block), :])
        own, merged, far = block_scores(
            block, upper, on_slot, query_two, key_ref, gkey_ref, bias_ref, klocal_ref, kglobal_ref, qfeat_ref
        )
        peak = jnp.maximum(
            jnp.maximum(
                jnp.max(own, axis=0, keepdims=True), jnp.max(merged, axis=0, keepdims=True)
            ),
            jnp.max(far, axis=0, keepdims=True),
        )
        own, merged, far = jnp.exp(own - peak), jnp.exp(merged - peak), jnp.exp(far - peak)
        total = (
            jnp.sum(own, axis=0, keepdims=True)
            + jnp.sum(merged, axis=0, keepdims=True)
            + jnp.sum(far, axis=0, keepdims=True)
        )
        near_low = spread_band(upper, own, merged)
        wide = dot_nn(value_turned[:, window], near_low) + dot_nn(
            gvalue_turned[...], far.astype(bf16)
        )
        out_ref[rows_of(block), :] = unstack_heads(wide * (1.0 / total)).astype(bf16)
        log_ref[0, pl.ds(block, 1), :] = peak + jnp.log(total)
        return carry

    lax.fori_loop(0, rows // 128, step, 0, unroll=4)


def align_offsets(sums, step_of_lane, bits, sign):
    for bit in range(bits):
        shift = sign * (1 << bit)
        moved = jnp.concatenate([sums[shift:], sums[:shift]], axis=0)
        sums = jnp.where((step_of_lane >> bit) & 1 == 1, moved, sums)
    return sums


def two_totals(left, right):
    lane = lax.broadcasted_iota(i32, (left.shape[0], 128), 1)
    first = jnp.sum(left, axis=1, keepdims=True)
    second = jnp.sum(right, axis=1, keepdims=True)
    return jnp.where(lane == 0, first, jnp.where(lane == 1, second, 0.0))


def attend_backward(
    query_ref, grad_ref, key_ref, value_ref, gkey_ref, gvalue_ref, normed_ref, pooled_ref, wq_ref, wk_ref, wv_ref,
    log_ref, bias_ref, klocal_ref, kglobal_ref, qfeat_ref,
    dwq_ref, dwk_ref, dwv_ref, dnormed_ref, dpooled_ref, near_ref, far_ref,
    key_turned, gkey_turned, dquery, key_sum, value_sum, gkey_sum, gvalue_sum, near_sum, far_sum, normed_turned, pooled_turned,
):
    rows = query_ref.shape[0]
    slots = gkey_ref.shape[0]

    @pl.when(pl.program_id(0) == 0)
    def start():
        normed_turned[...] = normed_ref[...].T
        pooled_turned[...] = pooled_ref[...].T
        dnormed_ref[...] = jnp.zeros_like(dnormed_ref)
        dpooled_ref[...] = jnp.zeros_like(dpooled_ref)

    key_turned[...] = key_ref[...].T
    gkey_turned[...] = gkey_ref[...].T
    for total_ref in (key_sum, value_sum, gkey_sum, gvalue_sum, near_sum, far_sum):
        total_ref[...] = jnp.zeros_like(total_ref)
    upper = upper_band()
    on_slot = slot_lanes()
    lane = lax.broadcasted_iota(i32, (256, 128), 0)
    column = lax.broadcasted_iota(i32, (256, 128), 1)
    slot_column = (lane // 128) * 64 + (lane % 128) // 16

    def step(block, carry):
        window = window_of(block)
        query_two = stack_heads(query_ref[rows_of(block), :])
        grad_two = stack_heads(grad_ref[rows_of(block), :])
        own, merged, far = block_scores(
            block, upper, on_slot, query_two, key_ref, gkey_ref, bias_ref, klocal_ref, kglobal_ref, qfeat_ref
        )
        logs = log_ref[0, pl.ds(block, 1), :]
        own, merged, far = jnp.exp(own - logs), jnp.exp(merged - logs), jnp.exp(far - logs)
        value_sum[window, :] += dot_nn(spread_band(upper, own, merged), grad_two)
        gvalue_sum[...] += dot_nn(far.astype(bf16), grad_two)
        near_dot = dot_nt(value_ref[window, :], grad_two)
        own_dot = near_dot[128:256]
        merged_dot = jnp.where(upper, near_dot[0:128], near_dot[256:384])
        far_dot = dot_nt(gvalue_ref[...], grad_two)
        centre = (
            jnp.sum(own * own_dot, axis=0, keepdims=True)
            + jnp.sum(merged * merged_dot, axis=0, keepdims=True)
            + jnp.sum(far * far_dot, axis=0, keepdims=True)
        )
        own = own * (own_dot - centre)
        merged = merged * (merged_dot - centre)
        far = (far * (far_dot - centre)).astype(bf16)
        near_sum[0:128, :] += own
        near_sum[128:256, :] += merged
        choose = (column == slot_column + block * 8).astype(bf16)
        far_sum[...] += dot_nn(far, choose)
        near_low = spread_band(upper, own, merged)
        key_sum[window, :] += dot_nn(near_low, query_two)
        gkey_sum[...] += dot_nn(far, query_two)
        wide = dot_nn(key_turned[:, window], near_low) + dot_nn(gkey_turned[...], far)
        dquery[rows_of(block), :] = unstack_heads(wide).astype(bf16)
        return carry

    lax.fori_loop(0, rows // 128, step, 0, unroll=4)

    lane_of = lax.broadcasted_iota(i32, (256, 256), 1)
    near = align_offsets(near_sum[...], lane_of & 127, 7, 1)
    near_ref[0] = two_totals(near[:, :128], near[:, 128:])
    lane_of = lax.broadcasted_iota(i32, (slots + 64, 128), 1)
    far = jnp.concatenate([far_sum[...], jnp.zeros((64, 128), f32)], axis=0)
    far = align_offsets(far, lane_of & 63, 6, 1)
    first = lane_of < 64
    far_ref[0] = two_totals(jnp.where(first, far, 0.0), jnp.where(first, 0.0, far))

    grad_low = dquery[...]
    dwq_ref[...] = dot_nn(normed_turned[:, 128 : 128 + rows], grad_low).astype(bf16)
    dnormed_ref[128 : 128 + rows, :] += dot_nt(grad_low, wq_ref[...])
    two = jnp.concatenate([key_sum[...], value_sum[...]], axis=1).astype(bf16)
    gtwo = jnp.concatenate([gkey_sum[...], gvalue_sum[...]], axis=1).astype(bf16)
    w_two = jnp.concatenate([wk_ref[...], wv_ref[...]], axis=1)
    dw_two = (dot_nn(normed_turned[...], two) + dot_nn(pooled_turned[...], gtwo)).astype(bf16)
    dwk_ref[...] = dw_two[:, :128]
    dwv_ref[...] = dw_two[:, 128:]
    dnormed_ref[...] += dot_nt(two, w_two)
    dpooled_ref[...] += dot_nt(gtwo, w_two)


def columns(rows, first):
    return pl.BlockSpec((rows, 128), lambda pair: (0, pair + first))


def of_pair(first, *shape):
    zeros = (0,) * len(shape)
    return pl.BlockSpec((1,) + shape, lambda pair: (pair + first,) + zeros)


def fixed(*shape):
    zeros = (0,) * len(shape)
    return pl.BlockSpec(shape, lambda pair: zeros, pipeline_mode=pl.Buffered(1))


def fixed_out(*shape):
    zeros = (0,) * len(shape)
    return pl.BlockSpec(shape, lambda pair: zeros)


def attention_forward(source_ext, raw_pool, weights, bias, klocal, kglobal, qfeat):
    width = source_ext.shape[1]
    rows = source_ext.shape[0] - 256
    slots = raw_pool.shape[0]
    blocks = rows // 128
    pairs = width // 128
    return pl.pallas_call(
        attend_forward,
        grid=(pairs,),
        in_specs=[
            fixed(rows + 256, width),
            fixed(slots, width),
            pl.BlockSpec((width, 128), lambda pair: (0, 4 * pairs), pipeline_mode=pl.Buffered(1)),
            columns(width, 0),
            columns(width, pairs),
            columns(width, 2 * pairs),
            fixed(256, 128),
            fixed(rows + 256, 128),
            columns(blocks * slots, 0),
            fixed(rows, 128),
        ],
        out_specs=[
            of_pair(0, 256, 256),
            columns(rows, 0),
            of_pair(0, blocks, 256),
            columns(rows, 0),
            columns(rows + 256, 0),
            columns(rows + 256, 0),
            columns(slots, 0),
            columns(slots, 0),
            fixed_out(rows + 256, width),
            fixed_out(slots, width),
            fixed_out(8, width),
        ],
        out_shape=[
            jax.ShapeDtypeStruct((pairs, 256, 256), f32),
            jax.ShapeDtypeStruct((rows, width), bf16),
            jax.ShapeDtypeStruct((pairs, blocks, 256), f32),
            jax.ShapeDtypeStruct((rows, width), bf16),
            jax.ShapeDtypeStruct((rows + 256, width), bf16),
            jax.ShapeDtypeStruct((rows + 256, width), bf16),
            jax.ShapeDtypeStruct((slots, width), bf16),
            jax.ShapeDtypeStruct((slots, width), bf16),
            jax.ShapeDtypeStruct((rows + 256, width), bf16),
            jax.ShapeDtypeStruct((slots, width), bf16),
            jax.ShapeDtypeStruct((8, width), f32),
        ],
        scratch_shapes=[pltpu.VMEM((128, rows + 256), bf16), pltpu.VMEM((128, slots), bf16)],
        compiler_params=pltpu.CompilerParams(vmem_limit_bytes=48 << 20),
        cost_estimate=pl.CostEstimate(
            flops=30 * rows * (384 + slots) * width, bytes_accessed=24 << 20, transcendentals=0
        ),
        name="attend_forward",
    )(source_ext, raw_pool, weights, weights, weights, weights, bias, klocal, kglobal, qfeat)


def attention_backward(
    first, count, queries, grads, keys, values, gkeys, gvalues, normed, pooled, weights, logs, bias, klocal, kglobal, qfeat
):
    rows, width = queries.shape
    slots = gkeys.shape[0]
    blocks = rows // 128
    pairs = width // 128
    return pl.pallas_call(
        attend_backward,
        grid=(count,),
        in_specs=[
            columns(rows, first),
            columns(rows, first),
            columns(rows + 256, first),
            columns(rows + 256, first),
            columns(slots, first),
            columns(slots, first),
            fixed(rows + 256, width),
            fixed(slots, width),
            columns(width, first),
            columns(width, pairs + first),
            columns(width, 2 * pairs + first),
            of_pair(first, blocks, 256),
            of_pair(first, 256, 256),
            fixed(rows + 256, 128),
            columns(blocks * slots, first),
            fixed(rows, 128),
        ],
        out_specs=[
            columns(width, 0),
            columns(width, 0),
            columns(width, 0),
            fixed_out(rows + 256, width),
            fixed_out(slots, width),
            of_pair(0, 256, 128),
            of_pair(0, slots + 64, 128),
        ],
        out_shape=[
            jax.ShapeDtypeStruct((width, count * 128), bf16),
            jax.ShapeDtypeStruct((width, count * 128), bf16),
            jax.ShapeDtypeStruct((width, count * 128), bf16),
            jax.ShapeDtypeStruct((rows + 256, width), f32),
            jax.ShapeDtypeStruct((slots, width), f32),
            jax.ShapeDtypeStruct((count, 256, 128), f32),
            jax.ShapeDtypeStruct((count, slots + 64, 128), f32),
        ],
        scratch_shapes=[
            pltpu.VMEM((128, rows + 256), bf16),
            pltpu.VMEM((128, slots), bf16),
            pltpu.VMEM((rows, 128), bf16),
            pltpu.VMEM((rows + 256, 128), f32),
            pltpu.VMEM((rows + 256, 128), f32),
            pltpu.VMEM((slots, 128), f32),
            pltpu.VMEM((slots, 128), f32),
            pltpu.VMEM((256, 256), f32),
            pltpu.VMEM((slots, 128), f32),
            pltpu.VMEM((width, rows + 256), bf16),
            pltpu.VMEM((width, slots), bf16),
        ],
        compiler_params=pltpu.CompilerParams(vmem_limit_bytes=48 << 20),
        cost_estimate=pl.CostEstimate(
            flops=60 * rows * (384 + slots) * 128 * count, bytes_accessed=count << 22, transcendentals=0
        ),
        name="attend_backward",
    )(
        queries, grads, keys, values, gkeys, gvalues, normed, pooled, weights, weights, weights, logs, bias, klocal,
        kglobal, qfeat,
    )


def feed_forward(
    source_ref, mixture_ref, wo_ref, gains_ref, cot_ref, wg_ref, wu_ref, wd_ref,
    out_ref, middle_grad_ref, dmixture_ref, dwo_ref, dgain_ref, dwg_ref, dwu_ref, dwd_ref,
    middle, normed, turned, out_sum, grad_sum, product, gate_low, lift_low,
):
    rows = source_ref.shape[0]
    part_rows = 256
    parts = rows // part_rows
    gain = gains_ref[2:3, :]

    @pl.when(pl.program_id(0) == 0)
    def start():
        def norm_rows(index, carry):
            part = pl.ds(pl.multiple_of(index * 128, 128), 128)
            values = source_ref[part, :].astype(f32) + dot_nn(mixture_ref[part, :], wo_ref[...])
            middle[part, :] = values
            low = (values * inverse_rms(values) * gain).astype(bf16)
            normed[part, :] = low
            turned[:, part] = low.T
            return carry

        lax.fori_loop(0, rows // 128, norm_rows, 0)
        out_sum[...] = jnp.zeros_like(out_sum)
        grad_sum[...] = jnp.zeros_like(grad_sum)

    root = 0.7978845608028654
    for index in range(parts):
        part = slice(index * part_rows, (index + 1) * part_rows)
        low = normed[part, :]
        gate_pre = dot_nn(low, wg_ref[...])
        lift_pre = dot_nn(low, wu_ref[...])
        grad = dot_nt(cot_ref[part, :], wd_ref[...])
        square = gate_pre * gate_pre
        bent = jnp.tanh(gate_pre * (root + (root * 0.044715) * square))
        half = 0.5 + 0.5 * bent
        gelu = gate_pre * half
        slope = half + gelu * (1.0 - bent) * (root + (3 * root * 0.044715) * square)
        product[part, :] = (gelu * lift_pre).astype(bf16)
        lift_low[part, :] = (grad * gelu).astype(bf16)
        gate_low[part, :] = (grad * lift_pre * slope).astype(bf16)
        out_sum[part, :] += dot_nn(product[part, :], wd_ref[...])
        grad_sum[part, :] += dot_nt(gate_low[part, :], wg_ref[...]) + dot_nt(
            lift_low[part, :], wu_ref[...]
        )
    dwg_ref[...] = dot_nn(turned[...], gate_low[...]).astype(bf16)
    dwu_ref[...] = dot_nn(turned[...], lift_low[...]).astype(bf16)
    dwd_ref[...] = dot_nn(product[...].T, cot_ref[...]).astype(bf16)

    @pl.when(pl.program_id(0) == pl.num_programs(0) - 1)
    def finish():
        dgain_ref[...] = jnp.zeros_like(dgain_ref)

        def back_rows(index, carry):
            part = pl.ds(pl.multiple_of(index * 128, 128), 128)
            values = middle[part, :]
            out_ref[part, :] = (values + out_sum[part, :]).astype(bf16)
            inverse = inverse_rms(values)
            grad = grad_sum[part, :]
            dgain_ref[0:1, :] += jnp.sum(grad * values * inverse, axis=0, keepdims=True)
            total = cot_ref[part, :].astype(f32) + norm_gradient(values, inverse, gain, grad)
            middle_grad_ref[part, :] = total
            low = total.astype(bf16)
            normed[part, :] = low
            dmixture_ref[part, :] = dot_nt(low, wo_ref[...]).astype(bf16)
            turned[:, part] = mixture_ref[part, :].T
            return carry

        lax.fori_loop(0, rows // 128, back_rows, 0)
        dwo_ref[...] = dot_nn(turned[...], normed[...]).astype(bf16)


def feed_forward_both(source, mixture, weights, gains, cotangent, w_gate_up, w_down):
    rows, width = source.shape
    hidden = w_down.shape[0]
    tile = 256
    tiles = hidden // tile
    return pl.pallas_call(
        feed_forward,
        grid=(tiles,),
        in_specs=[
            fixed(rows, width),
            fixed(rows, width),
            pl.BlockSpec((width, width), lambda step: (0, 3), pipeline_mode=pl.Buffered(1)),
            fixed(8, width),
            fixed(rows, width),
            pl.BlockSpec((width, tile), lambda step: (0, step)),
            pl.BlockSpec((width, tile), lambda step: (0, step + tiles)),
            pl.BlockSpec((tile, width), lambda step: (step, 0)),
        ],
        out_specs=[
            fixed_out(rows, width),
            fixed_out(rows, width),
            fixed_out(rows, width),
            fixed_out(width, width),
            fixed_out(8, width),
            pl.BlockSpec((width, tile), lambda step: (0, step)),
            pl.BlockSpec((width, tile), lambda step: (0, step)),
            pl.BlockSpec((tile, width), lambda step: (step, 0)),
        ],
        out_shape=[
            jax.ShapeDtypeStruct((rows, width), bf16),
            jax.ShapeDtypeStruct((rows, width), f32),
            jax.ShapeDtypeStruct((rows, width), bf16),
            jax.ShapeDtypeStruct((width, width), bf16),
            jax.ShapeDtypeStruct((8, width), f32),
            jax.ShapeDtypeStruct((width, hidden), bf16),
            jax.ShapeDtypeStruct((width, hidden), bf16),
            jax.ShapeDtypeStruct((hidden, width), bf16),
        ],
        scratch_shapes=[
            pltpu.VMEM((rows, width), f32),
            pltpu.VMEM((rows, width), bf16),
            pltpu.VMEM((width, rows), bf16),
            pltpu.VMEM((rows, width), f32),
            pltpu.VMEM((rows, width), f32),
            pltpu.VMEM((rows, tile), bf16),
            pltpu.VMEM((rows, tile), bf16),
            pltpu.VMEM((rows, tile), bf16),
        ],
        compiler_params=pltpu.CompilerParams(vmem_limit_bytes=56 << 20),
        cost_estimate=pl.CostEstimate(
            flops=20 * rows * width * hidden, bytes_accessed=40 << 20, transcendentals=0
        ),
        name="feed_forward",
    )(source, mixture, weights, gains, cotangent, w_gate_up, w_gate_up, w_down)


def near_offsets(local_bias):
    heads, buckets = local_bias.shape
    offset = (jnp.arange(256, dtype=i32) + 128) % 256 - 128
    table = (bucket_of(offset)[:, None] == jnp.arange(buckets, dtype=i32)).astype(f32)
    chosen = jnp.einsum("ob,hb->oh", table, local_bias, precision=highest)
    chosen = jnp.where((offset == -128)[:, None], never, chosen)
    return jnp.pad(chosen, ((0, 0), (0, 128 - heads)))


def far_features(global_bias, slot_segments, slot_live, first_slot, blocks):
    heads, buckets = global_bias.shape
    pairs = heads // 2
    slots = slot_segments.shape[0]
    wide = 8 * buckets + 8
    shape = (blocks * slots, wide)
    row = lax.broadcasted_iota(i32, shape, 0)
    column = lax.broadcasted_iota(i32, shape, 1)
    slot = row % slots
    query_slot = first_slot + (row // slots) * 8 + column // buckets
    code = jnp.tile(jnp.where(slot_live, slot_segments, 3), blocks)[:, None]
    picks = jnp.where(
        column < 8 * buckets,
        bucket_of(slot - query_slot) == column % buckets,
        code == column - 8 * buckets,
    ).astype(bf16)
    high = lax.reduce_precision(global_bias, 8, 7)
    middle = lax.reduce_precision(global_bias - high, 8, 7)
    lowest = lax.reduce_precision(global_bias - high - middle, 8, 7)
    parts = jnp.stack([high, middle, lowest]).reshape(3, pairs, 2, buckets)
    parts = parts.transpose(3, 1, 0, 2)
    same = jnp.eye(8, dtype=f32)[:, None, None, None, None, :]
    table = (parts[None, :, :, :, :, None] * same).reshape(8 * buckets, pairs, 48)
    table = jnp.pad(table, ((0, 8), (0, 0), (0, 80)))
    shape = (wide, 1, 128)
    lane = lax.broadcasted_iota(i32, shape, 2) - 48
    code_row = lax.broadcasted_iota(i32, shape, 0) - 8 * buckets
    barred = (code_row >= 0) & (lane >= 0) & (lane < 3) & (lane != code_row)
    table = jnp.where(barred, never, table).astype(bf16).reshape(wide, pairs * 128)
    return jnp.dot(picks, table, preferred_element_type=f32).astype(bf16)


def near_features(segments_ext, valid_ext):
    lane = lax.broadcasted_iota(i32, (segments_ext.shape[0], 128), 1)
    allowed = (segments_ext[:, None] == lane - 48) & (valid_ext[:, None] > 0)
    return jnp.where((lane >= 48) & (lane < 51) & ~allowed, never, 0.0).astype(bf16)


def query_features(own_segments):
    lane = lax.broadcasted_iota(i32, (own_segments.shape[0], 128), 1)
    return (own_segments[:, None] == lane - 48).astype(bf16)


def bucket_totals(near_sums, far_sums, first_slot, buckets):
    heads = near_sums.shape[0] * 2
    ids = jnp.arange(buckets, dtype=i32)
    span = near_sums.shape[1]
    offset = (jnp.arange(span, dtype=i32) + 128) % span - 128
    table = (bucket_of(offset)[:, None] == ids).astype(f32)
    near = jnp.einsum("poa,ob->pab", near_sums[:, :, :2], table, precision=highest)
    span = far_sums.shape[1]
    place = jnp.arange(span, dtype=i32)
    offset = jnp.where(place < span - 64, place, place - span) - first_slot
    table = (bucket_of(offset)[:, None] == ids).astype(f32)
    far = jnp.einsum("poa,ob->pab", far_sums[:, :, :2], table, precision=highest)
    return near.reshape(heads, buckets), far.reshape(heads, buckets)


def pick(values, index, dim):
    return lax.dynamic_index_in_dim(values, index, dim, keepdims=False)


def ring(size, hop):
    return [(i, (i + hop) % size) for i in range(size)]


def split_stage(values, axis, dim):
    size, me = lax.axis_size(axis), lax.axis_index(axis)
    keep = pick(values, me, dim)
    return keep, [pick(values, (me + hop) % size, dim) for hop in range(1, size)]


def send_all(axis, pieces):
    size = lax.axis_size(axis)
    return [lax.ppermute(piece, axis, ring(size, hop + 1)) for hop, piece in enumerate(pieces)]


def join_stage(keep, pieces):
    total = keep.astype(f32)
    for piece in pieces:
        total = total + piece.astype(f32)
    return total


def place_stage(values, pieces, axis, dim):
    size, me = lax.axis_size(axis), lax.axis_index(axis)
    shape = values.shape[:dim] + (size,) + values.shape[dim:]
    out = lax.dynamic_update_index_in_dim(jnp.zeros(shape, values.dtype), values, me, dim)
    for hop, piece in enumerate(pieces):
        out = lax.dynamic_update_index_in_dim(out, piece, (me - hop - 1) % size, dim)
    return out


def half_of(width):
    return (width // 256) * 128


def sum_rows(grads):
    y, x, z, core = (lax.axis_size(axis) for axis in everyone)
    width = grads.shape[1]
    half = half_of(width)
    values = grads.reshape(y, x, z, core, -1, width)
    sends = yield split_stage(values, "core", 3)
    held = yield sends[0], send_all("core", sends[1])
    values = join_stage(*held).astype(bf16)
    left, right = values[..., :half], values[..., half:]
    for left_axis, right_axis in (("x", "y"), ("y", "x")):
        dim = 1 if left_axis == "x" else 0
        sends = yield split_stage(left, left_axis, dim), split_stage(right, right_axis, 0)
        (keep_left, send_left), (keep_right, send_right) = sends
        held = yield (
            (keep_left, send_all(left_axis, send_left)),
            (keep_right, send_all(right_axis, send_right)),
        )
        left, right = (join_stage(*part).astype(bf16) for part in held)
    sends = yield split_stage(jnp.concatenate([left, right], axis=-1), "z", 0)
    held = yield sends[0], send_all("z", sends[1])
    return join_stage(*held)


def all_rows(shard):
    width = shard.shape[1]
    half = half_of(width)
    others = lax.axis_size("z") - 1
    shard = yield shard
    held = yield shard, send_all("z", [shard] * others)
    values = place_stage(*held, "z", 0)
    left, right = values[..., :half], values[..., half:]
    for left_axis, right_axis in (("x", "y"), ("y", "x")):
        dim = 1 if right_axis == "x" else 0
        left, right = yield left, right
        held = yield (
            (left, send_all(left_axis, [left] * (lax.axis_size(left_axis) - 1))),
            (right, send_all(right_axis, [right] * (lax.axis_size(right_axis) - 1))),
        )
        left, right = place_stage(*held[0], left_axis, 0), place_stage(*held[1], right_axis, dim)
    values = yield jnp.concatenate([left, right], axis=-1)
    held = yield values, send_all("core", [values])
    return place_stage(*held, "core", 3).reshape(-1, width)


class Chain:
    def __init__(self, steps):
        self.steps = steps
        self.value = next(steps)
        self.done = False

    def advance(self):
        try:
            self.value = self.steps.send(self.value)
        except StopIteration as end:
            self.value, self.done = end.value, True


def phase(chains, operand, work):
    chains = [chain for chain in chains if not chain.done]
    values, operand = lax.optimization_barrier(([chain.value for chain in chains], operand))
    for chain, value in zip(chains, values):
        chain.value = value
        chain.advance()
    result = work(operand)
    values, result = lax.optimization_barrier(([chain.value for chain in chains], result))
    for chain, value in zip(chains, values):
        chain.value = value
        chain.advance()
    return result


def neighbour_rows(to_after, to_before):
    count = lax.axis_size(seq)
    ends = count - 1
    before = lax.ppermute(to_after, seq, [(i, i + 1) for i in range(ends)])
    after = lax.ppermute(to_before, seq, [(i + 1, i) for i in range(ends)])
    return before, after


def on_device(
    hidden_state,
    segment_ids,
    valid_mask,
    cotangent,
    norm_gain,
    pool_gain,
    feed_gain,
    query_weight,
    key_weight,
    value_weight,
    output_weight,
    local_bias,
    global_bias,
    gate_weight,
    up_weight,
    down_weight,
):
    model_width = hidden_state.shape[2]
    hidden = gate_weight.shape[1]
    tok_rows = hidden_state.shape[1]
    own_part = norm_gain.shape[0]
    buckets = local_bias.shape[1]
    pairs = local_bias.shape[0] // 2
    blocks = tok_rows // 128
    own_slots = tok_rows // 16
    seq_count = lax.axis_size(seq)
    slot_count = own_slots * seq_count
    row_start = lax.axis_index(seq) * tok_rows
    first_slot = row_start // 16
    source = hidden_state[0]
    upstream = cotangent[0]
    own_segments = segment_ids[0]
    valid_float = valid_mask[0].astype(f32)

    gain_columns = jnp.pad(jnp.stack([norm_gain, pool_gain, feed_gain], axis=1), ((0, 0), (0, 125)))
    first = Chain(
        all_rows(
            jnp.concatenate(
                [query_weight, key_weight, value_weight, output_weight, gain_columns], axis=1
            )
        )
    )
    second = Chain(all_rows(down_weight))
    values = source.astype(f32)
    inverse = inverse_rms(values)

    def share(operands):
        values, gate_weight, up_weight = operands
        w_gate_up = lax.all_gather(
            jnp.concatenate([gate_weight, up_weight], axis=1), everyone, axis=0, tiled=True
        )
        before, after = neighbour_rows(source[-128:], source[:128])
        own_raw = jnp.sum(
            (values * (inverse * valid_float[:, None])).reshape(own_slots, 16, model_width), axis=1
        )
        marks = jnp.stack([own_segments, valid_mask[0]]).astype(bf16).reshape(-1)
        mark_rows = -(-marks.size // model_width)
        pad_rows = -(-mark_rows // 16) * 16
        marks = jnp.pad(marks, (0, pad_rows * model_width - marks.size))
        shared = lax.all_gather(
            jnp.concatenate([own_raw.astype(bf16), marks.reshape(pad_rows, model_width)], axis=0),
            seq, axis=0, tiled=False,
        )
        return own_raw, shared, before, after, w_gate_up

    own_raw, shared, before, after, w_gate_up = share((values, gate_weight, up_weight))
    shared = phase([first], shared, lambda shared: shared)

    def near_parts(operands):
        shared, local_bias = operands
        raw_pool = shared[:, :own_slots].reshape(slot_count, model_width)
        all_marks = shared[:, own_slots:].reshape(seq_count, -1)[:, : 2 * tok_rows].astype(i32)
        all_marks = all_marks.reshape(seq_count, 2, tok_rows)
        all_segments, all_valid = all_marks[:, 0].reshape(-1), all_marks[:, 1].reshape(-1)
        slot_segments = all_segments.reshape(slot_count, 16)[:, 0]
        slot_live = jnp.sum(all_valid.reshape(slot_count, 16), axis=1) > 0
        segments_ext = lax.dynamic_slice_in_dim(
            jnp.pad(all_segments, 128, constant_values=-1), row_start, tok_rows + 256
        )
        valid_ext = lax.dynamic_slice_in_dim(jnp.pad(all_valid, 128), row_start, tok_rows + 256)
        feat_near = near_features(segments_ext, valid_ext)
        source_ext = jnp.concatenate([before, source, after], axis=0)
        return raw_pool, slot_segments, slot_live, feat_near, near_offsets(local_bias), source_ext

    raw_pool, slot_segments, slot_live, feat_near, bias_near, source_ext = phase(
        [first, second], (shared, local_bias), near_parts
    )
    feat_query = query_features(own_segments)
    feat_far = phase(
        [first, second],
        (global_bias, slot_segments, slot_live),
        lambda operands: far_features(*operands, first_slot, blocks),
    )
    phase([first], (), lambda nothing: nothing)
    weights = first.value

    bias, mixture, logs, queries, keys, vals, gkeys, gvals, normed, pooled, gains = phase(
        [second],
        (source_ext, raw_pool, weights, bias_near, feat_near, feat_far, feat_query),
        lambda operands: attention_forward(*operands),
    )
    phase([second], (), lambda nothing: nothing)
    w_down = second.value
    layer_output, middle_grad, mixture_grad, d_output, d_feed, d_gate, d_up, d_down = feed_forward_both(
        source, mixture, weights, gains, upstream, w_gate_up, w_down
    )
    chains = [
        Chain(sum_rows(jnp.concatenate([d_gate, d_up, d_output], axis=1))),
        Chain(sum_rows(d_down)),
    ]
    calls = 3 if pairs % 3 == 0 else 1
    count = pairs // calls
    near_sums, far_sums = [], []
    normed_grad, pooled_grad = 0.0, 0.0
    for call in range(calls):
        dwq, dwk, dwv, dnormed, dpooled, near, far = phase(
            chains,
            mixture_grad,
            lambda grad: attention_backward(
                call * count, count, queries, grad, keys, vals, gkeys, gvals, normed, pooled, weights, logs,
                bias, feat_near, feat_far, feat_query,
            ),
        )
        chains.append(Chain(sum_rows(jnp.concatenate([dwq, dwk, dwv], axis=1))))
        near_sums.append(near)
        far_sums.append(far)
        normed_grad = normed_grad + dnormed
        pooled_grad = pooled_grad + dpooled

    def return_grads(operands):
        normed_grad, pooled_grad = operands
        spread = lax.all_to_all(
            pooled_grad.astype(bf16).reshape(seq_count, own_slots, model_width), seq, 0, 0, tiled=True
        )
        to_head, to_tail = neighbour_rows(
            normed_grad[-128:].astype(bf16), normed_grad[:128].astype(bf16)
        )
        return normed_grad, spread, to_head, to_tail

    normed_grad, spread, to_head, to_tail = phase(chains, (normed_grad, pooled_grad), return_grads)
    pooled_grad = jnp.sum(spread.astype(f32), axis=0)
    edges = jnp.concatenate(
        [to_head.astype(f32), jnp.zeros((tok_rows - 256, model_width), f32), to_tail.astype(f32)]
    )
    gain_one, gain_pool = gains[0:1], gains[1:2]

    def finish(operands):
        normed_grad, pooled_grad, edges = operands
        pooled_raw = own_raw * gain_one
        pool_inverse = inverse_rms(pooled_raw)
        pool_delta = jnp.sum(pooled_grad * pooled_raw * pool_inverse, axis=0)
        pooled_raw_grad = norm_gradient(pooled_raw, pool_inverse, gain_pool, pooled_grad)
        spread_grad = jnp.broadcast_to(
            pooled_raw_grad[:, None, :], (own_slots, 16, model_width)
        ).reshape(tok_rows, model_width)
        normed_grad = normed_grad[128:-128] + edges + spread_grad * valid_float[:, None]
        norm_delta = jnp.sum(normed_grad * values * inverse, axis=0)
        input_delta = middle_grad + norm_gradient(values, inverse, gain_one, normed_grad)
        local_delta, global_delta = bucket_totals(
            jnp.concatenate(near_sums), jnp.concatenate(far_sums), first_slot, buckets
        )
        small = jnp.concatenate(
            [norm_delta, pool_delta, d_feed[0], local_delta.reshape(-1), global_delta.reshape(-1)]
        ).reshape(1, -1)
        return input_delta, small

    input_delta, small = phase(chains, (normed_grad, pooled_grad, edges), finish)
    small = phase(
        chains,
        small,
        lambda small: jnp.sum(lax.all_gather(small, batch, axis=0, tiled=True), axis=0, keepdims=True),
    )
    small = phase(
        chains,
        small,
        lambda small: jnp.sum(lax.all_gather(small, seq, axis=0, tiled=True), axis=0),
    )
    rest_delta, down_delta = chains[0].value, chains[1].value
    size = count * 128
    query_deltas = [chain.value[:, :size] for chain in chains[2:]]
    key_deltas = [chain.value[:, size : 2 * size] for chain in chains[2:]]
    value_deltas = [chain.value[:, 2 * size :] for chain in chains[2:]]
    place = lax.axis_index(everyone) * own_part
    gain_deltas = [
        lax.dynamic_slice_in_dim(small[i * model_width : (i + 1) * model_width], place, own_part)
        for i in range(3)
    ]
    bias_size = local_bias.size
    local_total = small[3 * model_width : 3 * model_width + bias_size].reshape(local_bias.shape)
    global_total = small[3 * model_width + bias_size :].reshape(local_bias.shape)
    return (
        layer_output[None],
        input_delta[None],
        gain_deltas[0],
        gain_deltas[1],
        gain_deltas[2],
        jnp.concatenate(query_deltas, axis=1),
        jnp.concatenate(key_deltas, axis=1),
        jnp.concatenate(value_deltas, axis=1),
        rest_delta[:, 2 * hidden :],
        local_total,
        global_total,
        rest_delta[:, :hidden],
        rest_delta[:, hidden : 2 * hidden],
        down_delta,
    )


def solution(mesh):
    seq_size, batch_size = mesh.shape["seq"], mesh.shape["batch"]
    chips = Mesh(mesh.devices.reshape(2, seq_size // 2, batch_size // 2, 2), everyone)
    tokens = P(batch, seq, None)
    marks = P(batch, seq)
    row = P(everyone)
    matrix = P(everyone, None)
    whole = P()
    return jax.shard_map(
        on_device,
        mesh=chips,
        in_specs=(tokens, marks, marks, tokens, row, row, row)
        + (matrix,) * 4
        + (whole,) * 2
        + (matrix,) * 3,
        out_specs=(tokens, tokens, row, row, row)
        + (matrix,) * 4
        + (whole,) * 2
        + (matrix,) * 3,
        check_vma=False,
    )
```

time: 606 us -> 452 us (0.75)
  matrix products: 122 us -> 10 us
  waiting for transfers between devices: 148 us -> 38.7 us
  starting transfers between devices: 16.2 us -> 81.3 us
  Pallas kernels: 98.2 us -> 159 us
  blocking collectives: 63.8 us -> 33.5 us
  other arithmetic: 70.7 us -> 52.6 us
  local copies, waits for them, and re-layouts: 64.4 us -> 55.5 us
    reduce_scatter x2 -> x0, waiting for transfers between devices: 122 us -> none  [scatter_rows(): lax.psum_scatter(array.astype(bf16), both, scatter_dimension=0, tiled=True)]
    dot_general x29 -> x4, matrix products: 122 us -> 10 us  [the longest x1 8.78 us: far_features(): return jnp.dot(picks, table, preferred_element_type=f32).astype(bf16)]
    ppermute x4 -> x60, starting transfers between devices: 11.2 us -> 77.1 us  [the longest x56 66.2 us: send_all(): lax.ppermute(piece, axis, ring(size, hop + 1))]
    pallas_call x2 -> x5, Pallas kernels: 98.2 us -> 159 us  [the longest x3 74.3 us: attention_backward(): pl.pallas_call(attend_backward, grid=(count,), in_specs=[columns(rows, fi...]
    ppermute x4 -> x60, waiting for transfers between devices: 0.01 us -> 38.7 us  [the longest x56 32.7 us: send_all(): lax.ppermute(piece, axis, ring(size, hop + 1))]
    all_gather x6 -> x3, blocking collectives: 63.8 us -> 33.5 us  [the longest x1 13.9 us: on_device(): lax.all_gather(small, batch, axis=0, tiled=True)]
    all_gather x3 -> x1, waiting for transfers between devices: 19.3 us -> 0.01 us  [share(): lax.all_gather(jnp.concatenate([gate_weight, up_weight], axis=1), everyon...]
    unnamed x165 -> x167, local copies, waits for them, and re-layouts: 27.7 us -> 9.72 us
  transfers between devices with their start and end apart: 11 -> 62, of which waited for: 3 -> 13; matrix products, arithmetic and copies ran while one was open for 35% -> 12% of each run, Pallas kernels for 16% -> 24%
where the time goes in v2:
time: 452 us; the launch traced here: 447 us
  Pallas kernels  159 us (35%)
  starting transfers between devices  81.3 us (18%)
  local copies, waits for them, and re-layouts  55.5 us (12%)
  other arithmetic  52.6 us (12%)
  waiting for transfers between devices  38.7 us (9%)
  blocking collectives  33.5 us (7%)
  between operations  16.4 us (4%)
  matrix products  10 us (2%)
    pallas_call x3, Pallas kernels, attention_backward(): pl.pallas_call(attend_backward, grid=(count,), in_specs=[columns(rows, fi...  74.3 us
    ppermute x56, starting transfers between devices, send_all(): lax.ppermute(piece, axis, ring(size, hop + 1))  66.2 us
    pallas_call x1, Pallas kernels, feed_forward_both(): pl.pallas_call(feed_forward, grid=(tiles,), in_specs=[fixed(rows, width),...  52.1 us
    pallas_call x1, Pallas kernels, attention_forward(): pl.pallas_call(attend_forward, grid=(pairs,), in_specs=[fixed(rows + 256,...  32.8 us
    ppermute x56, waiting for transfers between devices, send_all(): lax.ppermute(piece, axis, ring(size, hop + 1))  32.7 us
    squeeze x25, local copies, waits for them, and re-layouts, pick(): return lax.dynamic_index_in_dim(values, index, dim, keepdims=False)  14.7 us
    all_gather x1, blocking collectives, on_device(): lax.all_gather(small, batch, axis=0, tiled=True)  13.9 us
    all_gather x1, blocking collectives, share(): lax.all_gather(jnp.concatenate([own_raw.astype(bf16), marks.reshape(pad_r...  11.4 us
  transfers between devices with their start and end apart: 62, of which 13 were waited for; matrix products, arithmetic and copies ran while one was open for 12% of the time, Pallas kernels for 24%

profile of v2, /device:TPU:0, one launch (start us, length us, event | category | flops | bytes accessed | tf_op | source)
XLA Modules:
  0.0 447.1 jit_solution(8200005898012961413)
XLA Ops:
  9.6 1.8 fusion
  12.7 2.4 fusion.8
  15.3 11.4 %all-gather = bf16[320,768]{1,0:T(8,128)(2,1)S(1)} all-gather(bf16[80,768]{1,0:T(8,128)(2,1)S(1)} %pad_maximum_fusion.13), channel_id=2, replica_groups=mesh['y'=2,'x'=2,'z'=4,'core'=2] {'y','x'}, dimensions={0}, use_global_device_ids=true | all-gather | bytes 614400 | tf_op jit(solution)/shard_map/all_gather | solution.py:797
  28.6 2.6 collective-permute-start.1
  33.3 4.1 collective-permute-start.8
  52.4 2.9 collective-permute-start.4
  57.2 3.4 collective-permute-start.7
  60.9 2.4 pad_maximum_fusion.3.source_ref
  64.0 3.4 collective-permute-done.3
  76.4 2.0 collective-permute-start.13
  79.4 8.8 %convolution_convert_fusion.kglobal_ref = bf16[2048,768]{1,0:T(8,128)(2,1)} fusion(s32[264]{0:T(512)S(1)} %get-tuple-element.725, s32[264]{0:T(512)} %get-tuple-element.723, s32[264]{0:T(512)} %get-tuple-element.724, s32[264]{0:T(512)} %get-tuple-element.722, s32[264]{0:T(512)} %broadcast_add_fusion.1, s32[2048]{0:T(1024)S(1)} %get-tuple-element.718, ...), kind=kOutput, calls=%fused_computation.10 | convolution fusion | flops 852793344 | bytes 3378108 | tf_op jit(solution)/shard_map/dot_general | solution.py:590
  88.2 7.0 %collective-permute-done.12 = bf16[4,64,384]{2,1,0:T(8,128)(2,1)S(1)} collective-permute-done((bf16[4,64,384]{2,1,0:T(8,128)(2,1)S(1)}, bf16[4,64,384]{2,1,0:T(8,128)(2,1)S(1)}, u32[]{:S(2)}, u32[]{:S(2)}) %collective-permute-start.12) | collective-permute-done | bytes 196640 | tf_op jit(solution)/shard_map/ppermute | solution.py:635
  98.2 4.5 %collective-permute-done.14 = bf16[2,2,4,24,3200]{4,3,2,1,0:T(8,128)(2,1)} collective-permute-done((bf16[2,2,4,24,3200]{4,3,2,1,0:T(8,128)(2,1)}, bf16[2,2,4,24,3200]{4,3,2,1,0:T(8,128)(2,1)}, u32[]{:S(2)}, u32[]{:S(2)}) %collective-permute-start.14) | collective-permute-done | bytes 2457632 | tf_op jit(solution)/shard_map/ppermute | solution.py:635
  103.1 2.0 bitcast_dynamic-update-slice_fusion
  105.1 2.1 bitcast_dynamic-update-slice_fusion.1
  109.4 32.8 %attend_forward.1 = (f32[6,256,256]{2,1,0:T(8,128)S(1)}, bf16[1024,768]{1,0:T(8,128)(2,1)S(1)}, f32[6,8,256]{2,1,0:T(8,128)S(1)}, bf16[1024,768]{1,0:T(8,128)(2,...) custom-call(bf16[1280,768]{1,0:T(8,128)(2,1)} %pad_maximum_fusion.3., ...), custom_call_target="tpu_custom_call" | custom-call | flops 15099494400 | bytes 25165824 | tf_op jit(solution)/shard_map/attend_forward/pallas_call | solution.py:305
  144.4 3.4 collective-permute-done.17
  147.8 2.0 broadcast_in_dim.226
  151.0 2.7 bitcast_dynamic-update-slice_fusion.3
  153.7 52.1 %feed_forward.1 = (bf16[1024,768]{1,0:T(8,128)(2,1)}, f32[1024,768]{1,0:T(8,128)}, bf16[1024,768]{1,0:T(8,128)(2,1)}, bf16[768,768]{1,0:T(8,128)(2,1)}, f32[8,76...) custom-call(bf16[1024,768]{1,0:T(8,128)(2,1)} %bitcast.297, ...), custom_call_target="tpu_custom_call" | custom-call | flops 32212254720 | bytes 41943040 | tf_op jit(solution)/shard_map/feed_forward/pallas_call | solution.py:501
  205.8 3.9 pad_maximum_fusion
  209.7 3.6 dynamic-slice_bitcast_fusion
  213.2 1.9 dynamic-slice_bitcast_fusion.2
  218.7 24.7 %attend_backward.3 = (bf16[768,256]{1,0:T(8,128)(2,1)S(1)}, bf16[768,256]{1,0:T(8,128)(2,1)S(1)}, bf16[768,256]{1,0:T(8,128)(2,1)S(1)}, f32[1280,768]{1,0:T(8,12...) custom-call(bf16[1024,768]{1,0:T(8,128)(2,1)S(1)} %copy-done.4, ...), custom_call_target="tpu_custom_call" | custom-call | flops 10066329600 | bytes 8388608 | tf_op jit(solution)/shard_map/attend_backward/pallas_call | solution.py:362
  244.8 2.0 add_convert_fusion.1
  247.3 2.9 add_convert_fusion
  257.6 25.0 %attend_backward.4 = (bf16[768,256]{1,0:T(8,128)(2,1)S(1)}, bf16[768,256]{1,0:T(8,128)(2,1)S(1)}, bf16[768,256]{1,0:T(8,128)(2,1)S(1)}, f32[1280,768]{1,0:T(8,12...) custom-call(bf16[1024,768]{1,0:T(8,128)(2,1)S(1)} %copy-done.5, ...), custom_call_target="tpu_custom_call" | custom-call | flops 10066329600 | bytes 8388608 | tf_op jit(solution)/shard_map/attend_backward/pallas_call | solution.py:362
  282.5 2.4 collective-permute-done.22
  297.6 24.6 %attend_backward.5 = (bf16[768,256]{1,0:T(8,128)(2,1)S(1)}, bf16[768,256]{1,0:T(8,128)(2,1)S(1)}, bf16[768,256]{1,0:T(8,128)(2,1)S(1)}, f32[1280,768]{1,0:T(8,12...) custom-call(bf16[1024,768]{1,0:T(8,128)(2,1)S(1)} %copy-done.5, ...), custom_call_target="tpu_custom_call" | custom-call | flops 10066329600 | bytes 8388608 | tf_op jit(solution)/shard_map/attend_backward/pallas_call | solution.py:362
  335.0 1.9 collective-permute-start.36
  338.9 4.1 all-to-all-start
  343.6 4.0 collective-permute-start.43
  349.3 1.8 collective-permute-start.37
  351.2 3.0 collective-permute-done.37
  355.0 1.9 collective-permute-done.40
  356.9 2.2 collective-permute-start.33
  362.3 6.0 %collective-permute-done.44 = bf16[128,768]{1,0:T(8,128)(2,1)S(1)} collective-permute-done((bf16[128,768]{1,0:T(8,128)(2,1)}, bf16[128,768]{1,0:T(8,128)(2,1)S(1)}, u32[]{:S(2)}, u32[]{:S(2)}) %collective-permute-start.44) | collective-permute-done | bytes 196640 | tf_op jit(solution)/shard_map/ppermute | solution.py:733
  368.3 3.8 collective-permute-done.33
  380.9 1.9 fusion.5
  386.1 5.5 %collective-permute-start.45 = (bf16[24,768]{1,0:T(8,128)(2,1)S(1)}, bf16[24,768]{1,0:T(8,128)(2,1)S(1)}, u32[]{:S(2)}, u32[]{:S(2)}) collective-permute-start(bf16[24,768]{1,0:T(8,128)(2,1)S(1)} %get-tuple-element.520), channel_id=1, source_target_pairs={{0,2},{2,4},{4,6},{6,0},{1,3},{3,5},{5,7},{7,1},{8,10},{10,12},{12... | collective-permute-start | bytes 110600 | tf_op jit(solution)/shard_map/ppermute | solution.py:635
  392.6 2.3 fusion.3
  395.0 1.7 convert_add_fusion.1
  396.8 1.9 collective-permute-start.47
  401.3 1.7 collective-permute-start.55
  404.2 3.3 collective-permute-start.53
  408.6 13.9 %all-gather.1 = f32[8,1,3072]{2,1,0:T(1,128)S(1)} all-gather(f32[1,1,3072]{2,1,0:T(1,128)S(1)} %bitcast.327), channel_id=1, replica_groups=mesh['y'=2,'x'=2,'z'=4,'core'=2] {'z','core'}, dimensions={0}, use_global_device_ids=true | all-gather | bytes 110592 | tf_op jit(solution)/shard_map/all_gather | solution.py:908
  424.2 2.3 collective-permute-start.59
  426.6 8.2 %all-gather.2 = f32[4,1,3072]{2,1,0:T(1,128)S(1)} all-gather(f32[1,1,3072]{2,1,0:T(1,128)S(1)} %bitcast.323), channel_id=1, replica_groups=mesh['y'=2,'x'=2,'z'=4,'core'=2] {'y','x'}, dimensions={0}, use_global_device_ids=true | all-gather | bytes 61440 | tf_op jit(solution)/shard_map/all_gather | solution.py:913
  (481 shorter events, 114.7 us)
Async XLA Ops:
  7.3 146.4 %all-gather.5.cloned.1.call-start = ((), (), s32[]{:S(2)}) async-start(), calls=%async_computation.1 | async-start | bytes 6488064 | tf_op jit(solution)/shard_map/all_gather | solution.py:786
  26.9 19.8 %collective-permute-start = (bf16[24,3200]{1,0:T(8,128)(2,1)S(1)}, bf16[24,3200]{1,0:T(8,128)(2,1)S(1)}, u32[]{:S(2)}, u32[]{:S(2)}) collective-permute-start(bf16[24,3200]{1,0:T(8,128)(2,1)S(1)} %constant_dynamic-update-slice_fusion), channel_id=1, source_target_pairs={{0,2},{2,4},{4,6},{6,0},{1,3},{3,5},{5,7},{7,1},{8,10},{10,12},{12... | collective-permute-start | bytes 460808 | tf_op jit(solution)/shard_map/ppermute | solution.py:635
  28.6 18.2 %collective-permute-start.1 = (bf16[24,3200]{1,0:T(8,128)(2,1)S(1)}, bf16[24,3200]{1,0:T(8,128)(2,1)S(1)}, u32[]{:S(2)}, u32[]{:S(2)}) collective-permute-start(bf16[24,3200]{1,0:T(8,128)(2,1)S(1)} %constant_dynamic-update-slice_fusion), channel_id=1, source_target_pairs={{0,4},{2,6},{4,0},{6,2},{1,5},{3,7},{5,1},{7,3},{8,12},{10,14},{12... | collective-permute-start | bytes 460808 | tf_op jit(solution)/shard_map/ppermute | solution.py:635
  31.1 16.3 %collective-permute-start.2 = (bf16[24,3200]{1,0:T(8,128)(2,1)S(1)}, bf16[24,3200]{1,0:T(8,128)(2,1)}, u32[]{:S(2)}, u32[]{:S(2)}) collective-permute-start(bf16[24,3200]{1,0:T(8,128)(2,1)S(1)} %constant_dynamic-update-slice_fusion), channel_id=1, source_target_pairs={{0,6},{2,0},{4,2},{6,4},{1,7},{3,1},{5,3},{7,5},{8,14},{10,8},{12,... | collective-permute-start | bytes 460808 | tf_op jit(solution)/shard_map/ppermute | solution.py:635
  33.3 24.0 %collective-permute-start.8 = (bf16[128,768]{1,0:T(8,128)(2,1)}, bf16[128,768]{1,0:T(8,128)(2,1)}, u32[]{:S(2)}, u32[]{:S(2)}) collective-permute-start(bf16[128,768]{1,0:T(8,128)(2,1)} %get-tuple-element.613), channel_id=1, source_target_pairs={{0,8},{8,16},{16,24},{1,9},{9,17},{17,25},{2,10},{10,18},{18,26},{... | collective-permute-start | bytes 589832 | tf_op jit(solution)/shard_map/ppermute | solution.py:732
  37.3 23.3 %collective-permute-start.9 = (bf16[128,768]{1,0:T(8,128)(2,1)}, bf16[128,768]{1,0:T(8,128)(2,1)}, u32[]{:S(2)}, u32[]{:S(2)}) collective-permute-start(bf16[128,768]{1,0:T(8,128)(2,1)} %get-tuple-element.614), channel_id=1, source_target_pairs={{8,0},{16,8},{24,16},{9,1},{17,9},{25,17},{10,2},{18,10},{26,18},{... | collective-permute-start | bytes 589832 | tf_op jit(solution)/shard_map/ppermute | solution.py:733
  49.6 13.8 %collective-permute-start.5 = (bf16[64,768]{1,0:T(8,128)(2,1)}, bf16[64,768]{1,0:T(8,128)(2,1)}, u32[]{:S(2)}, u32[]{:S(2)}) collective-permute-start(bf16[64,768]{1,0:T(8,128)(2,1)} %param.31), channel_id=1, source_target_pairs={{0,2},{2,4},{4,6},{6,0},{1,3},{3,5},{5,7},{7,1},{8,10},{10,12},{12... | collective-permute-start | bytes 294920 | tf_op jit(solution)/shard_map/ppermute | solution.py:635
  50.3 13.1 %collective-permute-start.6 = (bf16[64,768]{1,0:T(8,128)(2,1)}, bf16[64,768]{1,0:T(8,128)(2,1)}, u32[]{:S(2)}, u32[]{:S(2)}) collective-permute-start(bf16[64,768]{1,0:T(8,128)(2,1)} %param.31), channel_id=1, source_target_pairs={{0,4},{2,6},{4,0},{6,2},{1,5},{3,7},{5,1},{7,3},{8,12},{10,14},{12... | collective-permute-start | bytes 294920 | tf_op jit(solution)/shard_map/ppermute | solution.py:635
  52.4 14.9 %collective-permute-start.4 = (bf16[4,24,1664]{2,1,0:T(8,128)(2,1)S(1)}, bf16[4,24,1664]{2,1,0:T(8,128)(2,1)S(1)}, u32[]{:S(2)}, u32[]{:S(2)}) collective-permute-start(bf16[4,24,1664]{2,1,0:T(8,128)(2,1)S(1)} %slice.215), channel_id=1, source_target_pairs={{0,16},{16,0},{1,17},{17,1},{2,18},{18,2},{3,19},{19,3},{4,20},{20... | collective-permute-start | bytes 958472 | tf_op jit(solution)/shard_map/ppermute | solution.py:635
  74.3 21.0 %collective-permute-start.11 = (bf16[2,4,24,1664]{3,2,1,0:T(8,128)(2,1)S(1)}, bf16[2,4,24,1664]{3,2,1,0:T(8,128)(2,1)S(1)}, u32[]{:S(2)}, u32[]{:S(2)}) collective-permute-start(bf16[2,4,24,1664]{3,2,1,0:T(8,128)(2,1)S(1)} %bitcast_dynamic-update-slice_fusion.12), channel_id=1, source_target_pairs={{0,8},{8,0},{1,9},{9,1},{2,10},{10,2},{3,11},{11,3},{4,12},{12,4},... | collective-permute-start | bytes 1916936 | tf_op jit(solution)/shard_map/ppermute | solution.py:635
  74.7 20.6 %collective-permute-start.10 = (bf16[2,4,24,1536]{3,2,1,0:T(8,128)(2,1)S(1)}, bf16[2,4,24,1536]{3,2,1,0:T(8,128)(2,1)S(1)}, u32[]{:S(2)}, u32[]{:S(2)}) collective-permute-start(bf16[2,4,24,1536]{3,2,1,0:T(8,128)(2,1)S(1)} %bitcast_dynamic-update-slice_fusion.14), channel_id=1, source_target_pairs={{0,16},{16,0},{1,17},{17,1},{2,18},{18,2},{3,19},{19,3},{4,20},{20... | collective-permute-start | bytes 1769480 | tf_op jit(solution)/shard_map/ppermute | solution.py:635
  76.1 19.1 %collective-permute-start.12 = (bf16[4,64,384]{2,1,0:T(8,128)(2,1)S(1)}, bf16[4,64,384]{2,1,0:T(8,128)(2,1)S(1)}, u32[]{:S(2)}, u32[]{:S(2)}) collective-permute-start(bf16[4,64,384]{2,1,0:T(8,128)(2,1)S(1)} %get-tuple-element.332), channel_id=1, source_target_pairs={{0,8},{8,0},{1,9},{9,1},{2,10},{10,2},{3,11},{11,3},{4,12},{12,4},... | collective-permute-start | bytes 589832 | tf_op jit(solution)/shard_map/ppermute | solution.py:635
  76.4 18.8 %collective-permute-start.13 = (bf16[4,64,384]{2,1,0:T(8,128)(2,1)}, bf16[4,64,384]{2,1,0:T(8,128)(2,1)S(1)}, u32[]{:S(2)}, u32[]{:S(2)}) collective-permute-start(bf16[4,64,384]{2,1,0:T(8,128)(2,1)} %get-tuple-element.334), channel_id=1, source_target_pairs={{0,16},{16,0},{1,17},{17,1},{2,18},{18,2},{3,19},{19,3},{4,20},{20... | collective-permute-start | bytes 589832 | tf_op jit(solution)/shard_map/ppermute | solution.py:635
  107.2 35.1 %collective-permute-start.15 = (bf16[2,4,64,384]{3,2,1,0:T(8,128)(2,1)S(1)}, bf16[2,4,64,384]{3,2,1,0:T(8,128)(2,1)S(1)}, u32[]{:S(2)}, u32[]{:S(2)}) collective-permute-start(bf16[2,4,64,384]{3,2,1,0:T(8,128)(2,1)S(1)} %bitcast_dynamic-update-slice_fusion.18), channel_id=1, source_target_pairs={{0,16},{16,0},{1,17},{17,1},{2,18},{18,2},{3,19},{19,3},{4,20},{20... | collective-permute-start | bytes 1179656 | tf_op jit(solution)/shard_map/ppermute | solution.py:635
  108.7 33.6 %collective-permute-start.16 = (bf16[2,4,64,384]{3,2,1,0:T(8,128)(2,1)S(1)}, bf16[2,4,64,384]{3,2,1,0:T(8,128)(2,1)S(1)}, u32[]{:S(2)}, u32[]{:S(2)}) collective-permute-start(bf16[2,4,64,384]{3,2,1,0:T(8,128)(2,1)S(1)} %bitcast_dynamic-update-slice_fusion.16), channel_id=1, source_target_pairs={{0,8},{8,0},{1,9},{9,1},{2,10},{10,2},{3,11},{11,3},{4,12},{12,4},... | collective-permute-start | bytes 1179656 | tf_op jit(solution)/shard_map/ppermute | solution.py:635
  215.1 28.2 %collective-permute-start.18 = (bf16[2,2,4,24,4864]{4,3,2,1,0:T(8,128)(2,1)}, bf16[2,2,4,24,4864]{4,3,2,1,0:T(8,128)(2,1)}, u32[]{:S(2)}, u32[]{:S(2)}) collective-permute-start(bf16[2,2,4,24,4864]{4,3,2,1,0:T(8,128)(2,1)} %get-tuple-element.382), channel_id=1, source_target_pairs={{0,1},{1,0},{2,3},{3,2},{4,5},{5,4},{6,7},{7,6},{8,9},{9,8},{10,11... | collective-permute-start | bytes 11206664 | tf_op jit(solution)/shard_map/ppermute | solution.py:635
  215.3 28.1 %collective-permute-start.19 = (bf16[2,2,4,64,768]{4,3,2,1,0:T(8,128)(2,1)}, bf16[2,2,4,64,768]{4,3,2,1,0:T(8,128)(2,1)}, u32[]{:S(2)}, u32[]{:S(2)}) collective-permute-start(bf16[2,2,4,64,768]{4,3,2,1,0:T(8,128)(2,1)} %get-tuple-element.384), channel_id=1, source_target_pairs={{0,1},{1,0},{2,3},{3,2},{4,5},{5,4},{6,7},{7,6},{8,9},{9,8},{10,11... | collective-permute-start | bytes 4718600 | tf_op jit(solution)/shard_map/ppermute | solution.py:635
  253.5 32.3 %collective-permute-start.20 = (bf16[2,4,24,2432]{3,2,1,0:T(8,128)(2,1)}, bf16[2,4,24,2432]{3,2,1,0:T(8,128)(2,1)S(1)}, u32[]{:S(2)}, u32[]{:S(2)}) collective-permute-start(bf16[2,4,24,2432]{3,2,1,0:T(8,128)(2,1)} %get-tuple-element.410), channel_id=1, source_target_pairs={{0,8},{8,0},{1,9},{9,1},{2,10},{10,2},{3,11},{11,3},{4,12},{12,4},... | collective-permute-start | bytes 2801672 | tf_op jit(solution)/shard_map/ppermute | solution.py:635
  254.8 31.0 %collective-permute-start.21 = (bf16[2,4,24,2432]{3,2,1,0:T(8,128)(2,1)S(1)}, bf16[2,4,24,2432]{3,2,1,0:T(8,128)(2,1)S(1)}, u32[]{:S(2)}, u32[]{:S(2)}) collective-permute-start(bf16[2,4,24,2432]{3,2,1,0:T(8,128)(2,1)S(1)} %get-tuple-element.412), channel_id=1, source_target_pairs={{0,16},{16,0},{1,17},{17,1},{2,18},{18,2},{3,19},{19,3},{4,20},{20... | collective-permute-start | bytes 2801672 | tf_op jit(solution)/shard_map/ppermute | solution.py:635
  255.5 30.3 %collective-permute-start.24 = (bf16[2,2,4,24,768]{4,3,2,1,0:T(8,128)(2,1)S(1)}, bf16[2,2,4,24,768]{4,3,2,1,0:T(8,128)(2,1)S(1)}, u32[]{:S(2)}, u32[]{:S(2)}) collective-permute-start(bf16[2,2,4,24,768]{4,3,2,1,0:T(8,128)(2,1)S(1)} %get-tuple-element.418), channel_id=1, source_target_pairs={{0,1},{1,0},{2,3},{3,2},{4,5},{5,4},{6,7},{7,6},{8,9},{9,8},{10,11... | collective-permute-start | bytes 1769480 | tf_op jit(solution)/shard_map/ppermute | solution.py:635
  255.5 29.4 %collective-permute-start.22 = (bf16[2,4,64,384]{3,2,1,0:T(8,128)(2,1)}, bf16[2,4,64,384]{3,2,1,0:T(8,128)(2,1)S(1)}, u32[]{:S(2)}, u32[]{:S(2)}) collective-permute-start(bf16[2,4,64,384]{3,2,1,0:T(8,128)(2,1)} %get-tuple-element.414), channel_id=1, source_target_pairs={{0,8},{8,0},{1,9},{9,1},{2,10},{10,2},{3,11},{11,3},{4,12},{12,4},... | collective-permute-start | bytes 1179656 | tf_op jit(solution)/shard_map/ppermute | solution.py:635
  257.0 28.8 %collective-permute-start.23 = (bf16[2,4,64,384]{3,2,1,0:T(8,128)(2,1)}, bf16[2,4,64,384]{3,2,1,0:T(8,128)(2,1)}, u32[]{:S(2)}, u32[]{:S(2)}) collective-permute-start(bf16[2,4,64,384]{3,2,1,0:T(8,128)(2,1)} %get-tuple-element.416), channel_id=1, source_target_pairs={{0,16},{16,0},{1,17},{17,1},{2,18},{18,2},{3,19},{19,3},{4,20},{20... | collective-permute-start | bytes 1179656 | tf_op jit(solution)/shard_map/ppermute | solution.py:635
  293.4 28.9 %collective-permute-start.31 = (bf16[2,2,4,24,768]{4,3,2,1,0:T(8,128)(2,1)}, bf16[2,2,4,24,768]{4,3,2,1,0:T(8,128)(2,1)S(1)}, u32[]{:S(2)}, u32[]{:S(2)}) collective-permute-start(bf16[2,2,4,24,768]{4,3,2,1,0:T(8,128)(2,1)} %get-tuple-element.453), channel_id=1, source_target_pairs={{0,1},{1,0},{2,3},{3,2},{4,5},{5,4},{6,7},{7,6},{8,9},{9,8},{10,11... | collective-permute-start | bytes 1769480 | tf_op jit(solution)/shard_map/ppermute | solution.py:635
  293.5 28.8 %collective-permute-start.25 = (bf16[4,24,2432]{2,1,0:T(8,128)(2,1)S(1)}, bf16[4,24,2432]{2,1,0:T(8,128)(2,1)S(1)}, u32[]{:S(2)}, u32[]{:S(2)}) collective-permute-start(bf16[4,24,2432]{2,1,0:T(8,128)(2,1)S(1)} %get-tuple-element.441), channel_id=1, source_target_pairs={{0,16},{16,0},{1,17},{17,1},{2,18},{18,2},{3,19},{19,3},{4,20},{20... | collective-permute-start | bytes 1400840 | tf_op jit(solution)/shard_map/ppermute | solution.py:635
  294.4 27.9 %collective-permute-start.26 = (bf16[4,24,2432]{2,1,0:T(8,128)(2,1)S(1)}, bf16[4,24,2432]{2,1,0:T(8,128)(2,1)S(1)}, u32[]{:S(2)}, u32[]{:S(2)}) collective-permute-start(bf16[4,24,2432]{2,1,0:T(8,128)(2,1)S(1)} %get-tuple-element.443), channel_id=1, source_target_pairs={{0,8},{8,0},{1,9},{9,1},{2,10},{10,2},{3,11},{11,3},{4,12},{12,4},... | collective-permute-start | bytes 1400840 | tf_op jit(solution)/shard_map/ppermute | solution.py:635
  295.4 26.8 %collective-permute-start.27 = (bf16[4,64,384]{2,1,0:T(8,128)(2,1)}, bf16[4,64,384]{2,1,0:T(8,128)(2,1)S(1)}, u32[]{:S(2)}, u32[]{:S(2)}) collective-permute-start(bf16[4,64,384]{2,1,0:T(8,128)(2,1)} %get-tuple-element.445), channel_id=1, source_target_pairs={{0,16},{16,0},{1,17},{17,1},{2,18},{18,2},{3,19},{19,3},{4,20},{20... | collective-permute-start | bytes 589832 | tf_op jit(solution)/shard_map/ppermute | solution.py:635
  296.6 25.6 %collective-permute-start.28 = (bf16[4,64,384]{2,1,0:T(8,128)(2,1)S(1)}, bf16[4,64,384]{2,1,0:T(8,128)(2,1)S(1)}, u32[]{:S(2)}, u32[]{:S(2)}) collective-permute-start(bf16[4,64,384]{2,1,0:T(8,128)(2,1)S(1)} %get-tuple-element.447), channel_id=1, source_target_pairs={{0,8},{8,0},{1,9},{9,1},{2,10},{10,2},{3,11},{11,3},{4,12},{12,4},... | collective-permute-start | bytes 589832 | tf_op jit(solution)/shard_map/ppermute | solution.py:635
  333.5 38.7 %collective-permute-start.42 = (bf16[2,2,4,24,768]{4,3,2,1,0:T(8,128)(2,1)}, bf16[2,2,4,24,768]{4,3,2,1,0:T(8,128)(2,1)}, u32[]{:S(2)}, u32[]{:S(2)}) collective-permute-start(bf16[2,2,4,24,768]{4,3,2,1,0:T(8,128)(2,1)} %get-tuple-element.502), channel_id=1, source_target_pairs={{0,1},{1,0},{2,3},{3,2},{4,5},{5,4},{6,7},{7,6},{8,9},{9,8},{10,11... | collective-permute-start | bytes 1769480 | tf_op jit(solution)/shard_map/ppermute | solution.py:635
  333.5 15.7 %collective-permute-start.35 = (bf16[64,768]{1,0:T(8,128)(2,1)}, bf16[64,768]{1,0:T(8,128)(2,1)S(1)}, u32[]{:S(2)}, u32[]{:S(2)}) collective-permute-start(bf16[64,768]{1,0:T(8,128)(2,1)} %get-tuple-element.490), channel_id=1, source_target_pairs={{0,2},{2,4},{4,6},{6,0},{1,3},{3,5},{5,7},{7,1},{8,10},{10,12},{12... | collective-permute-start | bytes 294920 | tf_op jit(solution)/shard_map/ppermute | solution.py:635
  335.0 14.3 %collective-permute-start.36 = (bf16[64,768]{1,0:T(8,128)(2,1)}, bf16[64,768]{1,0:T(8,128)(2,1)}, u32[]{:S(2)}, u32[]{:S(2)}) collective-permute-start(bf16[64,768]{1,0:T(8,128)(2,1)} %get-tuple-element.491), channel_id=1, source_target_pairs={{0,4},{2,6},{4,0},{6,2},{1,5},{3,7},{5,1},{7,3},{8,12},{10,14},{12... | collective-permute-start | bytes 294920 | tf_op jit(solution)/shard_map/ppermute | solution.py:635
  338.9 33.2 %all-to-all-start = ((bf16[4,64,768]{2,1,0:T(8,128)(2,1)}), bf16[4,64,768]{2,1,0:T(8,128)(2,1)}, u32[]{:S(2)}, u32[]{:S(2)}) async-start(bf16[4,64,768]{2,1,0:T(8,128)(2,1)} %bitcast.100), calls=%async_computation | async-start | bytes 786432 | tf_op jit(solution)/shard_map/all_to_all | solution.py:869
  343.6 17.0 %collective-permute-start.43 = (bf16[128,768]{1,0:T(8,128)(2,1)}, bf16[128,768]{1,0:T(8,128)(2,1)S(1)}, u32[]{:S(2)}, u32[]{:S(2)}) collective-permute-start(bf16[128,768]{1,0:T(8,128)(2,1)} %get-tuple-element.606), channel_id=1, source_target_pairs={{0,8},{8,16},{16,24},{1,9},{9,17},{17,25},{2,10},{10,18},{18,26},{... | collective-permute-start | bytes 589832 | tf_op jit(solution)/shard_map/ppermute | solution.py:732
  349.2 9.9 %collective-permute-start.41 = (bf16[2,4,24,384]{3,2,1,0:T(8,128)(2,1)S(1)}, bf16[2,4,24,384]{3,2,1,0:T(8,128)(2,1)}, u32[]{:S(2)}, u32[]{:S(2)}) collective-permute-start(bf16[2,4,24,384]{3,2,1,0:T(8,128)(2,1)S(1)} %copy-done.45), channel_id=1, source_target_pairs={{0,16},{16,0},{1,17},{17,1},{2,18},{18,2},{3,19},{19,3},{4,20},{20... | collective-permute-start | bytes 442376 | tf_op jit(solution)/shard_map/ppermute | solution.py:635
  354.2 14.1 %collective-permute-start.32 = (bf16[24,4864]{1,0:T(8,128)(2,1)}, bf16[24,4864]{1,0:T(8,128)(2,1)S(1)}, u32[]{:S(2)}, u32[]{:S(2)}) collective-permute-start(bf16[24,4864]{1,0:T(8,128)(2,1)} %get-tuple-element.486), channel_id=1, source_target_pairs={{0,2},{2,4},{4,6},{6,0},{1,3},{3,5},{5,7},{7,1},{8,10},{10,12},{12... | collective-permute-start | bytes 700424 | tf_op jit(solution)/shard_map/ppermute | solution.py:635
  356.9 15.2 %collective-permute-start.33 = (bf16[24,4864]{1,0:T(8,128)(2,1)}, bf16[24,4864]{1,0:T(8,128)(2,1)S(1)}, u32[]{:S(2)}, u32[]{:S(2)}) collective-permute-start(bf16[24,4864]{1,0:T(8,128)(2,1)} %get-tuple-element.487), channel_id=1, source_target_pairs={{0,4},{2,6},{4,0},{6,2},{1,5},{3,7},{5,1},{7,3},{8,12},{10,14},{12... | collective-permute-start | bytes 700424 | tf_op jit(solution)/shard_map/ppermute | solution.py:635
  359.1 13.0 %collective-permute-start.34 = (bf16[24,4864]{1,0:T(8,128)(2,1)}, bf16[24,4864]{1,0:T(8,128)(2,1)S(1)}, u32[]{:S(2)}, u32[]{:S(2)}) collective-permute-start(bf16[24,4864]{1,0:T(8,128)(2,1)} %get-tuple-element.488), channel_id=1, source_target_pairs={{0,6},{2,0},{4,2},{6,4},{1,7},{3,1},{5,3},{7,5},{8,14},{10,8},{12,... | collective-permute-start | bytes 700424 | tf_op jit(solution)/shard_map/ppermute | solution.py:635
  382.8 18.2 %collective-permute-start.50 = (bf16[2,4,24,384]{3,2,1,0:T(8,128)(2,1)S(1)}, bf16[2,4,24,384]{3,2,1,0:T(8,128)(2,1)S(1)}, u32[]{:S(2)}, u32[]{:S(2)}) collective-permute-start(bf16[2,4,24,384]{3,2,1,0:T(8,128)(2,1)S(1)} %get-tuple-element.528), channel_id=1, source_target_pairs={{0,8},{8,0},{1,9},{9,1},{2,10},{10,2},{3,11},{11,3},{4,12},{12,4},... | collective-permute-start | bytes 442376 | tf_op jit(solution)/shard_map/ppermute | solution.py:635
  384.1 17.0 %collective-permute-start.51 = (bf16[2,4,24,384]{3,2,1,0:T(8,128)(2,1)S(1)}, bf16[2,4,24,384]{3,2,1,0:T(8,128)(2,1)S(1)}, u32[]{:S(2)}, u32[]{:S(2)}) collective-permute-start(bf16[2,4,24,384]{3,2,1,0:T(8,128)(2,1)S(1)} %get-tuple-element.530), channel_id=1, source_target_pairs={{0,16},{16,0},{1,17},{17,1},{2,18},{18,2},{3,19},{19,3},{4,20},{20... | collective-permute-start | bytes 442376 | tf_op jit(solution)/shard_map/ppermute | solution.py:635
  384.9 15.9 %collective-permute-start.48 = (bf16[4,24,384]{2,1,0:T(8,128)(2,1)S(1)}, bf16[4,24,384]{2,1,0:T(8,128)(2,1)S(1)}, u32[]{:S(2)}, u32[]{:S(2)}) collective-permute-start(bf16[4,24,384]{2,1,0:T(8,128)(2,1)S(1)} %get-tuple-element.524), channel_id=1, source_target_pairs={{0,16},{16,0},{1,17},{17,1},{2,18},{18,2},{3,19},{19,3},{4,20},{20... | collective-permute-start | bytes 221192 | tf_op jit(solution)/shard_map/ppermute | solution.py:635
  386.1 10.5 %collective-permute-start.45 = (bf16[24,768]{1,0:T(8,128)(2,1)S(1)}, bf16[24,768]{1,0:T(8,128)(2,1)S(1)}, u32[]{:S(2)}, u32[]{:S(2)}) collective-permute-start(bf16[24,768]{1,0:T(8,128)(2,1)S(1)} %get-tuple-element.520), channel_id=1, source_target_pairs={{0,2},{2,4},{4,6},{6,0},{1,3},{3,5},{5,7},{7,1},{8,10},{10,12},{12... | collective-permute-start | bytes 110600 | tf_op jit(solution)/shard_map/ppermute | solution.py:635
  401.3 21.3 %collective-permute-start.55 = (bf16[4,24,384]{2,1,0:T(8,128)(2,1)S(1)}, bf16[4,24,384]{2,1,0:T(8,128)(2,1)S(1)}, u32[]{:S(2)}, u32[]{:S(2)}) collective-permute-start(bf16[4,24,384]{2,1,0:T(8,128)(2,1)S(1)} %get-tuple-element.557), channel_id=1, source_target_pairs={{0,16},{16,0},{1,17},{17,1},{2,18},{18,2},{3,19},{19,3},{4,20},{20... | collective-permute-start | bytes 221192 | tf_op jit(solution)/shard_map/ppermute | solution.py:635
  403.0 19.5 %collective-permute-start.56 = (bf16[4,24,384]{2,1,0:T(8,128)(2,1)S(1)}, bf16[4,24,384]{2,1,0:T(8,128)(2,1)S(1)}, u32[]{:S(2)}, u32[]{:S(2)}) collective-permute-start(bf16[4,24,384]{2,1,0:T(8,128)(2,1)S(1)} %get-tuple-element.559), channel_id=1, source_target_pairs={{0,8},{8,0},{1,9},{9,1},{2,10},{10,2},{3,11},{11,3},{4,12},{12,4},... | collective-permute-start | bytes 221192 | tf_op jit(solution)/shard_map/ppermute | solution.py:635
  403.6 18.9 %collective-permute-start.52 = (bf16[24,768]{1,0:T(8,128)(2,1)S(1)}, bf16[24,768]{1,0:T(8,128)(2,1)S(1)}, u32[]{:S(2)}, u32[]{:S(2)}) collective-permute-start(bf16[24,768]{1,0:T(8,128)(2,1)S(1)} %get-tuple-element.553), channel_id=1, source_target_pairs={{0,2},{2,4},{4,6},{6,0},{1,3},{3,5},{5,7},{7,1},{8,10},{10,12},{12... | collective-permute-start | bytes 110600 | tf_op jit(solution)/shard_map/ppermute | solution.py:635
  404.2 18.4 %collective-permute-start.53 = (bf16[24,768]{1,0:T(8,128)(2,1)S(1)}, bf16[24,768]{1,0:T(8,128)(2,1)S(1)}, u32[]{:S(2)}, u32[]{:S(2)}) collective-permute-start(bf16[24,768]{1,0:T(8,128)(2,1)S(1)} %get-tuple-element.554), channel_id=1, source_target_pairs={{0,4},{2,6},{4,0},{6,2},{1,5},{3,7},{5,1},{7,3},{8,12},{10,14},{12... | collective-permute-start | bytes 110600 | tf_op jit(solution)/shard_map/ppermute | solution.py:635
  407.4 15.1 %collective-permute-start.54 = (bf16[24,768]{1,0:T(8,128)(2,1)S(1)}, bf16[24,768]{1,0:T(8,128)(2,1)S(1)}, u32[]{:S(2)}, u32[]{:S(2)}) collective-permute-start(bf16[24,768]{1,0:T(8,128)(2,1)S(1)} %get-tuple-element.555), channel_id=1, source_target_pairs={{0,6},{2,0},{4,2},{6,4},{1,7},{3,1},{5,3},{7,5},{8,14},{10,8},{12,... | collective-permute-start | bytes 110600 | tf_op jit(solution)/shard_map/ppermute | solution.py:635
  422.7 12.2 %collective-permute-start.57 = (bf16[24,768]{1,0:T(8,128)(2,1)S(1)}, bf16[24,768]{1,0:T(8,128)(2,1)S(1)}, u32[]{:S(2)}, u32[]{:S(2)}) collective-permute-start(bf16[24,768]{1,0:T(8,128)(2,1)S(1)} %get-tuple-element.567), channel_id=1, source_target_pairs={{0,2},{2,4},{4,6},{6,0},{1,3},{3,5},{5,7},{7,1},{8,10},{10,12},{12... | collective-permute-start | bytes 110600 | tf_op jit(solution)/shard_map/ppermute | solution.py:635
  422.8 12.1 %collective-permute-start.58 = (bf16[24,768]{1,0:T(8,128)(2,1)S(1)}, bf16[24,768]{1,0:T(8,128)(2,1)S(1)}, u32[]{:S(2)}, u32[]{:S(2)}) collective-permute-start(bf16[24,768]{1,0:T(8,128)(2,1)S(1)} %get-tuple-element.568), channel_id=1, source_target_pairs={{0,4},{2,6},{4,0},{6,2},{1,5},{3,7},{5,1},{7,3},{8,12},{10,14},{12... | collective-permute-start | bytes 110600 | tf_op jit(solution)/shard_map/ppermute | solution.py:635
  424.2 10.7 %collective-permute-start.59 = (bf16[24,768]{1,0:T(8,128)(2,1)S(1)}, bf16[24,768]{1,0:T(8,128)(2,1)S(1)}, u32[]{:S(2)}, u32[]{:S(2)}) collective-permute-start(bf16[24,768]{1,0:T(8,128)(2,1)S(1)} %get-tuple-element.569), channel_id=1, source_target_pairs={{0,6},{2,0},{4,2},{6,4},{1,7},{3,1},{5,3},{7,5},{8,14},{10,8},{12,... | collective-permute-start | bytes 110600 | tf_op jit(solution)/shard_map/ppermute | solution.py:635
  (90 other events, 926.7 us)
Sparse Core Ops, SparseCore 0:
  39.5 75.2 all-gather.4

commit v3 on v2

--- a/solution.py
+++ b/solution.py
@@ -1,3 +1,5 @@
+import functools
+
 import jax
 import jax.numpy as jnp
 from jax import lax
@@ -16,6 +18,7 @@
 f32 = jnp.float32
 i32 = jnp.int32
 highest = lax.Precision.HIGHEST
+calls = 3
 
 
 def bucket_of(offset):
@@ -40,6 +43,14 @@
     weighted = grad * gain
     mean = jnp.mean(weighted * values, axis=-1, keepdims=True)
     return inverse * weighted - (inverse * inverse * inverse * mean) * values
+
+
+def store_halves(keep_ref, send_ref, index, value, core, part):
+    rows, width = value.shape
+    value = value.reshape(rows // (2 * part), 2, part, width)
+    first, second = value[:, 0].reshape(rows // 2, width), value[:, 1].reshape(rows // 2, width)
+    keep_ref[index] = jnp.where(core == 0, first, second).astype(bf16)
+    send_ref[index] = jnp.where(core == 0, second, first).astype(bf16)
 
 
 def stack_heads(rows):
@@ -100,8 +111,8 @@
 
 def attend_forward(
     source_ref, raw_ref, gain_ref, wq_ref, wk_ref, wv_ref, offsets_ref, klocal_ref, kglobal_ref, qfeat_ref,
-    bias_ref, out_ref, log_ref, query_ref, key_ref, value_ref, gkey_ref, gvalue_ref, normed_ref, pooled_ref, gains_ref,
-    value_turned, gvalue_turned,
+    bias_ref, out_ref, log_ref, query_ref, key_ref, value_ref, gkey_ref, gvalue_ref, normed_ref, gains_ref,
+    normed_turned, pooled_turned, pooled_ref, value_turned, gvalue_turned,
 ):
     rows = query_ref.shape[0]
     slots = gkey_ref.shape[0]
@@ -115,7 +126,9 @@
         def norm_rows(index, carry):
             part = pl.ds(pl.multiple_of(index * 128, 128), 128)
             values = source_ref[part, :].astype(f32)
-            normed_ref[part, :] = (values * inverse_rms(values) * gain_one).astype(bf16)
+            low = (values * inverse_rms(values) * gain_one).astype(bf16)
+            normed_ref[part, :] = low
+            normed_turned[:, part] = low.T
             return carry
 
         lax.fori_loop(0, (rows + 256) // 128, norm_rows, 0)
@@ -123,7 +136,9 @@
         def pool_rows(index, carry):
             part = pl.ds(pl.multiple_of(index * 128, 128), 128)
             values = raw_ref[part, :].astype(f32) * gain_one
-            pooled_ref[part, :] = (values * inverse_rms(values) * gain_pool).astype(bf16)
+            low = (values * inverse_rms(values) * gain_pool).astype(bf16)
+            pooled_ref[part, :] = low
+            pooled_turned[:, part] = low.T
             return carry
 
         lax.fori_loop(0, slots // 128, pool_rows, 0)
@@ -193,21 +208,31 @@
     return jnp.where(lane == 0, first, jnp.where(lane == 1, second, 0.0))
 
 
+def add_buckets(table_ref, sums, offset, head):
+    hit = (bucket_of(offset) == lax.broadcasted_iota(i32, sums.shape, 1)).astype(f32)
+    totals = lax.dot_general(
+        sums, hit, (((0,), (0,)), ((), ())), precision=highest, preferred_element_type=f32
+    )
+    row = lax.broadcasted_iota(i32, table_ref.shape, 0)
+    table_ref[...] += jnp.where(
+        row == head, totals[0:1], jnp.where(row == head + 1, totals[1:2], 0.0)
+    )
+
+
 def attend_backward(
-    query_ref, grad_ref, key_ref, value_ref, gkey_ref, gvalue_ref, normed_ref, pooled_ref, wq_ref, wk_ref, wv_ref,
-    log_ref, bias_ref, klocal_ref, kglobal_ref, qfeat_ref,
-    dwq_ref, dwk_ref, dwv_ref, dnormed_ref, dpooled_ref, near_ref, far_ref,
-    key_turned, gkey_turned, dquery, key_sum, value_sum, gkey_sum, gvalue_sum, near_sum, far_sum, normed_turned, pooled_turned,
+    last, part, own_part, first_pair, query_ref, grad_ref, key_ref, value_ref, gkey_ref, gvalue_ref, normed_ref, normed_turned, pooled_turned, wq_ref, wk_ref, wv_ref,
+    log_ref, bias_ref, klocal_ref, kglobal_ref, qfeat_ref, raw_ref, gains_ref, place_ref, old_small_ref, old_table_ref,
+    keep_ref, send_ref, dnormed_ref, draw_ref, small_ref, table_ref,
+    dnormed_sum, dpooled_sum, key_turned, gkey_turned, dquery, key_sum, value_sum, gkey_sum, gvalue_sum, near_sum, far_sum,
 ):
     rows = query_ref.shape[0]
     slots = gkey_ref.shape[0]
 
     @pl.when(pl.program_id(0) == 0)
     def start():
-        normed_turned[...] = normed_ref[...].T
-        pooled_turned[...] = pooled_ref[...].T
-        dnormed_ref[...] = jnp.zeros_like(dnormed_ref)
-        dpooled_ref[...] = jnp.zeros_like(dpooled_ref)
+        dnormed_sum[...] = jnp.zeros_like(dnormed_sum)
+        dpooled_sum[...] = jnp.zeros_like(dpooled_sum)
+        table_ref[...] = old_table_ref[...]
 
     key_turned[...] = key_ref[...].T
     gkey_turned[...] = gkey_ref[...].T
@@ -255,26 +280,88 @@
 
     lax.fori_loop(0, rows // 128, step, 0, unroll=4)
 
+    core, first_slot = place_ref[0], place_ref[1]
+    head = 2 * (first_pair + pl.program_id(0))
     lane_of = lax.broadcasted_iota(i32, (256, 256), 1)
     near = align_offsets(near_sum[...], lane_of & 127, 7, 1)
-    near_ref[0] = two_totals(near[:, :128], near[:, 128:])
+    near = two_totals(near[:, :128], near[:, 128:])
+    place = lax.broadcasted_iota(i32, (256, 128), 0)
+    add_buckets(table_ref, near, ((place + 128) & 255) - 128, head)
     lane_of = lax.broadcasted_iota(i32, (slots + 64, 128), 1)
     far = jnp.concatenate([far_sum[...], jnp.zeros((64, 128), f32)], axis=0)
     far = align_offsets(far, lane_of & 63, 6, 1)
-    first = lane_of < 64
-    far_ref[0] = two_totals(jnp.where(first, far, 0.0), jnp.where(first, 0.0, far))
-
+    far = two_totals(jnp.where(lane_of < 64, far, 0.0), jnp.where(lane_of < 64, 0.0, far))
+    place = lax.broadcasted_iota(i32, (slots + 64, 128), 0)
+    heads = normed_ref.shape[1] // 64
+    add_buckets(table_ref, far, jnp.where(place < slots, place, place - slots - 64) - first_slot, heads + head)
+
+    width = normed_ref.shape[1]
     grad_low = dquery[...]
-    dwq_ref[...] = dot_nn(normed_turned[:, 128 : 128 + rows], grad_low).astype(bf16)
-    dnormed_ref[128 : 128 + rows, :] += dot_nt(grad_low, wq_ref[...])
+    dwq = dot_nn(normed_turned[:, 128 : 128 + rows], grad_low)
+    planes = 4 if last else 3
+    lead = pl.program_id(0) * planes
+    store_halves(keep_ref, send_ref, lead, dwq, core, part)
+    dnormed_sum[128 : 128 + rows, :] += dot_nt(grad_low, wq_ref[...])
     two = jnp.concatenate([key_sum[...], value_sum[...]], axis=1).astype(bf16)
     gtwo = jnp.concatenate([gkey_sum[...], gvalue_sum[...]], axis=1).astype(bf16)
     w_two = jnp.concatenate([wk_ref[...], wv_ref[...]], axis=1)
-    dw_two = (dot_nn(normed_turned[...], two) + dot_nn(pooled_turned[...], gtwo)).astype(bf16)
-    dwk_ref[...] = dw_two[:, :128]
-    dwv_ref[...] = dw_two[:, 128:]
-    dnormed_ref[...] += dot_nt(two, w_two)
-    dpooled_ref[...] += dot_nt(gtwo, w_two)
+    dw_two = dot_nn(normed_turned[...], two) + dot_nn(pooled_turned[...], gtwo)
+    store_halves(keep_ref, send_ref, lead + 1, dw_two[:, :128], core, part)
+    store_halves(keep_ref, send_ref, lead + 2, dw_two[:, 128:], core, part)
+    dnormed_sum[...] += dot_nt(two, w_two)
+    dpooled_sum[...] += dot_nt(gtwo, w_two)
+
+    @pl.when(pl.program_id(0) == pl.num_programs(0) - 1)
+    def finish():
+        gain_one, gain_pool = gains_ref[0:1, :], gains_ref[1:2, :]
+        small_ref[...] = old_small_ref[...]
+
+        def norm_rows(index, carry):
+            part = pl.ds(pl.multiple_of(index * 128, 128), 128)
+            grad = dnormed_sum[part, :]
+            dnormed_ref[part, :] = grad.astype(bf16)
+            return carry + jnp.sum(grad * normed_ref[part, :].astype(f32), axis=0, keepdims=True)
+
+        norm_part = lax.fori_loop(0, (rows + 256) // 128, norm_rows, jnp.zeros((1, width), f32))
+        norm_part = norm_part / gain_one
+
+        def pool_rows(index, carry):
+            norm_part, pool_part = carry
+            part = pl.ds(pl.multiple_of(index * 128, 128), 128)
+            raw = raw_ref[part, :].astype(f32)
+            values = raw * gain_one
+            inverse = inverse_rms(values)
+            grad = dpooled_sum[part, :]
+            back = norm_gradient(values, inverse, gain_pool, grad)
+            draw_ref[part, :] = back.astype(bf16)
+            return (
+                norm_part + jnp.sum(back * raw, axis=0, keepdims=True),
+                pool_part + jnp.sum(grad * values * inverse, axis=0, keepdims=True),
+            )
+
+        norm_part, pool_part = lax.fori_loop(
+            0, slots // 128, pool_rows, (norm_part, jnp.zeros((1, width), f32))
+        )
+        small_ref[0:1, :] += norm_part
+        small_ref[1:2, :] += pool_part
+        if not last:
+            return
+        rows_of_small = jnp.concatenate([small_ref[...], jnp.zeros((120, width), f32)], axis=0)
+        tables = jnp.zeros((width, 128), f32)
+        row = lax.broadcasted_iota(i32, (width, 32), 0)
+        column = lax.broadcasted_iota(i32, (width, 32), 1)
+        for block in range(-(-2 * heads // own_part)):
+            chosen = (column == row % own_part + block * own_part).astype(f32)
+            shifted = table_ref[...]
+            if block:
+                shifted = jnp.concatenate(
+                    [shifted[:, 128 - 32 * block :], shifted[:, : 128 - 32 * block]], axis=1
+                )
+            tables = tables + jnp.dot(
+                chosen, shifted, precision=highest, preferred_element_type=f32
+            )
+        store_halves(keep_ref, send_ref, 3, rows_of_small.T, core, part)
+        store_halves(keep_ref, send_ref, keep_ref.shape[0] - 1, tables, core, part)
 
 
 def columns(rows, first):
@@ -327,8 +414,9 @@
             columns(slots, 0),
             columns(slots, 0),
             fixed_out(rows + 256, width),
-            fixed_out(slots, width),
             fixed_out(8, width),
+            fixed_out(width, rows + 256),
+            fixed_out(width, slots),
         ],
         out_shape=[
             jax.ShapeDtypeStruct((pairs, 256, 256), f32),
@@ -340,10 +428,11 @@
             jax.ShapeDtypeStruct((slots, width), bf16),
             jax.ShapeDtypeStruct((slots, width), bf16),
             jax.ShapeDtypeStruct((rows + 256, width), bf16),
-            jax.ShapeDtypeStruct((slots, width), bf16),
             jax.ShapeDtypeStruct((8, width), f32),
-        ],
-        scratch_shapes=[pltpu.VMEM((128, rows + 256), bf16), pltpu.VMEM((128, slots), bf16)],
+            jax.ShapeDtypeStruct((width, rows + 256), bf16),
+            jax.ShapeDtypeStruct((width, slots), bf16),
+        ],
+        scratch_shapes=[pltpu.VMEM((slots, width), bf16), pltpu.VMEM((128, rows + 256), bf16), pltpu.VMEM((128, slots), bf16)],
         compiler_params=pltpu.CompilerParams(vmem_limit_bytes=48 << 20),
         cost_estimate=pl.CostEstimate(
             flops=30 * rows * (384 + slots) * width, bytes_accessed=24 << 20, transcendentals=0
@@ -353,14 +442,16 @@
 
 
 def attention_backward(
-    first, count, queries, grads, keys, values, gkeys, gvalues, normed, pooled, weights, logs, bias, klocal, kglobal, qfeat
+    first, count, part, queries, grads, keys, values, gkeys, gvalues, normed, turned, pooled, weights, logs, bias, klocal,
+    kglobal, qfeat, raw_pool, gains, place, old_small, old_table,
 ):
     rows, width = queries.shape
     slots = gkeys.shape[0]
     blocks = rows // 128
     pairs = width // 128
+    lead = count * (4 if first + count == pairs else 3)
     return pl.pallas_call(
-        attend_backward,
+        functools.partial(attend_backward, first + count == pairs, width // 32, part, first),
         grid=(count,),
         in_specs=[
             columns(rows, first),
@@ -370,7 +461,8 @@
             columns(slots, first),
             columns(slots, first),
             fixed(rows + 256, width),
-            fixed(slots, width),
+            fixed(width, rows + 256),
+            fixed(width, slots),
             columns(width, first),
             columns(width, pairs + first),
             columns(width, 2 * pairs + first),
@@ -379,26 +471,31 @@
             fixed(rows + 256, 128),
             columns(blocks * slots, first),
             fixed(rows, 128),
+            fixed(slots, width),
+            fixed(8, width),
+            pl.BlockSpec(memory_space=pltpu.SMEM),
+            fixed(8, width),
+            fixed(32, 128),
         ],
         out_specs=[
-            columns(width, 0),
-            columns(width, 0),
-            columns(width, 0),
+            fixed_out(lead, width // 2, 128),
+            fixed_out(lead, width // 2, 128),
             fixed_out(rows + 256, width),
             fixed_out(slots, width),
-            of_pair(0, 256, 128),
-            of_pair(0, slots + 64, 128),
+            fixed_out(8, width),
+            fixed_out(32, 128),
         ],
         out_shape=[
-            jax.ShapeDtypeStruct((width, count * 128), bf16),
-            jax.ShapeDtypeStruct((width, count * 128), bf16),
-            jax.ShapeDtypeStruct((width, count * 128), bf16),
-            jax.ShapeDtypeStruct((rows + 256, width), f32),
-            jax.ShapeDtypeStruct((slots, width), f32),
-            jax.ShapeDtypeStruct((count, 256, 128), f32),
-            jax.ShapeDtypeStruct((count, slots + 64, 128), f32),
+            jax.ShapeDtypeStruct((lead, width // 2, 128), bf16),
+            jax.ShapeDtypeStruct((lead, width // 2, 128), bf16),
+            jax.ShapeDtypeStruct((rows + 256, width), bf16),
+            jax.ShapeDtypeStruct((slots, width), bf16),
+            jax.ShapeDtypeStruct((8, width), f32),
+            jax.ShapeDtypeStruct((32, 128), f32),
         ],
         scratch_shapes=[
+            pltpu.VMEM((rows + 256, width), f32),
+            pltpu.VMEM((slots, width), f32),
             pltpu.VMEM((128, rows + 256), bf16),
             pltpu.VMEM((128, slots), bf16),
             pltpu.VMEM((rows, 128), bf16),
@@ -408,8 +505,6 @@
             pltpu.VMEM((slots, 128), f32),
             pltpu.VMEM((256, 256), f32),
             pltpu.VMEM((slots, 128), f32),
-            pltpu.VMEM((width, rows + 256), bf16),
-            pltpu.VMEM((width, slots), bf16),
         ],
         compiler_params=pltpu.CompilerParams(vmem_limit_bytes=48 << 20),
         cost_estimate=pl.CostEstimate(
@@ -417,20 +512,88 @@
         ),
         name="attend_backward",
     )(
-        queries, grads, keys, values, gkeys, gvalues, normed, pooled, weights, weights, weights, logs, bias, klocal,
-        kglobal, qfeat,
-    )
+        queries, grads, keys, values, gkeys, gvalues, normed, turned, pooled, weights, weights, weights, logs, bias, klocal,
+        kglobal, qfeat, raw_pool, gains, place, old_small, old_table,
+    )
+
+
+def interleave(held, other, core):
+    held, other = held.astype(f32), other.astype(f32)
+    both = jnp.stack([jnp.where(core == 0, held, other), jnp.where(core == 0, other, held)], axis=1)
+    return both.reshape(-1, both.shape[-1])
+
+
+def fold_rows(tall):
+    rows, width = tall.shape[1:]
+    return jnp.concatenate(
+        [
+            jnp.concatenate(
+                [tall[:, r : r + 8, c : c + 256] for r in range(0, rows, 8)], axis=2
+            )
+            for c in range(0, width, 256)
+        ],
+        axis=1,
+    )
+
+
+unfold_rows = fold_rows
+
+
+def pack(
+    source_ref, keep_ref, marks_ref, wq_ref, wk_ref, wv_ref, wo_ref, gains_ref, gate_ref, up_ref, down_ref,
+    first_ref, second_ref, shared_ref,
+):
+    width = source_ref.shape[1]
+    for index, weight_ref in enumerate((wq_ref, wk_ref, wv_ref, wo_ref)):
+        first_ref[:, index * width : (index + 1) * width] = weight_ref[...]
+    first_ref[:, 4 * width :] = gains_ref[...]
+    if second_ref.shape[1] > 128:
+        hidden = gate_ref.shape[1]
+        second_ref[:, :hidden] = gate_ref[...]
+        second_ref[:, hidden : 2 * hidden] = up_ref[...]
+        second_ref[:, 2 * hidden :] = fold_rows(down_ref[...].astype(f32)[None])[0].astype(bf16)
+    slots = source_ref.shape[0] // 16
+    for slot in range(0, slots, 16):
+        rows = slice(slot * 16, slot * 16 + 256)
+        values = source_ref[rows, :].astype(f32)
+        values = values * (inverse_rms(values) * keep_ref[rows, :])
+        shared_ref[slot : slot + 16, :] = jnp.sum(values.reshape(16, 16, width), axis=1).astype(bf16)
+    marks = marks_ref[...].astype(f32)
+    rest = jnp.zeros((marks.shape[0], width - 128), f32)
+    shared_ref[slots:, :] = jnp.concatenate([marks, rest], axis=1).astype(bf16)
+
+
+def pack_all(source, keep, marks, wq, wk, wv, wo, gains, gate, up, down, aligned):
+    rows, width = source.shape
+    part, hidden = gate.shape
+    return pl.pallas_call(
+        pack,
+        out_shape=[
+            jax.ShapeDtypeStruct((part, 4 * width + 128), bf16),
+            jax.ShapeDtypeStruct((part, 3 * hidden if aligned else 128), bf16),
+            jax.ShapeDtypeStruct((rows // 16 + marks.shape[0], width), bf16),
+        ],
+        compiler_params=pltpu.CompilerParams(vmem_limit_bytes=60 << 20),
+        name="pack",
+    )(source, keep, marks, wq, wk, wv, wo, gains, gate, up, down)
 
 
 def feed_forward(
-    source_ref, mixture_ref, wo_ref, gains_ref, cot_ref, wg_ref, wu_ref, wd_ref,
-    out_ref, middle_grad_ref, dmixture_ref, dwo_ref, dgain_ref, dwg_ref, dwu_ref, dwd_ref,
-    middle, normed, turned, out_sum, grad_sum, product, gate_low, lift_low,
+    source_ref, mixture_ref, wo_ref, gains_ref, cot_ref, gate_held, gate_other, up_held, up_other, down_held, down_other,
+    place_ref,
+    out_ref, middle_grad_ref, dmixture_ref, dgain_ref, keep_out, send_out, keep_wide, send_wide, keep_down, send_down,
+    middle, normed, turned, out_sum, grad_sum, product, gate_low, lift_low, wg_ref, wu_ref, wd_ref,
 ):
-    rows = source_ref.shape[0]
+    rows, width = source_ref.shape
     part_rows = 256
     parts = rows // part_rows
     gain = gains_ref[2:3, :]
+    core = place_ref[0]
+    wg_ref[...] = interleave(gate_held[...], gate_other[...], core).astype(bf16)
+    wu_ref[...] = interleave(up_held[...], up_other[...], core).astype(bf16)
+    wd_ref[...] = interleave(
+        unfold_rows(down_held[...].astype(f32)), unfold_rows(down_other[...].astype(f32)), core
+    ).astype(bf16)
 
     @pl.when(pl.program_id(0) == 0)
     def start():
@@ -466,9 +629,18 @@
         grad_sum[part, :] += dot_nt(gate_low[part, :], wg_ref[...]) + dot_nt(
             lift_low[part, :], wu_ref[...]
         )
-    dwg_ref[...] = dot_nn(turned[...], gate_low[...]).astype(bf16)
-    dwu_ref[...] = dot_nn(turned[...], lift_low[...]).astype(bf16)
-    dwd_ref[...] = dot_nn(product[...].T, cot_ref[...]).astype(bf16)
+    wide_part, down_part = width // 32, down_held.shape[1] * down_held.shape[2] // width
+    store_halves(keep_wide, send_wide, 0, dot_nn(turned[...], gate_low[...]), core, wide_part)
+    store_halves(keep_wide, send_wide, 1, dot_nn(turned[...], lift_low[...]), core, wide_part)
+    value = dot_nn(product[...].T, cot_ref[...]).reshape(-1, 2, down_part, width)
+    first, second = value[:, 0], value[:, 1]
+    for half_ref, chosen in (
+        (keep_down, jnp.where(core == 0, first, second)),
+        (send_down, jnp.where(core == 0, second, first)),
+    ):
+        folded = fold_rows(chosen)
+        folded = folded.reshape(-1, folded.shape[2]).astype(bf16)
+        half_ref[0], half_ref[1] = folded[:, : folded.shape[1] // 2], folded[:, folded.shape[1] // 2 :]
 
     @pl.when(pl.program_id(0) == pl.num_programs(0) - 1)
     def finish():
@@ -480,7 +652,7 @@
             out_ref[part, :] = (values + out_sum[part, :]).astype(bf16)
             inverse = inverse_rms(values)
             grad = grad_sum[part, :]
-            dgain_ref[0:1, :] += jnp.sum(grad * values * inverse, axis=0, keepdims=True)
+            dgain_ref[2:3, :] += jnp.sum(grad * values * inverse, axis=0, keepdims=True)
             total = cot_ref[part, :].astype(f32) + norm_gradient(values, inverse, gain, grad)
             middle_grad_ref[part, :] = total
             low = total.astype(bf16)
@@ -490,14 +662,24 @@
             return carry
 
         lax.fori_loop(0, rows // 128, back_rows, 0)
-        dwo_ref[...] = dot_nn(turned[...], normed[...]).astype(bf16)
-
-
-def feed_forward_both(source, mixture, weights, gains, cotangent, w_gate_up, w_down):
+        for side in range(2):
+            half = slice(side * width // 2, (side + 1) * width // 2)
+            store_halves(keep_out, send_out, side, dot_nn(turned[...], normed[:, half]), core, width // 32)
+
+
+def feed_forward_both(source, mixture, weights, gains, cotangent, held, other, place):
     rows, width = source.shape
-    hidden = w_down.shape[0]
-    tile = 256
+    groups, part, total = held.shape
+    hidden = total // 3
+    tile = 512
     tiles = hidden // tile
+    step_groups = groups // tiles
+    gate_spec = pl.BlockSpec((groups, part, tile), lambda step: (0, 0, step))
+    up_spec = pl.BlockSpec((groups, part, tile), lambda step: (0, 0, step + tiles))
+    down_spec = pl.BlockSpec((step_groups, part, hidden), lambda step: (step, 0, 2))
+    wide_spec = pl.BlockSpec((2, width // 2, tile), lambda step: (0, 0, step))
+    fold_spec = pl.BlockSpec((2, step_groups * part, hidden // 2), lambda step: (0, step, 0))
+    out_spec = fixed_out(2, width // 2, width // 2)
     return pl.pallas_call(
         feed_forward,
         grid=(tiles,),
@@ -507,29 +689,37 @@
             pl.BlockSpec((width, width), lambda step: (0, 3), pipeline_mode=pl.Buffered(1)),
             fixed(8, width),
             fixed(rows, width),
-            pl.BlockSpec((width, tile), lambda step: (0, step)),
-            pl.BlockSpec((width, tile), lambda step: (0, step + tiles)),
-            pl.BlockSpec((tile, width), lambda step: (step, 0)),
+            gate_spec,
+            gate_spec,
+            up_spec,
+            up_spec,
+            down_spec,
+            down_spec,
+            pl.BlockSpec(memory_space=pltpu.SMEM),
         ],
         out_specs=[
             fixed_out(rows, width),
             fixed_out(rows, width),
             fixed_out(rows, width),
-            fixed_out(width, width),
             fixed_out(8, width),
-            pl.BlockSpec((width, tile), lambda step: (0, step)),
-            pl.BlockSpec((width, tile), lambda step: (0, step)),
-            pl.BlockSpec((tile, width), lambda step: (step, 0)),
+            out_spec,
+            out_spec,
+            wide_spec,
+            wide_spec,
+            fold_spec,
+            fold_spec,
         ],
         out_shape=[
             jax.ShapeDtypeStruct((rows, width), bf16),
             jax.ShapeDtypeStruct((rows, width), f32),
             jax.ShapeDtypeStruct((rows, width), bf16),
-            jax.ShapeDtypeStruct((width, width), bf16),
             jax.ShapeDtypeStruct((8, width), f32),
-            jax.ShapeDtypeStruct((width, hidden), bf16),
-            jax.ShapeDtypeStruct((width, hidden), bf16),
-            jax.ShapeDtypeStruct((hidden, width), bf16),
+            jax.ShapeDtypeStruct((2, width // 2, width // 2), bf16),
+            jax.ShapeDtypeStruct((2, width // 2, width // 2), bf16),
+            jax.ShapeDtypeStruct((2, width // 2, hidden), bf16),
+            jax.ShapeDtypeStruct((2, width // 2, hidden), bf16),
+            jax.ShapeDtypeStruct((2, width // 2, hidden // 2), bf16),
+            jax.ShapeDtypeStruct((2, width // 2, hidden // 2), bf16),
         ],
         scratch_shapes=[
             pltpu.VMEM((rows, width), f32),
@@ -540,13 +730,16 @@
             pltpu.VMEM((rows, tile), bf16),
             pltpu.VMEM((rows, tile), bf16),
             pltpu.VMEM((rows, tile), bf16),
-        ],
-        compiler_params=pltpu.CompilerParams(vmem_limit_bytes=56 << 20),
+            pltpu.VMEM((width, tile), bf16),
+            pltpu.VMEM((width, tile), bf16),
+            pltpu.VMEM((tile, width), bf16),
+        ],
+        compiler_params=pltpu.CompilerParams(vmem_limit_bytes=60 << 20),
         cost_estimate=pl.CostEstimate(
             flops=20 * rows * width * hidden, bytes_accessed=40 << 20, transcendentals=0
         ),
         name="feed_forward",
-    )(source, mixture, weights, gains, cotangent, w_gate_up, w_gate_up, w_down)
+    )(source, mixture, weights, gains, cotangent, held, other, held, other, held, other, place)
 
 
 def near_offsets(local_bias):
@@ -601,21 +794,6 @@
     return (own_segments[:, None] == lane - 48).astype(bf16)
 
 
-def bucket_totals(near_sums, far_sums, first_slot, buckets):
-    heads = near_sums.shape[0] * 2
-    ids = jnp.arange(buckets, dtype=i32)
-    span = near_sums.shape[1]
-    offset = (jnp.arange(span, dtype=i32) + 128) % span - 128
-    table = (bucket_of(offset)[:, None] == ids).astype(f32)
-    near = jnp.einsum("poa,ob->pab", near_sums[:, :, :2], table, precision=highest)
-    span = far_sums.shape[1]
-    place = jnp.arange(span, dtype=i32)
-    offset = jnp.where(place < span - 64, place, place - span) - first_slot
-    table = (bucket_of(offset)[:, None] == ids).astype(f32)
-    far = jnp.einsum("poa,ob->pab", far_sums[:, :, :2], table, precision=highest)
-    return near.reshape(heads, buckets), far.reshape(heads, buckets)
-
-
 def pick(values, index, dim):
     return lax.dynamic_index_in_dim(values, index, dim, keepdims=False)
 
@@ -624,22 +802,27 @@
     return [(i, (i + hop) % size) for i in range(size)]
 
 
-def split_stage(values, axis, dim):
+def add_up(parts):
+    if len(parts) == 1:
+        return parts[0]
+    return sum((part.astype(f32) for part in parts[1:]), parts[0].astype(f32))
+
+
+def split_stage(side, labels, axis, join):
     size, me = lax.axis_size(axis), lax.axis_index(axis)
-    keep = pick(values, me, dim)
-    return keep, [pick(values, (me + hop) % size, dim) for hop in range(1, size)]
+    dim = labels.index(axis) - len(labels) - 2 + side[0][0].ndim
+    chosen = []
+    for hop in range(size):
+        pieces = [
+            add_up([pick(part, (me + hop) % size, dim) for part in piece]).astype(bf16) for piece in side
+        ]
+        chosen.append(pieces[0] if len(pieces) == 1 else jnp.concatenate(pieces, axis=join))
+    return chosen[1:], chosen[0]
 
 
 def send_all(axis, pieces):
     size = lax.axis_size(axis)
     return [lax.ppermute(piece, axis, ring(size, hop + 1)) for hop, piece in enumerate(pieces)]
-
-
-def join_stage(keep, pieces):
-    total = keep.astype(f32)
-    for piece in pieces:
-        total = total + piece.astype(f32)
-    return total
 
 
 def place_stage(values, pieces, axis, dim):
@@ -655,48 +838,78 @@
     return (width // 256) * 128
 
 
-def sum_rows(grads):
-    y, x, z, core = (lax.axis_size(axis) for axis in everyone)
-    width = grads.shape[1]
-    half = half_of(width)
-    values = grads.reshape(y, x, z, core, -1, width)
-    sends = yield split_stage(values, "core", 3)
-    held = yield sends[0], send_all("core", sends[1])
-    values = join_stage(*held).astype(bf16)
-    left, right = values[..., :half], values[..., half:]
-    for left_axis, right_axis in (("x", "y"), ("y", "x")):
-        dim = 1 if left_axis == "x" else 0
-        sends = yield split_stage(left, left_axis, dim), split_stage(right, right_axis, 0)
-        (keep_left, send_left), (keep_right, send_right) = sends
-        held = yield (
-            (keep_left, send_all(left_axis, send_left)),
-            (keep_right, send_all(right_axis, send_right)),
-        )
-        left, right = (join_stage(*part).astype(bf16) for part in held)
-    sends = yield split_stage(jnp.concatenate([left, right], axis=-1), "z", 0)
-    held = yield sends[0], send_all("z", sends[1])
-    return join_stage(*held)
-
-
-def all_rows(shard):
+def scatter_steps(sides, labels, stages, join):
+    labels = [list(labels) for _ in sides]
+    for axes in stages:
+        if len(axes) < len(sides):
+            sides, labels = [[piece for side in sides for piece in side]], labels[:1]
+        split = [split_stage(side, names, axis, join) for side, names, axis in zip(sides, labels, axes)]
+        sends = yield [send for send, _ in split]
+        gots = yield [send_all(axis, send) for axis, send in zip(axes, sends)]
+        sides = [[[keep] + got] for (_, keep), got in zip(split, gots)]
+        for names, axis in zip(labels, axes):
+            names.remove(axis)
+    return add_up(sides[0][0])
+
+
+across = (("x", "y"), ("y", "x"))
+
+
+stages = (("x", "y"), ("y", "x"), ("z",))
+labels = ("y", "x", "z")
+
+
+def core_steps(pairs, part):
+    y, x, z, _ = (lax.axis_size(axis) for axis in everyone)
+    keeps, sends = zip(*pairs)
+    if part != keeps[0].shape[1] // 16:
+        keeps, sends = zip(*(regroup(keep, send, part) for keep, send in pairs))
+    sends = yield sends
+    gots = yield [lax.ppermute(send, "core", ring(2, 1)) for send in sends]
+    sides = [[], []]
+    for keep, got in zip(keeps, gots):
+        lead, _, width = keep.shape
+        held, new = (values.reshape(lead, y, x, z, part, width) for values in (keep, got))
+        sides[0].append([held[: lead // 2], new[: lead // 2]])
+        sides[1].append([held[lead // 2 :], new[lead // 2 :]])
+    return sides
+
+
+def sum_rows(pairs, part, join):
+    sides = yield from core_steps(pairs, part)
+    return (yield from scatter_steps(sides, labels, stages, join))
+
+
+def regroup(keep, send, part):
+    lead, half, width = keep.shape
+    both = jnp.stack([keep.reshape(lead, 16, -1, width), send.reshape(lead, 16, -1, width)], axis=2)
+    both = both.reshape(lead, half // part, 2, part, width)
+    me = lax.axis_index("core")
+    return tuple(pick(both, index, 2).reshape(keep.shape) for index in (me, 1 - me))
+
+
+def all_rows(shard, last):
     width = shard.shape[1]
     half = half_of(width)
     others = lax.axis_size("z") - 1
     shard = yield shard
-    held = yield shard, send_all("z", [shard] * others)
-    values = place_stage(*held, "z", 0)
+    pieces = yield send_all("z", [shard] * others)
+    values = place_stage(shard, pieces, "z", 0)
     left, right = values[..., :half], values[..., half:]
-    for left_axis, right_axis in (("x", "y"), ("y", "x")):
+    for left_axis, right_axis in across:
         dim = 1 if right_axis == "x" else 0
         left, right = yield left, right
-        held = yield (
-            (left, send_all(left_axis, [left] * (lax.axis_size(left_axis) - 1))),
-            (right, send_all(right_axis, [right] * (lax.axis_size(right_axis) - 1))),
-        )
-        left, right = place_stage(*held[0], left_axis, 0), place_stage(*held[1], right_axis, dim)
+        got = yield (
+            send_all(left_axis, [left] * (lax.axis_size(left_axis) - 1)),
+            send_all(right_axis, [right] * (lax.axis_size(right_axis) - 1)),
+        )
+        left = place_stage(left, got[0], left_axis, 0)
+        right = place_stage(right, got[1], right_axis, dim)
     values = yield jnp.concatenate([left, right], axis=-1)
-    held = yield values, send_all("core", [values])
-    return place_stage(*held, "core", 3).reshape(-1, width)
+    got = yield send_all("core", [values])
+    if not last:
+        return values.reshape(-1, *values.shape[-2:]), got[0].reshape(-1, *values.shape[-2:])
+    return place_stage(values, got, "core", 3).reshape(-1, width)
 
 
 class Chain:
@@ -712,15 +925,15 @@
             self.value, self.done = end.value, True
 
 
-def phase(chains, operand, work):
-    chains = [chain for chain in chains if not chain.done]
-    values, operand = lax.optimization_barrier(([chain.value for chain in chains], operand))
-    for chain, value in zip(chains, values):
+def phase(operand, work, launch=(), collect=None):
+    collect = launch if collect is None else collect
+    values, operand = lax.optimization_barrier(([chain.value for chain in launch], operand))
+    for chain, value in zip(launch, values):
         chain.value = value
         chain.advance()
     result = work(operand)
-    values, result = lax.optimization_barrier(([chain.value for chain in chains], result))
-    for chain, value in zip(chains, values):
+    values, result = lax.optimization_barrier(([chain.value for chain in collect], result))
+    for chain, value in zip(collect, values):
         chain.value = value
         chain.advance()
     return result
@@ -769,45 +982,28 @@
     own_segments = segment_ids[0]
     valid_float = valid_mask[0].astype(f32)
 
+    aligned = own_part * 32 == model_width
     gain_columns = jnp.pad(jnp.stack([norm_gain, pool_gain, feed_gain], axis=1), ((0, 0), (0, 125)))
-    first = Chain(
-        all_rows(
-            jnp.concatenate(
-                [query_weight, key_weight, value_weight, output_weight, gain_columns], axis=1
-            )
-        )
-    )
-    second = Chain(all_rows(down_weight))
-    values = source.astype(f32)
-    inverse = inverse_rms(values)
-
-    def share(operands):
-        values, gate_weight, up_weight = operands
-        w_gate_up = lax.all_gather(
-            jnp.concatenate([gate_weight, up_weight], axis=1), everyone, axis=0, tiled=True
-        )
+    marks = jnp.concatenate([segment_ids.reshape(-1, 128), valid_mask.reshape(-1, 128)])
+    packed, packed_second, shared = pack_all(
+        source, valid_float[:, None], marks, query_weight, key_weight, value_weight, output_weight, gain_columns,
+        gate_weight, up_weight, down_weight, aligned,
+    )
+    first = Chain(all_rows(packed, True))
+    later = [Chain(all_rows(packed_second, False))] if aligned else []
+    place = jnp.stack([lax.axis_index("core"), first_slot]).astype(i32)
+
+    def share(shared):
         before, after = neighbour_rows(source[-128:], source[:128])
-        own_raw = jnp.sum(
-            (values * (inverse * valid_float[:, None])).reshape(own_slots, 16, model_width), axis=1
-        )
-        marks = jnp.stack([own_segments, valid_mask[0]]).astype(bf16).reshape(-1)
-        mark_rows = -(-marks.size // model_width)
-        pad_rows = -(-mark_rows // 16) * 16
-        marks = jnp.pad(marks, (0, pad_rows * model_width - marks.size))
-        shared = lax.all_gather(
-            jnp.concatenate([own_raw.astype(bf16), marks.reshape(pad_rows, model_width)], axis=0),
-            seq, axis=0, tiled=False,
-        )
-        return own_raw, shared, before, after, w_gate_up
-
-    own_raw, shared, before, after, w_gate_up = share((values, gate_weight, up_weight))
-    shared = phase([first], shared, lambda shared: shared)
+        copies = jnp.broadcast_to(shared, (seq_count,) + shared.shape)
+        return lax.all_to_all(copies, seq, 0, 0, tiled=True), before, after
+
+    shared, before, after = phase(shared, share, [first])
 
     def near_parts(operands):
-        shared, local_bias = operands
+        shared, before, after, local_bias = operands
         raw_pool = shared[:, :own_slots].reshape(slot_count, model_width)
-        all_marks = shared[:, own_slots:].reshape(seq_count, -1)[:, : 2 * tok_rows].astype(i32)
-        all_marks = all_marks.reshape(seq_count, 2, tok_rows)
+        all_marks = shared[:, own_slots:, :128].astype(i32).reshape(seq_count, 2, tok_rows)
         all_segments, all_valid = all_marks[:, 0].reshape(-1), all_marks[:, 1].reshape(-1)
         slot_segments = all_segments.reshape(slot_count, 16)[:, 0]
         slot_live = jnp.sum(all_valid.reshape(slot_count, 16), axis=1) > 0
@@ -820,125 +1016,161 @@
         return raw_pool, slot_segments, slot_live, feat_near, near_offsets(local_bias), source_ext
 
     raw_pool, slot_segments, slot_live, feat_near, bias_near, source_ext = phase(
-        [first, second], (shared, local_bias), near_parts
+        (shared, before, after, local_bias), near_parts, [first] + later, [first]
     )
     feat_query = query_features(own_segments)
     feat_far = phase(
-        [first, second],
         (global_bias, slot_segments, slot_live),
         lambda operands: far_features(*operands, first_slot, blocks),
-    )
-    phase([first], (), lambda nothing: nothing)
+        [first],
+        [first] + later,
+    )
+    phase((), lambda nothing: nothing, [first] + later)
     weights = first.value
 
-    bias, mixture, logs, queries, keys, vals, gkeys, gvals, normed, pooled, gains = phase(
-        [second],
+    bias, mixture, logs, queries, keys, vals, gkeys, gvals, normed, gains, turned, pooled = phase(
         (source_ext, raw_pool, weights, bias_near, feat_near, feat_far, feat_query),
         lambda operands: attention_forward(*operands),
-    )
-    phase([second], (), lambda nothing: nothing)
-    w_down = second.value
-    layer_output, middle_grad, mixture_grad, d_output, d_feed, d_gate, d_up, d_down = feed_forward_both(
-        source, mixture, weights, gains, upstream, w_gate_up, w_down
-    )
-    chains = [
-        Chain(sum_rows(jnp.concatenate([d_gate, d_up, d_output], axis=1))),
-        Chain(sum_rows(d_down)),
-    ]
-    calls = 3 if pairs % 3 == 0 else 1
+        later,
+    )
+    phase((), lambda nothing: nothing, later)
+    if aligned:
+        held, other = later[0].value
+        kernel_place = place
+    else:
+        wide = lax.all_gather(jnp.concatenate([gate_weight, up_weight], axis=1), everyone, axis=0, tiled=True)
+        tall = lax.all_gather(down_weight, everyone, axis=0, tiled=True)
+        tall = fold_rows(tall.reshape(32, -1, model_width))
+        both = jnp.concatenate([wide.reshape(32, -1, 2 * hidden), tall], axis=2)
+        both = both.reshape(16, 2, -1, 3 * hidden)
+        held, other = both[:, 0], both[:, 1]
+        kernel_place = place * jnp.array([0, 1], i32)
+    layer_output, middle_grad, mixture_grad, small, out_keep, out_send, wide_keep, wide_send, down_keep, down_send = (
+        feed_forward_both(source, mixture, weights, gains, upstream, held, other, kernel_place)
+    )
+    rest = []
+    if aligned:
+        pieces = [(wide_keep, wide_send), (down_keep, down_send), (out_keep, out_send)]
+        rest = [Chain(sum_rows(pieces, own_part, -1))]
+    table = jnp.zeros((32, 128), f32)
     count = pairs // calls
-    near_sums, far_sums = [], []
-    normed_grad, pooled_grad = 0.0, 0.0
+    dnormed, draw, waiting, started = [], [], [], []
     for call in range(calls):
-        dwq, dwk, dwv, dnormed, dpooled, near, far = phase(
-            chains,
-            mixture_grad,
-            lambda grad: attention_backward(
-                call * count, count, queries, grad, keys, vals, gkeys, gvals, normed, pooled, weights, logs,
-                bias, feat_near, feat_far, feat_query,
+        keep, send, dnormed_part, draw_part, small, table = phase(
+            (mixture_grad, small, table),
+            lambda operands: attention_backward(
+                call * count, count, own_part, queries, operands[0], keys, vals, gkeys, gvals, normed, turned, pooled, weights,
+                logs, bias, feat_near, feat_far, feat_query, raw_pool, gains, kernel_place, *operands[1:],
             ),
-        )
-        chains.append(Chain(sum_rows(jnp.concatenate([dwq, dwk, dwv], axis=1))))
-        near_sums.append(near)
-        far_sums.append(far)
-        normed_grad = normed_grad + dnormed
-        pooled_grad = pooled_grad + dpooled
+            rest + started,
+        )
+        waiting.append((keep, send))
+        if call > 0:
+            started.append(Chain(core_steps(waiting, own_part)))
+            waiting = []
+        dnormed.append(dnormed_part)
+        draw.append(draw_part)
 
     def return_grads(operands):
-        normed_grad, pooled_grad = operands
-        spread = lax.all_to_all(
-            pooled_grad.astype(bf16).reshape(seq_count, own_slots, model_width), seq, 0, 0, tiled=True
-        )
-        to_head, to_tail = neighbour_rows(
-            normed_grad[-128:].astype(bf16), normed_grad[:128].astype(bf16)
-        )
-        return normed_grad, spread, to_head, to_tail
-
-    normed_grad, spread, to_head, to_tail = phase(chains, (normed_grad, pooled_grad), return_grads)
-    pooled_grad = jnp.sum(spread.astype(f32), axis=0)
-    edges = jnp.concatenate(
-        [to_head.astype(f32), jnp.zeros((tok_rows - 256, model_width), f32), to_tail.astype(f32)]
-    )
-    gain_one, gain_pool = gains[0:1], gains[1:2]
+        dnormed, draw = operands
+        me = lax.axis_index(seq)
+        head, tail = (add_up([part[where] for part in dnormed]).astype(bf16) for where in (slice(128), slice(-128, None)))
+        target = lax.broadcasted_iota(i32, (seq_count, 1, 1), 0)
+        edges = jnp.where(target == me - 1, head[None], jnp.where(target == me + 1, tail[None], 0))
+        pools = add_up(draw).astype(bf16).reshape(seq_count, own_slots, model_width)
+        return lax.all_to_all(jnp.concatenate([pools, edges], axis=1), seq, 0, 0, tiled=True)
 
     def finish(operands):
-        normed_grad, pooled_grad, edges = operands
-        pooled_raw = own_raw * gain_one
-        pool_inverse = inverse_rms(pooled_raw)
-        pool_delta = jnp.sum(pooled_grad * pooled_raw * pool_inverse, axis=0)
-        pooled_raw_grad = norm_gradient(pooled_raw, pool_inverse, gain_pool, pooled_grad)
+        me = lax.axis_index(seq)
+        spread = operands[:, :own_slots]
+        to_head, to_tail = (
+            jnp.where(
+                (near >= 0) & (near < seq_count),
+                pick(operands[:, own_slots:], jnp.clip(near, 0, seq_count - 1), 0),
+                0,
+            )
+            for near in (me - 1, me + 1)
+        )
+        values = source.astype(f32)
+        inverse = inverse_rms(values)
+        edges = jnp.concatenate(
+            [to_head.astype(f32), jnp.zeros((tok_rows - 256, model_width), f32), to_tail.astype(f32)]
+        )
+        pooled_raw_grad = jnp.sum(spread.astype(f32), axis=0)
         spread_grad = jnp.broadcast_to(
             pooled_raw_grad[:, None, :], (own_slots, 16, model_width)
         ).reshape(tok_rows, model_width)
-        normed_grad = normed_grad[128:-128] + edges + spread_grad * valid_float[:, None]
-        norm_delta = jnp.sum(normed_grad * values * inverse, axis=0)
-        input_delta = middle_grad + norm_gradient(values, inverse, gain_one, normed_grad)
-        local_delta, global_delta = bucket_totals(
-            jnp.concatenate(near_sums), jnp.concatenate(far_sums), first_slot, buckets
-        )
-        small = jnp.concatenate(
-            [norm_delta, pool_delta, d_feed[0], local_delta.reshape(-1), global_delta.reshape(-1)]
-        ).reshape(1, -1)
-        return input_delta, small
-
-    input_delta, small = phase(chains, (normed_grad, pooled_grad, edges), finish)
-    small = phase(
-        chains,
-        small,
-        lambda small: jnp.sum(lax.all_gather(small, batch, axis=0, tiled=True), axis=0, keepdims=True),
-    )
-    small = phase(
-        chains,
-        small,
-        lambda small: jnp.sum(lax.all_gather(small, seq, axis=0, tiled=True), axis=0),
-    )
-    rest_delta, down_delta = chains[0].value, chains[1].value
-    size = count * 128
-    query_deltas = [chain.value[:, :size] for chain in chains[2:]]
-    key_deltas = [chain.value[:, size : 2 * size] for chain in chains[2:]]
-    value_deltas = [chain.value[:, 2 * size :] for chain in chains[2:]]
-    place = lax.axis_index(everyone) * own_part
-    gain_deltas = [
-        lax.dynamic_slice_in_dim(small[i * model_width : (i + 1) * model_width], place, own_part)
-        for i in range(3)
-    ]
-    bias_size = local_bias.size
-    local_total = small[3 * model_width : 3 * model_width + bias_size].reshape(local_bias.shape)
-    global_total = small[3 * model_width + bias_size :].reshape(local_bias.shape)
+        normed_grad = add_up([part[128:-128] for part in dnormed])
+        normed_grad = normed_grad + edges + spread_grad * valid_float[:, None]
+        return middle_grad + norm_gradient(values, inverse, gains[0:1], normed_grad)
+
+    def return_and_start(operands):
+        for chain in rest:
+            chain.advance()
+        return return_grads(operands)
+
+    held = []
+    phase((dnormed, draw), lambda operands: held.append(return_and_start(operands)), started[1:])
+    operands = held[0]
+    sides = [sum((chain.value[side] for chain in started), []) for side in range(2)]
+    last = Chain(scatter_steps(sides, labels, stages, 0))
+    operands = phase(operands, lambda operands: operands, [last])
+    input_delta = phase(operands, finish, [last], rest + [last])
+    phase((), lambda nothing: nothing, [last])
+    total = last.value
+    half = total.shape[0] // 2
+    sides = [total[:half], total[half:]]
+    extra = jnp.concatenate([side[half - 1] for side in sides], axis=-1)
+    blocks_of_table = -(-4 * pairs // own_part)
+    tables = extra[:, 128 : 128 + buckets * blocks_of_table].reshape(own_part, blocks_of_table, buckets)
+    tables = tables.transpose(1, 0, 2).reshape((2,) + local_bias.shape)
+    query_delta, key_delta, value_delta = (
+        jnp.concatenate(
+            [sides[pair % count][3 * (pair // count) + index] for pair in range(pairs)],
+            axis=-1,
+        )
+        for index in range(3)
+    )
+    if aligned:
+        total = rest[0].value[0]
+        side, fold, half = total.shape[1] // 2, hidden // 2, model_width // 2
+        left, right = total[:, :side], total[:, side:]
+        gate_delta, up_delta = left[:, :hidden], right[:, :hidden]
+        tall = jnp.concatenate([left[:, hidden : hidden + fold], right[:, hidden : hidden + fold]], axis=1)
+        down_delta = unfold_rows(tall[None])[0]
+        output_delta = jnp.concatenate([left[:, hidden + fold :], right[:, hidden + fold :]], axis=1)
+    else:
+
+        def whole_rows(keep, send):
+            width = keep.shape[-1]
+            both = jnp.stack([keep.reshape(16, -1, width), send.reshape(16, -1, width)], axis=1)
+            return both.reshape(32, -1, width)
+
+        def join(halves):
+            return jnp.concatenate([halves[0], halves[1]], axis=-1)
+
+        def scatter(grads):
+            grads = grads.reshape(-1, grads.shape[-1])
+            return lax.psum_scatter(grads, everyone, scatter_dimension=0, tiled=True).astype(f32)
+
+        gate_delta = scatter(whole_rows(wide_keep[0], wide_send[0]))
+        up_delta = scatter(whole_rows(wide_keep[1], wide_send[1]))
+        output_delta = scatter(whole_rows(join(out_keep), join(out_send)))
+        down_delta = scatter(unfold_rows(whole_rows(join(down_keep), join(down_send))))
     return (
         layer_output[None],
         input_delta[None],
-        gain_deltas[0],
-        gain_deltas[1],
-        gain_deltas[2],
-        jnp.concatenate(query_deltas, axis=1),
-        jnp.concatenate(key_deltas, axis=1),
-        jnp.concatenate(value_deltas, axis=1),
-        rest_delta[:, 2 * hidden :],
-        local_total,
-        global_total,
-        rest_delta[:, :hidden],
-        rest_delta[:, hidden : 2 * hidden],
+        extra[:, 0],
+        extra[:, 1],
+        extra[:, 2],
+        query_delta,
+        key_delta,
+        value_delta,
+        output_delta,
+        tables[0],
+        tables[1],
+        gate_delta,
+        up_delta,
         down_delta,
     )
 

time: 452 us -> 378 us (0.84)
  blocking collectives: 33.5 us -> 0 us
  starting transfers between devices: 81.3 us -> 52 us
  between operations: 16.4 us -> 2.9 us
  Pallas kernels: 159 us -> 171 us
  other arithmetic: 52.6 us -> 40.9 us
    all_gather x3 -> x0, blocking collectives: 33.5 us -> none  [the longest x1 13.9 us: on_device(): lax.all_gather(small, batch, axis=0, tiled=True)]
    ppermute x56 -> x30, starting transfers between devices: 66.2 us -> 37.4 us  [send_all(): lax.ppermute(piece, axis, ring(size, hop + 1))]
    squeeze x25 -> x1, local copies, waits for them, and re-layouts: 14.7 us -> 0.01 us  [on_device(): extra = jnp.concatenate([side[half - 1] for side in sides], axis=-1)]
    pallas_call x3 -> x4, Pallas kernels: 74.3 us -> 84.3 us  [the longest x3 80.8 us: attention_backward(): pl.pallas_call(functools.partial(attend_backward, first + count == pairs,...]
    reduce_sum x6 -> x1, other arithmetic: 5.83 us -> 0.06 us  [finish(): pooled_raw_grad = jnp.sum(spread.astype(f32), axis=0)]
    dynamic_update_slice x12 -> x11, local copies, waits for them, and re-layouts: 4.6 us -> 10.3 us  [place_stage(): lax.dynamic_update_index_in_dim(jnp.zeros(shape, values.dtype), values, m...]
    dynamic_update_slice x16 -> x15, local copies, waits for them, and re-layouts: 8.85 us -> 14.5 us  [place_stage(): lax.dynamic_update_index_in_dim(out, piece, (me - hop - 1) % size, dim)]
    dynamic_slice x3 -> x12, local copies, waits for them, and re-layouts: 1.75 us -> 7.26 us  [pick(): return lax.dynamic_index_in_dim(values, index, dim, keepdims=False)]
  transfers between devices with their start and end apart: 62 -> 40, of which waited for: 13 -> 13; matrix products, arithmetic and copies ran while one was open for 12% -> 18% of each run, Pallas kernels for 24% -> 31%
where the time goes in v3:
time: 378 us; the launch traced here: 374 us
  Pallas kernels  171 us (45%)
  local copies, waits for them, and re-layouts  59.7 us (16%)
  starting transfers between devices  52 us (14%)
  other arithmetic  40.9 us (11%)
  waiting for transfers between devices  40 us (11%)
  matrix products  8.08 us (2%)
    pallas_call x3, Pallas kernels, attention_backward(): pl.pallas_call(functools.partial(attend_backward, first + count == pairs,...  80.8 us
    pallas_call x1, Pallas kernels, feed_forward_both(): pl.pallas_call(feed_forward, grid=(tiles,), in_specs=[fixed(rows, width),...  52.1 us
    ppermute x30, starting transfers between devices, send_all(): lax.ppermute(piece, axis, ring(size, hop + 1))  37.4 us
    ppermute x30, waiting for transfers between devices, send_all(): lax.ppermute(piece, axis, ring(size, hop + 1))  36.4 us
    pallas_call x1, Pallas kernels, attention_forward(): pl.pallas_call(attend_forward, grid=(pairs,), in_specs=[fixed(rows + 256,...  34.2 us
    dynamic_update_slice x15, local copies, waits for them, and re-layouts, place_stage(): lax.dynamic_update_index_in_dim(out, piece, (me - hop - 1) % size, dim)  14.5 us
    dynamic_update_slice x11, local copies, waits for them, and re-layouts, place_stage(): lax.dynamic_update_index_in_dim(jnp.zeros(shape, values.dtype), values, m...  10.3 us
    convert_element_type x24, other arithmetic, split_stage(): add_up([pick(part, (me + hop) % size, dim) for part in piece]).astype(bf16)  8.68 us
  transfers between devices with their start and end apart: 40, of which 13 were waited for; matrix products, arithmetic and copies ran while one was open for 18% of the time, Pallas kernels for 31%

profile of v3, /device:TPU:0, one launch (start us, length us, event | category | flops | bytes accessed | tf_op | source)
XLA Modules:
  0.0 374.2 jit_solution(13133557786235307193)
XLA Ops:
  5.1 3.4 pack.1
  8.5 3.0 collective-permute-start
  11.6 2.6 collective-permute-start.1
  15.5 1.7 broadcast_in_dim.227
  17.2 3.7 all-to-all-start
  21.7 4.6 %collective-permute-start.3 = (bf16[128,768]{1,0:T(8,128)(2,1)}, bf16[128,768]{1,0:T(8,128)(2,1)}, u32[]{:S(2)}, u32[]{:S(2)}) collective-permute-start(bf16[128,768]{1,0:T(8,128)(2,1)} %get-tuple-element.394), channel_id=1, source_target_pairs={{0,8},{8,16},{16,24},{1,9},{9,17},{17,25},{2,10},{10,18},{18,26},{... | collective-permute-start | bytes 589832 | tf_op jit(solution)/shard_map/ppermute | solution.py:945
  33.0 3.4 collective-permute-done.4
  41.2 2.6 collective-permute-start.11
  44.3 1.4 collective-permute-start.5
  47.8 1.5 bitcast_dynamic-update-slice_fusion.15
  50.2 1.7 bitcast_dynamic-update-slice_fusion.21
  53.3 2.5 pad_maximum_fusion.2.source_ref
  56.8 1.7 bitcast_dynamic-update-slice_fusion.20
  60.2 1.9 collective-permute-start.7
  62.3 7.8 %convolution_convert_fusion.kglobal_ref = bf16[2048,768]{1,0:T(8,128)(2,1)} fusion(s32[264]{0:T(512)S(1)} %get-tuple-element.537, s32[264]{0:T(512)S(1)} %copy-done.63, s32[264]{0:T(512)S(1)} %copy-done.59, s32[264]{0:T(512)S(1)} %copy-done.62, s32[264]{0:T(512)S(1)} %copy-done.64, s32[2048]{0:T(1024)S(1)} %get-tuple-element.530, ...), kind=kOutput, calls=%fused_computation.5 | convolution fusion | flops 852793344 | bytes 3378108 | tf_op jit(solution)/shard_map/dot_general | solution.py:783
  71.6 1.6 collective-permute-done.7
  78.2 1.7 collective-permute-start.14
  84.5 8.4 %collective-permute-done.13 = bf16[4,24,3072]{2,1,0:T(8,128)(2,1)S(1)} collective-permute-done((bf16[4,24,3072]{2,1,0:T(8,128)(2,1)S(1)}, bf16[4,24,3072]{2,1,0:T(8,128)(2,1)S(1)}, u32[]{:S(2)}, u32[]{:S(2)}) %collective-permute-start.13) | collective-permute-done | bytes 589856 | tf_op jit(solution)/shard_map/ppermute | solution.py:825
  95.6 1.7 collective-permute-start.15
  98.8 1.4 bitcast_dynamic-update-slice_fusion.5
  100.4 1.4 bitcast_dynamic-update-slice_fusion.2
  101.9 34.2 %attend_forward.1 = (f32[6,256,256]{2,1,0:T(8,128)S(1)}, bf16[1024,768]{1,0:T(8,128)(2,1)S(1)}, f32[6,8,256]{2,1,0:T(8,128)S(1)}, bf16[1024,768]{1,0:T(8,128)(2,...) custom-call(bf16[1280,768]{1,0:T(8,128)(2,1)} %pad_maximum_fusion.2., ...), custom_call_target="tpu_custom_call" | custom-call | flops 15099494400 | bytes 25165824 | tf_op jit(solution)/shard_map/attend_forward/pallas_call | solution.py:392
  136.1 2.3 bitcast_dynamic-update-slice_fusion.4
  138.4 1.4 bitcast_dynamic-update-slice_fusion.3
  141.1 7.2 %collective-permute-done.17 = bf16[2,2,4,24,6144]{4,3,2,1,0:T(8,128)(2,1)S(1)} collective-permute-done((bf16[2,2,4,24,6144]{4,3,2,1,0:T(8,128)(2,1)S(1)}, bf16[2,2,4,24,6144]{4,3,2,1,0:T(8,128)(2,1)S(1)}, u32[]{:S(2)}, u32[]{:S(2)}) %collective-permute-start.17) | collective-permute-done | bytes 4718624 | tf_op jit(solution)/shard_map/ppermute | solution.py:825
  148.2 2.1 copy-done.68
  150.3 52.1 %feed_forward.1 = (bf16[1024,768]{1,0:T(8,128)(2,1)}, f32[1024,768]{1,0:T(8,128)}, bf16[1024,768]{1,0:T(8,128)(2,1)}, f32[8,768]{1,0:T(8,128)}, bf16[2,384,384]{...) custom-call(bf16[1024,768]{1,0:T(8,128)(2,1)} %bitcast.392, ...), custom_call_target="tpu_custom_call" | custom-call | flops 32212254720 | bytes 41943040 | tf_op jit(solution)/shard_map/feed_forward/pallas_call | solution.py:683
  203.4 1.5 fusion.145
  206.9 27.0 %attend_backward.3 = (bf16[6,384,128]{2,1,0:T(8,128)(2,1)S(1)}, bf16[6,384,128]{2,1,0:T(8,128)(2,1)S(1)}, bf16[1280,768]{1,0:T(8,128)(2,1)}, bf16[256,768]{1,0:T...) custom-call(bf16[1024,768]{1,0:T(8,128)(2,1)S(1)} %copy-done.6, ...), custom_call_target="tpu_custom_call" | custom-call | flops 10066329600 | bytes 8388608 | tf_op jit(solution)/shard_map/attend_backward/pallas_call | solution.py:453
  234.3 2.1 fusion.144
  236.4 1.5 fusion.146
  245.3 26.6 %attend_backward.4 = (bf16[6,384,128]{2,1,0:T(8,128)(2,1)S(1)}, bf16[6,384,128]{2,1,0:T(8,128)(2,1)S(1)}, bf16[1280,768]{1,0:T(8,128)(2,1)}, bf16[256,768]{1,0:T...) custom-call(bf16[1024,768]{1,0:T(8,128)(2,1)S(1)} %copy-done.6, ...), custom_call_target="tpu_custom_call" | custom-call | flops 10066329600 | bytes 8388608 | tf_op jit(solution)/shard_map/attend_backward/pallas_call | solution.py:453
  273.4 2.5 add_convert_fusion.4
  280.7 27.2 %attend_backward.5 = (bf16[8,384,128]{2,1,0:T(8,128)(2,1)S(1)}, bf16[8,384,128]{2,1,0:T(8,128)(2,1)S(1)}, bf16[1280,768]{1,0:T(8,128)(2,1)}, bf16[256,768]{1,0:T...) custom-call(bf16[1024,768]{1,0:T(8,128)(2,1)S(1)} %copy-done.6, bf16[1024,768]{1,0:T(8,128)(2,1)} %get-tuple-element.314.grad_ref, ...), custom_call_target="tpu_custom_call" | custom-call | flops 10066329600 | bytes 8388608 | tf_op jit(solution)/shard_map/attend_backward/pallas_call | solution.py:453
  311.4 1.5 add_convert_fusion.19
  314.1 3.7 all-to-all-start.1
  319.6 1.5 fusion.78
  322.2 3.5 collective-permute-start.29
  333.7 1.7 collective-permute-start.31
  335.4 1.5 collective-permute-start.32
  337.2 9.7 %collective-permute-done.31 = bf16[10,2,4,24,128]{4,3,0,2,1:T(8,128)(2,1)S(1)} collective-permute-done((bf16[10,2,4,24,128]{4,3,0,2,1:T(8,128)(2,1)}, bf16[10,2,4,24,128]{4,3,0,2,1:T(8,128)(2,1)S(1)}, u32[]{:S(2)}, u32[]{:S(2)}) %collective-permute-start.31) | collective-permute-done | bytes 491552 | tf_op jit(solution)/shard_map/ppermute | solution.py:825
  348.6 1.5 collective-permute-start.33
  350.8 2.5 fusion
  353.3 4.3 %fusion.3 = f32[1024,768]{1,0:T(8,128)} fusion(f32[1024,768]{1,0:T(8,128)S(1)} %copy-done.27, f32[1024]{0:T(1024)S(1)} %get-tuple-element.521, f32[1024]{0:T(1024)S(1)} %get-tuple-element.520, bf16[1,1024,768]{2,1,0:T(8,128)(2,1)S(1)} %copy-done.18, f32[768]{0:T(1024)S(1)} %slice_reduce_fusion.4, f32[1024]{0:T(1024)S(1)} %bitcast.440, ...), kind=kLoop, calls=%fused_computation.9 | loop fusion | flops 12582912 | bytes 13585408 | tf_op jit(solution)/shard_map/add | solution.py:1105
  360.1 2.7 collective-permute-start.35
  362.8 1.4 collective-permute-start.36
  366.2 2.1 collective-permute-done.35
  368.3 3.5 collective-permute-done.36
  (387 shorter events, 82.7 us)
Async XLA Ops:
  0.6 52.1 %copy-start = (f32[12,32]{1,0:T(8,128)S(1)}, f32[12,32]{1,0:T(8,128)}, u32[]{:S(2)}) copy-start(f32[12,32]{1,0:T(8,128)} %param.27) | copy-start | bytes 4612
  1.4 19.6 %copy-start.17 = (bf16[1,1024,768]{2,1,0:T(8,128)(2,1)S(1)}, bf16[1,1024,768]{2,1,0:T(8,128)(2,1)}, u32[]{:S(2)}) copy-start(bf16[1,1024,768]{2,1,0:T(8,128)(2,1)} %param.16) | copy-start | bytes 4718596
  5.1 26.0 %copy-start.53 = (s32[1,1024]{1,0:T(1,128)S(1)}, s32[1,1024]{1,0:T(1,128)}, u32[]{:S(2)}) copy-start(s32[1,1024]{1,0:T(1,128)} %param.17) | copy-start | bytes 12292
  8.5 22.6 %copy-start.52 = (bf16[24,3200]{1,0:T(8,128)(2,1)S(1)}, bf16[24,3200]{1,0:T(8,128)(2,1)}, u32[]{:S(2)}) copy-start(bf16[24,3200]{1,0:T(8,128)(2,1)} %get-tuple-element.191) | copy-start | bytes 460804
  8.5 24.4 %collective-permute-start = (bf16[24,3200]{1,0:T(8,128)(2,1)}, bf16[24,3200]{1,0:T(8,128)(2,1)}, u32[]{:S(2)}, u32[]{:S(2)}) collective-permute-start(bf16[24,3200]{1,0:T(8,128)(2,1)} %get-tuple-element.191), channel_id=1, source_target_pairs={{0,2},{2,4},{4,6},{6,0},{1,3},{3,5},{5,7},{7,1},{8,10},{10,12},{12... | collective-permute-start | bytes 460808 | tf_op jit(solution)/shard_map/ppermute | solution.py:825
  11.6 21.4 %collective-permute-start.1 = (bf16[24,3200]{1,0:T(8,128)(2,1)}, bf16[24,3200]{1,0:T(8,128)(2,1)}, u32[]{:S(2)}, u32[]{:S(2)}) collective-permute-start(bf16[24,3200]{1,0:T(8,128)(2,1)} %get-tuple-element.191), channel_id=1, source_target_pairs={{0,4},{2,6},{4,0},{6,2},{1,5},{3,7},{5,1},{7,3},{8,12},{10,14},{12... | collective-permute-start | bytes 460808 | tf_op jit(solution)/shard_map/ppermute | solution.py:825
  14.2 18.8 %collective-permute-start.2 = (bf16[24,3200]{1,0:T(8,128)(2,1)}, bf16[24,3200]{1,0:T(8,128)(2,1)}, u32[]{:S(2)}, u32[]{:S(2)}) collective-permute-start(bf16[24,3200]{1,0:T(8,128)(2,1)} %get-tuple-element.191), channel_id=1, source_target_pairs={{0,6},{2,0},{4,2},{6,4},{1,7},{3,1},{5,3},{7,5},{8,14},{10,8},{12,... | collective-permute-start | bytes 460808 | tf_op jit(solution)/shard_map/ppermute | solution.py:825
  17.2 19.1 %all-to-all-start = ((bf16[4,80,768]{2,1,0:T(8,128)(2,1)}), bf16[4,80,768]{2,1,0:T(8,128)(2,1)S(1)}, u32[]{:S(2)}, u32[]{:S(2)}) async-start(bf16[4,80,768]{2,1,0:T(8,128)(2,1)} %broadcast_in_dim.227), calls=%async_computation | async-start | bytes 983040 | tf_op jit(solution)/shard_map/all_to_all | solution.py:999
  21.7 11.3 %collective-permute-start.3 = (bf16[128,768]{1,0:T(8,128)(2,1)}, bf16[128,768]{1,0:T(8,128)(2,1)}, u32[]{:S(2)}, u32[]{:S(2)}) collective-permute-start(bf16[128,768]{1,0:T(8,128)(2,1)} %get-tuple-element.394), channel_id=1, source_target_pairs={{0,8},{8,16},{16,24},{1,9},{9,17},{17,25},{2,10},{10,18},{18,26},{... | collective-permute-start | bytes 589832 | tf_op jit(solution)/shard_map/ppermute | solution.py:945
  26.3 10.0 %collective-permute-start.4 = (bf16[128,768]{1,0:T(8,128)(2,1)}, bf16[128,768]{1,0:T(8,128)(2,1)}, u32[]{:S(2)}, u32[]{:S(2)}) collective-permute-start(bf16[128,768]{1,0:T(8,128)(2,1)} %get-tuple-element.393), channel_id=1, source_target_pairs={{8,0},{16,8},{24,16},{9,1},{17,9},{25,17},{10,2},{18,10},{26,18},{... | collective-permute-start | bytes 589832 | tf_op jit(solution)/shard_map/ppermute | solution.py:946
  40.8 30.8 %collective-permute-start.10 = (bf16[24,6144]{1,0:T(8,128)(2,1)}, bf16[24,6144]{1,0:T(8,128)(2,1)}, u32[]{:S(2)}, u32[]{:S(2)}) collective-permute-start(bf16[24,6144]{1,0:T(8,128)(2,1)} %get-tuple-element.212), channel_id=1, source_target_pairs={{0,4},{2,6},{4,0},{6,2},{1,5},{3,7},{5,1},{7,3},{8,12},{10,14},{12... | collective-permute-start | bytes 884744 | tf_op jit(solution)/shard_map/ppermute | solution.py:825
  41.2 30.4 %collective-permute-start.11 = (bf16[24,6144]{1,0:T(8,128)(2,1)}, bf16[24,6144]{1,0:T(8,128)(2,1)}, u32[]{:S(2)}, u32[]{:S(2)}) collective-permute-start(bf16[24,6144]{1,0:T(8,128)(2,1)} %get-tuple-element.212), channel_id=1, source_target_pairs={{0,6},{2,0},{4,2},{6,4},{1,7},{3,1},{5,3},{7,5},{8,14},{10,8},{12,... | collective-permute-start | bytes 884744 | tf_op jit(solution)/shard_map/ppermute | solution.py:825
  43.8 27.8 %collective-permute-start.9 = (bf16[24,6144]{1,0:T(8,128)(2,1)}, bf16[24,6144]{1,0:T(8,128)(2,1)}, u32[]{:S(2)}, u32[]{:S(2)}) collective-permute-start(bf16[24,6144]{1,0:T(8,128)(2,1)} %get-tuple-element.212), channel_id=1, source_target_pairs={{0,2},{2,4},{4,6},{6,0},{1,3},{3,5},{5,7},{7,1},{8,10},{10,12},{12... | collective-permute-start | bytes 884744 | tf_op jit(solution)/shard_map/ppermute | solution.py:825
  44.3 11.5 %collective-permute-start.6 = (bf16[4,24,1664]{2,1,0:T(8,128)(2,1)}, bf16[4,24,1664]{2,1,0:T(8,128)(2,1)}, u32[]{:S(2)}, u32[]{:S(2)}) collective-permute-start(bf16[4,24,1664]{2,1,0:T(8,128)(2,1)} %slice.549), channel_id=1, source_target_pairs={{0,16},{16,0},{1,17},{17,1},{2,18},{18,2},{3,19},{19,3},{4,20},{20... | collective-permute-start | bytes 958472 | tf_op jit(solution)/shard_map/ppermute | solution.py:825
  44.3 11.4 %collective-permute-start.5 = (bf16[4,24,1536]{2,1,0:T(8,128)(2,1)}, bf16[4,24,1536]{2,1,0:T(8,128)(2,1)}, u32[]{:S(2)}, u32[]{:S(2)}) collective-permute-start(bf16[4,24,1536]{2,1,0:T(8,128)(2,1)} %slice.548), channel_id=1, source_target_pairs={{0,8},{8,0},{1,9},{9,1},{2,10},{10,2},{3,11},{11,3},{4,12},{12,4},... | collective-permute-start | bytes 884744 | tf_op jit(solution)/shard_map/ppermute | solution.py:825
  59.5 14.3 %collective-permute-start.8 = (bf16[2,4,24,1664]{3,2,1,0:T(8,128)(2,1)S(1)}, bf16[2,4,24,1664]{3,2,1,0:T(8,128)(2,1)S(1)}, u32[]{:S(2)}, u32[]{:S(2)}) collective-permute-start(bf16[2,4,24,1664]{3,2,1,0:T(8,128)(2,1)S(1)} %bitcast_dynamic-update-slice_fusion.14), channel_id=1, source_target_pairs={{0,8},{8,0},{1,9},{9,1},{2,10},{10,2},{3,11},{11,3},{4,12},{12,4},... | collective-permute-start | bytes 1916936 | tf_op jit(solution)/shard_map/ppermute | solution.py:825
  60.2 13.0 %collective-permute-start.7 = (bf16[2,4,24,1536]{3,2,1,0:T(8,128)(2,1)}, bf16[2,4,24,1536]{3,2,1,0:T(8,128)(2,1)S(1)}, u32[]{:S(2)}, u32[]{:S(2)}) collective-permute-start(bf16[2,4,24,1536]{3,2,1,0:T(8,128)(2,1)} %bitcast_dynamic-update-slice_fusion.20), channel_id=1, source_target_pairs={{0,16},{16,0},{1,17},{17,1},{2,18},{18,2},{3,19},{19,3},{4,20},{20... | collective-permute-start | bytes 1769480 | tf_op jit(solution)/shard_map/ppermute | solution.py:825
  77.1 16.5 %collective-permute-start.12 = (bf16[2,2,4,24,3200]{4,3,2,1,0:T(8,128)(2,1)S(1)}, bf16[2,2,4,24,3200]{4,3,2,1,0:T(8,128)(2,1)S(1)}, u32[]{:S(2)}, u32[]{:S(2)}) collective-permute-start(bf16[2,2,4,24,3200]{4,3,2,1,0:T(8,128)(2,1)S(1)} %pad_maximum_fusion.1), channel_id=1, source_target_pairs={{0,1},{1,0},{2,3},{3,2},{4,5},{5,4},{6,7},{7,6},{8,9},{9,8},{10,11... | collective-permute-start | bytes 7372808 | tf_op jit(solution)/shard_map/ppermute | solution.py:825
  77.2 15.7 %collective-permute-start.13 = (bf16[4,24,3072]{2,1,0:T(8,128)(2,1)S(1)}, bf16[4,24,3072]{2,1,0:T(8,128)(2,1)S(1)}, u32[]{:S(2)}, u32[]{:S(2)}) collective-permute-start(bf16[4,24,3072]{2,1,0:T(8,128)(2,1)S(1)} %get-tuple-element.221), channel_id=1, source_target_pairs={{0,8},{8,0},{1,9},{9,1},{2,10},{10,2},{3,11},{11,3},{4,12},{12,4},... | collective-permute-start | bytes 1769480 | tf_op jit(solution)/shard_map/ppermute | solution.py:825
  78.2 15.4 %collective-permute-start.14 = (bf16[4,24,3072]{2,1,0:T(8,128)(2,1)S(1)}, bf16[4,24,3072]{2,1,0:T(8,128)(2,1)S(1)}, u32[]{:S(2)}, u32[]{:S(2)}) collective-permute-start(bf16[4,24,3072]{2,1,0:T(8,128)(2,1)S(1)} %get-tuple-element.223), channel_id=1, source_target_pairs={{0,16},{16,0},{1,17},{17,1},{2,18},{18,2},{3,19},{19,3},{4,20},{20... | collective-permute-start | bytes 1769480 | tf_op jit(solution)/shard_map/ppermute | solution.py:825
  95.6 40.5 %collective-permute-start.15 = (bf16[2,4,24,3072]{3,2,1,0:T(8,128)(2,1)}, bf16[2,4,24,3072]{3,2,1,0:T(8,128)(2,1)}, u32[]{:S(2)}, u32[]{:S(2)}) collective-permute-start(bf16[2,4,24,3072]{3,2,1,0:T(8,128)(2,1)} %bitcast_dynamic-update-slice_fusion.10), channel_id=1, source_target_pairs={{0,16},{16,0},{1,17},{17,1},{2,18},{18,2},{3,19},{19,3},{4,20},{20... | collective-permute-start | bytes 3538952 | tf_op jit(solution)/shard_map/ppermute | solution.py:825
  97.3 38.8 %collective-permute-start.16 = (bf16[2,4,24,3072]{3,2,1,0:T(8,128)(2,1)}, bf16[2,4,24,3072]{3,2,1,0:T(8,128)(2,1)}, u32[]{:S(2)}, u32[]{:S(2)}) collective-permute-start(bf16[2,4,24,3072]{3,2,1,0:T(8,128)(2,1)} %bitcast_dynamic-update-slice_fusion.8), channel_id=1, source_target_pairs={{0,8},{8,0},{1,9},{9,1},{2,10},{10,2},{3,11},{11,3},{4,12},{12,4},... | collective-permute-start | bytes 3538952 | tf_op jit(solution)/shard_map/ppermute | solution.py:825
  136.1 108.3 %copy-start.7 = (bf16[256,768]{1,0:T(8,128)(2,1)}, bf16[256,768]{1,0:T(8,128)(2,1)S(1)}, u32[]{:S(2)}) copy-start(bf16[256,768]{1,0:T(8,128)(2,1)S(1)} %get-tuple-element.271.gkey_ref) | copy-start | bytes 1179652
  140.3 8.0 %collective-permute-start.17 = (bf16[2,2,4,24,6144]{4,3,2,1,0:T(8,128)(2,1)S(1)}, bf16[2,2,4,24,6144]{4,3,2,1,0:T(8,128)(2,1)S(1)}, u32[]{:S(2)}, u32[]{:S(2)}) collective-permute-start(bf16[2,2,4,24,6144]{4,3,2,1,0:T(8,128)(2,1)S(1)} %pad_maximum_fusion), channel_id=1, source_target_pairs={{0,1},{1,0},{2,3},{3,2},{4,5},{5,4},{6,7},{7,6},{8,9},{9,8},{10,11... | collective-permute-start | bytes 14155784 | tf_op jit(solution)/shard_map/ppermute | solution.py:825
  150.3 52.4 %copy-start.3 = (f32[8,768]{1,0:T(8,128)S(1)}, f32[8,768]{1,0:T(8,128)}, u32[]{:S(2)}) copy-start(f32[8,768]{1,0:T(8,128)} %copy-done.2) | copy-start | bytes 73732
  202.5 31.8 %collective-permute-start.18 = (bf16[2,384,2048]{2,1,0:T(8,128)(2,1)}, bf16[2,384,2048]{2,1,0:T(8,128)(2,1)}, u32[]{:S(2)}, u32[]{:S(2)}) collective-permute-start(bf16[2,384,2048]{2,1,0:T(8,128)(2,1)} %get-tuple-element.264), channel_id=1, source_target_pairs={{0,1},{1,0},{2,3},{3,2},{4,5},{5,4},{6,7},{7,6},{8,9},{9,8},{10,11... | collective-permute-start | bytes 9437192 | tf_op jit(solution)/shard_map/ppermute | solution.py:868
  202.8 31.5 %collective-permute-start.19 = (bf16[2,384,1024]{2,1,0:T(8,128)(2,1)}, bf16[2,384,1024]{2,1,0:T(8,128)(2,1)}, u32[]{:S(2)}, u32[]{:S(2)}) collective-permute-start(bf16[2,384,1024]{2,1,0:T(8,128)(2,1)} %get-tuple-element.265), channel_id=1, source_target_pairs={{0,1},{1,0},{2,3},{3,2},{4,5},{5,4},{6,7},{7,6},{8,9},{9,8},{10,11... | collective-permute-start | bytes 4718600 | tf_op jit(solution)/shard_map/ppermute | solution.py:868
  203.2 31.1 %collective-permute-start.20 = (bf16[2,384,384]{2,1,0:T(8,128)(2,1)}, bf16[2,384,384]{2,1,0:T(8,128)(2,1)S(1)}, u32[]{:S(2)}, u32[]{:S(2)}) collective-permute-start(bf16[2,384,384]{2,1,0:T(8,128)(2,1)} %get-tuple-element.266), channel_id=1, source_target_pairs={{0,1},{1,0},{2,3},{3,2},{4,5},{5,4},{6,7},{7,6},{8,9},{9,8},{10,11... | collective-permute-start | bytes 1769480 | tf_op jit(solution)/shard_map/ppermute | solution.py:868
  206.9 27.0 %copy-start.37 = (bf16[2,384,384]{2,1,0:T(8,128)(2,1)S(1)}, bf16[2,384,384]{2,1,0:T(8,128)(2,1)}, u32[]{:S(2)}) copy-start(bf16[2,384,384]{2,1,0:T(8,128)(2,1)} %get-tuple-element.289) | copy-start | bytes 1769476
  206.9 27.1 %copy-start.26 = (bf16[2,384,2048]{2,1,0:T(8,128)(2,1)S(1)}, bf16[2,384,2048]{2,1,0:T(8,128)(2,1)}, u32[]{:S(2)}) copy-start(bf16[2,384,2048]{2,1,0:T(8,128)(2,1)} %get-tuple-element.258) | copy-start | bytes 9437188
  241.3 31.6 %collective-permute-start.21 = (bf16[1,2,4,24,3456]{4,3,2,1,0:T(8,128)(2,1)}, bf16[1,2,4,24,3456]{4,3,2,1,0:T(8,128)(2,1)S(1)}, u32[]{:S(2)}, u32[]{:S(2)}) collective-permute-start(bf16[1,2,4,24,3456]{4,3,2,1,0:T(8,128)(2,1)} %pad_maximum_fusion.4), channel_id=1, source_target_pairs={{0,8},{8,0},{1,9},{9,1},{2,10},{10,2},{3,11},{11,3},{4,12},{12,4},... | collective-permute-start | bytes 3981320 | tf_op jit(solution)/shard_map/ppermute | solution.py:825
  242.2 31.2 %collective-permute-start.22 = (bf16[1,2,4,24,3456]{4,3,2,1,0:T(8,128)(2,1)S(1)}, bf16[1,2,4,24,3456]{4,3,2,1,0:T(8,128)(2,1)}, u32[]{:S(2)}, u32[]{:S(2)}) collective-permute-start(bf16[1,2,4,24,3456]{4,3,2,1,0:T(8,128)(2,1)S(1)} %pad_maximum_fusion.5), channel_id=1, source_target_pairs={{0,16},{16,0},{1,17},{17,1},{2,18},{18,2},{3,19},{19,3},{4,20},{20... | collective-permute-start | bytes 3981320 | tf_op jit(solution)/shard_map/ppermute | solution.py:825
  277.1 30.8 %collective-permute-start.23 = (bf16[1,4,24,3456]{3,2,1,0:T(8,128)(2,1)S(1)}, bf16[1,4,24,3456]{3,2,1,0:T(8,128)(2,1)S(1)}, u32[]{:S(2)}, u32[]{:S(2)}) collective-permute-start(bf16[1,4,24,3456]{3,2,1,0:T(8,128)(2,1)S(1)} %get-tuple-element.310), channel_id=1, source_target_pairs={{0,16},{16,0},{1,17},{17,1},{2,18},{18,2},{3,19},{19,3},{4,20},{20... | collective-permute-start | bytes 1990664 | tf_op jit(solution)/shard_map/ppermute | solution.py:825
  277.5 30.5 %collective-permute-start.24 = (bf16[1,4,24,3456]{3,2,1,0:T(8,128)(2,1)S(1)}, bf16[1,4,24,3456]{3,2,1,0:T(8,128)(2,1)S(1)}, u32[]{:S(2)}, u32[]{:S(2)}) collective-permute-start(bf16[1,4,24,3456]{3,2,1,0:T(8,128)(2,1)S(1)} %get-tuple-element.311), channel_id=1, source_target_pairs={{0,8},{8,0},{1,9},{9,1},{2,10},{10,2},{3,11},{11,3},{4,12},{12,4},... | collective-permute-start | bytes 1990664 | tf_op jit(solution)/shard_map/ppermute | solution.py:825
  278.6 29.3 %collective-permute-start.25 = (bf16[6,384,128]{2,1,0:T(8,128)(2,1)S(1)}, bf16[6,384,128]{2,1,0:T(8,128)(2,1)S(1)}, u32[]{:S(2)}, u32[]{:S(2)}) collective-permute-start(bf16[6,384,128]{2,1,0:T(8,128)(2,1)S(1)} %get-tuple-element.312), channel_id=1, source_target_pairs={{0,1},{1,0},{2,3},{3,2},{4,5},{5,4},{6,7},{7,6},{8,9},{9,8},{10,11... | collective-permute-start | bytes 1769480 | tf_op jit(solution)/shard_map/ppermute | solution.py:868
  278.6 29.3 %collective-permute-start.26 = (bf16[6,384,128]{2,1,0:T(8,128)(2,1)S(1)}, bf16[6,384,128]{2,1,0:T(8,128)(2,1)S(1)}, u32[]{:S(2)}, u32[]{:S(2)}) collective-permute-start(bf16[6,384,128]{2,1,0:T(8,128)(2,1)S(1)} %get-tuple-element.313), channel_id=1, source_target_pairs={{0,1},{1,0},{2,3},{3,2},{4,5},{5,4},{6,7},{7,6},{8,9},{9,8},{10,11... | collective-permute-start | bytes 1769480 | tf_op jit(solution)/shard_map/ppermute | solution.py:868
  310.3 20.0 %collective-permute-start.30 = (bf16[8,384,128]{2,1,0:T(8,128)(2,1)S(1)}, bf16[8,384,128]{2,1,0:T(8,128)(2,1)}, u32[]{:S(2)}, u32[]{:S(2)}) collective-permute-start(bf16[8,384,128]{2,1,0:T(8,128)(2,1)S(1)} %get-tuple-element.335), channel_id=1, source_target_pairs={{0,1},{1,0},{2,3},{3,2},{4,5},{5,4},{6,7},{7,6},{8,9},{9,8},{10,11... | collective-permute-start | bytes 2359304 | tf_op jit(solution)/shard_map/ppermute | solution.py:868
  314.1 19.6 %all-to-all-start.1 = ((bf16[4,192,768]{2,1,0:T(8,128)(2,1)}), bf16[4,192,768]{2,1,0:T(8,128)(2,1)S(1)}, u32[]{:S(2)}, u32[]{:S(2)}) async-start(bf16[4,192,768]{2,1,0:T(8,128)(2,1)} %pad_maximum_fusion.7), calls=%async_computation.1 | async-start | bytes 2359296 | tf_op jit(solution)/shard_map/all_to_all | solution.py:1081
  322.2 35.4 %collective-permute-start.29 = (bf16[1,24,6912]{2,1,0:T(8,128)(2,1)}, bf16[1,24,6912]{2,1,0:T(8,128)(2,1)}, u32[]{:S(2)}, u32[]{:S(2)}) collective-permute-start(bf16[1,24,6912]{2,1,0:T(8,128)(2,1)} %pad_maximum_fusion.14), channel_id=1, source_target_pairs={{0,6},{2,0},{4,2},{6,4},{1,7},{3,1},{5,3},{7,5},{8,14},{10,8},{12,... | collective-permute-start | bytes 995336 | tf_op jit(solution)/shard_map/ppermute | solution.py:825
  326.5 31.1 %collective-permute-start.28 = (bf16[1,24,6912]{2,1,0:T(8,128)(2,1)}, bf16[1,24,6912]{2,1,0:T(8,128)(2,1)}, u32[]{:S(2)}, u32[]{:S(2)}) collective-permute-start(bf16[1,24,6912]{2,1,0:T(8,128)(2,1)} %pad_maximum_fusion.13), channel_id=1, source_target_pairs={{0,4},{2,6},{4,0},{6,2},{1,5},{3,7},{5,1},{7,3},{8,12},{10,14},{12... | collective-permute-start | bytes 995336 | tf_op jit(solution)/shard_map/ppermute | solution.py:825
  327.2 30.4 %collective-permute-start.27 = (bf16[1,24,6912]{2,1,0:T(8,128)(2,1)}, bf16[1,24,6912]{2,1,0:T(8,128)(2,1)}, u32[]{:S(2)}, u32[]{:S(2)}) collective-permute-start(bf16[1,24,6912]{2,1,0:T(8,128)(2,1)} %pad_maximum_fusion.12), channel_id=1, source_target_pairs={{0,2},{2,4},{4,6},{6,0},{1,3},{3,5},{5,7},{7,1},{8,10},{10,12},{12... | collective-permute-start | bytes 995336 | tf_op jit(solution)/shard_map/ppermute | solution.py:825
  333.7 13.2 %collective-permute-start.31 = (bf16[10,2,4,24,128]{4,3,0,2,1:T(8,128)(2,1)}, bf16[10,2,4,24,128]{4,3,0,2,1:T(8,128)(2,1)S(1)}, u32[]{:S(2)}, u32[]{:S(2)}) collective-permute-start(bf16[10,2,4,24,128]{4,3,0,2,1:T(8,128)(2,1)} %pad_maximum_fusion.9), channel_id=1, source_target_pairs={{0,8},{8,0},{1,9},{9,1},{2,10},{10,2},{3,11},{11,3},{4,12},{12,4},... | collective-permute-start | bytes 1474568 | tf_op jit(solution)/shard_map/ppermute | solution.py:825
  335.4 12.7 %collective-permute-start.32 = (bf16[10,2,4,24,128]{4,3,0,2,1:T(8,128)(2,1)}, bf16[10,2,4,24,128]{4,3,0,2,1:T(8,128)(2,1)S(1)}, u32[]{:S(2)}, u32[]{:S(2)}) collective-permute-start(bf16[10,2,4,24,128]{4,3,0,2,1:T(8,128)(2,1)} %pad_maximum_fusion.10), channel_id=1, source_target_pairs={{0,16},{16,0},{1,17},{17,1},{2,18},{18,2},{3,19},{19,3},{4,20},{20... | collective-permute-start | bytes 1474568 | tf_op jit(solution)/shard_map/ppermute | solution.py:825
  348.6 9.0 %collective-permute-start.33 = (bf16[10,4,24,128]{3,2,0,1:T(8,128)(2,1)S(1)}, bf16[10,4,24,128]{3,2,0,1:T(8,128)(2,1)S(1)}, u32[]{:S(2)}, u32[]{:S(2)}) collective-permute-start(bf16[10,4,24,128]{3,2,0,1:T(8,128)(2,1)S(1)} %get-tuple-element.348), channel_id=1, source_target_pairs={{0,16},{16,0},{1,17},{17,1},{2,18},{18,2},{3,19},{19,3},{4,20},{20... | collective-permute-start | bytes 737288 | tf_op jit(solution)/shard_map/ppermute | solution.py:825
  350.1 7.5 %collective-permute-start.34 = (bf16[10,4,24,128]{3,2,0,1:T(8,128)(2,1)S(1)}, bf16[10,4,24,128]{3,2,0,1:T(8,128)(2,1)S(1)}, u32[]{:S(2)}, u32[]{:S(2)}) collective-permute-start(bf16[10,4,24,128]{3,2,0,1:T(8,128)(2,1)S(1)} %get-tuple-element.349), channel_id=1, source_target_pairs={{0,8},{8,0},{1,9},{9,1},{2,10},{10,2},{3,11},{11,3},{4,12},{12,4},... | collective-permute-start | bytes 737288 | tf_op jit(solution)/shard_map/ppermute | solution.py:825
  360.1 8.2 %collective-permute-start.35 = (bf16[20,24,128]{2,1,0:T(8,128)(2,1)S(1)}, bf16[20,24,128]{2,1,0:T(8,128)(2,1)S(1)}, u32[]{:S(2)}, u32[]{:S(2)}) collective-permute-start(bf16[20,24,128]{2,1,0:T(8,128)(2,1)S(1)} %pad_maximum_fusion.15), channel_id=1, source_target_pairs={{0,2},{2,4},{4,6},{6,0},{1,3},{3,5},{5,7},{7,1},{8,10},{10,12},{12... | collective-permute-start | bytes 368648 | tf_op jit(solution)/shard_map/ppermute | solution.py:825
  362.8 9.0 %collective-permute-start.36 = (bf16[20,24,128]{2,1,0:T(8,128)(2,1)S(1)}, bf16[20,24,128]{2,1,0:T(8,128)(2,1)S(1)}, u32[]{:S(2)}, u32[]{:S(2)}) collective-permute-start(bf16[20,24,128]{2,1,0:T(8,128)(2,1)S(1)} %pad_maximum_fusion.16), channel_id=1, source_target_pairs={{0,4},{2,6},{4,0},{6,2},{1,5},{3,7},{5,1},{7,3},{8,12},{10,14},{12... | collective-permute-start | bytes 368648 | tf_op jit(solution)/shard_map/ppermute | solution.py:825
  364.1 7.6 %collective-permute-start.37 = (bf16[20,24,128]{2,1,0:T(8,128)(2,1)S(1)}, bf16[20,24,128]{2,1,0:T(8,128)(2,1)S(1)}, u32[]{:S(2)}, u32[]{:S(2)}) collective-permute-start(bf16[20,24,128]{2,1,0:T(8,128)(2,1)S(1)} %pad_maximum_fusion.17), channel_id=1, source_target_pairs={{0,6},{2,0},{4,2},{6,4},{1,7},{3,1},{5,3},{7,5},{8,14},{10,8},{12,... | collective-permute-start | bytes 368648 | tf_op jit(solution)/shard_map/ppermute | solution.py:825
  (64 other events, 301.7 us)

commit v4 on v3

--- a/solution.py
+++ b/solution.py
@@ -190,7 +190,7 @@
         log_ref[0, pl.ds(block, 1), :] = peak + jnp.log(total)
         return carry
 
-    lax.fori_loop(0, rows // 128, step, 0, unroll=4)
+    lax.fori_loop(0, rows // 128, step, 0, unroll=8)
 
 
 def align_offsets(sums, step_of_lane, bits, sign):
@@ -221,9 +221,9 @@
 
 def attend_backward(
     last, part, own_part, first_pair, query_ref, grad_ref, key_ref, value_ref, gkey_ref, gvalue_ref, normed_ref, normed_turned, pooled_turned, wq_ref, wk_ref, wv_ref,
-    log_ref, bias_ref, klocal_ref, kglobal_ref, qfeat_ref, raw_ref, gains_ref, place_ref, old_small_ref, old_table_ref,
+    log_ref, bias_ref, klocal_ref, kglobal_ref, qfeat_ref, raw_ref, gains_ref, place_ref, old_small_ref, old_table_ref, old_dnormed_ref, old_draw_ref,
     keep_ref, send_ref, dnormed_ref, draw_ref, small_ref, table_ref,
-    dnormed_sum, dpooled_sum, key_turned, gkey_turned, dquery, key_sum, value_sum, gkey_sum, gvalue_sum, near_sum, far_sum,
+    dnormed_sum, dpooled_sum, draw_sum, key_turned, gkey_turned, dquery, key_sum, value_sum, gkey_sum, gvalue_sum, near_sum, far_sum,
 ):
     rows = query_ref.shape[0]
     slots = gkey_ref.shape[0]
@@ -278,7 +278,7 @@
         dquery[rows_of(block), :] = unstack_heads(wide).astype(bf16)
         return carry
 
-    lax.fori_loop(0, rows // 128, step, 0, unroll=4)
+    lax.fori_loop(0, rows // 128, step, 0, unroll=8)
 
     core, first_slot = place_ref[0], place_ref[1]
     head = 2 * (first_pair + pl.program_id(0))
@@ -319,7 +319,8 @@
         def norm_rows(index, carry):
             part = pl.ds(pl.multiple_of(index * 128, 128), 128)
             grad = dnormed_sum[part, :]
-            dnormed_ref[part, :] = grad.astype(bf16)
+            total = grad if first_pair == 0 else grad + old_dnormed_ref[part, :].astype(f32)
+            dnormed_ref[part, :] = total.astype(bf16)
             return carry + jnp.sum(grad * normed_ref[part, :].astype(f32), axis=0, keepdims=True)
 
         norm_part = lax.fori_loop(0, (rows + 256) // 128, norm_rows, jnp.zeros((1, width), f32))
@@ -333,7 +334,8 @@
             inverse = inverse_rms(values)
             grad = dpooled_sum[part, :]
             back = norm_gradient(values, inverse, gain_pool, grad)
-            draw_ref[part, :] = back.astype(bf16)
+            total = back if first_pair == 0 else back + old_draw_ref[part, :].astype(f32)
+            draw_sum[part, :] = total.astype(bf16)
             return (
                 norm_part + jnp.sum(back * raw, axis=0, keepdims=True),
                 pool_part + jnp.sum(grad * values * inverse, axis=0, keepdims=True),
@@ -345,7 +347,25 @@
         small_ref[0:1, :] += norm_part
         small_ref[1:2, :] += pool_part
         if not last:
+            draw_ref[...] = draw_sum[...]
             return
+        own_slots = rows // 16
+        me = lax.axis_index("y") * lax.axis_size("x") + lax.axis_index("x")
+        for hop in range(draw_ref.shape[0]):
+            target = lax.rem(me + hop, draw_ref.shape[0])
+            draw_ref[hop, :own_slots, :] = draw_sum[
+                pl.ds(pl.multiple_of(target * own_slots, own_slots), own_slots), :
+            ]
+            before = target == me - 1
+
+            @pl.when(before)
+            def head():
+                draw_ref[hop, own_slots:, :] = dnormed_ref[:128, :]
+
+            @pl.when(jnp.logical_not(before))
+            def tail():
+                draw_ref[hop, own_slots:, :] = dnormed_ref[rows + 128 :, :]
+
         rows_of_small = jnp.concatenate([small_ref[...], jnp.zeros((120, width), f32)], axis=0)
         tables = jnp.zeros((width, 128), f32)
         row = lax.broadcasted_iota(i32, (width, 32), 0)
@@ -443,13 +463,15 @@
 
 def attention_backward(
     first, count, part, queries, grads, keys, values, gkeys, gvalues, normed, turned, pooled, weights, logs, bias, klocal,
-    kglobal, qfeat, raw_pool, gains, place, old_small, old_table,
+    kglobal, qfeat, raw_pool, gains, place, old_small, old_table, old_dnormed, old_draw,
 ):
     rows, width = queries.shape
     slots = gkeys.shape[0]
     blocks = rows // 128
     pairs = width // 128
     lead = count * (4 if first + count == pairs else 3)
+    own_slots = rows // 16
+    draw_shape = (slots // own_slots, own_slots + 128, width) if first + count == pairs else (slots, width)
     return pl.pallas_call(
         functools.partial(attend_backward, first + count == pairs, width // 32, part, first),
         grid=(count,),
@@ -476,12 +498,14 @@
             pl.BlockSpec(memory_space=pltpu.SMEM),
             fixed(8, width),
             fixed(32, 128),
+            fixed(rows + 256, width) if first else fixed(8, width),
+            fixed(slots, width) if first else fixed(8, width),
         ],
         out_specs=[
             fixed_out(lead, width // 2, 128),
             fixed_out(lead, width // 2, 128),
             fixed_out(rows + 256, width),
-            fixed_out(slots, width),
+            fixed_out(*draw_shape),
             fixed_out(8, width),
             fixed_out(32, 128),
         ],
@@ -489,13 +513,14 @@
             jax.ShapeDtypeStruct((lead, width // 2, 128), bf16),
             jax.ShapeDtypeStruct((lead, width // 2, 128), bf16),
             jax.ShapeDtypeStruct((rows + 256, width), bf16),
-            jax.ShapeDtypeStruct((slots, width), bf16),
+            jax.ShapeDtypeStruct(draw_shape, bf16),
             jax.ShapeDtypeStruct((8, width), f32),
             jax.ShapeDtypeStruct((32, 128), f32),
         ],
         scratch_shapes=[
             pltpu.VMEM((rows + 256, width), f32),
             pltpu.VMEM((slots, width), f32),
+            pltpu.VMEM((slots, width), bf16),
             pltpu.VMEM((128, rows + 256), bf16),
             pltpu.VMEM((128, slots), bf16),
             pltpu.VMEM((rows, 128), bf16),
@@ -513,7 +538,7 @@
         name="attend_backward",
     )(
         queries, grads, keys, values, gkeys, gvalues, normed, turned, pooled, weights, weights, weights, logs, bias, klocal,
-        kglobal, qfeat, raw_pool, gains, place, old_small, old_table,
+        kglobal, qfeat, raw_pool, gains, place, old_small, old_table, old_dnormed, old_draw,
     )
 
 
@@ -539,11 +564,8 @@
 unfold_rows = fold_rows
 
 
-def pack(
-    source_ref, keep_ref, marks_ref, wq_ref, wk_ref, wv_ref, wo_ref, gains_ref, gate_ref, up_ref, down_ref,
-    first_ref, second_ref, shared_ref,
-):
-    width = source_ref.shape[1]
+def pack_weights(wq_ref, wk_ref, wv_ref, wo_ref, gains_ref, gate_ref, up_ref, down_ref, first_ref, second_ref):
+    width = wq_ref.shape[1]
     for index, weight_ref in enumerate((wq_ref, wk_ref, wv_ref, wo_ref)):
         first_ref[:, index * width : (index + 1) * width] = weight_ref[...]
     first_ref[:, 4 * width :] = gains_ref[...]
@@ -552,30 +574,55 @@
         second_ref[:, :hidden] = gate_ref[...]
         second_ref[:, hidden : 2 * hidden] = up_ref[...]
         second_ref[:, 2 * hidden :] = fold_rows(down_ref[...].astype(f32)[None])[0].astype(bf16)
+
+
+def pack_tokens(source_ref, keep_ref, marks_ref, shared_ref):
+    width = source_ref.shape[1]
     slots = source_ref.shape[0] // 16
     for slot in range(0, slots, 16):
         rows = slice(slot * 16, slot * 16 + 256)
         values = source_ref[rows, :].astype(f32)
         values = values * (inverse_rms(values) * keep_ref[rows, :])
-        shared_ref[slot : slot + 16, :] = jnp.sum(values.reshape(16, 16, width), axis=1).astype(bf16)
+        shared_ref[0, slot : slot + 16, :] = jnp.sum(values.reshape(16, 16, width), axis=1).astype(bf16)
     marks = marks_ref[...].astype(f32)
     rest = jnp.zeros((marks.shape[0], width - 128), f32)
-    shared_ref[slots:, :] = jnp.concatenate([marks, rest], axis=1).astype(bf16)
-
-
-def pack_all(source, keep, marks, wq, wk, wv, wo, gains, gate, up, down, aligned):
-    rows, width = source.shape
-    part, hidden = gate.shape
+    count = slots + marks.shape[0]
+    shared_ref[0, slots:count, :] = jnp.concatenate([marks, rest], axis=1).astype(bf16)
+    for target in range(1, shared_ref.shape[0]):
+        shared_ref[target, :count, :] = shared_ref[0, :count, :]
+    for target in range(shared_ref.shape[0]):
+        before = target == lax.axis_index("y") * lax.axis_size("x") + lax.axis_index("x") - 1
+
+        @pl.when(before)
+        def head():
+            shared_ref[target, count:, :] = source_ref[:128, :]
+
+        @pl.when(jnp.logical_not(before))
+        def tail():
+            shared_ref[target, count:, :] = source_ref[source_ref.shape[0] - 128 :, :]
+
+
+def pack_all(wq, wk, wv, wo, gains, gate, up, down, aligned):
+    part, width = wq.shape
     return pl.pallas_call(
-        pack,
+        pack_weights,
         out_shape=[
             jax.ShapeDtypeStruct((part, 4 * width + 128), bf16),
-            jax.ShapeDtypeStruct((part, 3 * hidden if aligned else 128), bf16),
-            jax.ShapeDtypeStruct((rows // 16 + marks.shape[0], width), bf16),
+            jax.ShapeDtypeStruct((part, 3 * gate.shape[1] if aligned else 128), bf16),
         ],
         compiler_params=pltpu.CompilerParams(vmem_limit_bytes=60 << 20),
-        name="pack",
-    )(source, keep, marks, wq, wk, wv, wo, gains, gate, up, down)
+        name="pack_weights",
+    )(wq, wk, wv, wo, gains, gate, up, down)
+
+
+def pack_shared(source, keep, marks, count):
+    rows, width = source.shape
+    return pl.pallas_call(
+        pack_tokens,
+        out_shape=jax.ShapeDtypeStruct((count, rows // 16 + marks.shape[0] + 128, width), bf16),
+        compiler_params=pltpu.CompilerParams(vmem_limit_bytes=60 << 20),
+        name="pack_tokens",
+    )(source, keep, marks)
 
 
 def feed_forward(
@@ -598,7 +645,7 @@
     @pl.when(pl.program_id(0) == 0)
     def start():
         def norm_rows(index, carry):
-            part = pl.ds(pl.multiple_of(index * 128, 128), 128)
+            part = pl.ds(pl.multiple_of(index * 256, 256), 256)
             values = source_ref[part, :].astype(f32) + dot_nn(mixture_ref[part, :], wo_ref[...])
             middle[part, :] = values
             low = (values * inverse_rms(values) * gain).astype(bf16)
@@ -606,7 +653,7 @@
             turned[:, part] = low.T
             return carry
 
-        lax.fori_loop(0, rows // 128, norm_rows, 0)
+        lax.fori_loop(0, rows // 256, norm_rows, 0, unroll=True)
         out_sum[...] = jnp.zeros_like(out_sum)
         grad_sum[...] = jnp.zeros_like(grad_sum)
 
@@ -647,7 +694,7 @@
         dgain_ref[...] = jnp.zeros_like(dgain_ref)
 
         def back_rows(index, carry):
-            part = pl.ds(pl.multiple_of(index * 128, 128), 128)
+            part = pl.ds(pl.multiple_of(index * 256, 256), 256)
             values = middle[part, :]
             out_ref[part, :] = (values + out_sum[part, :]).astype(bf16)
             inverse = inverse_rms(values)
@@ -661,7 +708,7 @@
             turned[:, part] = mixture_ref[part, :].T
             return carry
 
-        lax.fori_loop(0, rows // 128, back_rows, 0)
+        lax.fori_loop(0, rows // 256, back_rows, 0, unroll=True)
         for side in range(2):
             half = slice(side * width // 2, (side + 1) * width // 2)
             store_halves(keep_out, send_out, side, dot_nn(turned[...], normed[:, half]), core, width // 32)
@@ -742,6 +789,56 @@
     )(source, mixture, weights, gains, cotangent, held, other, held, other, held, other, place)
 
 
+def source_gradient(source_ref, keep_ref, middle_grad_ref, gains_ref, dnormed_ref, payload_ref, *refs):
+    step, steps = pl.program_id(0), pl.num_programs(0)
+    received, out_ref = refs[:-1], refs[-1]
+    seq_count = len(received) + 1
+    own_slots = payload_ref.shape[1] - 128
+    rows, width = source_ref.shape
+    slots = pl.ds(pl.multiple_of(step * (rows // 16), rows // 16), rows // 16)
+    pooled = payload_ref[0, slots, :].astype(f32)
+    for other_ref in received:
+        pooled = pooled + other_ref[slots, :].astype(f32)
+    pooled = jnp.broadcast_to(pooled[:, None, :], (rows // 16, 16, width)).reshape(rows, width)
+    own = pl.ds(pl.multiple_of(128 + step * rows, 128), rows)
+    grad = dnormed_ref[own, :].astype(f32) + pooled * keep_ref[...]
+    me = lax.axis_index("y") * lax.axis_size("x") + lax.axis_index("x")
+    before = (step == 0) & (me > 0)
+    after = (step == steps - 1) & (me < seq_count - 1)
+    head = received[0][own_slots:, :].astype(f32)
+    tail = received[-1][own_slots:, :].astype(f32)
+    edges = [jnp.where(before, head, 0.0), jnp.zeros((rows - 256, width), f32), jnp.where(after, tail, 0.0)]
+    grad = grad + jnp.concatenate([edge for edge in edges if edge.shape[0]], axis=0)
+    values = source_ref[...].astype(f32)
+    out_ref[...] = middle_grad_ref[...] + norm_gradient(values, inverse_rms(values), gains_ref[0:1, :], grad)
+
+
+def input_gradient(source, keep, middle_grad, gains, dnormed, payload, received):
+    rows, width = source.shape
+    tile = 256
+    row_spec = pl.BlockSpec((tile, width), lambda step: (step, 0))
+    return pl.pallas_call(
+        source_gradient,
+        grid=(rows // tile,),
+        in_specs=[
+            row_spec,
+            pl.BlockSpec((tile, 1), lambda step: (step, 0)),
+            row_spec,
+            fixed(8, width),
+            fixed(*dnormed.shape),
+            pl.BlockSpec((1,) + payload.shape[1:], lambda step: (0, 0, 0), pipeline_mode=pl.Buffered(1)),
+        ]
+        + [fixed(*other.shape) for other in received],
+        out_specs=row_spec,
+        out_shape=jax.ShapeDtypeStruct((rows, width), f32),
+        compiler_params=pltpu.CompilerParams(vmem_limit_bytes=60 << 20),
+        cost_estimate=pl.CostEstimate(
+            flops=20 * rows * width, bytes_accessed=14 << 20, transcendentals=0
+        ),
+        name="source_gradient",
+    )(source, keep, middle_grad, gains, dnormed, payload, *received)
+
+
 def near_offsets(local_bias):
     heads, buckets = local_bias.shape
     offset = (jnp.arange(256, dtype=i32) + 128) % 256 - 128
@@ -841,6 +938,12 @@
 def scatter_steps(sides, labels, stages, join):
     labels = [list(labels) for _ in sides]
     for axes in stages:
+        if axes == ("all z",):
+            merged = [add_up(piece).astype(bf16) for side in sides for piece in side]
+            merged = yield jnp.concatenate(merged, axis=join)
+            dim = merged.ndim - 3
+            got = yield lax.all_to_all(merged, "z", dim, dim, tiled=True)
+            return jnp.sum(got.astype(f32), axis=dim)
         if len(axes) < len(sides):
             sides, labels = [[piece for side in sides for piece in side]], labels[:1]
         split = [split_stage(side, names, axis, join) for side, names, axis in zip(sides, labels, axes)]
@@ -877,7 +980,7 @@
 
 def sum_rows(pairs, part, join):
     sides = yield from core_steps(pairs, part)
-    return (yield from scatter_steps(sides, labels, stages, join))
+    return (yield from scatter_steps(sides, labels, across + (("all z",),), join))
 
 
 def regroup(keep, send, part):
@@ -937,14 +1040,6 @@
         chain.value = value
         chain.advance()
     return result
-
-
-def neighbour_rows(to_after, to_before):
-    count = lax.axis_size(seq)
-    ends = count - 1
-    before = lax.ppermute(to_after, seq, [(i, i + 1) for i in range(ends)])
-    after = lax.ppermute(to_before, seq, [(i + 1, i) for i in range(ends)])
-    return before, after
 
 
 def on_device(
@@ -983,27 +1078,34 @@
     valid_float = valid_mask[0].astype(f32)
 
     aligned = own_part * 32 == model_width
+    place = jnp.stack([lax.axis_index("core"), first_slot]).astype(i32)
     gain_columns = jnp.pad(jnp.stack([norm_gain, pool_gain, feed_gain], axis=1), ((0, 0), (0, 125)))
     marks = jnp.concatenate([segment_ids.reshape(-1, 128), valid_mask.reshape(-1, 128)])
-    packed, packed_second, shared = pack_all(
-        source, valid_float[:, None], marks, query_weight, key_weight, value_weight, output_weight, gain_columns,
-        gate_weight, up_weight, down_weight, aligned,
+    packed, packed_second = pack_all(
+        query_weight, key_weight, value_weight, output_weight, gain_columns, gate_weight, up_weight, down_weight, aligned
     )
     first = Chain(all_rows(packed, True))
     later = [Chain(all_rows(packed_second, False))] if aligned else []
-    place = jnp.stack([lax.axis_index("core"), first_slot]).astype(i32)
-
-    def share(shared):
-        before, after = neighbour_rows(source[-128:], source[:128])
-        copies = jnp.broadcast_to(shared, (seq_count,) + shared.shape)
-        return lax.all_to_all(copies, seq, 0, 0, tiled=True), before, after
-
-    shared, before, after = phase(shared, share, [first])
+
+    def share(operands):
+        shared = pack_shared(*operands, seq_count)
+        return lax.all_to_all(shared, seq, 0, 0, tiled=True)
+
+    held = []
+    phase(
+        (source, valid_float[:, None], marks), lambda operands: held.append(share(operands)), [first] + later, [first]
+    )
 
     def near_parts(operands):
-        shared, before, after, local_bias = operands
+        shared, local_bias = operands
+        me = lax.axis_index(seq)
+        edge = own_slots + marks.shape[0]
         raw_pool = shared[:, :own_slots].reshape(slot_count, model_width)
-        all_marks = shared[:, own_slots:, :128].astype(i32).reshape(seq_count, 2, tok_rows)
+        all_marks = shared[:, own_slots:edge, :128].astype(i32).reshape(seq_count, 2, tok_rows)
+        before, after = (
+            jnp.where((near >= 0) & (near < seq_count), pick(shared[:, edge:], jnp.clip(near, 0, seq_count - 1), 0), 0)
+            for near in (me - 1, me + 1)
+        )
         all_segments, all_valid = all_marks[:, 0].reshape(-1), all_marks[:, 1].reshape(-1)
         slot_segments = all_segments.reshape(slot_count, 16)[:, 0]
         slot_live = jnp.sum(all_valid.reshape(slot_count, 16), axis=1) > 0
@@ -1016,16 +1118,17 @@
         return raw_pool, slot_segments, slot_live, feat_near, near_offsets(local_bias), source_ext
 
     raw_pool, slot_segments, slot_live, feat_near, bias_near, source_ext = phase(
-        (shared, before, after, local_bias), near_parts, [first] + later, [first]
+        (held[0], local_bias), near_parts, [first], [first] + later
     )
     feat_query = query_features(own_segments)
     feat_far = phase(
         (global_bias, slot_segments, slot_live),
         lambda operands: far_features(*operands, first_slot, blocks),
         [first],
-        [first] + later,
-    )
-    phase((), lambda nothing: nothing, [first] + later)
+        [],
+    )
+    feat_far = phase(feat_far, lambda operands: operands, later, [first])
+    phase((), lambda nothing: nothing, [first], [first] + later)
     weights = first.value
 
     bias, mixture, logs, queries, keys, vals, gkeys, gvals, normed, gains, turned, pooled = phase(
@@ -1054,10 +1157,12 @@
         rest = [Chain(sum_rows(pieces, own_part, -1))]
     table = jnp.zeros((32, 128), f32)
     count = pairs // calls
-    dnormed, draw, waiting, started = [], [], [], []
+    waiting, started = [], []
+    dnormed, draw = gains, gains
+    keep_column = valid_float[:, None]
     for call in range(calls):
-        keep, send, dnormed_part, draw_part, small, table = phase(
-            (mixture_grad, small, table),
+        keep, send, dnormed, draw, small, table = phase(
+            (mixture_grad, small, table, dnormed, draw),
             lambda operands: attention_backward(
                 call * count, count, own_part, queries, operands[0], keys, vals, gkeys, gvals, normed, turned, pooled, weights,
                 logs, bias, feat_near, feat_far, feat_query, raw_pool, gains, kernel_place, *operands[1:],
@@ -1068,54 +1173,22 @@
         if call > 0:
             started.append(Chain(core_steps(waiting, own_part)))
             waiting = []
-        dnormed.append(dnormed_part)
-        draw.append(draw_part)
-
-    def return_grads(operands):
-        dnormed, draw = operands
-        me = lax.axis_index(seq)
-        head, tail = (add_up([part[where] for part in dnormed]).astype(bf16) for where in (slice(128), slice(-128, None)))
-        target = lax.broadcasted_iota(i32, (seq_count, 1, 1), 0)
-        edges = jnp.where(target == me - 1, head[None], jnp.where(target == me + 1, tail[None], 0))
-        pools = add_up(draw).astype(bf16).reshape(seq_count, own_slots, model_width)
-        return lax.all_to_all(jnp.concatenate([pools, edges], axis=1), seq, 0, 0, tiled=True)
-
-    def finish(operands):
-        me = lax.axis_index(seq)
-        spread = operands[:, :own_slots]
-        to_head, to_tail = (
-            jnp.where(
-                (near >= 0) & (near < seq_count),
-                pick(operands[:, own_slots:], jnp.clip(near, 0, seq_count - 1), 0),
-                0,
-            )
-            for near in (me - 1, me + 1)
-        )
-        values = source.astype(f32)
-        inverse = inverse_rms(values)
-        edges = jnp.concatenate(
-            [to_head.astype(f32), jnp.zeros((tok_rows - 256, model_width), f32), to_tail.astype(f32)]
-        )
-        pooled_raw_grad = jnp.sum(spread.astype(f32), axis=0)
-        spread_grad = jnp.broadcast_to(
-            pooled_raw_grad[:, None, :], (own_slots, 16, model_width)
-        ).reshape(tok_rows, model_width)
-        normed_grad = add_up([part[128:-128] for part in dnormed])
-        normed_grad = normed_grad + edges + spread_grad * valid_float[:, None]
-        return middle_grad + norm_gradient(values, inverse, gains[0:1], normed_grad)
-
-    def return_and_start(operands):
-        for chain in rest:
-            chain.advance()
-        return return_grads(operands)
+
+    def return_rows(payload):
+        return [lax.ppermute(payload[hop], seq, ring(seq_count, hop)) for hop in range(1, seq_count)]
 
     held = []
-    phase((dnormed, draw), lambda operands: held.append(return_and_start(operands)), started[1:])
+    phase(draw, lambda operands: held.append(return_rows(operands)), started[1:] + rest, started[1:])
     operands = held[0]
     sides = [sum((chain.value[side] for chain in started), []) for side in range(2)]
     last = Chain(scatter_steps(sides, labels, stages, 0))
     operands = phase(operands, lambda operands: operands, [last])
-    input_delta = phase(operands, finish, [last], rest + [last])
+    input_delta = phase(
+        operands,
+        lambda received: input_gradient(source, keep_column, middle_grad, gains, dnormed, draw, received),
+        [last],
+        rest + [last],
+    )
     phase((), lambda nothing: nothing, [last])
     total = last.value
     half = total.shape[0] // 2

time: 378 us -> 360 us (0.952)
  other arithmetic: 40.9 us -> 28.8 us
    pallas_call x1 -> x3, Pallas kernels: 3.44 us -> 12.2 us  [the longest x1 6.6 us: input_gradient(): pl.pallas_call(source_gradient, grid=(rows // tile,), in_specs=[row_spec,...]
    concatenate x16 -> x11, other arithmetic: 7.25 us -> 0.63 us  [split_stage(): jnp.concatenate(pieces, axis=join)]
    pallas_call x1, Pallas kernels: 52.1 us -> 47.5 us  [feed_forward_both(): pl.pallas_call(feed_forward, grid=(tiles,), in_specs=[fixed(rows, width),...]
    add x1 -> x0, other arithmetic: 4.31 us -> none  [finish(): return middle_grad + norm_gradient(values, inverse, gains[0:1], normed_grad)]
    pallas_call x3, Pallas kernels: 80.8 us -> 76.7 us  [attention_backward(): pl.pallas_call(functools.partial(attend_backward, first + count == pairs,...]
    ppermute x30 -> x27, starting transfers between devices: 37.4 us -> 35.7 us  [send_all(): lax.ppermute(piece, axis, ring(size, hop + 1))]
    unnamed x151 -> x127, local copies, waits for them, and re-layouts: 6.01 us -> 7.61 us
    ppermute x30 -> x27, waiting for transfers between devices: 36.4 us -> 36.2 us  [send_all(): lax.ppermute(piece, axis, ring(size, hop + 1))]
  transfers between devices with their start and end apart: 40 -> 38, of which waited for: 13 -> 10; matrix products, arithmetic and copies ran while one was open for 18% -> 16% of each run, Pallas kernels for 31% -> 33%
where the time goes in v4:
time: 360 us; the launch traced here: 355 us
  Pallas kernels  168 us (47%)
  local copies, waits for them, and re-layouts  59 us (16%)
  starting transfers between devices  51.2 us (14%)
  waiting for transfers between devices  37.4 us (10%)
  other arithmetic  28.8 us (8%)
  matrix products  8.05 us (2%)
    pallas_call x3, Pallas kernels, attention_backward(): pl.pallas_call(functools.partial(attend_backward, first + count == pairs,...  76.7 us
    pallas_call x1, Pallas kernels, feed_forward_both(): pl.pallas_call(feed_forward, grid=(tiles,), in_specs=[fixed(rows, width),...  47.5 us
    ppermute x27, waiting for transfers between devices, send_all(): lax.ppermute(piece, axis, ring(size, hop + 1))  36.2 us
    ppermute x27, starting transfers between devices, send_all(): lax.ppermute(piece, axis, ring(size, hop + 1))  35.7 us
    pallas_call x1, Pallas kernels, attention_forward(): pl.pallas_call(attend_forward, grid=(pairs,), in_specs=[fixed(rows + 256,...  31.6 us
    dynamic_update_slice x15, local copies, waits for them, and re-layouts, place_stage(): lax.dynamic_update_index_in_dim(out, piece, (me - hop - 1) % size, dim)  14.2 us
    convert_element_type x24, other arithmetic, split_stage(): add_up([pick(part, (me + hop) % size, dim) for part in piece]).astype(bf16)  9.53 us
    dot_general x1, matrix products, far_features(): return jnp.dot(picks, table, preferred_element_type=f32).astype(bf16)  7.8 us
  transfers between devices with their start and end apart: 38, of which 10 were waited for; matrix products, arithmetic and copies ran while one was open for 16% of the time, Pallas kernels for 33%

profile of v4, /device:TPU:0, one launch (start us, length us, event | category | flops | bytes accessed | tf_op | source)
XLA Modules:
  0.0 354.9 jit_solution(4965450416268798088)
XLA Ops:
  2.8 1.3 pad_add_fusion.marks_ref
  4.1 1.9 pack_weights.1
  5.9 3.0 collective-permute-start
  8.9 2.6 collective-permute-start.1
  11.5 1.3 collective-permute-start.2
  14.9 3.7 %pack_tokens.1 = bf16[4,208,768]{2,1,0:T(8,128)(2,1)} custom-call(bf16[1024,768]{1,0:T(8,128)(2,1)} %bitcast.356, f32[1024,1]{1,0:T(8,128)} %copy.165.keep_ref, s32[16,128]{1,0:T(8,128)} %pad_add_fusion.marks_ref), custom_call_target="tpu_custom_call" | custom-call | tf_op jit(solution)/shard_map/pack_tokens/pallas_call | solution.py:620
  18.6 3.8 %all-to-all-start = ((bf16[4,208,768]{2,1,0:T(8,128)(2,1)}), bf16[4,208,768]{2,1,0:T(8,128)(2,1)S(1)}, u32[]{:S(2)}, u32[]{:S(2)}) async-start(bf16[4,208,768]{2,1,0:T(8,128)(2,1)} %pack_tokens.1), calls=%async_computation | async-start | bytes 2555904 | tf_op jit(solution)/shard_map/all_to_all | solution.py:1092
  31.9 2.8 collective-permute-start.7
  35.4 1.6 bitcast_dynamic-update-slice_fusion.23
  37.0 1.6 bitcast_dynamic-update-slice_fusion.22
  38.5 1.7 slice.501
  40.3 1.7 slice.500
  43.2 2.0 collective-permute-start.4
  45.2 1.5 collective-permute-start.3
  53.1 1.5 pad_maximum_fusion.2.source_ref
  65.0 7.8 %convolution_convert_fusion.kglobal_ref = bf16[2048,768]{1,0:T(8,128)(2,1)} fusion(s32[264]{0:T(512)S(1)} %get-tuple-element.520, s32[264]{0:T(512)S(1)} %copy-done.52, s32[264]{0:T(512)S(1)} %copy-done.48, s32[264]{0:T(512)S(1)} %copy-done.51, s32[264]{0:T(512)S(1)} %copy-done.53, s32[2048]{0:T(1024)S(1)} %copy-done.38, s32[2048]{0:T(1024)S(1)} %copy-done.41, ...), kind=kOutput, calls=%fused_computation.2 | convolution fusion | flops 852793344 | bytes 3378108 | tf_op jit(solution)/shard_map/dot_general | solution.py:880
  73.0 2.0 collective-permute-start.11
  75.0 1.5 collective-permute-start.12
  76.6 3.3 collective-permute-done.8
  80.0 1.5 collective-permute-done.9
  84.7 5.7 %collective-permute-done.11 = bf16[4,24,3072]{2,1,0:T(8,128)(2,1)S(1)} collective-permute-done((bf16[4,24,3072]{2,1,0:T(8,128)(2,1)S(1)}, bf16[4,24,3072]{2,1,0:T(8,128)(2,1)S(1)}, u32[]{:S(2)}, u32[]{:S(2)}) %collective-permute-start.11) | collective-permute-done | bytes 589856 | tf_op jit(solution)/shard_map/ppermute | solution.py:922
  93.3 1.4 bitcast_dynamic-update-slice_fusion.5
  95.2 31.6 %attend_forward.1 = (f32[6,256,256]{2,1,0:T(8,128)S(1)}, bf16[1024,768]{1,0:T(8,128)(2,1)S(1)}, f32[6,8,256]{2,1,0:T(8,128)S(1)}, bf16[1024,768]{1,0:T(8,128)(2,...) custom-call(bf16[1280,768]{1,0:T(8,128)(2,1)} %pad_maximum_fusion.2., ...), custom_call_target="tpu_custom_call" | custom-call | flops 15099494400 | bytes 25165824 | tf_op jit(solution)/shard_map/attend_forward/pallas_call | solution.py:412
  126.9 2.3 bitcast_dynamic-update-slice_fusion.4
  129.2 1.4 bitcast_dynamic-update-slice_fusion.3
  130.9 2.2 copy-done.16
  133.7 7.3 %collective-permute-done.15 = bf16[2,2,4,24,6144]{4,3,2,1,0:T(8,128)(2,1)S(1)} collective-permute-done((bf16[2,2,4,24,6144]{4,3,2,1,0:T(8,128)(2,1)S(1)}, bf16[2,2,4,24,6144]{4,3,2,1,0:T(8,128)(2,1)S(1)}, u32[]{:S(2)}, u32[]{:S(2)}) %collective-permute-start.15) | collective-permute-done | bytes 4718624 | tf_op jit(solution)/shard_map/ppermute | solution.py:922
  141.0 2.1 copy-done.55
  143.1 47.5 %feed_forward.1 = (bf16[1024,768]{1,0:T(8,128)(2,1)}, f32[1024,768]{1,0:T(8,128)}, bf16[1024,768]{1,0:T(8,128)(2,1)}, f32[8,768]{1,0:T(8,128)}, bf16[2,384,384]{...) custom-call(bf16[1024,768]{1,0:T(8,128)(2,1)} %bitcast.357, ...), custom_call_target="tpu_custom_call" | custom-call | flops 32212254720 | bytes 41943040 | tf_op jit(solution)/shard_map/feed_forward/pallas_call | solution.py:730
  191.4 1.6 fusion.126
  193.3 24.6 %attend_backward.3 = (bf16[6,384,128]{2,1,0:T(8,128)(2,1)S(1)}, bf16[6,384,128]{2,1,0:T(8,128)(2,1)S(1)}, bf16[1280,768]{1,0:T(8,128)(2,1)}, bf16[256,768]{1,0:T...) custom-call(bf16[1024,768]{1,0:T(8,128)(2,1)S(1)} %copy-done.7, ...), custom_call_target="tpu_custom_call" | custom-call | flops 10066329600 | bytes 8388608 | tf_op jit(solution)/shard_map/attend_backward/pallas_call | solution.py:475
  219.6 2.4 fusion.125
  224.6 1.4 collective-permute-start.19
  226.0 1.5 collective-permute-start.20
  229.2 25.6 %attend_backward.4 = (bf16[6,384,128]{2,1,0:T(8,128)(2,1)S(1)}, bf16[6,384,128]{2,1,0:T(8,128)(2,1)S(1)}, bf16[1280,768]{1,0:T(8,128)(2,1)}, bf16[256,768]{1,0:T...) custom-call(bf16[1024,768]{1,0:T(8,128)(2,1)S(1)} %copy-done.7, ...), custom_call_target="tpu_custom_call" | custom-call | flops 10066329600 | bytes 8388608 | tf_op jit(solution)/shard_map/attend_backward/pallas_call | solution.py:475
  258.6 1.5 collective-permute-start.21
  263.0 26.4 %attend_backward.5 = (bf16[8,384,128]{2,1,0:T(8,128)(2,1)S(1)}, bf16[8,384,128]{2,1,0:T(8,128)(2,1)S(1)}, bf16[1280,768]{1,0:T(8,128)(2,1)}, bf16[4,192,768]{2,1...) custom-call(bf16[1024,768]{1,0:T(8,128)(2,1)} %get-tuple-element.265.query_ref, ...), custom_call_target="tpu_custom_call" | custom-call | flops 10066329600 | bytes 8388608 | tf_op jit(solution)/shard_map/attend_backward/pallas_call | solution.py:475
  291.5 1.4 fusion.39
  299.2 1.7 collective-permute-start.28
  300.9 6.8 %all-to-all-start.1 = ((bf16[1,4,24,6912]{3,2,0,1:T(8,128)(2,1)}), bf16[1,4,24,6912]{3,2,0,1:T(8,128)(2,1)S(1)}, u32[]{:S(2)}, u32[]{:S(2)}) async-start(bf16[1,4,24,6912]{3,2,0,1:T(8,128)(2,1)} %pad_maximum_fusion.7), calls=%async_computation.1 | async-start | bytes 2654208 | tf_op jit(solution)/shard_map/all_to_all | solution.py:945
  315.2 1.4 collective-permute-start.30
  316.9 10.6 %collective-permute-done.29 = bf16[10,2,4,24,128]{4,3,0,2,1:T(8,128)(2,1)S(1)} collective-permute-done((bf16[10,2,4,24,128]{4,3,0,2,1:T(8,128)(2,1)S(1)}, bf16[10,2,4,24,128]{4,3,0,2,1:T(8,128)(2,1)S(1)}, u32[]{:S(2)}, u32[]{:S(2)}) %collective-permute-start.29) | collective-permute-done | bytes 491552 | tf_op jit(solution)/shard_map/ppermute | solution.py:922
  327.8 1.3 collective-permute-start.31
  329.1 1.3 collective-permute-start.32
  331.4 6.6 %source_gradient.1 = f32[1024,768]{1,0:T(8,128)} custom-call(bf16[1024,768]{1,0:T(8,128)(2,1)} %bitcast.358, f32[1024,1]{1,0:T(8,128)} %copy.214.keep_ref, f32[1024,768]{1,0:T(8,128)} %get-tuple-element.353.middle_grad_ref, f32[8,768]{1,0:T(8,128)} %copy-done.3, bf16[1280,768]{1,0:T(8,128)(2,1)} %get-tuple-element.354.dnormed_ref, ...), custom_call_target="tpu_custom_call" | custom-call | flops 15728640 | bytes 14680064 | tf_op jit(solution)/shard_map/source_gradient/pallas_call | solution.py:820
  340.6 3.6 %collective-permute-start.33 = (bf16[20,24,128]{2,1,0:T(8,128)(2,1)S(1)}, bf16[20,24,128]{2,1,0:T(8,128)(2,1)S(1)}, u32[]{:S(2)}, u32[]{:S(2)}) collective-permute-start(bf16[20,24,128]{2,1,0:T(8,128)(2,1)S(1)} %pad_maximum_fusion.12), channel_id=1, source_target_pairs={{0,2},{2,4},{4,6},{6,0},{1,3},{3,5},{5,7},{7,1},{8,10},{10,12},{12... | collective-permute-start | bytes 368648 | tf_op jit(solution)/shard_map/ppermute | solution.py:922
  344.1 2.4 collective-permute-start.35
  348.6 4.0 %collective-permute-done.34 = bf16[20,24,128]{2,1,0:T(8,128)(2,1)S(1)} collective-permute-done((bf16[20,24,128]{2,1,0:T(8,128)(2,1)S(1)}, bf16[20,24,128]{2,1,0:T(8,128)(2,1)S(1)}, u32[]{:S(2)}, u32[]{:S(2)}) %collective-permute-start.34) | collective-permute-done | bytes 122912 | tf_op jit(solution)/shard_map/ppermute | solution.py:922
  (347 shorter events, 76.4 us)
Async XLA Ops:
  0.6 52.1 %copy-start = (f32[12,32]{1,0:T(8,128)S(1)}, f32[12,32]{1,0:T(8,128)}, u32[]{:S(2)}) copy-start(f32[12,32]{1,0:T(8,128)} %param.27) | copy-start | bytes 4612
  5.9 26.0 %collective-permute-start = (bf16[24,3200]{1,0:T(8,128)(2,1)}, bf16[24,3200]{1,0:T(8,128)(2,1)S(1)}, u32[]{:S(2)}, u32[]{:S(2)}) collective-permute-start(bf16[24,3200]{1,0:T(8,128)(2,1)} %get-tuple-element.194), channel_id=1, source_target_pairs={{0,2},{2,4},{4,6},{6,0},{1,3},{3,5},{5,7},{7,1},{8,10},{10,12},{12... | collective-permute-start | bytes 460808 | tf_op jit(solution)/shard_map/ppermute | solution.py:922
  8.9 25.8 %collective-permute-start.1 = (bf16[24,3200]{1,0:T(8,128)(2,1)}, bf16[24,3200]{1,0:T(8,128)(2,1)}, u32[]{:S(2)}, u32[]{:S(2)}) collective-permute-start(bf16[24,3200]{1,0:T(8,128)(2,1)} %get-tuple-element.194), channel_id=1, source_target_pairs={{0,4},{2,6},{4,0},{6,2},{1,5},{3,7},{5,1},{7,3},{8,12},{10,14},{12... | collective-permute-start | bytes 460808 | tf_op jit(solution)/shard_map/ppermute | solution.py:922
  11.5 23.2 %collective-permute-start.2 = (bf16[24,3200]{1,0:T(8,128)(2,1)}, bf16[24,3200]{1,0:T(8,128)(2,1)}, u32[]{:S(2)}, u32[]{:S(2)}) collective-permute-start(bf16[24,3200]{1,0:T(8,128)(2,1)} %get-tuple-element.194), channel_id=1, source_target_pairs={{0,6},{2,0},{4,2},{6,4},{1,7},{3,1},{5,3},{7,5},{8,14},{10,8},{12,... | collective-permute-start | bytes 460808 | tf_op jit(solution)/shard_map/ppermute | solution.py:922
  12.9 41.7 %collective-permute-start.5 = (bf16[24,6144]{1,0:T(8,128)(2,1)}, bf16[24,6144]{1,0:T(8,128)(2,1)}, u32[]{:S(2)}, u32[]{:S(2)}) collective-permute-start(bf16[24,6144]{1,0:T(8,128)(2,1)} %get-tuple-element.193), channel_id=1, source_target_pairs={{0,2},{2,4},{4,6},{6,0},{1,3},{3,5},{5,7},{7,1},{8,10},{10,12},{12... | collective-permute-start | bytes 884744 | tf_op jit(solution)/shard_map/ppermute | solution.py:922
  13.6 41.0 %collective-permute-start.6 = (bf16[24,6144]{1,0:T(8,128)(2,1)}, bf16[24,6144]{1,0:T(8,128)(2,1)}, u32[]{:S(2)}, u32[]{:S(2)}) collective-permute-start(bf16[24,6144]{1,0:T(8,128)(2,1)} %get-tuple-element.193), channel_id=1, source_target_pairs={{0,4},{2,6},{4,0},{6,2},{1,5},{3,7},{5,1},{7,3},{8,12},{10,14},{12... | collective-permute-start | bytes 884744 | tf_op jit(solution)/shard_map/ppermute | solution.py:922
  18.6 8.4 %copy-start.35 = (bf16[24,3200]{1,0:T(8,128)(2,1)S(1)}, bf16[24,3200]{1,0:T(8,128)(2,1)}, u32[]{:S(2)}) copy-start(bf16[24,3200]{1,0:T(8,128)(2,1)} %get-tuple-element.194) | copy-start | bytes 460804
  18.6 23.4 %all-to-all-start = ((bf16[4,208,768]{2,1,0:T(8,128)(2,1)}), bf16[4,208,768]{2,1,0:T(8,128)(2,1)S(1)}, u32[]{:S(2)}, u32[]{:S(2)}) async-start(bf16[4,208,768]{2,1,0:T(8,128)(2,1)} %pack_tokens.1), calls=%async_computation | async-start | bytes 2555904 | tf_op jit(solution)/shard_map/all_to_all | solution.py:1092
  22.5 6.3 %copy-start.37 = (s32[1,1024]{1,0:T(1,128)S(1)}, s32[1,1024]{1,0:T(1,128)}, u32[]{:S(2)}) copy-start(s32[1,1024]{1,0:T(1,128)} %param.17) | copy-start | bytes 12292
  31.9 22.7 %collective-permute-start.7 = (bf16[24,6144]{1,0:T(8,128)(2,1)}, bf16[24,6144]{1,0:T(8,128)(2,1)}, u32[]{:S(2)}, u32[]{:S(2)}) collective-permute-start(bf16[24,6144]{1,0:T(8,128)(2,1)} %get-tuple-element.193), channel_id=1, source_target_pairs={{0,6},{2,0},{4,2},{6,4},{1,7},{3,1},{5,3},{7,5},{8,14},{10,8},{12,... | collective-permute-start | bytes 884744 | tf_op jit(solution)/shard_map/ppermute | solution.py:922
  43.2 11.4 %collective-permute-start.4 = (bf16[4,24,1664]{2,1,0:T(8,128)(2,1)}, bf16[4,24,1664]{2,1,0:T(8,128)(2,1)}, u32[]{:S(2)}, u32[]{:S(2)}) collective-permute-start(bf16[4,24,1664]{2,1,0:T(8,128)(2,1)} %slice.501), channel_id=1, source_target_pairs={{0,16},{16,0},{1,17},{17,1},{2,18},{18,2},{3,19},{19,3},{4,20},{20... | collective-permute-start | bytes 958472 | tf_op jit(solution)/shard_map/ppermute | solution.py:922
  45.2 9.3 %collective-permute-start.3 = (bf16[4,24,1536]{2,1,0:T(8,128)(2,1)}, bf16[4,24,1536]{2,1,0:T(8,128)(2,1)}, u32[]{:S(2)}, u32[]{:S(2)}) collective-permute-start(bf16[4,24,1536]{2,1,0:T(8,128)(2,1)} %slice.500), channel_id=1, source_target_pairs={{0,8},{8,0},{1,9},{9,1},{2,10},{10,2},{3,11},{11,3},{4,12},{12,4},... | collective-permute-start | bytes 884744 | tf_op jit(solution)/shard_map/ppermute | solution.py:922
  64.1 17.4 %collective-permute-start.9 = (bf16[2,4,24,1664]{3,2,1,0:T(8,128)(2,1)S(1)}, bf16[2,4,24,1664]{3,2,1,0:T(8,128)(2,1)S(1)}, u32[]{:S(2)}, u32[]{:S(2)}) collective-permute-start(bf16[2,4,24,1664]{3,2,1,0:T(8,128)(2,1)S(1)} %copy-done.19), channel_id=1, source_target_pairs={{0,8},{8,0},{1,9},{9,1},{2,10},{10,2},{3,11},{11,3},{4,12},{12,4},... | collective-permute-start | bytes 1916936 | tf_op jit(solution)/shard_map/ppermute | solution.py:922
  64.7 15.2 %collective-permute-start.8 = (bf16[2,4,24,1536]{3,2,1,0:T(8,128)(2,1)S(1)}, bf16[2,4,24,1536]{3,2,1,0:T(8,128)(2,1)S(1)}, u32[]{:S(2)}, u32[]{:S(2)}) collective-permute-start(bf16[2,4,24,1536]{3,2,1,0:T(8,128)(2,1)S(1)} %copy-done.21), channel_id=1, source_target_pairs={{0,16},{16,0},{1,17},{17,1},{2,18},{18,2},{3,19},{19,3},{4,20},{20... | collective-permute-start | bytes 1769480 | tf_op jit(solution)/shard_map/ppermute | solution.py:922
  73.0 17.5 %collective-permute-start.11 = (bf16[4,24,3072]{2,1,0:T(8,128)(2,1)S(1)}, bf16[4,24,3072]{2,1,0:T(8,128)(2,1)S(1)}, u32[]{:S(2)}, u32[]{:S(2)}) collective-permute-start(bf16[4,24,3072]{2,1,0:T(8,128)(2,1)S(1)} %get-tuple-element.215), channel_id=1, source_target_pairs={{0,8},{8,0},{1,9},{9,1},{2,10},{10,2},{3,11},{11,3},{4,12},{12,4},... | collective-permute-start | bytes 1769480 | tf_op jit(solution)/shard_map/ppermute | solution.py:922
  75.0 15.5 %collective-permute-start.12 = (bf16[4,24,3072]{2,1,0:T(8,128)(2,1)S(1)}, bf16[4,24,3072]{2,1,0:T(8,128)(2,1)S(1)}, u32[]{:S(2)}, u32[]{:S(2)}) collective-permute-start(bf16[4,24,3072]{2,1,0:T(8,128)(2,1)S(1)} %get-tuple-element.221), channel_id=1, source_target_pairs={{0,16},{16,0},{1,17},{17,1},{2,18},{18,2},{3,19},{19,3},{4,20},{20... | collective-permute-start | bytes 1769480 | tf_op jit(solution)/shard_map/ppermute | solution.py:922
  81.8 8.7 %collective-permute-start.10 = (bf16[2,2,4,24,3200]{4,3,2,1,0:T(8,128)(2,1)S(1)}, bf16[2,2,4,24,3200]{4,3,2,1,0:T(8,128)(2,1)S(1)}, u32[]{:S(2)}, u32[]{:S(2)}) collective-permute-start(bf16[2,2,4,24,3200]{4,3,2,1,0:T(8,128)(2,1)S(1)} %pad_maximum_fusion.1), channel_id=1, source_target_pairs={{0,1},{1,0},{2,3},{3,2},{4,5},{5,4},{6,7},{7,6},{8,9},{9,8},{10,11... | collective-permute-start | bytes 7372808 | tf_op jit(solution)/shard_map/ppermute | solution.py:922
  91.8 35.1 %collective-permute-start.13 = (bf16[2,4,24,3072]{3,2,1,0:T(8,128)(2,1)}, bf16[2,4,24,3072]{3,2,1,0:T(8,128)(2,1)}, u32[]{:S(2)}, u32[]{:S(2)}) collective-permute-start(bf16[2,4,24,3072]{3,2,1,0:T(8,128)(2,1)} %bitcast_dynamic-update-slice_fusion.10), channel_id=1, source_target_pairs={{0,16},{16,0},{1,17},{17,1},{2,18},{18,2},{3,19},{19,3},{4,20},{20... | collective-permute-start | bytes 3538952 | tf_op jit(solution)/shard_map/ppermute | solution.py:922
  92.4 34.5 %collective-permute-start.14 = (bf16[2,4,24,3072]{3,2,1,0:T(8,128)(2,1)S(1)}, bf16[2,4,24,3072]{3,2,1,0:T(8,128)(2,1)}, u32[]{:S(2)}, u32[]{:S(2)}) collective-permute-start(bf16[2,4,24,3072]{3,2,1,0:T(8,128)(2,1)S(1)} %bitcast_dynamic-update-slice_fusion.8), channel_id=1, source_target_pairs={{0,8},{8,0},{1,9},{9,1},{2,10},{10,2},{3,11},{11,3},{4,12},{12,4},... | collective-permute-start | bytes 3538952 | tf_op jit(solution)/shard_map/ppermute | solution.py:922
  126.8 102.4 %copy-start.8 = (bf16[256,768]{1,0:T(8,128)(2,1)}, bf16[256,768]{1,0:T(8,128)(2,1)S(1)}, u32[]{:S(2)}) copy-start(bf16[256,768]{1,0:T(8,128)(2,1)S(1)} %get-tuple-element.270.gvalue_ref) | copy-start | bytes 1179652
  126.8 102.4 %copy-start.10 = (bf16[768,256]{1,0:T(8,128)(2,1)}, bf16[768,256]{1,0:T(8,128)(2,1)S(1)}, u32[]{:S(2)}) copy-start(bf16[768,256]{1,0:T(8,128)(2,1)S(1)} %get-tuple-element.273.pooled_turned) | copy-start | bytes 1179652
  133.1 7.9 %collective-permute-start.15 = (bf16[2,2,4,24,6144]{4,3,2,1,0:T(8,128)(2,1)S(1)}, bf16[2,2,4,24,6144]{4,3,2,1,0:T(8,128)(2,1)S(1)}, u32[]{:S(2)}, u32[]{:S(2)}) collective-permute-start(bf16[2,2,4,24,6144]{4,3,2,1,0:T(8,128)(2,1)S(1)} %pad_maximum_fusion), channel_id=1, source_target_pairs={{0,1},{1,0},{2,3},{3,2},{4,5},{5,4},{6,7},{7,6},{8,9},{9,8},{10,11... | collective-permute-start | bytes 14155784 | tf_op jit(solution)/shard_map/ppermute | solution.py:922
  190.6 27.8 %collective-permute-start.16 = (bf16[2,384,2048]{2,1,0:T(8,128)(2,1)}, bf16[2,384,2048]{2,1,0:T(8,128)(2,1)}, u32[]{:S(2)}, u32[]{:S(2)}) collective-permute-start(bf16[2,384,2048]{2,1,0:T(8,128)(2,1)} %get-tuple-element.262), channel_id=1, source_target_pairs={{0,1},{1,0},{2,3},{3,2},{4,5},{5,4},{6,7},{7,6},{8,9},{9,8},{10,11... | collective-permute-start | bytes 9437192 | tf_op jit(solution)/shard_map/ppermute | solution.py:971
  190.8 27.6 %collective-permute-start.17 = (bf16[2,384,1024]{2,1,0:T(8,128)(2,1)}, bf16[2,384,1024]{2,1,0:T(8,128)(2,1)S(1)}, u32[]{:S(2)}, u32[]{:S(2)}) collective-permute-start(bf16[2,384,1024]{2,1,0:T(8,128)(2,1)} %get-tuple-element.263), channel_id=1, source_target_pairs={{0,1},{1,0},{2,3},{3,2},{4,5},{5,4},{6,7},{7,6},{8,9},{9,8},{10,11... | collective-permute-start | bytes 4718600 | tf_op jit(solution)/shard_map/ppermute | solution.py:971
  191.2 27.2 %collective-permute-start.18 = (bf16[2,384,384]{2,1,0:T(8,128)(2,1)}, bf16[2,384,384]{2,1,0:T(8,128)(2,1)S(1)}, u32[]{:S(2)}, u32[]{:S(2)}) collective-permute-start(bf16[2,384,384]{2,1,0:T(8,128)(2,1)} %get-tuple-element.264), channel_id=1, source_target_pairs={{0,1},{1,0},{2,3},{3,2},{4,5},{5,4},{6,7},{7,6},{8,9},{9,8},{10,11... | collective-permute-start | bytes 1769480 | tf_op jit(solution)/shard_map/ppermute | solution.py:971
  193.3 24.6 %copy-start.29 = (bf16[2,384,384]{2,1,0:T(8,128)(2,1)S(1)}, bf16[2,384,384]{2,1,0:T(8,128)(2,1)}, u32[]{:S(2)}) copy-start(bf16[2,384,384]{2,1,0:T(8,128)(2,1)} %get-tuple-element.289) | copy-start | bytes 1769476
  193.3 24.7 %copy-start.17 = (bf16[2,384,2048]{2,1,0:T(8,128)(2,1)S(1)}, bf16[2,384,2048]{2,1,0:T(8,128)(2,1)}, u32[]{:S(2)}) copy-start(bf16[2,384,2048]{2,1,0:T(8,128)(2,1)} %get-tuple-element.256) | copy-start | bytes 9437188
  224.6 31.5 %collective-permute-start.19 = (bf16[1,2,4,24,3456]{4,3,2,1,0:T(8,128)(2,1)S(1)}, bf16[1,2,4,24,3456]{4,3,2,1,0:T(8,128)(2,1)S(1)}, u32[]{:S(2)}, u32[]{:S(2)}) collective-permute-start(bf16[1,2,4,24,3456]{4,3,2,1,0:T(8,128)(2,1)S(1)} %pad_maximum_fusion.4), channel_id=1, source_target_pairs={{0,8},{8,0},{1,9},{9,1},{2,10},{10,2},{3,11},{11,3},{4,12},{12,4},... | collective-permute-start | bytes 3981320 | tf_op jit(solution)/shard_map/ppermute | solution.py:922
  226.0 31.2 %collective-permute-start.20 = (bf16[1,2,4,24,3456]{4,3,2,1,0:T(8,128)(2,1)S(1)}, bf16[1,2,4,24,3456]{4,3,2,1,0:T(8,128)(2,1)}, u32[]{:S(2)}, u32[]{:S(2)}) collective-permute-start(bf16[1,2,4,24,3456]{4,3,2,1,0:T(8,128)(2,1)S(1)} %pad_maximum_fusion.5), channel_id=1, source_target_pairs={{0,16},{16,0},{1,17},{17,1},{2,18},{18,2},{3,19},{19,3},{4,20},{20... | collective-permute-start | bytes 3981320 | tf_op jit(solution)/shard_map/ppermute | solution.py:922
  258.6 30.8 %collective-permute-start.21 = (bf16[1,4,24,3456]{3,2,0,1:T(8,128)(2,1)S(1)}, bf16[1,4,24,3456]{3,2,0,1:T(8,128)(2,1)S(1)}, u32[]{:S(2)}, u32[]{:S(2)}) collective-permute-start(bf16[1,4,24,3456]{3,2,0,1:T(8,128)(2,1)S(1)} %fusion.45), channel_id=1, source_target_pairs={{0,16},{16,0},{1,17},{17,1},{2,18},{18,2},{3,19},{19,3},{4,20},{20... | collective-permute-start | bytes 1990664 | tf_op jit(solution)/shard_map/ppermute | solution.py:922
  260.2 29.3 %collective-permute-start.22 = (bf16[1,4,24,3456]{3,2,0,1:T(8,128)(2,1)S(1)}, bf16[1,4,24,3456]{3,2,0,1:T(8,128)(2,1)S(1)}, u32[]{:S(2)}, u32[]{:S(2)}) collective-permute-start(bf16[1,4,24,3456]{3,2,0,1:T(8,128)(2,1)S(1)} %fusion.46), channel_id=1, source_target_pairs={{0,8},{8,0},{1,9},{9,1},{2,10},{10,2},{3,11},{11,3},{4,12},{12,4},... | collective-permute-start | bytes 1990664 | tf_op jit(solution)/shard_map/ppermute | solution.py:922
  260.9 28.5 %collective-permute-start.23 = (bf16[6,384,128]{2,1,0:T(8,128)(2,1)S(1)}, bf16[6,384,128]{2,1,0:T(8,128)(2,1)S(1)}, u32[]{:S(2)}, u32[]{:S(2)}) collective-permute-start(bf16[6,384,128]{2,1,0:T(8,128)(2,1)S(1)} %get-tuple-element.318), channel_id=1, source_target_pairs={{0,1},{1,0},{2,3},{3,2},{4,5},{5,4},{6,7},{7,6},{8,9},{9,8},{10,11... | collective-permute-start | bytes 1769480 | tf_op jit(solution)/shard_map/ppermute | solution.py:971
  260.9 28.5 %collective-permute-start.24 = (bf16[6,384,128]{2,1,0:T(8,128)(2,1)S(1)}, bf16[6,384,128]{2,1,0:T(8,128)(2,1)S(1)}, u32[]{:S(2)}, u32[]{:S(2)}) collective-permute-start(bf16[6,384,128]{2,1,0:T(8,128)(2,1)S(1)} %get-tuple-element.319), channel_id=1, source_target_pairs={{0,1},{1,0},{2,3},{3,2},{4,5},{5,4},{6,7},{7,6},{8,9},{9,8},{10,11... | collective-permute-start | bytes 1769480 | tf_op jit(solution)/shard_map/ppermute | solution.py:971
  289.4 7.0 %copy-start.2 = (bf16[4,192,768]{2,1,0:T(8,128)(2,1)}, bf16[4,192,768]{2,1,0:T(8,128)(2,1)S(1)}, u32[]{:S(2)}) copy-start(bf16[4,192,768]{2,1,0:T(8,128)(2,1)S(1)} %get-tuple-element.340.payload_ref) | copy-start | bytes 3538948
  294.1 19.2 %collective-permute-start.25 = (bf16[8,384,128]{2,1,0:T(8,128)(2,1)S(1)}, bf16[8,384,128]{2,1,0:T(8,128)(2,1)S(1)}, u32[]{:S(2)}, u32[]{:S(2)}) collective-permute-start(bf16[8,384,128]{2,1,0:T(8,128)(2,1)S(1)} %get-tuple-element.339), channel_id=1, source_target_pairs={{0,1},{1,0},{2,3},{3,2},{4,5},{5,4},{6,7},{7,6},{8,9},{9,8},{10,11... | collective-permute-start | bytes 2359304 | tf_op jit(solution)/shard_map/ppermute | solution.py:971
  297.4 17.1 %collective-permute-start.26 = (bf16[192,768]{1,0:T(8,128)(2,1)}, bf16[192,768]{1,0:T(8,128)(2,1)}, u32[]{:S(2)}, u32[]{:S(2)}) collective-permute-start(bf16[192,768]{1,0:T(8,128)(2,1)} %get-tuple-element.389), channel_id=1, source_target_pairs={{0,8},{8,16},{16,24},{24,0},{1,9},{9,17},{17,25},{25,1},{2,10},{10... | collective-permute-start | bytes 884744 | tf_op jit(solution)/shard_map/ppermute | solution.py:1178
  298.6 15.9 %collective-permute-start.27 = (bf16[192,768]{1,0:T(8,128)(2,1)}, bf16[192,768]{1,0:T(8,128)(2,1)}, u32[]{:S(2)}, u32[]{:S(2)}) collective-permute-start(bf16[192,768]{1,0:T(8,128)(2,1)} %get-tuple-element.388), channel_id=1, source_target_pairs={{0,16},{8,24},{16,0},{24,8},{1,17},{9,25},{17,1},{25,9},{2,18},{10... | collective-permute-start | bytes 884744 | tf_op jit(solution)/shard_map/ppermute | solution.py:1178
  299.2 15.3 %collective-permute-start.28 = (bf16[192,768]{1,0:T(8,128)(2,1)}, bf16[192,768]{1,0:T(8,128)(2,1)}, u32[]{:S(2)}, u32[]{:S(2)}) collective-permute-start(bf16[192,768]{1,0:T(8,128)(2,1)} %get-tuple-element.387), channel_id=1, source_target_pairs={{0,24},{8,0},{16,8},{24,16},{1,25},{9,1},{17,9},{25,17},{2,26},{10... | collective-permute-start | bytes 884744 | tf_op jit(solution)/shard_map/ppermute | solution.py:1178
  300.9 38.4 %all-to-all-start.1 = ((bf16[1,4,24,6912]{3,2,0,1:T(8,128)(2,1)}), bf16[1,4,24,6912]{3,2,0,1:T(8,128)(2,1)S(1)}, u32[]{:S(2)}, u32[]{:S(2)}) async-start(bf16[1,4,24,6912]{3,2,0,1:T(8,128)(2,1)} %pad_maximum_fusion.7), calls=%async_computation.1 | async-start | bytes 2654208 | tf_op jit(solution)/shard_map/all_to_all | solution.py:945
  314.5 13.0 %collective-permute-start.29 = (bf16[10,2,4,24,128]{4,3,0,2,1:T(8,128)(2,1)S(1)}, bf16[10,2,4,24,128]{4,3,0,2,1:T(8,128)(2,1)S(1)}, u32[]{:S(2)}, u32[]{:S(2)}) collective-permute-start(bf16[10,2,4,24,128]{4,3,0,2,1:T(8,128)(2,1)S(1)} %pad_maximum_fusion.9), channel_id=1, source_target_pairs={{0,8},{8,0},{1,9},{9,1},{2,10},{10,2},{3,11},{11,3},{4,12},{12,4},... | collective-permute-start | bytes 1474568 | tf_op jit(solution)/shard_map/ppermute | solution.py:922
  315.2 12.3 %collective-permute-start.30 = (bf16[10,2,4,24,128]{4,3,0,2,1:T(8,128)(2,1)S(1)}, bf16[10,2,4,24,128]{4,3,0,2,1:T(8,128)(2,1)S(1)}, u32[]{:S(2)}, u32[]{:S(2)}) collective-permute-start(bf16[10,2,4,24,128]{4,3,0,2,1:T(8,128)(2,1)S(1)} %pad_maximum_fusion.10), channel_id=1, source_target_pairs={{0,16},{16,0},{1,17},{17,1},{2,18},{18,2},{3,19},{19,3},{4,20},{20... | collective-permute-start | bytes 1474568 | tf_op jit(solution)/shard_map/ppermute | solution.py:922
  327.8 10.3 %collective-permute-start.31 = (bf16[10,4,24,128]{3,2,0,1:T(8,128)(2,1)S(1)}, bf16[10,4,24,128]{3,2,0,1:T(8,128)(2,1)S(1)}, u32[]{:S(2)}, u32[]{:S(2)}) collective-permute-start(bf16[10,4,24,128]{3,2,0,1:T(8,128)(2,1)S(1)} %get-tuple-element.351), channel_id=1, source_target_pairs={{0,16},{16,0},{1,17},{17,1},{2,18},{18,2},{3,19},{19,3},{4,20},{20... | collective-permute-start | bytes 737288 | tf_op jit(solution)/shard_map/ppermute | solution.py:922
  329.1 8.9 %collective-permute-start.32 = (bf16[10,4,24,128]{3,2,0,1:T(8,128)(2,1)S(1)}, bf16[10,4,24,128]{3,2,0,1:T(8,128)(2,1)S(1)}, u32[]{:S(2)}, u32[]{:S(2)}) collective-permute-start(bf16[10,4,24,128]{3,2,0,1:T(8,128)(2,1)S(1)} %get-tuple-element.352), channel_id=1, source_target_pairs={{0,8},{8,0},{1,9},{9,1},{2,10},{10,2},{3,11},{11,3},{4,12},{12,4},... | collective-permute-start | bytes 737288 | tf_op jit(solution)/shard_map/ppermute | solution.py:922
  340.4 14.4 %copy-start.1 = (f32[12,32]{1,0:T(8,128)S(1)}, f32[12,32]{1,0:T(8,128)}, u32[]{:S(2)}) copy-start(f32[12,32]{1,0:T(8,128)} %param.27) | copy-start | bytes 4612
  340.6 8.1 %collective-permute-start.33 = (bf16[20,24,128]{2,1,0:T(8,128)(2,1)S(1)}, bf16[20,24,128]{2,1,0:T(8,128)(2,1)S(1)}, u32[]{:S(2)}, u32[]{:S(2)}) collective-permute-start(bf16[20,24,128]{2,1,0:T(8,128)(2,1)S(1)} %pad_maximum_fusion.12), channel_id=1, source_target_pairs={{0,2},{2,4},{4,6},{6,0},{1,3},{3,5},{5,7},{7,1},{8,10},{10,12},{12... | collective-permute-start | bytes 368648 | tf_op jit(solution)/shard_map/ppermute | solution.py:922
  344.1 8.5 %collective-permute-start.34 = (bf16[20,24,128]{2,1,0:T(8,128)(2,1)S(1)}, bf16[20,24,128]{2,1,0:T(8,128)(2,1)S(1)}, u32[]{:S(2)}, u32[]{:S(2)}) collective-permute-start(bf16[20,24,128]{2,1,0:T(8,128)(2,1)S(1)} %pad_maximum_fusion.13), channel_id=1, source_target_pairs={{0,4},{2,6},{4,0},{6,2},{1,5},{3,7},{5,1},{7,3},{8,12},{10,14},{12... | collective-permute-start | bytes 368648 | tf_op jit(solution)/shard_map/ppermute | solution.py:922
  344.1 8.5 %collective-permute-start.35 = (bf16[20,24,128]{2,1,0:T(8,128)(2,1)S(1)}, bf16[20,24,128]{2,1,0:T(8,128)(2,1)S(1)}, u32[]{:S(2)}, u32[]{:S(2)}) collective-permute-start(bf16[20,24,128]{2,1,0:T(8,128)(2,1)S(1)} %pad_maximum_fusion.14), channel_id=1, source_target_pairs={{0,6},{2,0},{4,2},{6,4},{1,7},{3,1},{5,3},{7,5},{8,14},{10,8},{12,... | collective-permute-start | bytes 368648 | tf_op jit(solution)/shard_map/ppermute | solution.py:922
  346.6 7.5 %copy-start.44 = (f32[1,64,768]{2,1,0:T(8,128)}, f32[1,64,768]{2,1,0:T(8,128)S(1)}, u32[]{:S(2)}) copy-start(f32[1,64,768]{2,1,0:T(8,128)S(1)} %constant_dynamic-update-slice_fusion.18) | copy-start | bytes 589828
  (49 other events, 106.7 us)

commit v5 on v4

--- a/solution.py
+++ b/solution.py
@@ -789,26 +789,29 @@
     )(source, mixture, weights, gains, cotangent, held, other, held, other, held, other, place)
 
 
-def source_gradient(source_ref, keep_ref, middle_grad_ref, gains_ref, dnormed_ref, payload_ref, *refs):
+def source_gradient(source_ref, keep_ref, middle_grad_ref, gains_ref, upper_ref, lower_ref, *refs):
     step, steps = pl.program_id(0), pl.num_programs(0)
-    received, out_ref = refs[:-1], refs[-1]
-    seq_count = len(received) + 1
-    own_slots = payload_ref.shape[1] - 128
+    pooled_refs, edge_refs, out_ref = refs[:-5], refs[-5:-1], refs[-1]
     rows, width = source_ref.shape
-    slots = pl.ds(pl.multiple_of(step * (rows // 16), rows // 16), rows // 16)
-    pooled = payload_ref[0, slots, :].astype(f32)
-    for other_ref in received:
-        pooled = pooled + other_ref[slots, :].astype(f32)
+    pooled = pooled_refs[0][0].astype(f32)
+    for other_ref in pooled_refs[1:]:
+        pooled = pooled + other_ref[...].astype(f32)
     pooled = jnp.broadcast_to(pooled[:, None, :], (rows // 16, 16, width)).reshape(rows, width)
-    own = pl.ds(pl.multiple_of(128 + step * rows, 128), rows)
-    grad = dnormed_ref[own, :].astype(f32) + pooled * keep_ref[...]
     me = lax.axis_index("y") * lax.axis_size("x") + lax.axis_index("x")
     before = (step == 0) & (me > 0)
-    after = (step == steps - 1) & (me < seq_count - 1)
-    head = received[0][own_slots:, :].astype(f32)
-    tail = received[-1][own_slots:, :].astype(f32)
-    edges = [jnp.where(before, head, 0.0), jnp.zeros((rows - 256, width), f32), jnp.where(after, tail, 0.0)]
-    grad = grad + jnp.concatenate([edge for edge in edges if edge.shape[0]], axis=0)
+    after = (step == steps - 1) & (me < len(pooled_refs) - 1)
+    head, tail = (
+        jnp.concatenate([first[...], second[...]], axis=0).astype(f32)
+        for first, second in (edge_refs[:2], edge_refs[2:])
+    )
+    grad = jnp.concatenate(
+        [
+            upper_ref[...].astype(f32) + jnp.where(before, head, 0.0),
+            lower_ref[...].astype(f32) + jnp.where(after, tail, 0.0),
+        ],
+        axis=0,
+    )
+    grad = grad + pooled * keep_ref[...]
     values = source_ref[...].astype(f32)
     out_ref[...] = middle_grad_ref[...] + norm_gradient(values, inverse_rms(values), gains_ref[0:1, :], grad)
 
@@ -816,7 +819,12 @@
 def input_gradient(source, keep, middle_grad, gains, dnormed, payload, received):
     rows, width = source.shape
     tile = 256
+    own_slots = rows // 16
     row_spec = pl.BlockSpec((tile, width), lambda step: (step, 0))
+    edges = [
+        pl.BlockSpec((64, width), lambda step, index=index: (own_slots // 64 + index, 0), pipeline_mode=pl.Buffered(1))
+        for index in range(2)
+    ]
     return pl.pallas_call(
         source_gradient,
         grid=(rows // tile,),
@@ -825,10 +833,12 @@
             pl.BlockSpec((tile, 1), lambda step: (step, 0)),
             row_spec,
             fixed(8, width),
-            fixed(*dnormed.shape),
-            pl.BlockSpec((1,) + payload.shape[1:], lambda step: (0, 0, 0), pipeline_mode=pl.Buffered(1)),
+            pl.BlockSpec((128, width), lambda step: (1 + 2 * step, 0)),
+            pl.BlockSpec((128, width), lambda step: (2 + 2 * step, 0)),
+            pl.BlockSpec((1, tile // 16, width), lambda step: (0, step, 0)),
         ]
-        + [fixed(*other.shape) for other in received],
+        + [pl.BlockSpec((tile // 16, width), lambda step: (step, 0)) for _ in received]
+        + edges * 2,
         out_specs=row_spec,
         out_shape=jax.ShapeDtypeStruct((rows, width), f32),
         compiler_params=pltpu.CompilerParams(vmem_limit_bytes=60 << 20),
@@ -836,7 +846,10 @@
             flops=20 * rows * width, bytes_accessed=14 << 20, transcendentals=0
         ),
         name="source_gradient",
-    )(source, keep, middle_grad, gains, dnormed, payload, *received)
+    )(
+        source, keep, middle_grad, gains, dnormed, dnormed, payload, *received, received[0], received[0], received[-1],
+        received[-1],
+    )
 
 
 def near_offsets(local_bias):
@@ -1080,7 +1093,6 @@
     aligned = own_part * 32 == model_width
     place = jnp.stack([lax.axis_index("core"), first_slot]).astype(i32)
     gain_columns = jnp.pad(jnp.stack([norm_gain, pool_gain, feed_gain], axis=1), ((0, 0), (0, 125)))
-    marks = jnp.concatenate([segment_ids.reshape(-1, 128), valid_mask.reshape(-1, 128)])
     packed, packed_second = pack_all(
         query_weight, key_weight, value_weight, output_weight, gain_columns, gate_weight, up_weight, down_weight, aligned
     )
@@ -1088,18 +1100,20 @@
     later = [Chain(all_rows(packed_second, False))] if aligned else []
 
     def share(operands):
-        shared = pack_shared(*operands, seq_count)
+        source, segments, valid = operands
+        marks = jnp.concatenate([segments.reshape(-1, 128), valid.reshape(-1, 128)])
+        shared = pack_shared(source, valid[0].astype(f32)[:, None], marks, seq_count)
         return lax.all_to_all(shared, seq, 0, 0, tiled=True)
 
     held = []
     phase(
-        (source, valid_float[:, None], marks), lambda operands: held.append(share(operands)), [first] + later, [first]
+        (source, segment_ids, valid_mask), lambda operands: held.append(share(operands)), [first] + later, [first]
     )
 
     def near_parts(operands):
         shared, local_bias = operands
         me = lax.axis_index(seq)
-        edge = own_slots + marks.shape[0]
+        edge = own_slots + 2 * (tok_rows // 128)
         raw_pool = shared[:, :own_slots].reshape(slot_count, model_width)
         all_marks = shared[:, own_slots:edge, :128].astype(i32).reshape(seq_count, 2, tok_rows)
         before, after = (

time: 360 us -> 357 us (level)
    unnamed x127 -> x135, local copies, waits for them, and re-layouts: 7.61 us -> 7.58 us
  transfers between devices with their start and end apart: 38 -> 38, of which waited for: 10 -> 11; matrix products, arithmetic and copies ran while one was open for 16% -> 17% of each run, Pallas kernels for 33% -> 34%
where the time goes in v5:
time: 357 us; the launch traced here: 352 us
  Pallas kernels  168 us (47%)
  local copies, waits for them, and re-layouts  59.5 us (17%)
  starting transfers between devices  48.8 us (14%)
  waiting for transfers between devices  37.7 us (11%)
  other arithmetic  28 us (8%)
  matrix products  8.05 us (2%)
    pallas_call x3, Pallas kernels, attention_backward(): pl.pallas_call(functools.partial(attend_backward, first + count == pairs,...  76.6 us
    pallas_call x1, Pallas kernels, feed_forward_both(): pl.pallas_call(feed_forward, grid=(tiles,), in_specs=[fixed(rows, width),...  47.5 us
    ppermute x27, waiting for transfers between devices, send_all(): lax.ppermute(piece, axis, ring(size, hop + 1))  36.4 us
    ppermute x27, starting transfers between devices, send_all(): lax.ppermute(piece, axis, ring(size, hop + 1))  35.2 us
    pallas_call x1, Pallas kernels, attention_forward(): pl.pallas_call(attend_forward, grid=(pairs,), in_specs=[fixed(rows + 256,...  31.5 us
    dynamic_update_slice x15, local copies, waits for them, and re-layouts, place_stage(): lax.dynamic_update_index_in_dim(out, piece, (me - hop - 1) % size, dim)  14.2 us
    convert_element_type x24, other arithmetic, split_stage(): add_up([pick(part, (me + hop) % size, dim) for part in piece]).astype(bf16)  9.54 us
    dot_general x1, matrix products, far_features(): return jnp.dot(picks, table, preferred_element_type=f32).astype(bf16)  7.79 us
  transfers between devices with their start and end apart: 38, of which 11 were waited for; matrix products, arithmetic and copies ran while one was open for 17% of the time, Pallas kernels for 34%

profile of v5, /device:TPU:0, one launch (start us, length us, event | category | flops | bytes accessed | tf_op | source)
XLA Modules:
  0.0 352.2 jit_solution(2824378357443719372)
XLA Ops:
  2.1 1.8 pack_weights.1
  3.9 3.0 collective-permute-start
  6.9 2.6 collective-permute-start.1
  9.5 1.3 collective-permute-start.2
  13.6 1.3 pad_add_fusion.marks_ref
  14.9 3.7 %pack_tokens.1 = bf16[4,208,768]{2,1,0:T(8,128)(2,1)} custom-call(bf16[1024,768]{1,0:T(8,128)(2,1)} %bitcast.358, f32[1024,1]{1,0:T(8,128)} %copy.165.keep_ref, s32[16,128]{1,0:T(8,128)} %pad_add_fusion.marks_ref), custom_call_target="tpu_custom_call" | custom-call | tf_op jit(solution)/shard_map/pack_tokens/pallas_call | solution.py:620
  18.6 3.8 %all-to-all-start = ((bf16[4,208,768]{2,1,0:T(8,128)(2,1)}), bf16[4,208,768]{2,1,0:T(8,128)(2,1)S(1)}, u32[]{:S(2)}, u32[]{:S(2)}) async-start(bf16[4,208,768]{2,1,0:T(8,128)(2,1)} %pack_tokens.1), calls=%async_computation | async-start | bytes 2555904 | tf_op jit(solution)/shard_map/all_to_all | solution.py:1106
  31.7 2.8 collective-permute-start.7
  35.2 1.6 bitcast_dynamic-update-slice_fusion.23
  36.8 1.6 bitcast_dynamic-update-slice_fusion.22
  38.4 1.7 slice.501
  40.1 1.7 slice.500
  43.1 2.0 collective-permute-start.4
  45.1 1.5 collective-permute-start.3
  53.0 1.5 pad_maximum_fusion.2.source_ref
  64.3 7.8 %convolution_convert_fusion.kglobal_ref = bf16[2048,768]{1,0:T(8,128)(2,1)} fusion(s32[264]{0:T(512)S(1)} %copy-done.41, s32[264]{0:T(512)S(1)} %copy-done.56, s32[264]{0:T(512)S(1)} %copy-done.52, s32[264]{0:T(512)S(1)} %copy-done.55, s32[264]{0:T(512)S(1)} %copy-done.57, s32[2048]{0:T(1024)S(1)} %copy-done.42, s32[2048]{0:T(1024)S(1)} %copy-done.45, ...), kind=kOutput, calls=%fused_computation.2 | convolution fusion | flops 852793344 | bytes 3378108 | tf_op jit(solution)/shard_map/dot_general | solution.py:893
  72.2 2.0 collective-permute-start.11
  74.2 1.5 collective-permute-start.12
  75.8 3.3 collective-permute-done.8
  79.2 1.5 collective-permute-done.9
  84.0 5.7 %collective-permute-done.11 = bf16[4,24,3072]{2,1,0:T(8,128)(2,1)S(1)} collective-permute-done((bf16[4,24,3072]{2,1,0:T(8,128)(2,1)S(1)}, bf16[4,24,3072]{2,1,0:T(8,128)(2,1)S(1)}, u32[]{:S(2)}, u32[]{:S(2)}) %collective-permute-start.11) | collective-permute-done | bytes 589856 | tf_op jit(solution)/shard_map/ppermute | solution.py:935
  92.6 1.4 bitcast_dynamic-update-slice_fusion.5
  94.4 31.5 %attend_forward.1 = (f32[6,256,256]{2,1,0:T(8,128)S(1)}, bf16[1024,768]{1,0:T(8,128)(2,1)S(1)}, f32[6,8,256]{2,1,0:T(8,128)S(1)}, bf16[1024,768]{1,0:T(8,128)(2,...) custom-call(bf16[1280,768]{1,0:T(8,128)(2,1)} %pad_maximum_fusion.2., ...), custom_call_target="tpu_custom_call" | custom-call | flops 15099494400 | bytes 25165824 | tf_op jit(solution)/shard_map/attend_forward/pallas_call | solution.py:412
  126.0 2.3 bitcast_dynamic-update-slice_fusion.4
  128.3 1.4 bitcast_dynamic-update-slice_fusion.3
  130.1 2.2 copy-done.16
  132.9 7.3 %collective-permute-done.15 = bf16[2,2,4,24,6144]{4,3,2,1,0:T(8,128)(2,1)S(1)} collective-permute-done((bf16[2,2,4,24,6144]{4,3,2,1,0:T(8,128)(2,1)S(1)}, bf16[2,2,4,24,6144]{4,3,2,1,0:T(8,128)(2,1)S(1)}, u32[]{:S(2)}, u32[]{:S(2)}) %collective-permute-start.15) | collective-permute-done | bytes 4718624 | tf_op jit(solution)/shard_map/ppermute | solution.py:935
  140.2 2.1 copy-done.59
  142.3 47.5 %feed_forward.1 = (bf16[1024,768]{1,0:T(8,128)(2,1)}, f32[1024,768]{1,0:T(8,128)}, bf16[1024,768]{1,0:T(8,128)(2,1)}, f32[8,768]{1,0:T(8,128)}, bf16[2,384,384]{...) custom-call(bf16[1024,768]{1,0:T(8,128)(2,1)} %bitcast.359, ...), custom_call_target="tpu_custom_call" | custom-call | flops 32212254720 | bytes 41943040 | tf_op jit(solution)/shard_map/feed_forward/pallas_call | solution.py:730
  190.5 1.6 fusion.126
  192.4 24.6 %attend_backward.3 = (bf16[6,384,128]{2,1,0:T(8,128)(2,1)S(1)}, bf16[6,384,128]{2,1,0:T(8,128)(2,1)S(1)}, bf16[1280,768]{1,0:T(8,128)(2,1)}, bf16[256,768]{1,0:T...) custom-call(bf16[1024,768]{1,0:T(8,128)(2,1)S(1)} %copy-done.7, ...), custom_call_target="tpu_custom_call" | custom-call | flops 10066329600 | bytes 8388608 | tf_op jit(solution)/shard_map/attend_backward/pallas_call | solution.py:475
  218.7 2.4 fusion.125
  223.7 1.4 collective-permute-start.19
  225.1 1.5 collective-permute-start.20
  228.4 25.6 %attend_backward.4 = (bf16[6,384,128]{2,1,0:T(8,128)(2,1)S(1)}, bf16[6,384,128]{2,1,0:T(8,128)(2,1)S(1)}, bf16[1280,768]{1,0:T(8,128)(2,1)}, bf16[256,768]{1,0:T...) custom-call(bf16[1024,768]{1,0:T(8,128)(2,1)S(1)} %copy-done.7, ...), custom_call_target="tpu_custom_call" | custom-call | flops 10066329600 | bytes 8388608 | tf_op jit(solution)/shard_map/attend_backward/pallas_call | solution.py:475
  257.8 1.5 collective-permute-start.21
  262.1 26.4 %attend_backward.5 = (bf16[8,384,128]{2,1,0:T(8,128)(2,1)S(1)}, bf16[8,384,128]{2,1,0:T(8,128)(2,1)S(1)}, bf16[1280,768]{1,0:T(8,128)(2,1)}, bf16[4,192,768]{2,1...) custom-call(bf16[1024,768]{1,0:T(8,128)(2,1)} %get-tuple-element.265.query_ref, ...), custom_call_target="tpu_custom_call" | custom-call | flops 10066329600 | bytes 8388608 | tf_op jit(solution)/shard_map/attend_backward/pallas_call | solution.py:475
  290.7 1.4 fusion.39
  296.5 1.3 collective-permute-start.26
  298.3 1.7 collective-permute-start.28
  300.0 5.0 %all-to-all-start.1 = ((bf16[1,4,24,6912]{3,2,0,1:T(8,128)(2,1)}), bf16[1,4,24,6912]{3,2,0,1:T(8,128)(2,1)S(1)}, u32[]{:S(2)}, u32[]{:S(2)}) async-start(bf16[1,4,24,6912]{3,2,0,1:T(8,128)(2,1)} %pad_maximum_fusion.7), calls=%async_computation.1 | async-start | bytes 2654208 | tf_op jit(solution)/shard_map/all_to_all | solution.py:958
  314.3 1.4 collective-permute-start.30
  316.0 10.6 %collective-permute-done.29 = bf16[10,2,4,24,128]{4,3,0,2,1:T(8,128)(2,1)S(1)} collective-permute-done((bf16[10,2,4,24,128]{4,3,0,2,1:T(8,128)(2,1)S(1)}, bf16[10,2,4,24,128]{4,3,0,2,1:T(8,128)(2,1)S(1)}, u32[]{:S(2)}, u32[]{:S(2)}) %collective-permute-start.29) | collective-permute-done | bytes 491552 | tf_op jit(solution)/shard_map/ppermute | solution.py:935
  330.3 6.3 %source_gradient.1 = f32[1024,768]{1,0:T(8,128)} custom-call(bf16[1024,768]{1,0:T(8,128)(2,1)} %bitcast.360, f32[1024,1]{1,0:T(8,128)} %copy.214.keep_ref, f32[1024,768]{1,0:T(8,128)} %get-tuple-element.353.middle_grad_ref, f32[8,768]{1,0:T(8,128)} %copy-done.3, bf16[1280,768]{1,0:T(8,128)(2,1)} %get-tuple-element.354.upper_ref.lower_ref, ...), custom_call_target="tpu_custom_call" | custom-call | flops 15728640 | bytes 14680064 | tf_op jit(solution)/shard_map/source_gradient/pallas_call | solution.py:828
  338.0 3.2 collective-permute-start.33
  341.1 2.4 collective-permute-start.35
  344.4 1.8 collective-permute-done.33
  346.2 3.7 %collective-permute-done.34 = bf16[20,24,128]{2,1,0:T(8,128)(2,1)S(1)} collective-permute-done((bf16[20,24,128]{2,1,0:T(8,128)(2,1)S(1)}, bf16[20,24,128]{2,1,0:T(8,128)(2,1)S(1)}, u32[]{:S(2)}, u32[]{:S(2)}) %collective-permute-start.34) | collective-permute-done | bytes 122912 | tf_op jit(solution)/shard_map/ppermute | solution.py:935
  (356 shorter events, 76.1 us)
Async XLA Ops:
  0.6 52.0 %copy-start = (f32[12,32]{1,0:T(8,128)S(1)}, f32[12,32]{1,0:T(8,128)}, u32[]{:S(2)}) copy-start(f32[12,32]{1,0:T(8,128)} %param.27) | copy-start | bytes 4612
  3.9 27.8 %collective-permute-start = (bf16[24,3200]{1,0:T(8,128)(2,1)}, bf16[24,3200]{1,0:T(8,128)(2,1)S(1)}, u32[]{:S(2)}, u32[]{:S(2)}) collective-permute-start(bf16[24,3200]{1,0:T(8,128)(2,1)} %get-tuple-element.194), channel_id=1, source_target_pairs={{0,2},{2,4},{4,6},{6,0},{1,3},{3,5},{5,7},{7,1},{8,10},{10,12},{12... | collective-permute-start | bytes 460808 | tf_op jit(solution)/shard_map/ppermute | solution.py:935
  6.9 27.6 %collective-permute-start.1 = (bf16[24,3200]{1,0:T(8,128)(2,1)}, bf16[24,3200]{1,0:T(8,128)(2,1)}, u32[]{:S(2)}, u32[]{:S(2)}) collective-permute-start(bf16[24,3200]{1,0:T(8,128)(2,1)} %get-tuple-element.194), channel_id=1, source_target_pairs={{0,4},{2,6},{4,0},{6,2},{1,5},{3,7},{5,1},{7,3},{8,12},{10,14},{12... | collective-permute-start | bytes 460808 | tf_op jit(solution)/shard_map/ppermute | solution.py:935
  9.5 25.0 %collective-permute-start.2 = (bf16[24,3200]{1,0:T(8,128)(2,1)}, bf16[24,3200]{1,0:T(8,128)(2,1)}, u32[]{:S(2)}, u32[]{:S(2)}) collective-permute-start(bf16[24,3200]{1,0:T(8,128)(2,1)} %get-tuple-element.194), channel_id=1, source_target_pairs={{0,6},{2,0},{4,2},{6,4},{1,7},{3,1},{5,3},{7,5},{8,14},{10,8},{12,... | collective-permute-start | bytes 460808 | tf_op jit(solution)/shard_map/ppermute | solution.py:935
  10.9 43.5 %collective-permute-start.5 = (bf16[24,6144]{1,0:T(8,128)(2,1)}, bf16[24,6144]{1,0:T(8,128)(2,1)}, u32[]{:S(2)}, u32[]{:S(2)}) collective-permute-start(bf16[24,6144]{1,0:T(8,128)(2,1)} %get-tuple-element.193), channel_id=1, source_target_pairs={{0,2},{2,4},{4,6},{6,0},{1,3},{3,5},{5,7},{7,1},{8,10},{10,12},{12... | collective-permute-start | bytes 884744 | tf_op jit(solution)/shard_map/ppermute | solution.py:935
  11.6 42.9 %collective-permute-start.6 = (bf16[24,6144]{1,0:T(8,128)(2,1)}, bf16[24,6144]{1,0:T(8,128)(2,1)}, u32[]{:S(2)}, u32[]{:S(2)}) collective-permute-start(bf16[24,6144]{1,0:T(8,128)(2,1)} %get-tuple-element.193), channel_id=1, source_target_pairs={{0,4},{2,6},{4,0},{6,2},{1,5},{3,7},{5,1},{7,3},{8,12},{10,14},{12... | collective-permute-start | bytes 884744 | tf_op jit(solution)/shard_map/ppermute | solution.py:935
  18.6 8.3 %copy-start.36 = (bf16[24,3200]{1,0:T(8,128)(2,1)S(1)}, bf16[24,3200]{1,0:T(8,128)(2,1)}, u32[]{:S(2)}) copy-start(bf16[24,3200]{1,0:T(8,128)(2,1)} %get-tuple-element.194) | copy-start | bytes 460804
  18.6 23.2 %all-to-all-start = ((bf16[4,208,768]{2,1,0:T(8,128)(2,1)}), bf16[4,208,768]{2,1,0:T(8,128)(2,1)S(1)}, u32[]{:S(2)}, u32[]{:S(2)}) async-start(bf16[4,208,768]{2,1,0:T(8,128)(2,1)} %pack_tokens.1), calls=%async_computation | async-start | bytes 2555904 | tf_op jit(solution)/shard_map/all_to_all | solution.py:1106
  23.1 7.1 %copy-start.40 = (s32[264]{0:T(512)}, s32[264]{0:T(512)S(1)}, u32[]{:S(2)}) copy-start(s32[264]{0:T(512)S(1)} %get-tuple-element.520) | copy-start | bytes 3172
  31.7 22.7 %collective-permute-start.7 = (bf16[24,6144]{1,0:T(8,128)(2,1)}, bf16[24,6144]{1,0:T(8,128)(2,1)}, u32[]{:S(2)}, u32[]{:S(2)}) collective-permute-start(bf16[24,6144]{1,0:T(8,128)(2,1)} %get-tuple-element.193), channel_id=1, source_target_pairs={{0,6},{2,0},{4,2},{6,4},{1,7},{3,1},{5,3},{7,5},{8,14},{10,8},{12,... | collective-permute-start | bytes 884744 | tf_op jit(solution)/shard_map/ppermute | solution.py:935
  43.1 11.4 %collective-permute-start.4 = (bf16[4,24,1664]{2,1,0:T(8,128)(2,1)}, bf16[4,24,1664]{2,1,0:T(8,128)(2,1)}, u32[]{:S(2)}, u32[]{:S(2)}) collective-permute-start(bf16[4,24,1664]{2,1,0:T(8,128)(2,1)} %slice.501), channel_id=1, source_target_pairs={{0,16},{16,0},{1,17},{17,1},{2,18},{18,2},{3,19},{19,3},{4,20},{20... | collective-permute-start | bytes 958472 | tf_op jit(solution)/shard_map/ppermute | solution.py:935
  45.1 9.3 %collective-permute-start.3 = (bf16[4,24,1536]{2,1,0:T(8,128)(2,1)}, bf16[4,24,1536]{2,1,0:T(8,128)(2,1)}, u32[]{:S(2)}, u32[]{:S(2)}) collective-permute-start(bf16[4,24,1536]{2,1,0:T(8,128)(2,1)} %slice.500), channel_id=1, source_target_pairs={{0,8},{8,0},{1,9},{9,1},{2,10},{10,2},{3,11},{11,3},{4,12},{12,4},... | collective-permute-start | bytes 884744 | tf_op jit(solution)/shard_map/ppermute | solution.py:935
  63.3 17.4 %collective-permute-start.9 = (bf16[2,4,24,1664]{3,2,1,0:T(8,128)(2,1)S(1)}, bf16[2,4,24,1664]{3,2,1,0:T(8,128)(2,1)S(1)}, u32[]{:S(2)}, u32[]{:S(2)}) collective-permute-start(bf16[2,4,24,1664]{3,2,1,0:T(8,128)(2,1)S(1)} %copy-done.21), channel_id=1, source_target_pairs={{0,8},{8,0},{1,9},{9,1},{2,10},{10,2},{3,11},{11,3},{4,12},{12,4},... | collective-permute-start | bytes 1916936 | tf_op jit(solution)/shard_map/ppermute | solution.py:935
  63.9 15.2 %collective-permute-start.8 = (bf16[2,4,24,1536]{3,2,1,0:T(8,128)(2,1)S(1)}, bf16[2,4,24,1536]{3,2,1,0:T(8,128)(2,1)S(1)}, u32[]{:S(2)}, u32[]{:S(2)}) collective-permute-start(bf16[2,4,24,1536]{3,2,1,0:T(8,128)(2,1)S(1)} %copy-done.23), channel_id=1, source_target_pairs={{0,16},{16,0},{1,17},{17,1},{2,18},{18,2},{3,19},{19,3},{4,20},{20... | collective-permute-start | bytes 1769480 | tf_op jit(solution)/shard_map/ppermute | solution.py:935
  72.2 17.5 %collective-permute-start.11 = (bf16[4,24,3072]{2,1,0:T(8,128)(2,1)S(1)}, bf16[4,24,3072]{2,1,0:T(8,128)(2,1)S(1)}, u32[]{:S(2)}, u32[]{:S(2)}) collective-permute-start(bf16[4,24,3072]{2,1,0:T(8,128)(2,1)S(1)} %get-tuple-element.215), channel_id=1, source_target_pairs={{0,8},{8,0},{1,9},{9,1},{2,10},{10,2},{3,11},{11,3},{4,12},{12,4},... | collective-permute-start | bytes 1769480 | tf_op jit(solution)/shard_map/ppermute | solution.py:935
  74.2 15.5 %collective-permute-start.12 = (bf16[4,24,3072]{2,1,0:T(8,128)(2,1)S(1)}, bf16[4,24,3072]{2,1,0:T(8,128)(2,1)S(1)}, u32[]{:S(2)}, u32[]{:S(2)}) collective-permute-start(bf16[4,24,3072]{2,1,0:T(8,128)(2,1)S(1)} %get-tuple-element.221), channel_id=1, source_target_pairs={{0,16},{16,0},{1,17},{17,1},{2,18},{18,2},{3,19},{19,3},{4,20},{20... | collective-permute-start | bytes 1769480 | tf_op jit(solution)/shard_map/ppermute | solution.py:935
  81.0 8.7 %collective-permute-start.10 = (bf16[2,2,4,24,3200]{4,3,2,1,0:T(8,128)(2,1)S(1)}, bf16[2,2,4,24,3200]{4,3,2,1,0:T(8,128)(2,1)S(1)}, u32[]{:S(2)}, u32[]{:S(2)}) collective-permute-start(bf16[2,2,4,24,3200]{4,3,2,1,0:T(8,128)(2,1)S(1)} %pad_maximum_fusion.1), channel_id=1, source_target_pairs={{0,1},{1,0},{2,3},{3,2},{4,5},{5,4},{6,7},{7,6},{8,9},{9,8},{10,11... | collective-permute-start | bytes 7372808 | tf_op jit(solution)/shard_map/ppermute | solution.py:935
  91.0 35.1 %collective-permute-start.13 = (bf16[2,4,24,3072]{3,2,1,0:T(8,128)(2,1)}, bf16[2,4,24,3072]{3,2,1,0:T(8,128)(2,1)}, u32[]{:S(2)}, u32[]{:S(2)}) collective-permute-start(bf16[2,4,24,3072]{3,2,1,0:T(8,128)(2,1)} %bitcast_dynamic-update-slice_fusion.10), channel_id=1, source_target_pairs={{0,16},{16,0},{1,17},{17,1},{2,18},{18,2},{3,19},{19,3},{4,20},{20... | collective-permute-start | bytes 3538952 | tf_op jit(solution)/shard_map/ppermute | solution.py:935
  91.6 34.4 %collective-permute-start.14 = (bf16[2,4,24,3072]{3,2,1,0:T(8,128)(2,1)S(1)}, bf16[2,4,24,3072]{3,2,1,0:T(8,128)(2,1)}, u32[]{:S(2)}, u32[]{:S(2)}) collective-permute-start(bf16[2,4,24,3072]{3,2,1,0:T(8,128)(2,1)S(1)} %bitcast_dynamic-update-slice_fusion.8), channel_id=1, source_target_pairs={{0,8},{8,0},{1,9},{9,1},{2,10},{10,2},{3,11},{11,3},{4,12},{12,4},... | collective-permute-start | bytes 3538952 | tf_op jit(solution)/shard_map/ppermute | solution.py:935
  126.0 102.4 %copy-start.8 = (bf16[256,768]{1,0:T(8,128)(2,1)}, bf16[256,768]{1,0:T(8,128)(2,1)S(1)}, u32[]{:S(2)}) copy-start(bf16[256,768]{1,0:T(8,128)(2,1)S(1)} %get-tuple-element.270.gvalue_ref) | copy-start | bytes 1179652
  126.0 102.4 %copy-start.10 = (bf16[768,256]{1,0:T(8,128)(2,1)}, bf16[768,256]{1,0:T(8,128)(2,1)S(1)}, u32[]{:S(2)}) copy-start(bf16[768,256]{1,0:T(8,128)(2,1)S(1)} %get-tuple-element.273.pooled_turned) | copy-start | bytes 1179652
  132.3 7.9 %collective-permute-start.15 = (bf16[2,2,4,24,6144]{4,3,2,1,0:T(8,128)(2,1)S(1)}, bf16[2,2,4,24,6144]{4,3,2,1,0:T(8,128)(2,1)S(1)}, u32[]{:S(2)}, u32[]{:S(2)}) collective-permute-start(bf16[2,2,4,24,6144]{4,3,2,1,0:T(8,128)(2,1)S(1)} %pad_maximum_fusion), channel_id=1, source_target_pairs={{0,1},{1,0},{2,3},{3,2},{4,5},{5,4},{6,7},{7,6},{8,9},{9,8},{10,11... | collective-permute-start | bytes 14155784 | tf_op jit(solution)/shard_map/ppermute | solution.py:935
  189.8 27.8 %collective-permute-start.16 = (bf16[2,384,2048]{2,1,0:T(8,128)(2,1)}, bf16[2,384,2048]{2,1,0:T(8,128)(2,1)}, u32[]{:S(2)}, u32[]{:S(2)}) collective-permute-start(bf16[2,384,2048]{2,1,0:T(8,128)(2,1)} %get-tuple-element.262), channel_id=1, source_target_pairs={{0,1},{1,0},{2,3},{3,2},{4,5},{5,4},{6,7},{7,6},{8,9},{9,8},{10,11... | collective-permute-start | bytes 9437192 | tf_op jit(solution)/shard_map/ppermute | solution.py:984
  190.0 27.6 %collective-permute-start.17 = (bf16[2,384,1024]{2,1,0:T(8,128)(2,1)}, bf16[2,384,1024]{2,1,0:T(8,128)(2,1)S(1)}, u32[]{:S(2)}, u32[]{:S(2)}) collective-permute-start(bf16[2,384,1024]{2,1,0:T(8,128)(2,1)} %get-tuple-element.263), channel_id=1, source_target_pairs={{0,1},{1,0},{2,3},{3,2},{4,5},{5,4},{6,7},{7,6},{8,9},{9,8},{10,11... | collective-permute-start | bytes 4718600 | tf_op jit(solution)/shard_map/ppermute | solution.py:984
  190.4 27.2 %collective-permute-start.18 = (bf16[2,384,384]{2,1,0:T(8,128)(2,1)}, bf16[2,384,384]{2,1,0:T(8,128)(2,1)S(1)}, u32[]{:S(2)}, u32[]{:S(2)}) collective-permute-start(bf16[2,384,384]{2,1,0:T(8,128)(2,1)} %get-tuple-element.264), channel_id=1, source_target_pairs={{0,1},{1,0},{2,3},{3,2},{4,5},{5,4},{6,7},{7,6},{8,9},{9,8},{10,11... | collective-permute-start | bytes 1769480 | tf_op jit(solution)/shard_map/ppermute | solution.py:984
  192.4 24.6 %copy-start.30 = (bf16[2,384,384]{2,1,0:T(8,128)(2,1)S(1)}, bf16[2,384,384]{2,1,0:T(8,128)(2,1)}, u32[]{:S(2)}) copy-start(bf16[2,384,384]{2,1,0:T(8,128)(2,1)} %get-tuple-element.289) | copy-start | bytes 1769476
  192.4 24.7 %copy-start.17 = (bf16[2,384,2048]{2,1,0:T(8,128)(2,1)S(1)}, bf16[2,384,2048]{2,1,0:T(8,128)(2,1)}, u32[]{:S(2)}) copy-start(bf16[2,384,2048]{2,1,0:T(8,128)(2,1)} %get-tuple-element.256) | copy-start | bytes 9437188
  223.7 31.5 %collective-permute-start.19 = (bf16[1,2,4,24,3456]{4,3,2,1,0:T(8,128)(2,1)S(1)}, bf16[1,2,4,24,3456]{4,3,2,1,0:T(8,128)(2,1)S(1)}, u32[]{:S(2)}, u32[]{:S(2)}) collective-permute-start(bf16[1,2,4,24,3456]{4,3,2,1,0:T(8,128)(2,1)S(1)} %pad_maximum_fusion.4), channel_id=1, source_target_pairs={{0,8},{8,0},{1,9},{9,1},{2,10},{10,2},{3,11},{11,3},{4,12},{12,4},... | collective-permute-start | bytes 3981320 | tf_op jit(solution)/shard_map/ppermute | solution.py:935
  225.1 31.2 %collective-permute-start.20 = (bf16[1,2,4,24,3456]{4,3,2,1,0:T(8,128)(2,1)S(1)}, bf16[1,2,4,24,3456]{4,3,2,1,0:T(8,128)(2,1)}, u32[]{:S(2)}, u32[]{:S(2)}) collective-permute-start(bf16[1,2,4,24,3456]{4,3,2,1,0:T(8,128)(2,1)S(1)} %pad_maximum_fusion.5), channel_id=1, source_target_pairs={{0,16},{16,0},{1,17},{17,1},{2,18},{18,2},{3,19},{19,3},{4,20},{20... | collective-permute-start | bytes 3981320 | tf_op jit(solution)/shard_map/ppermute | solution.py:935
  257.8 30.8 %collective-permute-start.21 = (bf16[1,4,24,3456]{3,2,0,1:T(8,128)(2,1)S(1)}, bf16[1,4,24,3456]{3,2,0,1:T(8,128)(2,1)S(1)}, u32[]{:S(2)}, u32[]{:S(2)}) collective-permute-start(bf16[1,4,24,3456]{3,2,0,1:T(8,128)(2,1)S(1)} %fusion.45), channel_id=1, source_target_pairs={{0,16},{16,0},{1,17},{17,1},{2,18},{18,2},{3,19},{19,3},{4,20},{20... | collective-permute-start | bytes 1990664 | tf_op jit(solution)/shard_map/ppermute | solution.py:935
  259.3 29.3 %collective-permute-start.22 = (bf16[1,4,24,3456]{3,2,0,1:T(8,128)(2,1)S(1)}, bf16[1,4,24,3456]{3,2,0,1:T(8,128)(2,1)S(1)}, u32[]{:S(2)}, u32[]{:S(2)}) collective-permute-start(bf16[1,4,24,3456]{3,2,0,1:T(8,128)(2,1)S(1)} %fusion.46), channel_id=1, source_target_pairs={{0,8},{8,0},{1,9},{9,1},{2,10},{10,2},{3,11},{11,3},{4,12},{12,4},... | collective-permute-start | bytes 1990664 | tf_op jit(solution)/shard_map/ppermute | solution.py:935
  260.0 28.5 %collective-permute-start.23 = (bf16[6,384,128]{2,1,0:T(8,128)(2,1)S(1)}, bf16[6,384,128]{2,1,0:T(8,128)(2,1)S(1)}, u32[]{:S(2)}, u32[]{:S(2)}) collective-permute-start(bf16[6,384,128]{2,1,0:T(8,128)(2,1)S(1)} %get-tuple-element.318), channel_id=1, source_target_pairs={{0,1},{1,0},{2,3},{3,2},{4,5},{5,4},{6,7},{7,6},{8,9},{9,8},{10,11... | collective-permute-start | bytes 1769480 | tf_op jit(solution)/shard_map/ppermute | solution.py:984
  260.0 28.5 %collective-permute-start.24 = (bf16[6,384,128]{2,1,0:T(8,128)(2,1)S(1)}, bf16[6,384,128]{2,1,0:T(8,128)(2,1)S(1)}, u32[]{:S(2)}, u32[]{:S(2)}) collective-permute-start(bf16[6,384,128]{2,1,0:T(8,128)(2,1)S(1)} %get-tuple-element.319), channel_id=1, source_target_pairs={{0,1},{1,0},{2,3},{3,2},{4,5},{5,4},{6,7},{7,6},{8,9},{9,8},{10,11... | collective-permute-start | bytes 1769480 | tf_op jit(solution)/shard_map/ppermute | solution.py:984
  293.3 17.3 %collective-permute-start.25 = (bf16[8,384,128]{2,1,0:T(8,128)(2,1)S(1)}, bf16[8,384,128]{2,1,0:T(8,128)(2,1)}, u32[]{:S(2)}, u32[]{:S(2)}) collective-permute-start(bf16[8,384,128]{2,1,0:T(8,128)(2,1)S(1)} %get-tuple-element.339), channel_id=1, source_target_pairs={{0,1},{1,0},{2,3},{3,2},{4,5},{5,4},{6,7},{7,6},{8,9},{9,8},{10,11... | collective-permute-start | bytes 2359304 | tf_op jit(solution)/shard_map/ppermute | solution.py:984
  296.5 15.7 %collective-permute-start.26 = (bf16[192,768]{1,0:T(8,128)(2,1)}, bf16[192,768]{1,0:T(8,128)(2,1)S(1)}, u32[]{:S(2)}, u32[]{:S(2)}) collective-permute-start(bf16[192,768]{1,0:T(8,128)(2,1)} %get-tuple-element.389), channel_id=1, source_target_pairs={{0,8},{8,16},{16,24},{24,0},{1,9},{9,17},{17,25},{25,1},{2,10},{10... | collective-permute-start | bytes 884744 | tf_op jit(solution)/shard_map/ppermute | solution.py:1192
  297.7 15.7 %collective-permute-start.27 = (bf16[192,768]{1,0:T(8,128)(2,1)}, bf16[192,768]{1,0:T(8,128)(2,1)}, u32[]{:S(2)}, u32[]{:S(2)}) collective-permute-start(bf16[192,768]{1,0:T(8,128)(2,1)} %get-tuple-element.388), channel_id=1, source_target_pairs={{0,16},{8,24},{16,0},{24,8},{1,17},{9,25},{17,1},{25,9},{2,18},{10... | collective-permute-start | bytes 884744 | tf_op jit(solution)/shard_map/ppermute | solution.py:1192
  298.3 15.1 %collective-permute-start.28 = (bf16[192,768]{1,0:T(8,128)(2,1)}, bf16[192,768]{1,0:T(8,128)(2,1)S(1)}, u32[]{:S(2)}, u32[]{:S(2)}) collective-permute-start(bf16[192,768]{1,0:T(8,128)(2,1)} %get-tuple-element.387), channel_id=1, source_target_pairs={{0,24},{8,0},{16,8},{24,16},{1,25},{9,1},{17,9},{25,17},{2,26},{10... | collective-permute-start | bytes 884744 | tf_op jit(solution)/shard_map/ppermute | solution.py:1192
  300.0 36.7 %all-to-all-start.1 = ((bf16[1,4,24,6912]{3,2,0,1:T(8,128)(2,1)}), bf16[1,4,24,6912]{3,2,0,1:T(8,128)(2,1)S(1)}, u32[]{:S(2)}, u32[]{:S(2)}) async-start(bf16[1,4,24,6912]{3,2,0,1:T(8,128)(2,1)} %pad_maximum_fusion.7), calls=%async_computation.1 | async-start | bytes 2654208 | tf_op jit(solution)/shard_map/all_to_all | solution.py:958
  313.4 13.2 %collective-permute-start.29 = (bf16[10,2,4,24,128]{4,3,0,2,1:T(8,128)(2,1)S(1)}, bf16[10,2,4,24,128]{4,3,0,2,1:T(8,128)(2,1)S(1)}, u32[]{:S(2)}, u32[]{:S(2)}) collective-permute-start(bf16[10,2,4,24,128]{4,3,0,2,1:T(8,128)(2,1)S(1)} %pad_maximum_fusion.9), channel_id=1, source_target_pairs={{0,8},{8,0},{1,9},{9,1},{2,10},{10,2},{3,11},{11,3},{4,12},{12,4},... | collective-permute-start | bytes 1474568 | tf_op jit(solution)/shard_map/ppermute | solution.py:935
  314.3 12.4 %collective-permute-start.30 = (bf16[10,2,4,24,128]{4,3,0,2,1:T(8,128)(2,1)S(1)}, bf16[10,2,4,24,128]{4,3,0,2,1:T(8,128)(2,1)S(1)}, u32[]{:S(2)}, u32[]{:S(2)}) collective-permute-start(bf16[10,2,4,24,128]{4,3,0,2,1:T(8,128)(2,1)S(1)} %pad_maximum_fusion.10), channel_id=1, source_target_pairs={{0,16},{16,0},{1,17},{17,1},{2,18},{18,2},{3,19},{19,3},{4,20},{20... | collective-permute-start | bytes 1474568 | tf_op jit(solution)/shard_map/ppermute | solution.py:935
  316.0 13.3 %copy-start.37 = (s32[1,1024]{1,0:T(1,128)S(1)}, s32[1,1024]{1,0:T(1,128)}, u32[]{:S(2)}) copy-start(s32[1,1024]{1,0:T(1,128)} %param.18) | copy-start | bytes 12292
  326.9 9.7 %collective-permute-start.31 = (bf16[10,4,24,128]{3,2,0,1:T(8,128)(2,1)S(1)}, bf16[10,4,24,128]{3,2,0,1:T(8,128)(2,1)S(1)}, u32[]{:S(2)}, u32[]{:S(2)}) collective-permute-start(bf16[10,4,24,128]{3,2,0,1:T(8,128)(2,1)S(1)} %get-tuple-element.351), channel_id=1, source_target_pairs={{0,16},{16,0},{1,17},{17,1},{2,18},{18,2},{3,19},{19,3},{4,20},{20... | collective-permute-start | bytes 737288 | tf_op jit(solution)/shard_map/ppermute | solution.py:935
  328.1 8.5 %collective-permute-start.32 = (bf16[10,4,24,128]{3,2,0,1:T(8,128)(2,1)S(1)}, bf16[10,4,24,128]{3,2,0,1:T(8,128)(2,1)S(1)}, u32[]{:S(2)}, u32[]{:S(2)}) collective-permute-start(bf16[10,4,24,128]{3,2,0,1:T(8,128)(2,1)S(1)} %get-tuple-element.352), channel_id=1, source_target_pairs={{0,8},{8,0},{1,9},{9,1},{2,10},{10,2},{3,11},{11,3},{4,12},{12,4},... | collective-permute-start | bytes 737288 | tf_op jit(solution)/shard_map/ppermute | solution.py:935
  337.8 14.2 %copy-start.1 = (f32[12,32]{1,0:T(8,128)S(1)}, f32[12,32]{1,0:T(8,128)}, u32[]{:S(2)}) copy-start(f32[12,32]{1,0:T(8,128)} %param.27) | copy-start | bytes 4612
  338.0 8.2 %collective-permute-start.33 = (bf16[20,24,128]{2,1,0:T(8,128)(2,1)S(1)}, bf16[20,24,128]{2,1,0:T(8,128)(2,1)S(1)}, u32[]{:S(2)}, u32[]{:S(2)}) collective-permute-start(bf16[20,24,128]{2,1,0:T(8,128)(2,1)S(1)} %pad_maximum_fusion.12), channel_id=1, source_target_pairs={{0,2},{2,4},{4,6},{6,0},{1,3},{3,5},{5,7},{7,1},{8,10},{10,12},{12... | collective-permute-start | bytes 368648 | tf_op jit(solution)/shard_map/ppermute | solution.py:935
  341.1 8.7 %collective-permute-start.34 = (bf16[20,24,128]{2,1,0:T(8,128)(2,1)S(1)}, bf16[20,24,128]{2,1,0:T(8,128)(2,1)S(1)}, u32[]{:S(2)}, u32[]{:S(2)}) collective-permute-start(bf16[20,24,128]{2,1,0:T(8,128)(2,1)S(1)} %pad_maximum_fusion.13), channel_id=1, source_target_pairs={{0,4},{2,6},{4,0},{6,2},{1,5},{3,7},{5,1},{7,3},{8,12},{10,14},{12... | collective-permute-start | bytes 368648 | tf_op jit(solution)/shard_map/ppermute | solution.py:935
  341.1 8.7 %collective-permute-start.35 = (bf16[20,24,128]{2,1,0:T(8,128)(2,1)S(1)}, bf16[20,24,128]{2,1,0:T(8,128)(2,1)S(1)}, u32[]{:S(2)}, u32[]{:S(2)}) collective-permute-start(bf16[20,24,128]{2,1,0:T(8,128)(2,1)S(1)} %pad_maximum_fusion.14), channel_id=1, source_target_pairs={{0,6},{2,0},{4,2},{6,4},{1,7},{3,1},{5,3},{7,5},{8,14},{10,8},{12,... | collective-permute-start | bytes 368648 | tf_op jit(solution)/shard_map/ppermute | solution.py:935
  343.7 7.7 %copy-start.48 = (f32[1,64,768]{2,1,0:T(8,128)}, f32[1,64,768]{2,1,0:T(8,128)S(1)}, u32[]{:S(2)}) copy-start(f32[1,64,768]{2,1,0:T(8,128)S(1)} %constant_dynamic-update-slice_fusion.18) | copy-start | bytes 589828
  (53 other events, 124.0 us)

commit v6 on v5

--- a/solution.py
+++ b/solution.py
@@ -453,7 +453,7 @@
             jax.ShapeDtypeStruct((width, slots), bf16),
         ],
         scratch_shapes=[pltpu.VMEM((slots, width), bf16), pltpu.VMEM((128, rows + 256), bf16), pltpu.VMEM((128, slots), bf16)],
-        compiler_params=pltpu.CompilerParams(vmem_limit_bytes=48 << 20),
+        compiler_params=pltpu.CompilerParams(vmem_limit_bytes=52 << 20),
         cost_estimate=pl.CostEstimate(
             flops=30 * rows * (384 + slots) * width, bytes_accessed=24 << 20, transcendentals=0
         ),
@@ -531,7 +531,7 @@
             pltpu.VMEM((256, 256), f32),
             pltpu.VMEM((slots, 128), f32),
         ],
-        compiler_params=pltpu.CompilerParams(vmem_limit_bytes=48 << 20),
+        compiler_params=pltpu.CompilerParams(vmem_limit_bytes=52 << 20),
         cost_estimate=pl.CostEstimate(
             flops=60 * rows * (384 + slots) * 128 * count, bytes_accessed=count << 22, transcendentals=0
         ),

time: 357 us -> 353 us (0.989)
  local copies, waits for them, and re-layouts: 59.5 us -> 55 us
    unnamed x135 -> x131, local copies, waits for them, and re-layouts: 7.58 us -> 8.95 us
where the time goes in v6:
time: 353 us; the launch traced here: 349 us
  Pallas kernels  169 us (48%)
  local copies, waits for them, and re-layouts  55 us (16%)
  starting transfers between devices  47.8 us (14%)
  waiting for transfers between devices  37.9 us (11%)
  other arithmetic  28.2 us (8%)
  matrix products  8.06 us (2%)
    pallas_call x3, Pallas kernels, attention_backward(): pl.pallas_call(functools.partial(attend_backward, first + count == pairs,...  78.8 us
    pallas_call x1, Pallas kernels, feed_forward_both(): pl.pallas_call(feed_forward, grid=(tiles,), in_specs=[fixed(rows, width),...  47.5 us
    ppermute x27, waiting for transfers between devices, send_all(): lax.ppermute(piece, axis, ring(size, hop + 1))  35.9 us
    ppermute x27, starting transfers between devices, send_all(): lax.ppermute(piece, axis, ring(size, hop + 1))  34.6 us
    pallas_call x1, Pallas kernels, attention_forward(): pl.pallas_call(attend_forward, grid=(pairs,), in_specs=[fixed(rows + 256,...  31.1 us
    dynamic_update_slice x15, local copies, waits for them, and re-layouts, place_stage(): lax.dynamic_update_index_in_dim(out, piece, (me - hop - 1) % size, dim)  11.1 us
    convert_element_type x24, other arithmetic, split_stage(): add_up([pick(part, (me + hop) % size, dim) for part in piece]).astype(bf16)  9.59 us
    unnamed x131, local copies, waits for them, and re-layouts  8.95 us
  transfers between devices with their start and end apart: 38, of which 11 were waited for; matrix products, arithmetic and copies ran while one was open for 17% of the time, Pallas kernels for 34%

profile of v6, /device:TPU:0, one launch (start us, length us, event | category | flops | bytes accessed | tf_op | source)
XLA Modules:
  0.0 348.7 jit_solution(5854687336659916344)
XLA Ops:
  2.1 1.9 pack_weights.1
  3.9 3.0 collective-permute-start
  7.0 2.6 collective-permute-start.1
  9.6 1.3 collective-permute-start.2
  13.6 1.3 pad_add_fusion.marks_ref
  14.9 3.7 %pack_tokens.1 = bf16[4,208,768]{2,1,0:T(8,128)(2,1)} custom-call(bf16[1024,768]{1,0:T(8,128)(2,1)} %bitcast.354, f32[1024,1]{1,0:T(8,128)} %copy.165.keep_ref, s32[16,128]{1,0:T(8,128)} %pad_add_fusion.marks_ref), custom_call_target="tpu_custom_call" | custom-call | tf_op jit(solution)/shard_map/pack_tokens/pallas_call | solution.py:620
  18.6 3.8 %all-to-all-start = ((bf16[4,208,768]{2,1,0:T(8,128)(2,1)}), bf16[4,208,768]{2,1,0:T(8,128)(2,1)S(1)}, u32[]{:S(2)}, u32[]{:S(2)}) async-start(bf16[4,208,768]{2,1,0:T(8,128)(2,1)} %pack_tokens.1), calls=%async_computation | async-start | bytes 2555904 | tf_op jit(solution)/shard_map/all_to_all | solution.py:1106
  32.3 2.8 collective-permute-start.7
  35.8 1.6 bitcast_dynamic-update-slice_fusion.23
  37.4 1.6 bitcast_dynamic-update-slice_fusion.22
  39.9 1.7 slice.500
  43.7 2.0 collective-permute-start.4
  45.7 1.5 collective-permute-start.3
  51.2 1.7 bitcast_dynamic-update-slice_fusion.17
  54.5 1.5 pad_maximum_fusion.2.source_ref
  56.0 1.7 bitcast_dynamic-update-slice_fusion.14
  57.8 1.7 bitcast_dynamic-update-slice_fusion.16
  64.5 7.8 %convolution_convert_fusion.kglobal_ref = bf16[2048,768]{1,0:T(8,128)(2,1)} fusion(s32[264]{0:T(512)S(1)} %get-tuple-element.520, s32[264]{0:T(512)S(1)} %copy-done.49, s32[264]{0:T(512)S(1)} %copy-done.45, s32[264]{0:T(512)S(1)} %copy-done.48, s32[264]{0:T(512)S(1)} %copy-done.50, s32[2048]{0:T(1024)S(1)} %copy-done.33, s32[2048]{0:T(1024)S(1)} %copy-done.36, ...), kind=kOutput, calls=%fused_computation.2 | convolution fusion | flops 852793344 | bytes 3378108 | tf_op jit(solution)/shard_map/dot_general | solution.py:893
  73.5 2.0 collective-permute-start.11
  75.5 1.5 collective-permute-start.12
  78.8 2.4 collective-permute-done.9
  82.6 7.5 %collective-permute-done.11 = bf16[4,24,3072]{2,1,0:T(8,128)(2,1)S(1)} collective-permute-done((bf16[4,24,3072]{2,1,0:T(8,128)(2,1)S(1)}, bf16[4,24,3072]{2,1,0:T(8,128)(2,1)S(1)}, u32[]{:S(2)}, u32[]{:S(2)}) %collective-permute-start.11) | collective-permute-done | bytes 589856 | tf_op jit(solution)/shard_map/ppermute | solution.py:935
  93.0 31.1 %attend_forward.1 = (f32[6,256,256]{2,1,0:T(8,128)}, bf16[1024,768]{1,0:T(8,128)(2,1)}, f32[6,8,256]{2,1,0:T(8,128)S(1)}, bf16[1024,768]{1,0:T(8,128)(2,1)}, bf1...) custom-call(bf16[1280,768]{1,0:T(8,128)(2,1)} %pad_maximum_fusion.2., ...), custom_call_target="tpu_custom_call" | custom-call | flops 15099494400 | bytes 25165824 | tf_op jit(solution)/shard_map/attend_forward/pallas_call | solution.py:412
  125.3 2.2 copy-done.12
  128.1 7.3 %collective-permute-done.15 = bf16[2,2,4,24,6144]{4,3,2,1,0:T(8,128)(2,1)S(1)} collective-permute-done((bf16[2,2,4,24,6144]{4,3,2,1,0:T(8,128)(2,1)S(1)}, bf16[2,2,4,24,6144]{4,3,2,1,0:T(8,128)(2,1)S(1)}, u32[]{:S(2)}, u32[]{:S(2)}) %collective-permute-start.15) | collective-permute-done | bytes 4718624 | tf_op jit(solution)/shard_map/ppermute | solution.py:935
  135.4 2.1 copy-done.55
  137.5 47.5 %feed_forward.1 = (bf16[1024,768]{1,0:T(8,128)(2,1)}, f32[1024,768]{1,0:T(8,128)}, bf16[1024,768]{1,0:T(8,128)(2,1)}, f32[8,768]{1,0:T(8,128)}, bf16[2,384,384]{...) custom-call(bf16[1024,768]{1,0:T(8,128)(2,1)} %bitcast.355, ...), custom_call_target="tpu_custom_call" | custom-call | flops 32212254720 | bytes 41943040 | tf_op jit(solution)/shard_map/feed_forward/pallas_call | solution.py:730
  185.7 1.5 fusion.126
  187.3 25.1 %attend_backward.3 = (bf16[6,384,128]{2,1,0:T(8,128)(2,1)}, bf16[6,384,128]{2,1,0:T(8,128)(2,1)}, bf16[1280,768]{1,0:T(8,128)(2,1)}, bf16[256,768]{1,0:T(8,128)(...) custom-call(bf16[1024,768]{1,0:T(8,128)(2,1)} %get-tuple-element.265.query_ref, ...), custom_call_target="tpu_custom_call" | custom-call | flops 10066329600 | bytes 8388608 | tf_op jit(solution)/shard_map/attend_backward/pallas_call | solution.py:475
  214.0 2.3 fusion.125
  221.0 1.5 collective-permute-start.20
  224.2 26.2 %attend_backward.4 = (bf16[6,384,128]{2,1,0:T(8,128)(2,1)}, bf16[6,384,128]{2,1,0:T(8,128)(2,1)}, bf16[1280,768]{1,0:T(8,128)(2,1)}, bf16[256,768]{1,0:T(8,128)(...) custom-call(bf16[1024,768]{1,0:T(8,128)(2,1)} %get-tuple-element.265.query_ref, ...), custom_call_target="tpu_custom_call" | custom-call | flops 10066329600 | bytes 8388608 | tf_op jit(solution)/shard_map/attend_backward/pallas_call | solution.py:475
  252.2 1.4 fusion.46
  253.7 1.5 collective-permute-start.21
  258.1 27.5 %attend_backward.5 = (bf16[8,384,128]{2,1,0:T(8,128)(2,1)}, bf16[8,384,128]{2,1,0:T(8,128)(2,1)}, bf16[1280,768]{1,0:T(8,128)(2,1)}, bf16[4,192,768]{2,1,0:T(8,1...) custom-call(bf16[1024,768]{1,0:T(8,128)(2,1)} %get-tuple-element.265.query_ref, ...), custom_call_target="tpu_custom_call" | custom-call | flops 10066329600 | bytes 8388608 | tf_op jit(solution)/shard_map/attend_backward/pallas_call | solution.py:475
  287.4 1.4 fusion.39
  293.5 1.3 collective-permute-start.26
  295.3 1.9 collective-permute-start.28
  297.2 4.3 %all-to-all-start.1 = ((bf16[1,4,24,6912]{3,2,0,1:T(8,128)(2,1)}), bf16[1,4,24,6912]{3,2,0,1:T(8,128)(2,1)S(1)}, u32[]{:S(2)}, u32[]{:S(2)}) async-start(bf16[1,4,24,6912]{3,2,0,1:T(8,128)(2,1)} %pad_maximum_fusion.7), calls=%async_computation.1 | async-start | bytes 2654208 | tf_op jit(solution)/shard_map/all_to_all | solution.py:958
  308.2 1.9 collective-permute-done.27.refs_2_
  311.3 1.2 collective-permute-start.30
  312.8 10.6 %collective-permute-done.29 = bf16[10,2,4,24,128]{4,3,0,2,1:T(8,128)(2,1)S(1)} collective-permute-done((bf16[10,2,4,24,128]{4,3,0,2,1:T(8,128)(2,1)S(1)}, bf16[10,2,4,24,128]{4,3,0,2,1:T(8,128)(2,1)S(1)}, u32[]{:S(2)}, u32[]{:S(2)}) %collective-permute-start.29) | collective-permute-done | bytes 491552 | tf_op jit(solution)/shard_map/ppermute | solution.py:935
  324.6 1.4 collective-permute-start.32
  327.0 6.3 %source_gradient.1 = f32[1024,768]{1,0:T(8,128)} custom-call(bf16[1024,768]{1,0:T(8,128)(2,1)} %bitcast.356, f32[1024,1]{1,0:T(8,128)} %copy.214.keep_ref, f32[1024,768]{1,0:T(8,128)} %get-tuple-element.353.middle_grad_ref, f32[8,768]{1,0:T(8,128)} %copy-done.2, bf16[1280,768]{1,0:T(8,128)(2,1)} %get-tuple-element.354.upper_ref.lower_ref, ...), custom_call_target="tpu_custom_call" | custom-call | flops 15728640 | bytes 14680064 | tf_op jit(solution)/shard_map/source_gradient/pallas_call | solution.py:828
  334.7 2.8 collective-permute-start.33
  337.5 2.4 collective-permute-start.35
  340.7 2.1 collective-permute-done.33
  342.8 3.5 %collective-permute-done.34 = bf16[20,24,128]{2,1,0:T(8,128)(2,1)S(1)} collective-permute-done((bf16[20,24,128]{2,1,0:T(8,128)(2,1)S(1)}, bf16[20,24,128]{2,1,0:T(8,128)(2,1)S(1)}, u32[]{:S(2)}, u32[]{:S(2)}) %collective-permute-start.34) | collective-permute-done | bytes 122912 | tf_op jit(solution)/shard_map/ppermute | solution.py:935
  (352 shorter events, 71.2 us)
Async XLA Ops:
  0.6 53.5 %copy-start = (f32[12,32]{1,0:T(8,128)S(1)}, f32[12,32]{1,0:T(8,128)}, u32[]{:S(2)}) copy-start(f32[12,32]{1,0:T(8,128)} %param.27) | copy-start | bytes 4612
  3.9 28.3 %collective-permute-start = (bf16[24,3200]{1,0:T(8,128)(2,1)}, bf16[24,3200]{1,0:T(8,128)(2,1)S(1)}, u32[]{:S(2)}, u32[]{:S(2)}) collective-permute-start(bf16[24,3200]{1,0:T(8,128)(2,1)} %get-tuple-element.194), channel_id=1, source_target_pairs={{0,2},{2,4},{4,6},{6,0},{1,3},{3,5},{5,7},{7,1},{8,10},{10,12},{12... | collective-permute-start | bytes 460808 | tf_op jit(solution)/shard_map/ppermute | solution.py:935
  7.0 28.1 %collective-permute-start.1 = (bf16[24,3200]{1,0:T(8,128)(2,1)}, bf16[24,3200]{1,0:T(8,128)(2,1)}, u32[]{:S(2)}, u32[]{:S(2)}) collective-permute-start(bf16[24,3200]{1,0:T(8,128)(2,1)} %get-tuple-element.194), channel_id=1, source_target_pairs={{0,4},{2,6},{4,0},{6,2},{1,5},{3,7},{5,1},{7,3},{8,12},{10,14},{12... | collective-permute-start | bytes 460808 | tf_op jit(solution)/shard_map/ppermute | solution.py:935
  9.6 25.5 %collective-permute-start.2 = (bf16[24,3200]{1,0:T(8,128)(2,1)}, bf16[24,3200]{1,0:T(8,128)(2,1)}, u32[]{:S(2)}, u32[]{:S(2)}) collective-permute-start(bf16[24,3200]{1,0:T(8,128)(2,1)} %get-tuple-element.194), channel_id=1, source_target_pairs={{0,6},{2,0},{4,2},{6,4},{1,7},{3,1},{5,3},{7,5},{8,14},{10,8},{12,... | collective-permute-start | bytes 460808 | tf_op jit(solution)/shard_map/ppermute | solution.py:935
  10.9 45.1 %collective-permute-start.5 = (bf16[24,6144]{1,0:T(8,128)(2,1)}, bf16[24,6144]{1,0:T(8,128)(2,1)}, u32[]{:S(2)}, u32[]{:S(2)}) collective-permute-start(bf16[24,6144]{1,0:T(8,128)(2,1)} %get-tuple-element.193), channel_id=1, source_target_pairs={{0,2},{2,4},{4,6},{6,0},{1,3},{3,5},{5,7},{7,1},{8,10},{10,12},{12... | collective-permute-start | bytes 884744 | tf_op jit(solution)/shard_map/ppermute | solution.py:935
  11.6 44.4 %collective-permute-start.6 = (bf16[24,6144]{1,0:T(8,128)(2,1)}, bf16[24,6144]{1,0:T(8,128)(2,1)}, u32[]{:S(2)}, u32[]{:S(2)}) collective-permute-start(bf16[24,6144]{1,0:T(8,128)(2,1)} %get-tuple-element.193), channel_id=1, source_target_pairs={{0,4},{2,6},{4,0},{6,2},{1,5},{3,7},{5,1},{7,3},{8,12},{10,14},{12... | collective-permute-start | bytes 884744 | tf_op jit(solution)/shard_map/ppermute | solution.py:935
  18.6 9.9 %copy-start.30 = (bf16[24,3200]{1,0:T(8,128)(2,1)S(1)}, bf16[24,3200]{1,0:T(8,128)(2,1)}, u32[]{:S(2)}) copy-start(bf16[24,3200]{1,0:T(8,128)(2,1)} %get-tuple-element.194) | copy-start | bytes 460804
  18.6 23.0 %all-to-all-start = ((bf16[4,208,768]{2,1,0:T(8,128)(2,1)}), bf16[4,208,768]{2,1,0:T(8,128)(2,1)S(1)}, u32[]{:S(2)}, u32[]{:S(2)}) async-start(bf16[4,208,768]{2,1,0:T(8,128)(2,1)} %pack_tokens.1), calls=%async_computation | async-start | bytes 2555904 | tf_op jit(solution)/shard_map/all_to_all | solution.py:1106
  22.5 8.8 %copy-start.38 = (s32[128]{0:T(128)}, s32[128]{0:T(128)S(1)}, u32[]{:S(2)}) copy-start(s32[128]{0:T(128)S(1)} %iota_add_fusion.1) | copy-start | bytes 1540
  32.3 23.7 %collective-permute-start.7 = (bf16[24,6144]{1,0:T(8,128)(2,1)}, bf16[24,6144]{1,0:T(8,128)(2,1)}, u32[]{:S(2)}, u32[]{:S(2)}) collective-permute-start(bf16[24,6144]{1,0:T(8,128)(2,1)} %get-tuple-element.193), channel_id=1, source_target_pairs={{0,6},{2,0},{4,2},{6,4},{1,7},{3,1},{5,3},{7,5},{8,14},{10,8},{12,... | collective-permute-start | bytes 884744 | tf_op jit(solution)/shard_map/ppermute | solution.py:935
  43.4 9.5 %copy-start.39 = (s32[128]{0:T(128)S(1)}, s32[128]{0:T(128)}, u32[]{:S(2)}) copy-start(s32[128]{0:T(128)} %copy-done.38) | copy-start | bytes 1540
  43.5 9.4 %copy-start.53 = (pred[128]{0:T(512)(128)(4,1)S(1)}, pred[128]{0:T(512)(128)(4,1)}, u32[]{:S(2)}) copy-start(pred[128]{0:T(512)(128)(4,1)} %compare_and_fusion.1) | copy-start | bytes 388
  43.7 12.4 %collective-permute-start.4 = (bf16[4,24,1664]{2,1,0:T(8,128)(2,1)S(1)}, bf16[4,24,1664]{2,1,0:T(8,128)(2,1)}, u32[]{:S(2)}, u32[]{:S(2)}) collective-permute-start(bf16[4,24,1664]{2,1,0:T(8,128)(2,1)S(1)} %slice.501), channel_id=1, source_target_pairs={{0,16},{16,0},{1,17},{17,1},{2,18},{18,2},{3,19},{19,3},{4,20},{20... | collective-permute-start | bytes 958472 | tf_op jit(solution)/shard_map/ppermute | solution.py:935
  45.7 10.3 %collective-permute-start.3 = (bf16[4,24,1536]{2,1,0:T(8,128)(2,1)}, bf16[4,24,1536]{2,1,0:T(8,128)(2,1)}, u32[]{:S(2)}, u32[]{:S(2)}) collective-permute-start(bf16[4,24,1536]{2,1,0:T(8,128)(2,1)} %slice.500), channel_id=1, source_target_pairs={{0,8},{8,0},{1,9},{9,1},{2,10},{10,2},{3,11},{11,3},{4,12},{12,4},... | collective-permute-start | bytes 884744 | tf_op jit(solution)/shard_map/ppermute | solution.py:935
  63.5 17.6 %collective-permute-start.9 = (bf16[2,4,24,1664]{3,2,1,0:T(8,128)(2,1)}, bf16[2,4,24,1664]{3,2,1,0:T(8,128)(2,1)S(1)}, u32[]{:S(2)}, u32[]{:S(2)}) collective-permute-start(bf16[2,4,24,1664]{3,2,1,0:T(8,128)(2,1)} %bitcast_dynamic-update-slice_fusion.14), channel_id=1, source_target_pairs={{0,8},{8,0},{1,9},{9,1},{2,10},{10,2},{3,11},{11,3},{4,12},{12,4},... | collective-permute-start | bytes 1916936 | tf_op jit(solution)/shard_map/ppermute | solution.py:935
  64.2 14.6 %collective-permute-start.8 = (bf16[2,4,24,1536]{3,2,1,0:T(8,128)(2,1)}, bf16[2,4,24,1536]{3,2,1,0:T(8,128)(2,1)S(1)}, u32[]{:S(2)}, u32[]{:S(2)}) collective-permute-start(bf16[2,4,24,1536]{3,2,1,0:T(8,128)(2,1)} %bitcast_dynamic-update-slice_fusion.16), channel_id=1, source_target_pairs={{0,16},{16,0},{1,17},{17,1},{2,18},{18,2},{3,19},{19,3},{4,20},{20... | collective-permute-start | bytes 1769480 | tf_op jit(solution)/shard_map/ppermute | solution.py:935
  73.5 16.7 %collective-permute-start.11 = (bf16[4,24,3072]{2,1,0:T(8,128)(2,1)S(1)}, bf16[4,24,3072]{2,1,0:T(8,128)(2,1)S(1)}, u32[]{:S(2)}, u32[]{:S(2)}) collective-permute-start(bf16[4,24,3072]{2,1,0:T(8,128)(2,1)S(1)} %get-tuple-element.215), channel_id=1, source_target_pairs={{0,8},{8,0},{1,9},{9,1},{2,10},{10,2},{3,11},{11,3},{4,12},{12,4},... | collective-permute-start | bytes 1769480 | tf_op jit(solution)/shard_map/ppermute | solution.py:935
  75.5 14.7 %collective-permute-start.12 = (bf16[4,24,3072]{2,1,0:T(8,128)(2,1)S(1)}, bf16[4,24,3072]{2,1,0:T(8,128)(2,1)S(1)}, u32[]{:S(2)}, u32[]{:S(2)}) collective-permute-start(bf16[4,24,3072]{2,1,0:T(8,128)(2,1)S(1)} %get-tuple-element.221), channel_id=1, source_target_pairs={{0,16},{16,0},{1,17},{17,1},{2,18},{18,2},{3,19},{19,3},{4,20},{20... | collective-permute-start | bytes 1769480 | tf_op jit(solution)/shard_map/ppermute | solution.py:935
  81.5 8.7 %collective-permute-start.10 = (bf16[2,2,4,24,3200]{4,3,2,1,0:T(8,128)(2,1)S(1)}, bf16[2,2,4,24,3200]{4,3,2,1,0:T(8,128)(2,1)S(1)}, u32[]{:S(2)}, u32[]{:S(2)}) collective-permute-start(bf16[2,2,4,24,3200]{4,3,2,1,0:T(8,128)(2,1)S(1)} %pad_maximum_fusion.1), channel_id=1, source_target_pairs={{0,1},{1,0},{2,3},{3,2},{4,5},{5,4},{6,7},{7,6},{8,9},{9,8},{10,11... | collective-permute-start | bytes 7372808 | tf_op jit(solution)/shard_map/ppermute | solution.py:935
  90.6 33.5 %collective-permute-start.13 = (bf16[2,4,24,3072]{3,2,1,0:T(8,128)(2,1)S(1)}, bf16[2,4,24,3072]{3,2,1,0:T(8,128)(2,1)S(1)}, u32[]{:S(2)}, u32[]{:S(2)}) collective-permute-start(bf16[2,4,24,3072]{3,2,1,0:T(8,128)(2,1)S(1)} %bitcast_dynamic-update-slice_fusion.10), channel_id=1, source_target_pairs={{0,16},{16,0},{1,17},{17,1},{2,18},{18,2},{3,19},{19,3},{4,20},{20... | collective-permute-start | bytes 3538952 | tf_op jit(solution)/shard_map/ppermute | solution.py:935
  91.2 32.9 %collective-permute-start.14 = (bf16[2,4,24,3072]{3,2,1,0:T(8,128)(2,1)S(1)}, bf16[2,4,24,3072]{3,2,1,0:T(8,128)(2,1)S(1)}, u32[]{:S(2)}, u32[]{:S(2)}) collective-permute-start(bf16[2,4,24,3072]{3,2,1,0:T(8,128)(2,1)S(1)} %bitcast_dynamic-update-slice_fusion.8), channel_id=1, source_target_pairs={{0,8},{8,0},{1,9},{9,1},{2,10},{10,2},{3,11},{11,3},{4,12},{12,4},... | collective-permute-start | bytes 3538952 | tf_op jit(solution)/shard_map/ppermute | solution.py:935
  127.5 7.9 %collective-permute-start.15 = (bf16[2,2,4,24,6144]{4,3,2,1,0:T(8,128)(2,1)S(1)}, bf16[2,2,4,24,6144]{4,3,2,1,0:T(8,128)(2,1)S(1)}, u32[]{:S(2)}, u32[]{:S(2)}) collective-permute-start(bf16[2,2,4,24,6144]{4,3,2,1,0:T(8,128)(2,1)S(1)} %pad_maximum_fusion), channel_id=1, source_target_pairs={{0,1},{1,0},{2,3},{3,2},{4,5},{5,4},{6,7},{7,6},{8,9},{9,8},{10,11... | collective-permute-start | bytes 14155784 | tf_op jit(solution)/shard_map/ppermute | solution.py:935
  185.0 28.2 %collective-permute-start.16 = (bf16[2,384,2048]{2,1,0:T(8,128)(2,1)}, bf16[2,384,2048]{2,1,0:T(8,128)(2,1)}, u32[]{:S(2)}, u32[]{:S(2)}) collective-permute-start(bf16[2,384,2048]{2,1,0:T(8,128)(2,1)} %get-tuple-element.262), channel_id=1, source_target_pairs={{0,1},{1,0},{2,3},{3,2},{4,5},{5,4},{6,7},{7,6},{8,9},{9,8},{10,11... | collective-permute-start | bytes 9437192 | tf_op jit(solution)/shard_map/ppermute | solution.py:984
  185.2 28.0 %collective-permute-start.17 = (bf16[2,384,1024]{2,1,0:T(8,128)(2,1)}, bf16[2,384,1024]{2,1,0:T(8,128)(2,1)S(1)}, u32[]{:S(2)}, u32[]{:S(2)}) collective-permute-start(bf16[2,384,1024]{2,1,0:T(8,128)(2,1)} %get-tuple-element.263), channel_id=1, source_target_pairs={{0,1},{1,0},{2,3},{3,2},{4,5},{5,4},{6,7},{7,6},{8,9},{9,8},{10,11... | collective-permute-start | bytes 4718600 | tf_op jit(solution)/shard_map/ppermute | solution.py:984
  185.6 27.6 %collective-permute-start.18 = (bf16[2,384,384]{2,1,0:T(8,128)(2,1)}, bf16[2,384,384]{2,1,0:T(8,128)(2,1)S(1)}, u32[]{:S(2)}, u32[]{:S(2)}) collective-permute-start(bf16[2,384,384]{2,1,0:T(8,128)(2,1)} %get-tuple-element.264), channel_id=1, source_target_pairs={{0,1},{1,0},{2,3},{3,2},{4,5},{5,4},{6,7},{7,6},{8,9},{9,8},{10,11... | collective-permute-start | bytes 1769480 | tf_op jit(solution)/shard_map/ppermute | solution.py:984
  187.3 25.1 %copy-start.21 = (bf16[2,384,384]{2,1,0:T(8,128)(2,1)S(1)}, bf16[2,384,384]{2,1,0:T(8,128)(2,1)}, u32[]{:S(2)}) copy-start(bf16[2,384,384]{2,1,0:T(8,128)(2,1)} %get-tuple-element.289) | copy-start | bytes 1769476
  187.3 25.2 %copy-start.14 = (bf16[2,384,2048]{2,1,0:T(8,128)(2,1)S(1)}, bf16[2,384,2048]{2,1,0:T(8,128)(2,1)}, u32[]{:S(2)}) copy-start(bf16[2,384,2048]{2,1,0:T(8,128)(2,1)} %get-tuple-element.256) | copy-start | bytes 9437188
  219.8 31.5 %collective-permute-start.19 = (bf16[1,2,4,24,3456]{4,3,2,1,0:T(8,128)(2,1)S(1)}, bf16[1,2,4,24,3456]{4,3,2,1,0:T(8,128)(2,1)S(1)}, u32[]{:S(2)}, u32[]{:S(2)}) collective-permute-start(bf16[1,2,4,24,3456]{4,3,2,1,0:T(8,128)(2,1)S(1)} %pad_maximum_fusion.4), channel_id=1, source_target_pairs={{0,8},{8,0},{1,9},{9,1},{2,10},{10,2},{3,11},{11,3},{4,12},{12,4},... | collective-permute-start | bytes 3981320 | tf_op jit(solution)/shard_map/ppermute | solution.py:935
  221.0 31.2 %collective-permute-start.20 = (bf16[1,2,4,24,3456]{4,3,2,1,0:T(8,128)(2,1)S(1)}, bf16[1,2,4,24,3456]{4,3,2,1,0:T(8,128)(2,1)}, u32[]{:S(2)}, u32[]{:S(2)}) collective-permute-start(bf16[1,2,4,24,3456]{4,3,2,1,0:T(8,128)(2,1)S(1)} %pad_maximum_fusion.5), channel_id=1, source_target_pairs={{0,16},{16,0},{1,17},{17,1},{2,18},{18,2},{3,19},{19,3},{4,20},{20... | collective-permute-start | bytes 3981320 | tf_op jit(solution)/shard_map/ppermute | solution.py:935
  253.7 31.8 %collective-permute-start.21 = (bf16[1,4,24,3456]{3,2,0,1:T(8,128)(2,1)S(1)}, bf16[1,4,24,3456]{3,2,0,1:T(8,128)(2,1)S(1)}, u32[]{:S(2)}, u32[]{:S(2)}) collective-permute-start(bf16[1,4,24,3456]{3,2,0,1:T(8,128)(2,1)S(1)} %fusion.45), channel_id=1, source_target_pairs={{0,16},{16,0},{1,17},{17,1},{2,18},{18,2},{3,19},{19,3},{4,20},{20... | collective-permute-start | bytes 1990664 | tf_op jit(solution)/shard_map/ppermute | solution.py:935
  255.3 30.3 %collective-permute-start.22 = (bf16[1,4,24,3456]{3,2,0,1:T(8,128)(2,1)S(1)}, bf16[1,4,24,3456]{3,2,0,1:T(8,128)(2,1)S(1)}, u32[]{:S(2)}, u32[]{:S(2)}) collective-permute-start(bf16[1,4,24,3456]{3,2,0,1:T(8,128)(2,1)S(1)} %fusion.46), channel_id=1, source_target_pairs={{0,8},{8,0},{1,9},{9,1},{2,10},{10,2},{3,11},{11,3},{4,12},{12,4},... | collective-permute-start | bytes 1990664 | tf_op jit(solution)/shard_map/ppermute | solution.py:935
  256.0 29.5 %collective-permute-start.23 = (bf16[6,384,128]{2,1,0:T(8,128)(2,1)S(1)}, bf16[6,384,128]{2,1,0:T(8,128)(2,1)S(1)}, u32[]{:S(2)}, u32[]{:S(2)}) collective-permute-start(bf16[6,384,128]{2,1,0:T(8,128)(2,1)S(1)} %copy-done.56), channel_id=1, source_target_pairs={{0,1},{1,0},{2,3},{3,2},{4,5},{5,4},{6,7},{7,6},{8,9},{9,8},{10,11... | collective-permute-start | bytes 1769480 | tf_op jit(solution)/shard_map/ppermute | solution.py:984
  256.0 29.5 %collective-permute-start.24 = (bf16[6,384,128]{2,1,0:T(8,128)(2,1)S(1)}, bf16[6,384,128]{2,1,0:T(8,128)(2,1)S(1)}, u32[]{:S(2)}, u32[]{:S(2)}) collective-permute-start(bf16[6,384,128]{2,1,0:T(8,128)(2,1)S(1)} %copy-done.57), channel_id=1, source_target_pairs={{0,1},{1,0},{2,3},{3,2},{4,5},{5,4},{6,7},{7,6},{8,9},{9,8},{10,11... | collective-permute-start | bytes 1769480 | tf_op jit(solution)/shard_map/ppermute | solution.py:984
  290.0 17.0 %collective-permute-start.25 = (bf16[8,384,128]{2,1,0:T(8,128)(2,1)}, bf16[8,384,128]{2,1,0:T(8,128)(2,1)S(1)}, u32[]{:S(2)}, u32[]{:S(2)}) collective-permute-start(bf16[8,384,128]{2,1,0:T(8,128)(2,1)} %get-tuple-element.339), channel_id=1, source_target_pairs={{0,1},{1,0},{2,3},{3,2},{4,5},{5,4},{6,7},{7,6},{8,9},{9,8},{10,11... | collective-permute-start | bytes 2359304 | tf_op jit(solution)/shard_map/ppermute | solution.py:984
  293.5 14.7 %collective-permute-start.26 = (bf16[192,768]{1,0:T(8,128)(2,1)}, bf16[192,768]{1,0:T(8,128)(2,1)S(1)}, u32[]{:S(2)}, u32[]{:S(2)}) collective-permute-start(bf16[192,768]{1,0:T(8,128)(2,1)} %get-tuple-element.389), channel_id=1, source_target_pairs={{0,8},{8,16},{16,24},{24,0},{1,9},{9,17},{17,25},{25,1},{2,10},{10... | collective-permute-start | bytes 884744 | tf_op jit(solution)/shard_map/ppermute | solution.py:1192
  294.8 15.4 %collective-permute-start.27 = (bf16[192,768]{1,0:T(8,128)(2,1)}, bf16[192,768]{1,0:T(8,128)(2,1)}, u32[]{:S(2)}, u32[]{:S(2)}) collective-permute-start(bf16[192,768]{1,0:T(8,128)(2,1)} %get-tuple-element.388), channel_id=1, source_target_pairs={{0,16},{8,24},{16,0},{24,8},{1,17},{9,25},{17,1},{25,9},{2,18},{10... | collective-permute-start | bytes 884744 | tf_op jit(solution)/shard_map/ppermute | solution.py:1192
  295.3 14.9 %collective-permute-start.28 = (bf16[192,768]{1,0:T(8,128)(2,1)}, bf16[192,768]{1,0:T(8,128)(2,1)S(1)}, u32[]{:S(2)}, u32[]{:S(2)}) collective-permute-start(bf16[192,768]{1,0:T(8,128)(2,1)} %get-tuple-element.387), channel_id=1, source_target_pairs={{0,24},{8,0},{16,8},{24,16},{1,25},{9,1},{17,9},{25,17},{2,26},{10... | collective-permute-start | bytes 884744 | tf_op jit(solution)/shard_map/ppermute | solution.py:1192
  297.2 36.1 %all-to-all-start.1 = ((bf16[1,4,24,6912]{3,2,0,1:T(8,128)(2,1)}), bf16[1,4,24,6912]{3,2,0,1:T(8,128)(2,1)S(1)}, u32[]{:S(2)}, u32[]{:S(2)}) async-start(bf16[1,4,24,6912]{3,2,0,1:T(8,128)(2,1)} %pad_maximum_fusion.7), calls=%async_computation.1 | async-start | bytes 2654208 | tf_op jit(solution)/shard_map/all_to_all | solution.py:958
  310.2 13.1 %collective-permute-start.29 = (bf16[10,2,4,24,128]{4,3,0,2,1:T(8,128)(2,1)S(1)}, bf16[10,2,4,24,128]{4,3,0,2,1:T(8,128)(2,1)S(1)}, u32[]{:S(2)}, u32[]{:S(2)}) collective-permute-start(bf16[10,2,4,24,128]{4,3,0,2,1:T(8,128)(2,1)S(1)} %pad_maximum_fusion.9), channel_id=1, source_target_pairs={{0,8},{8,0},{1,9},{9,1},{2,10},{10,2},{3,11},{11,3},{4,12},{12,4},... | collective-permute-start | bytes 1474568 | tf_op jit(solution)/shard_map/ppermute | solution.py:935
  311.3 12.1 %collective-permute-start.30 = (bf16[10,2,4,24,128]{4,3,0,2,1:T(8,128)(2,1)S(1)}, bf16[10,2,4,24,128]{4,3,0,2,1:T(8,128)(2,1)S(1)}, u32[]{:S(2)}, u32[]{:S(2)}) collective-permute-start(bf16[10,2,4,24,128]{4,3,0,2,1:T(8,128)(2,1)S(1)} %pad_maximum_fusion.10), channel_id=1, source_target_pairs={{0,16},{16,0},{1,17},{17,1},{2,18},{18,2},{3,19},{19,3},{4,20},{20... | collective-permute-start | bytes 1474568 | tf_op jit(solution)/shard_map/ppermute | solution.py:935
  312.8 13.2 %copy-start.31 = (s32[1,1024]{1,0:T(1,128)S(1)}, s32[1,1024]{1,0:T(1,128)}, u32[]{:S(2)}) copy-start(s32[1,1024]{1,0:T(1,128)} %param.18) | copy-start | bytes 12292
  323.7 9.6 %collective-permute-start.31 = (bf16[10,4,24,128]{3,2,0,1:T(8,128)(2,1)S(1)}, bf16[10,4,24,128]{3,2,0,1:T(8,128)(2,1)S(1)}, u32[]{:S(2)}, u32[]{:S(2)}) collective-permute-start(bf16[10,4,24,128]{3,2,0,1:T(8,128)(2,1)S(1)} %get-tuple-element.351), channel_id=1, source_target_pairs={{0,16},{16,0},{1,17},{17,1},{2,18},{18,2},{3,19},{19,3},{4,20},{20... | collective-permute-start | bytes 737288 | tf_op jit(solution)/shard_map/ppermute | solution.py:935
  324.6 8.7 %collective-permute-start.32 = (bf16[10,4,24,128]{3,2,0,1:T(8,128)(2,1)S(1)}, bf16[10,4,24,128]{3,2,0,1:T(8,128)(2,1)S(1)}, u32[]{:S(2)}, u32[]{:S(2)}) collective-permute-start(bf16[10,4,24,128]{3,2,0,1:T(8,128)(2,1)S(1)} %get-tuple-element.352), channel_id=1, source_target_pairs={{0,8},{8,0},{1,9},{9,1},{2,10},{10,2},{3,11},{11,3},{4,12},{12,4},... | collective-permute-start | bytes 737288 | tf_op jit(solution)/shard_map/ppermute | solution.py:935
  334.5 14.0 %copy-start.1 = (f32[12,32]{1,0:T(8,128)S(1)}, f32[12,32]{1,0:T(8,128)}, u32[]{:S(2)}) copy-start(f32[12,32]{1,0:T(8,128)} %param.27) | copy-start | bytes 4612
  334.7 8.2 %collective-permute-start.33 = (bf16[20,24,128]{2,1,0:T(8,128)(2,1)S(1)}, bf16[20,24,128]{2,1,0:T(8,128)(2,1)S(1)}, u32[]{:S(2)}, u32[]{:S(2)}) collective-permute-start(bf16[20,24,128]{2,1,0:T(8,128)(2,1)S(1)} %pad_maximum_fusion.12), channel_id=1, source_target_pairs={{0,2},{2,4},{4,6},{6,0},{1,3},{3,5},{5,7},{7,1},{8,10},{10,12},{12... | collective-permute-start | bytes 368648 | tf_op jit(solution)/shard_map/ppermute | solution.py:935
  337.5 8.9 %collective-permute-start.34 = (bf16[20,24,128]{2,1,0:T(8,128)(2,1)S(1)}, bf16[20,24,128]{2,1,0:T(8,128)(2,1)S(1)}, u32[]{:S(2)}, u32[]{:S(2)}) collective-permute-start(bf16[20,24,128]{2,1,0:T(8,128)(2,1)S(1)} %pad_maximum_fusion.13), channel_id=1, source_target_pairs={{0,4},{2,6},{4,0},{6,2},{1,5},{3,7},{5,1},{7,3},{8,12},{10,14},{12... | collective-permute-start | bytes 368648 | tf_op jit(solution)/shard_map/ppermute | solution.py:935
  337.5 8.9 %collective-permute-start.35 = (bf16[20,24,128]{2,1,0:T(8,128)(2,1)S(1)}, bf16[20,24,128]{2,1,0:T(8,128)(2,1)S(1)}, u32[]{:S(2)}, u32[]{:S(2)}) collective-permute-start(bf16[20,24,128]{2,1,0:T(8,128)(2,1)S(1)} %pad_maximum_fusion.14), channel_id=1, source_target_pairs={{0,6},{2,0},{4,2},{6,4},{1,7},{3,1},{5,3},{7,5},{8,14},{10,8},{12,... | collective-permute-start | bytes 368648 | tf_op jit(solution)/shard_map/ppermute | solution.py:935
  340.0 7.9 %copy-start.41 = (f32[1,64,768]{2,1,0:T(8,128)}, f32[1,64,768]{2,1,0:T(8,128)S(1)}, u32[]{:S(2)}) copy-start(f32[1,64,768]{2,1,0:T(8,128)S(1)} %constant_dynamic-update-slice_fusion.18) | copy-start | bytes 589828
  (51 other events, 121.1 us)
